TPU v7x, 32 devices: a whole 2x2x4 slice. The times are simulated.
32 devices in a mesh: dp: 16 (over z, y, x), seq: 2 (over core).
Axes of the slice: x: 2, y: 2, z: 4, core: 2. Of those that a mesh axis runs over, the one named last changes fastest.
Arguments:
- layer_input: bfloat16 [2, 16, 1024, 1152], P(None, 'dp', 'seq'), may hold values from -6 to 6
- w_query: bfloat16 [1152, 1152], P('dp', 'seq'), may hold values from -0.1875 to 0.1875
- w_key: bfloat16 [1152, 384], P('dp', 'seq'), may hold values from -0.1875 to 0.1875
- w_value: bfloat16 [1152, 384], P('dp', 'seq'), may hold values from -0.1875 to 0.1875
- w_out: bfloat16 [1152, 1152], P('dp', 'seq'), may hold values from -1.5 to 1.5
- gain_attn: bfloat16 [1152], P('dp'), may hold values from 0.099609375 to 1.8984375
- w_gate: bfloat16 [1152, 3072], P('dp', 'seq'), may hold values from -0.1875 to 0.1875
- w_up: bfloat16 [1152, 3072], P('dp', 'seq'), may hold values from -0.1875 to 0.1875
- w_down: bfloat16 [3072, 1152], P('dp', 'seq'), may hold values from -0.109375 to 0.109375
- gain_mlp: bfloat16 [1152], P('dp'), may hold values from 0.099609375 to 1.8984375
- cotangent: bfloat16 [2, 16, 1024, 1152], P(None, 'dp', 'seq'), may hold values from -6 to 6
Outputs:
- output: bfloat16 [2, 16, 1024, 1152], P(None, 'dp', 'seq')
- grad_input: bfloat16 [2, 16, 1024, 1152], P(None, 'dp', 'seq')
- grad_query: float32 [1152, 1152], P('dp', 'seq')
- grad_key: float32 [1152, 384], P('dp', 'seq')
- grad_value: float32 [1152, 384], P('dp', 'seq')
- grad_out: float32 [1152, 1152], P('dp', 'seq')
- grad_gain_attn: float32 [1152], P('dp')
- grad_gate: float32 [1152, 3072], P('dp', 'seq')
- grad_up: float32 [1152, 3072], P('dp', 'seq')
- grad_down: float32 [3072, 1152], P('dp', 'seq')
- grad_gain_mlp: float32 [1152], P('dp')
All inputs are finite; a program needn't handle non-finite values.
Results may differ from a plain program's by a relative error of at most 0.018.
Values may be sent and summed in bfloat16 or wider, within the bound.
A program may use at most 256 MiB of HBM per device.

v0:
```python
import jax
import jax.numpy as jnp
from jax import lax
from jax.sharding import PartitionSpec as P

D = 1152
QUERY_HEADS = 18
KEY_VALUE_HEADS = 6
HEAD_SIZE = 64
FF = 3072
BLOCK = 256
QD = 1152
KVD = 384


epsilon = 1e-05


def rope_tables(position_shift, count_rows):
    half_dim = HEAD_SIZE // 2
    places = (position_shift + jnp.arange(count_rows)).astype(jnp.float32)
    frequency = 10000.0 ** (-2.0 * jnp.arange(half_dim).astype(jnp.float32) / HEAD_SIZE)
    angles = places[:, None] * frequency[None, :]
    return (jnp.cos(angles)[:, None, :], jnp.sin(angles)[:, None, :])


def apply_rotary(values_in, position_shift, head_count, inverse):
    count_rows = values_in.shape[0]
    half_dim = HEAD_SIZE // 2
    cosine, sine_part = rope_tables(position_shift, count_rows)
    if inverse:
        sine_part = -sine_part
    split_heads = values_in.reshape(count_rows, head_count, HEAD_SIZE)
    first_half = split_heads[..., :half_dim]
    second = split_heads[..., half_dim:]
    turned = jnp.concatenate(
        [first_half * cosine - second * sine_part, second * cosine + first_half * sine_part],
        axis=-1,
    )
    return turned.reshape(count_rows, head_count * HEAD_SIZE)


def norm_back(grad_norm, rows_in, scale_rows, gain_rows):
    weighted = grad_norm * gain_rows
    cube_rows = scale_rows * scale_rows * scale_rows
    return scale_rows * weighted - rows_in * cube_rows * jnp.mean(
        weighted * rows_in, -1, keepdims=True
    )


def fetch_attention(w_query, w_key, w_value, w_out, gain_attn):
    columns = (
        lax.all_gather(w_query, "seq", axis=1, tiled=True),
        lax.all_gather(w_key, "seq", axis=1, tiled=True),
        lax.all_gather(w_value, "seq", axis=1, tiled=True),
        lax.all_gather(w_out, "seq", axis=1, tiled=True),
    )
    return (
        lax.all_gather(columns[0], "dp", axis=0, tiled=True),
        lax.all_gather(columns[1], "dp", axis=0, tiled=True),
        lax.all_gather(columns[2], "dp", axis=0, tiled=True),
        lax.all_gather(columns[3], "dp", axis=0, tiled=True),
        lax.all_gather(gain_attn, "dp", axis=0, tiled=True),
    )


def fetch_mlp(w_gate, w_up, w_down, gain_mlp):
    columns = (
        lax.all_gather(w_gate, "seq", axis=1, tiled=True),
        lax.all_gather(w_up, "seq", axis=1, tiled=True),
        lax.all_gather(w_down, "seq", axis=1, tiled=True),
    )
    return (
        lax.all_gather(columns[0], "dp", axis=0, tiled=True),
        lax.all_gather(columns[1], "dp", axis=0, tiled=True),
        lax.all_gather(columns[2], "dp", axis=0, tiled=True),
        lax.all_gather(gain_mlp, "dp", axis=0, tiled=True),
    )


def masked_scores(query_part, key_part, allowed):
    logits = (
        jnp.einsum("tjh,kh->jtk", query_part, key_part, preferred_element_type=jnp.float32) * 0.125
    )
    return jnp.where(allowed[None], logits, -jnp.inf)


def attend_forward(query_head_rows, key_head_rows, value_head_rows, allowed):

    def per_head(head_parts):
        query_part, key_part, value_part = head_parts
        scores = masked_scores(query_part, key_part, allowed)
        highest = jnp.max(scores, -1, keepdims=True)
        powers = jnp.exp(scores - highest)
        summed = jnp.sum(powers, -1, keepdims=True)
        prob_low = (powers / summed).astype(jnp.bfloat16)
        mixed_out = jnp.einsum(
            "jtk,kh->tjh", prob_low, value_part, preferred_element_type=jnp.float32
        )
        return (mixed_out, highest + jnp.log(summed))

    return lax.map(per_head, (query_head_rows, key_head_rows, value_head_rows))


def attend_back(query_head_rows, key_head_rows, value_head_rows, grad_heads, log_total, allowed):

    def per_head(head_parts):
        query_part, key_part, value_part, grad_part, log_part = head_parts
        scores = masked_scores(query_part, key_part, allowed)
        attn_prob = jnp.exp(scores - log_part)
        grad_prob = jnp.einsum(
            "tjh,kh->jtk", grad_part, value_part, preferred_element_type=jnp.float32
        )
        inner_sum = jnp.sum(attn_prob * grad_prob, -1, keepdims=True)
        grad_score = (attn_prob * (grad_prob - inner_sum)).astype(jnp.bfloat16)
        grad_query_rot = (
            jnp.einsum("jtk,kh->tjh", grad_score, key_part, preferred_element_type=jnp.float32)
            * 0.125
        )
        grad_keys_rot = (
            jnp.einsum("jtk,tjh->kh", grad_score, query_part, preferred_element_type=jnp.float32)
            * 0.125
        )
        grad_values = jnp.einsum(
            "jtk,tjh->kh",
            attn_prob.astype(jnp.bfloat16),
            grad_part,
            preferred_element_type=jnp.float32,
        )
        return (grad_query_rot, grad_keys_rot, grad_values)

    return lax.map(
        per_head, (query_head_rows, key_head_rows, value_head_rows, grad_heads, log_total)
    )


def flatten_rows(matrices):
    return tuple((matrix.reshape(-1) for matrix in matrices))


def restore_rows(pieces, widths):
    return tuple((piece.reshape(-1, width) for piece, width in zip(pieces, widths)))


def local(
    layer_input,
    w_query,
    w_key,
    w_value,
    w_out,
    gain_attn,
    w_gate,
    w_up,
    w_down,
    gain_mlp,
    cotangent,
):
    piece_length = layer_input.shape[2]
    query_group_width = QUERY_HEADS // KEY_VALUE_HEADS
    position_shift = lax.axis_index("seq") * piece_length
    places = position_shift + jnp.arange(piece_length)
    key_blocks = jnp.arange(piece_length * lax.axis_size("seq")) // BLOCK
    allowed = key_blocks[None, :] <= (places // BLOCK)[:, None]

    def fetch_all():
        return (
            fetch_attention(w_query, w_key, w_value, w_out, gain_attn),
            fetch_mlp(w_gate, w_up, w_down, gain_mlp),
        )

    def micro_step(grad_sums, inputs_pair):
        rows_in, cot_in = inputs_pair
        attn_set, mlp_set = fetch_all()
        full_query, complete_key_weight, full_value, full_out, full_gain_attn = attn_set
        full_gate, full_up, full_down, full_gain_mlp = mlp_set
        gain_one = full_gain_attn.astype(jnp.float32)
        gain_two = full_gain_mlp.astype(jnp.float32)
        floats = rows_in.astype(jnp.float32)
        scale_attn = lax.rsqrt(jnp.mean(floats * floats, -1, keepdims=True) + epsilon)
        normalized_attention_input = (floats * scale_attn * gain_one).astype(jnp.bfloat16)
        query_rotated = apply_rotary(
            jnp.dot(normalized_attention_input, full_query, preferred_element_type=jnp.float32),
            position_shift,
            QUERY_HEADS,
            False,
        ).astype(jnp.bfloat16)
        keys_rotated = apply_rotary(
            jnp.dot(
                normalized_attention_input, complete_key_weight, preferred_element_type=jnp.float32
            ),
            position_shift,
            KEY_VALUE_HEADS,
            False,
        ).astype(jnp.bfloat16)
        values_lower_precision = jnp.dot(
            normalized_attention_input, full_value, preferred_element_type=jnp.float32
        ).astype(jnp.bfloat16)
        keys_gathered_total, values_gathered_total = (
            lax.all_gather(keys_rotated, "seq", axis=0, tiled=True),
            lax.all_gather(values_lower_precision, "seq", axis=0, tiled=True),
        )
        query_head_rows = jnp.transpose(
            query_rotated.reshape(piece_length, KEY_VALUE_HEADS, query_group_width, HEAD_SIZE),
            (1, 0, 2, 3),
        )
        key_head_rows = jnp.transpose(
            keys_gathered_total.reshape(-1, KEY_VALUE_HEADS, HEAD_SIZE), (1, 0, 2)
        )
        value_head_rows = jnp.transpose(
            values_gathered_total.reshape(-1, KEY_VALUE_HEADS, HEAD_SIZE), (1, 0, 2)
        )
        mixed_out, log_total = attend_forward(
            query_head_rows, key_head_rows, value_head_rows, allowed
        )
        merged = (
            jnp.transpose(mixed_out, (1, 0, 2, 3)).reshape(piece_length, QD).astype(jnp.bfloat16)
        )
        residual = floats + jnp.dot(merged, full_out, preferred_element_type=jnp.float32)
        scale_mlp = lax.rsqrt(jnp.mean(residual * residual, -1, keepdims=True) + epsilon)
        normed_mlp = (residual * scale_mlp * gain_two).astype(jnp.bfloat16)
        gate_val = jnp.dot(normed_mlp, full_gate, preferred_element_type=jnp.float32)
        up_val = jnp.dot(normed_mlp, full_up, preferred_element_type=jnp.float32)
        sig_gate = jax.nn.sigmoid(gate_val)
        gate_act = gate_val * sig_gate
        hidden = (gate_act * up_val).astype(jnp.bfloat16)
        layer_out = (
            residual + jnp.dot(hidden, full_down, preferred_element_type=jnp.float32)
        ).astype(jnp.bfloat16)
        attn_again, mlp_again = fetch_all()
        full_query, complete_key_weight, full_value, full_out, full_gain_attn = attn_again
        full_gate, full_up, full_down, full_gain_mlp = mlp_again
        gain_one = full_gain_attn.astype(jnp.float32)
        gain_two = full_gain_mlp.astype(jnp.float32)
        grad_down = jnp.einsum("tf,td->fd", hidden, cot_in, preferred_element_type=jnp.float32)
        grad_hidden = jnp.einsum("td,fd->tf", cot_in, full_down, preferred_element_type=jnp.float32)
        grad_gate_val = (
            grad_hidden * up_val * sig_gate * (1.0 + gate_val * (1.0 - sig_gate))
        ).astype(jnp.bfloat16)
        grad_up_val = (grad_hidden * gate_act).astype(jnp.bfloat16)
        grad_gate = jnp.einsum(
            "td,tf->df", normed_mlp, grad_gate_val, preferred_element_type=jnp.float32
        )
        grad_up = jnp.einsum(
            "td,tf->df", normed_mlp, grad_up_val, preferred_element_type=jnp.float32
        )
        grad_normed_mlp = jnp.einsum(
            "tf,df->td", grad_gate_val, full_gate, preferred_element_type=jnp.float32
        ) + jnp.einsum("tf,df->td", grad_up_val, full_up, preferred_element_type=jnp.float32)
        grad_gain_mlp = jnp.sum(grad_normed_mlp * residual * scale_mlp, 0)
        grad_residual = cot_in.astype(jnp.float32) + norm_back(
            grad_normed_mlp, residual, scale_mlp, gain_two
        )
        grad_res_low = grad_residual.astype(jnp.bfloat16)
        grad_out = jnp.einsum("tq,td->qd", merged, grad_res_low, preferred_element_type=jnp.float32)
        grad_joined_heads = jnp.einsum(
            "td,qd->tq", grad_res_low, full_out, preferred_element_type=jnp.float32
        ).astype(jnp.bfloat16)
        grad_heads = jnp.transpose(
            grad_joined_heads.reshape(piece_length, KEY_VALUE_HEADS, query_group_width, HEAD_SIZE),
            (1, 0, 2, 3),
        )
        grad_query_rot, grad_keys_rot, grad_values = attend_back(
            query_head_rows, key_head_rows, value_head_rows, grad_heads, log_total, allowed
        )
        grad_query_flat = jnp.transpose(grad_query_rot, (1, 0, 2, 3)).reshape(piece_length, QD)
        grad_keys_flat = jnp.transpose(grad_keys_rot, (1, 0, 2)).reshape(-1, KVD)
        grad_values_flat = jnp.transpose(grad_values, (1, 0, 2)).reshape(-1, KVD)
        keys_local_part, values_own = (
            lax.psum_scatter(
                grad_keys_flat.astype(jnp.bfloat16), "seq", scatter_dimension=0, tiled=True
            ).astype(jnp.float32),
            lax.psum_scatter(
                grad_values_flat.astype(jnp.bfloat16), "seq", scatter_dimension=0, tiled=True
            ).astype(jnp.float32),
        )
        grad_query_lin = apply_rotary(grad_query_flat, position_shift, QUERY_HEADS, True).astype(
            jnp.bfloat16
        )
        grad_keys_linear = apply_rotary(
            keys_local_part, position_shift, KEY_VALUE_HEADS, True
        ).astype(jnp.bfloat16)
        grad_values_low = values_own.astype(jnp.bfloat16)
        grad_query = jnp.einsum(
            "td,tq->dq",
            normalized_attention_input,
            grad_query_lin,
            preferred_element_type=jnp.float32,
        )
        grad_key = jnp.einsum(
            "td,tq->dq",
            normalized_attention_input,
            grad_keys_linear,
            preferred_element_type=jnp.float32,
        )
        grad_value = jnp.einsum(
            "td,tq->dq",
            normalized_attention_input,
            grad_values_low,
            preferred_element_type=jnp.float32,
        )
        grad_normed_attn = jnp.einsum(
            "tq,dq->td", grad_query_lin, full_query, preferred_element_type=jnp.float32
        )
        grad_normed_attn = grad_normed_attn + jnp.einsum(
            "tq,dq->td", grad_keys_linear, complete_key_weight, preferred_element_type=jnp.float32
        )
        grad_normed_attn = grad_normed_attn + jnp.einsum(
            "tq,dq->td", grad_values_low, full_value, preferred_element_type=jnp.float32
        )
        grad_gain_attn = jnp.sum(grad_normed_attn * floats * scale_attn, 0)
        grad_input = (
            grad_residual + norm_back(grad_normed_attn, floats, scale_attn, gain_one)
        ).astype(jnp.bfloat16)
        grad_terms = (
            grad_query,
            grad_key,
            grad_value,
            grad_out,
            grad_gain_attn,
            grad_gate,
            grad_up,
            grad_down,
            grad_gain_mlp,
        )
        new_sums = tuple((earlier + added for earlier, added in zip(grad_sums, grad_terms)))
        return (new_sums, (layer_out, grad_input))

    start_sums = (
        jnp.zeros((D, QD), jnp.float32),
        jnp.zeros((D, KVD), jnp.float32),
        jnp.zeros((D, KVD), jnp.float32),
        jnp.zeros((QD, D), jnp.float32),
        jnp.zeros((D,), jnp.float32),
        jnp.zeros((D, FF), jnp.float32),
        jnp.zeros((D, FF), jnp.float32),
        jnp.zeros((FF, D), jnp.float32),
        jnp.zeros((D,), jnp.float32),
    )
    grad_sums, (outputs, grad_inputs) = lax.scan(
        micro_step, start_sums, (layer_input[:, 0], cotangent[:, 0])
    )
    (
        sum_query,
        sum_key,
        sum_value,
        sum_out,
        sum_gain_attn,
        sum_gate,
        sum_up,
        sum_down,
        sum_gain_mlp,
    ) = grad_sums
    matrices = (sum_query, sum_key, sum_value, sum_out, sum_gate, sum_up, sum_down)
    widths = tuple((matrix.shape[1] for matrix in matrices))
    flat_mats = flatten_rows(matrices)
    reduced = (
        lax.psum_scatter(flat_mats[0], "dp", scatter_dimension=0, tiled=True),
        lax.psum_scatter(flat_mats[1], "dp", scatter_dimension=0, tiled=True),
        lax.psum_scatter(flat_mats[2], "dp", scatter_dimension=0, tiled=True),
        lax.psum_scatter(flat_mats[3], "dp", scatter_dimension=0, tiled=True),
        lax.psum_scatter(flat_mats[4], "dp", scatter_dimension=0, tiled=True),
        lax.psum_scatter(flat_mats[5], "dp", scatter_dimension=0, tiled=True),
        lax.psum_scatter(flat_mats[6], "dp", scatter_dimension=0, tiled=True),
        lax.psum_scatter(sum_gain_attn, "dp", scatter_dimension=0, tiled=True),
        lax.psum_scatter(sum_gain_mlp, "dp", scatter_dimension=0, tiled=True),
    )
    row_parts = restore_rows(reduced[:7], widths)
    final_mats = (
        lax.psum_scatter(
            row_parts[0].astype(jnp.bfloat16), "seq", scatter_dimension=1, tiled=True
        ).astype(jnp.float32),
        lax.psum_scatter(
            row_parts[1].astype(jnp.bfloat16), "seq", scatter_dimension=1, tiled=True
        ).astype(jnp.float32),
        lax.psum_scatter(
            row_parts[2].astype(jnp.bfloat16), "seq", scatter_dimension=1, tiled=True
        ).astype(jnp.float32),
        lax.psum_scatter(
            row_parts[3].astype(jnp.bfloat16), "seq", scatter_dimension=1, tiled=True
        ).astype(jnp.float32),
        lax.psum_scatter(
            row_parts[4].astype(jnp.bfloat16), "seq", scatter_dimension=1, tiled=True
        ).astype(jnp.float32),
        lax.psum_scatter(
            row_parts[5].astype(jnp.bfloat16), "seq", scatter_dimension=1, tiled=True
        ).astype(jnp.float32),
        lax.psum_scatter(
            row_parts[6].astype(jnp.bfloat16), "seq", scatter_dimension=1, tiled=True
        ).astype(jnp.float32),
    )
    gain_parts = (reduced[7], reduced[8])
    gains_done = lax.psum((gain_parts[0], gain_parts[1]), "seq")
    return (
        outputs[:, None],
        grad_inputs[:, None],
        final_mats[0],
        final_mats[1],
        final_mats[2],
        final_mats[3],
        gains_done[0],
        final_mats[4],
        final_mats[5],
        final_mats[6],
        gains_done[1],
    )


def solution(mesh):
    placed = (
        P(None, "dp", "seq", None),
        P("dp", "seq"),
        P("dp", "seq"),
        P("dp", "seq"),
        P("dp", "seq"),
        P("dp"),
        P("dp", "seq"),
        P("dp", "seq"),
        P("dp", "seq"),
        P("dp"),
        P(None, "dp", "seq", None),
    )
    return jax.shard_map(
        local,
        mesh=mesh,
        in_specs=placed,
        out_specs=(
            P(None, "dp", "seq", None),
            P(None, "dp", "seq", None),
            P("dp", "seq"),
            P("dp", "seq"),
            P("dp", "seq"),
            P("dp", "seq"),
            P("dp"),
            P("dp", "seq"),
            P("dp", "seq"),
            P("dp", "seq"),
            P("dp"),
        ),
        check_vma=False,
    )
```

profile of v0, /device:TPU:0, one launch (start us, length us, event | category | flops | bytes accessed | tf_op | source)
XLA Modules:
  0.0 3833.3 jit_solution(704685637766157771)
XLA Ops:
  8.2 1292.5 %while.95 = (s32[]{:T(128)}, f32[1152,1152]{1,0:T(8,128)}, f32[1152,384]{1,0:T(8,128)}, f32[1152,384]{1,0:T(8,128)}, f32[1152,1152]{1,0:T(8,128)}, /*index=5*/f3...) while((s32[]{:T(128)}, f32[1152,1152]{1,0:T(8,128)}, ...), condition=%wide.region_16.17_spmd.clone.clone, body=%wide.region_0.16_spmd.clone.sunk.clone | while | flops 45045784576 | bytes 843582016 | solution.py:339
  27.8 44.8 %all-reduce.18 = (bf16[1152]{0:T(1024)(128)(2,1)S(1)}, bf16[1152]{0:T(1024)(128)(2,1)S(1)}) all-reduce(bf16[1152]{0:T(1024)(128)(2,1)S(1)} %dynamic-update-slice.8, bf16[1152]{0:T(1024)(128)(2,1)S(1)} %dynamic-update-slice.9), channel_id=1, replica_groups=mesh['dp'=16,'seq'=2] {'dp'}, use_global_device_ids=true, to_apply=%add | all-reduce | flops 2304 | bytes 9216 | tf_op jit(solution)/shard_map/while
  74.7 42.3 %all_gather.157 = bf16[1152,384]{1,0:T(8,128)(2,1)S(1)} all-gather(bf16[72,384]{1,0:T(8,128)(2,1)S(1)} %bitcast.590), channel_id=1, replica_groups=mesh['dp'=16,'seq'=2] {'dp'}, dimensions={0}, use_global_device_ids=true | all-gather | bytes 940032 | tf_op jit(solution)/shard_map/while/body/eval_jaxpr/all_gather | solution.py:60
  126.1 50.3 %all_gather.160 = bf16[1152,384]{1,0:T(8,128)(2,1)S(1)} all-gather(bf16[72,384]{1,0:T(8,128)(2,1)S(1)} %bitcast.591), channel_id=1, replica_groups=mesh['dp'=16,'seq'=2] {'dp'}, dimensions={0}, use_global_device_ids=true | all-gather | bytes 940032 | tf_op jit(solution)/shard_map/while/body/eval_jaxpr/all_gather | solution.py:61
  182.6 5.2 copy.102
  187.8 3.9 fusion.338
  193.2 44.1 %while.93 = (s32[]{:T(128)}, bf16[6,512,3,64]{1,3,2,0:T(8,128)(2,1)}, f32[6,3,512,1]{2,1,3,0:T(4,128)S(1)}, bf16[6,1024,64]{1,2,0:T(8,128)(2,1)}, pred[512,1024]...) while((s32[]{:T(128)}, ...), condition=%wide.region_5.5_spmd, body=%wide.region_2.4_spmd.sunk | while | flops 421526016 | bytes 21356632 | solution.py:102
  197.0 3.6 fusion.278
  204.4 3.6 fusion.278
  233.7 3.6 fusion.278
  237.3 4.2 multiply_reduce_fusion.7
  243.3 17.3 all-gather.37.cloned.1.call-done
  260.6 10.2 fusion.340
  270.8 91.4 %all-gather.35.cloned.1.call-done = bf16[1152,3072]{1,0:T(8,128)(2,1)} async-done(((bf16[72,3072]{1,0:T(8,128)(2,1)}), bf16[1152,3072]{1,0:T(8,128)(2,1)}) %all-gather.35.cloned.1.call-update) | async-done | bytes 7077904 | tf_op jit(solution)/shard_map/while/body/eval_jaxpr/all_gather | solution.py:74
  362.3 9.3 fusion.339
  371.5 92.4 %all-gather.39.cloned.1.call-done = bf16[1152,3072]{1,0:T(8,128)(2,1)} async-done(((bf16[72,3072]{1,0:T(8,128)(2,1)}), bf16[1152,3072]{1,0:T(8,128)(2,1)}) %all-gather.39.cloned.1.call-update) | async-done | bytes 7077904 | tf_op jit(solution)/shard_map/while/body/eval_jaxpr/all_gather | solution.py:75
  463.9 12.4 multiply_convert_fusion.9
  476.4 4.3 fusion.341
  480.7 8.5 multiply_reduce_fusion.8
  495.7 89.2 %while.94 = (s32[]{:T(128)}, f32[6,512,3,64]{1,3,2,0:T(8,128)}, bf16[6,1024,64]{1,2,0:T(8,128)(2,1)}, bf16[6,1024,64]{1,2,0:T(8,128)(2,1)}, bf16[6,1024,64]{1,2,...) while((s32[]{:T(128)}, f32[6,512,3,64]{1,3,2,0:T(8,128)}, ...), condition=%wide.region_10.10_spmd, body=%wide.region_8.9_spmd.sunk | while | flops 1030388224 | bytes 57199784 | solution.py:132
  585.1 9.8 select_add_fusion.16
  597.1 7.2 select_add_fusion.17
  604.3 4.6 convolution_add_fusion.19
  609.0 7.6 select_add_fusion.18
  616.7 4.3 fusion.344
  625.1 5.4 convolution_add_fusion.22
  664.4 40.6 %all-reduce.18 = (bf16[1152]{0:T(1024)(128)(2,1)S(1)}, bf16[1152]{0:T(1024)(128)(2,1)S(1)}) all-reduce(bf16[1152]{0:T(1024)(128)(2,1)S(1)} %dynamic-update-slice.8, bf16[1152]{0:T(1024)(128)(2,1)S(1)} %dynamic-update-slice.9), channel_id=1, replica_groups=mesh['dp'=16,'seq'=2] {'dp'}, use_global_device_ids=true, to_apply=%add | all-reduce | flops 2304 | bytes 9216 | tf_op jit(solution)/shard_map/while
  707.0 42.0 %all_gather.157 = bf16[1152,384]{1,0:T(8,128)(2,1)S(1)} all-gather(bf16[72,384]{1,0:T(8,128)(2,1)S(1)} %bitcast.590), channel_id=1, replica_groups=mesh['dp'=16,'seq'=2] {'dp'}, dimensions={0}, use_global_device_ids=true | all-gather | bytes 940032 | tf_op jit(solution)/shard_map/while/body/eval_jaxpr/all_gather | solution.py:60
  758.2 48.5 %all_gather.160 = bf16[1152,384]{1,0:T(8,128)(2,1)S(1)} all-gather(bf16[72,384]{1,0:T(8,128)(2,1)S(1)} %bitcast.591), channel_id=1, replica_groups=mesh['dp'=16,'seq'=2] {'dp'}, dimensions={0}, use_global_device_ids=true | all-gather | bytes 940032 | tf_op jit(solution)/shard_map/while/body/eval_jaxpr/all_gather | solution.py:61
  812.8 5.2 copy.102
  823.1 44.0 %while.93 = (s32[]{:T(128)}, bf16[6,512,3,64]{1,3,2,0:T(8,128)(2,1)}, f32[6,3,512,1]{2,1,3,0:T(4,128)S(1)}, bf16[6,1024,64]{1,2,0:T(8,128)(2,1)}, pred[512,1024]...) while((s32[]{:T(128)}, ...), condition=%wide.region_5.5_spmd, body=%wide.region_2.4_spmd.sunk | while | flops 421526016 | bytes 21356632 | solution.py:102
  826.8 3.6 fusion.278
  834.1 3.6 fusion.278
  848.8 3.7 fusion.278
  863.5 3.6 fusion.278
  867.1 4.2 multiply_reduce_fusion.7
  873.1 19.1 all-gather.37.cloned.1.call-done
  892.2 10.2 fusion.340
  902.4 91.6 %all-gather.35.cloned.1.call-done = bf16[1152,3072]{1,0:T(8,128)(2,1)} async-done(((bf16[72,3072]{1,0:T(8,128)(2,1)}), bf16[1152,3072]{1,0:T(8,128)(2,1)}) %all-gather.35.cloned.1.call-update) | async-done | bytes 7077904 | tf_op jit(solution)/shard_map/while/body/eval_jaxpr/all_gather | solution.py:74
  994.0 9.3 fusion.339
  1003.3 92.4 %all-gather.39.cloned.1.call-done = bf16[1152,3072]{1,0:T(8,128)(2,1)} async-done(((bf16[72,3072]{1,0:T(8,128)(2,1)}), bf16[1152,3072]{1,0:T(8,128)(2,1)}) %all-gather.39.cloned.1.call-update) | async-done | bytes 7077904 | tf_op jit(solution)/shard_map/while/body/eval_jaxpr/all_gather | solution.py:75
  1095.6 12.4 multiply_convert_fusion.9
  1108.1 4.3 fusion.341
  1112.4 8.5 multiply_reduce_fusion.8
  1127.5 89.2 %while.94 = (s32[]{:T(128)}, f32[6,512,3,64]{1,3,2,0:T(8,128)}, bf16[6,1024,64]{1,2,0:T(8,128)(2,1)}, bf16[6,1024,64]{1,2,0:T(8,128)(2,1)}, bf16[6,1024,64]{1,2,...) while((s32[]{:T(128)}, f32[6,512,3,64]{1,3,2,0:T(8,128)}, ...), condition=%wide.region_10.10_spmd, body=%wide.region_8.9_spmd.sunk | while | flops 1030388224 | bytes 57199784 | solution.py:132
  1216.8 14.7 select_add_fusion.16
  1233.8 10.3 select_add_fusion.17
  1244.1 7.0 convolution_add_fusion.19
  1251.2 11.0 select_add_fusion.18
  1262.3 4.3 fusion.344
  1270.7 6.9 convolution_add_fusion.22
  1300.8 15.3 reshape.418
  1316.0 13.4 copy.79
  1329.5 13.4 copy.80
  1342.9 6.6 reshape.412
  1349.5 6.7 reshape.415
  1361.5 2359.0 %all-reduce.20 = (bf16[1327104]{0:T(1024)(128)(2,1)}, bf16[442368]{0:T(1024)(128)(2,1)S(1)}, bf16[442368]{0:T(1024)(128)(2,1)S(1)}, bf16[1327104]{0:T(1024)(128)...) all-reduce(f32[1327104]{0:T(1024)} %reshape.412, ...), channel_id=4, replica_groups=mesh['dp'=16,'seq'=2] {'dp'}, use_global_device_ids=true, to_apply=%region_17.18.clone | all-reduce | flops 14158080 | bytes 84953088
  3740.2 15.3 reduce-scatter.26.cloned.1.call-done
  3757.0 9.7 reduce-scatter.28.cloned.1.call-done
  3768.3 10.0 reduce-scatter.24.cloned.1.call-done
  3780.0 9.9 reduce-scatter.30.cloned.1.call-done
  3791.7 9.6 reduce-scatter.32.cloned.1.call-done
  3803.2 9.9 reduce-scatter.20.cloned.1.call-done
  3814.8 9.3 reduce-scatter.22.cloned.1.call-done
  (672 shorter events, 410.0 us)
Async XLA Ops:
  8.6 173.6 %copy-start.57 = (s32[1024]{0:T(1024)}, s32[1024]{0:T(1024)S(1)}, u32[]{:S(2)}) copy-start(s32[1024]{0:T(1024)S(1)} %get-tuple-element.1324) | copy-start | bytes 12292 | tf_op jit(solution)/shard_map/while
  8.6 173.6 %copy-start.59 = (s32[512]{0:T(512)}, s32[512]{0:T(512)S(1)}, u32[]{:S(2)}) copy-start(s32[512]{0:T(512)S(1)} %get-tuple-element.1323) | copy-start | bytes 6148 | tf_op jit(solution)/shard_map/while
  8.6 173.9 %all-gather.31.cloned.1.call-start = ((), (), s32[]{:S(2)}) async-start(), calls=%async_computation.16 | async-start | bytes 2820096 | tf_op jit(solution)/shard_map/while/body/eval_jaxpr/all_gather | solution.py:59
  11.2 8.1 copy-start.44
  12.1 225.2 %all-gather.33.cloned.1.call-start = ((), (), s32[]{:S(2)}) async-start(), calls=%async_computation.17 | async-start | bytes 2820096 | tf_op jit(solution)/shard_map/while/body/eval_jaxpr/all_gather | solution.py:62
  15.3 245.3 %all-gather.37.cloned.1.call-start = ((), (), s32[]{:S(2)}) async-start(), calls=%async_computation.19 | async-start | bytes 7520256 | tf_op jit(solution)/shard_map/while/body/eval_jaxpr/all_gather | solution.py:76
  19.2 8.1 copy-start.64
  19.2 8.4 copy-start.65
  19.2 53.4 %copy-start.47 = (bf16[72,192]{1,0:T(8,128)(2,1)S(1)}, bf16[72,192]{1,0:T(8,128)(2,1)}, u32[]{:S(2)}) copy-start(bf16[72,192]{1,0:T(8,128)(2,1)} %get-tuple-element.1315) | copy-start | bytes 82948 | tf_op jit(solution)/shard_map/while
  19.2 343.1 %all-gather.35.cloned.1.call-start = ((), (), s32[]{:S(2)}) async-start(), calls=%async_computation.18 | async-start | bytes 7520256 | tf_op jit(solution)/shard_map/while/body/eval_jaxpr/all_gather | solution.py:74
  21.6 442.3 %all-gather.39.cloned.1.call-start = ((), (), s32[]{:S(2)}) async-start(), calls=%async_computation.20 | async-start | bytes 7520256 | tf_op jit(solution)/shard_map/while/body/eval_jaxpr/all_gather | solution.py:75
  23.9 606.5 %reduce-scatter.34.cloned.1.call-start = ((), (), s32[]{:S(2)}) async-start(), calls=%async_computation.21 | async-start | bytes 1179648 | tf_op jit(solution)/shard_map/while/body/eval_jaxpr/reduce_scatter | solution.py:269
  26.0 161.8 %copy-start.45 = (f32[512]{0:T(512)}, f32[512]{0:T(512)S(1)}, u32[]{:S(2)}) copy-start(f32[512]{0:T(512)S(1)} %get-tuple-element.1101) | copy-start | bytes 6148 | tf_op jit(solution)/shard_map/while
  72.6 115.2 %copy-start.39 = (f32[1152]{0:T(1024)}, f32[1152]{0:T(1024)S(1)}, u32[]{:S(2)}) copy-start(f32[1152]{0:T(1024)S(1)} %convert_element_type.568) | copy-start | bytes 13828 | tf_op jit(solution)/shard_map/while
  119.4 72.3 %copy-start.31 = (f32[512,32]{0,1:T(8,128)}, f32[512,32]{0,1:T(8,128)S(1)}, u32[]{:S(2)}) copy-start(f32[512,32]{0,1:T(8,128)S(1)} %get-tuple-element.1103) | copy-start | bytes 196612 | tf_op jit(solution)/shard_map/while
  243.3 341.7 %copy-start.8 = (bf16[512,1152]{1,0:T(8,128)(2,1)}, bf16[512,1152]{1,0:T(8,128)(2,1)S(1)}, u32[]{:S(2)}) copy-start(bf16[512,1152]{1,0:T(8,128)(2,1)S(1)} %multiply_convert_fusion.8) | copy-start | bytes 3538948 | tf_op jit(solution)/shard_map/while
  463.9 12.4 copy-start.61
  480.7 8.5 copy-start.27
  585.0 50.0 %reduce-scatter.36.cloned.1.call-start = ((), (), s32[]{:S(2)}) async-start(), calls=%async_computation.22 | async-start | bytes 1179648 | tf_op jit(solution)/shard_map/while/body/eval_jaxpr/reduce_scatter | solution.py:272
  585.0 9.8 copy-start.29
  585.0 9.8 copy-start.32
  585.0 9.8 copy-start.37
  604.3 12.3 slice-start
  609.0 7.7 copy-start.7
  609.0 7.7 slice-start.1
  609.0 7.7 copy-start.66
  645.3 167.1 %copy-start.57 = (s32[1024]{0:T(1024)}, s32[1024]{0:T(1024)S(1)}, u32[]{:S(2)}) copy-start(s32[1024]{0:T(1024)S(1)} %get-tuple-element.1324) | copy-start | bytes 12292 | tf_op jit(solution)/shard_map/while
  645.3 167.1 %copy-start.59 = (s32[512]{0:T(512)}, s32[512]{0:T(512)S(1)}, u32[]{:S(2)}) copy-start(s32[512]{0:T(512)S(1)} %get-tuple-element.1323) | copy-start | bytes 6148 | tf_op jit(solution)/shard_map/while
  645.3 167.5 %all-gather.31.cloned.1.call-start = ((), (), s32[]{:S(2)}) async-start(), calls=%async_computation.16 | async-start | bytes 2820096 | tf_op jit(solution)/shard_map/while/body/eval_jaxpr/all_gather | solution.py:59
  647.8 8.1 copy-start.44
  648.7 218.4 %all-gather.33.cloned.1.call-start = ((), (), s32[]{:S(2)}) async-start(), calls=%async_computation.17 | async-start | bytes 2820096 | tf_op jit(solution)/shard_map/while/body/eval_jaxpr/all_gather | solution.py:62
  651.9 240.3 %all-gather.37.cloned.1.call-start = ((), (), s32[]{:S(2)}) async-start(), calls=%async_computation.19 | async-start | bytes 7520256 | tf_op jit(solution)/shard_map/while/body/eval_jaxpr/all_gather | solution.py:76
  655.8 8.1 copy-start.64
  655.8 8.4 copy-start.65
  655.8 49.2 %copy-start.47 = (bf16[72,192]{1,0:T(8,128)(2,1)S(1)}, bf16[72,192]{1,0:T(8,128)(2,1)}, u32[]{:S(2)}) copy-start(bf16[72,192]{1,0:T(8,128)(2,1)} %get-tuple-element.1315) | copy-start | bytes 82948 | tf_op jit(solution)/shard_map/while
  655.8 338.2 %all-gather.35.cloned.1.call-start = ((), (), s32[]{:S(2)}) async-start(), calls=%async_computation.18 | async-start | bytes 7520256 | tf_op jit(solution)/shard_map/while/body/eval_jaxpr/all_gather | solution.py:74
  658.1 437.5 %all-gather.39.cloned.1.call-start = ((), (), s32[]{:S(2)}) async-start(), calls=%async_computation.20 | async-start | bytes 7520256 | tf_op jit(solution)/shard_map/while/body/eval_jaxpr/all_gather | solution.py:75
  660.5 617.1 %reduce-scatter.34.cloned.1.call-start = ((), (), s32[]{:S(2)}) async-start(), calls=%async_computation.21 | async-start | bytes 1179648 | tf_op jit(solution)/shard_map/while/body/eval_jaxpr/reduce_scatter | solution.py:269
  662.6 155.4 %copy-start.45 = (f32[512]{0:T(512)}, f32[512]{0:T(512)S(1)}, u32[]{:S(2)}) copy-start(f32[512]{0:T(512)S(1)} %get-tuple-element.1101) | copy-start | bytes 6148 | tf_op jit(solution)/shard_map/while
  705.0 113.1 %copy-start.39 = (f32[1152]{0:T(1024)}, f32[1152]{0:T(1024)S(1)}, u32[]{:S(2)}) copy-start(f32[1152]{0:T(1024)S(1)} %convert_element_type.568) | copy-start | bytes 13828 | tf_op jit(solution)/shard_map/while
  751.5 70.1 %copy-start.31 = (f32[512,32]{0,1:T(8,128)}, f32[512,32]{0,1:T(8,128)S(1)}, u32[]{:S(2)}) copy-start(f32[512,32]{0,1:T(8,128)S(1)} %get-tuple-element.1103) | copy-start | bytes 196612 | tf_op jit(solution)/shard_map/while
  873.1 343.7 %copy-start.8 = (bf16[512,1152]{1,0:T(8,128)(2,1)}, bf16[512,1152]{1,0:T(8,128)(2,1)S(1)}, u32[]{:S(2)}) copy-start(bf16[512,1152]{1,0:T(8,128)(2,1)S(1)} %multiply_convert_fusion.8) | copy-start | bytes 3538948 | tf_op jit(solution)/shard_map/while
  1095.6 12.4 copy-start.61
  1112.4 8.5 copy-start.27
  1216.7 65.4 %reduce-scatter.36.cloned.1.call-start = ((), (), s32[]{:S(2)}) async-start(), calls=%async_computation.22 | async-start | bytes 1179648 | tf_op jit(solution)/shard_map/while/body/eval_jaxpr/reduce_scatter | solution.py:272
  1216.8 14.7 copy-start.29
  1216.8 14.7 copy-start.32
  1216.8 14.7 copy-start.37
  1233.7 10.3 copy-start.1
  1233.7 10.3 copy-start.40
  1233.8 10.3 copy-start.46
  1244.1 18.1 slice-start
  1251.2 11.1 copy-start.7
  1251.2 11.1 slice-start.1
  1251.2 11.1 copy-start.66
  1270.7 8.2 copy-start.33
  1270.7 8.2 copy-start.38
  1300.7 2454.8 %reduce-scatter.26.cloned.1.call-start = ((), (), s32[]{:S(2)}) async-start(), calls=%async_computation.12 | async-start | bytes 147456
  3721.4 45.4 %reduce-scatter.28.cloned.1.call-start = ((), (), s32[]{:S(2)}) async-start(), calls=%async_computation.13 | async-start | bytes 147456
  3722.3 56.0 %reduce-scatter.24.cloned.1.call-start = ((), (), s32[]{:S(2)}) async-start(), calls=%async_computation.11 | async-start | bytes 442368
  3725.0 64.9 %reduce-scatter.30.cloned.1.call-start = ((), (), s32[]{:S(2)}) async-start(), calls=%async_computation.14 | async-start | bytes 442368
  3727.5 73.8 %reduce-scatter.32.cloned.1.call-start = ((), (), s32[]{:S(2)}) async-start(), calls=%async_computation.15 | async-start | bytes 884736
  3730.9 82.2 %reduce-scatter.20.cloned.1.call-start = ((), (), s32[]{:S(2)}) async-start(), calls=%async_computation.9 | async-start | bytes 663552 | tf_op jit(solution)/shard_map/reduce_scatter | solution.py:381
  3733.0 91.2 %reduce-scatter.22.cloned.1.call-start = ((), (), s32[]{:S(2)}) async-start(), calls=%async_computation.10 | async-start | bytes 663552 | tf_op jit(solution)/shard_map/reduce_scatter | solution.py:384
  (114 other events, 340.7 us)
Sparse Core Ops, SparseCore 0:
  12.7 71.0 all-gather.30
  87.0 68.8 all-gather.32
  159.3 101.3 all-gather.36
  263.3 98.9 all-gather.34
  364.9 98.9 all-gather.38
  585.1 6.5 reduce-scatter.33
  604.4 6.5 reduce-scatter.35
  649.4 66.7 all-gather.30
  719.5 69.4 all-gather.32
  792.2 100.0 all-gather.36
  895.0 98.9 all-gather.34
  996.7 98.9 all-gather.38
  1216.8 6.4 reduce-scatter.33
  1244.2 6.5 reduce-scatter.35
Sparse Core Ops, SparseCore 1:
  3721.4 34.0 reduce-scatter.25
  3758.1 8.6 reduce-scatter.27
  3769.4 8.8 reduce-scatter.23
  3781.1 8.8 reduce-scatter.29
  3792.2 9.0 reduce-scatter.31
  3804.1 8.9 reduce-scatter.19
  3815.2 8.9 reduce-scatter.21
where the time goes:
time: 3840 us; the launch traced here: 3830 us
  blocking collectives  2670 us (70%)
  waiting for transfers between devices  478 us (12%)
  matrix products  448 us (12%)
  local copies, waits for them, and re-layouts  138 us (4%)
  other arithmetic  64.8 us (2%)
    unnamed x1, blocking collectives  2360 us
    all_gather x2, waiting for transfers between devices, fetch_mlp(): lax.all_gather(columns[1], 'dp', axis=0, tiled=True)  185 us
    all_gather x2, waiting for transfers between devices, fetch_mlp(): lax.all_gather(columns[0], 'dp', axis=0, tiled=True)  183 us
    all_gather x2, blocking collectives, fetch_attention(): lax.all_gather(columns[2], 'dp', axis=0, tiled=True)  98.8 us
    while x2, blocking collectives  85.3 us
    all_gather x2, blocking collectives, fetch_attention(): lax.all_gather(columns[1], 'dp', axis=0, tiled=True)  84.3 us
  transfers between devices with their start and end apart: 21, of which 13 were waited for; matrix products, arithmetic and copies ran while one was open for 8% of the time, Pallas kernels for 0%

commit v1 on v0

v1 whole, which is shorter than its diff:
```python
import functools

import jax
import jax.numpy as jnp
from jax import lax
from jax.experimental import pallas as pl
from jax.experimental.pallas import tpu as pltpu
from jax.sharding import PartitionSpec as P

D = 1152
QUERY_HEADS = 18
KEY_VALUE_HEADS = 6
HEAD_SIZE = 64
FF = 3072
BLOCK = 256
QD = 1152
KVD = 384
HQ, HK = QUERY_HEADS // 2, KEY_VALUE_HEADS // 2
HALL = HQ + 2 * HK
QKV = HALL * HEAD_SIZE
FT = 256

epsilon = 1e-05
bf16, f32 = jnp.bfloat16, jnp.float32
NT = (((1,), (1,)), ((), ()))
NN = (((1,), (0,)), ((), ()))
TN = (((0,), (0,)), ((), ()))
VMEM_BYTES = 62 << 20


def dg(a, b, dims):
    return lax.dot_general(a, b, dims, preferred_element_type=f32)


def fwd_body(me, q, k, v, o, lse, kf, vf):
    piece = q.shape[3]
    shift = me[0]

    @pl.when(pl.program_id(1) % 3 == 0)
    def _():
        for a in range(2):
            kf[pl.ds(a * piece, piece), :] = k[shift ^ a, 0, 0]
            vf[pl.ds(a * piece, piece), :] = v[shift ^ a, 0, 0]

    for i in range(2 * piece // BLOCK):
        half, row = divmod(i * BLOCK, piece)
        r = pl.ds(row, BLOCK)
        kw = (i + 1) * BLOCK
        qs = q[shift ^ half, 0, 0, r, :] * jnp.asarray(0.125, bf16)
        s = dg(qs, kf[:kw, :], NT)
        m = jnp.max(s, axis=1, keepdims=True)
        p = jnp.exp(s - m)
        l = jnp.sum(p, axis=1, keepdims=True)
        mix = dg(p.astype(bf16), vf[:kw, :], NN)
        o[shift ^ half, 0, 0, r, :] = (mix / l).astype(bf16)
        lse[0, 0, pl.ds(i * BLOCK, BLOCK), :] = jnp.broadcast_to(m + jnp.log(l), (BLOCK, 128))


def bwd_body(me, q, k, v, o, do, lse, dq, dk, dv, kf, vf, dka, dva):
    piece = q.shape[3]
    shift = me[0]
    j = pl.program_id(2)

    @pl.when(j == 0)
    def _():
        for a in range(2):
            kf[pl.ds(a * piece, piece), :] = k[shift ^ a, 0, 0]
            vf[pl.ds(a * piece, piece), :] = v[shift ^ a, 0, 0]
        dka[...] = jnp.zeros_like(dka)
        dva[...] = jnp.zeros_like(dva)

    for i in range(2 * piece // BLOCK):
        half, row = divmod(i * BLOCK, piece)
        r = pl.ds(row, BLOCK)
        kw = (i + 1) * BLOCK
        at = shift ^ half
        qs = q[at, 0, 0, r, :] * jnp.asarray(0.125, bf16)
        dO = do[at, 0, 0, r, :]
        kk = kf[:kw, :]
        s = dg(qs, kk, NT)
        p = jnp.exp(s - lse[0, 0, pl.ds(i * BLOCK, BLOCK), :1])
        dp = dg(dO, vf[:kw, :], NT)
        inner = jnp.sum(dO.astype(f32) * o[at, 0, 0, r, :].astype(f32), axis=1, keepdims=True)
        ds = (p * (dp - inner)).astype(bf16)
        dq[at, 0, 0, r, :] = (dg(ds, kk, NN) * 0.125).astype(bf16)
        dka[:, :kw] += dg(qs.T, ds, NN)
        dva[:, :kw] += dg(dO.T, p.astype(bf16), NN)

    @pl.when(j == pl.num_programs(2) - 1)
    def _():
        for a in range(2):
            c = pl.ds(a * piece, piece)
            dk[shift ^ a, 0, 0] = dka[:, c].T.astype(bf16)
            dv[shift ^ a, 0, 0] = dva[:, c].T.astype(bf16)


def attend(me, heads):
    _, batch, _, piece, width = heads.shape
    at = lambda f: pl.BlockSpec((2, 1, 1, piece, width), lambda b, h, *_: (0, b, f(h), 0, 0))
    return pl.pallas_call(
        fwd_body,
        grid_spec=pltpu.PrefetchScalarGridSpec(
            num_scalar_prefetch=1,
            grid=(batch, HQ),
            in_specs=[at(lambda h: h), at(lambda h: HQ + h // 3), at(lambda h: HQ + HK + h // 3)],
            out_specs=[
                at(lambda h: h),
                pl.BlockSpec((1, 1, 2 * piece, 128), lambda b, h, *_: (b, h, 0, 0)),
            ],
            scratch_shapes=[pltpu.VMEM((2 * piece, width), bf16)] * 2,
        ),
        out_shape=[
            jax.ShapeDtypeStruct((2, batch, HQ, piece, width), bf16),
            jax.ShapeDtypeStruct((batch, HQ, 2 * piece, 128), f32),
        ],
        compiler_params=pltpu.CompilerParams(vmem_limit_bytes=VMEM_BYTES),
        cost_estimate=pl.CostEstimate(flops=24 * 10**9, bytes_accessed=20 * 10**6, transcendentals=12 * 10**6),
        name="attend",
    )(me, heads, heads, heads)


def attend_back(me, heads, mixed, grads, lse):
    _, batch, _, piece, width = heads.shape
    at = lambda f: pl.BlockSpec((2, 1, 1, piece, width), lambda b, g, j, *_: (0, b, f(g, j), 0, 0))
    query = at(lambda g, j: g * 3 + j)
    key = at(lambda g, j: g)
    return pl.pallas_call(
        bwd_body,
        grid_spec=pltpu.PrefetchScalarGridSpec(
            num_scalar_prefetch=1,
            grid=(batch, HK, 3),
            in_specs=[
                query,
                at(lambda g, j: HQ + g),
                at(lambda g, j: HQ + HK + g),
                query,
                query,
                pl.BlockSpec((1, 1, 2 * piece, 128), lambda b, g, j, *_: (b, g * 3 + j, 0, 0)),
            ],
            out_specs=[query, key, key],
            scratch_shapes=[pltpu.VMEM((2 * piece, width), bf16)] * 2
            + [pltpu.VMEM((width, 2 * piece), f32)] * 2,
        ),
        out_shape=[
            jax.ShapeDtypeStruct((2, batch, HQ, piece, width), bf16),
            jax.ShapeDtypeStruct((2, batch, HK, piece, width), bf16),
            jax.ShapeDtypeStruct((2, batch, HK, piece, width), bf16),
        ],
        compiler_params=pltpu.CompilerParams(vmem_limit_bytes=VMEM_BYTES),
        cost_estimate=pl.CostEstimate(flops=27 * 10**9, bytes_accessed=40 * 10**6, transcendentals=12 * 10**6),
        name="attend_back",
    )(me, heads, heads, heads, mixed, grads, lse)


def mlp_body(n2, n2t, cot, res, wg, wu, wd, out, gn, gg, gu, gd, y):
    t = pl.program_id(0)

    @pl.when(t == 0)
    def _():
        y[...] = res[...]
        gn[...] = jnp.zeros_like(gn)

    half = wd.shape[2]
    wdt = jnp.concatenate([wd[0], wd[1]], axis=1)
    gate = dg(n2[...], wg[0], NN)
    up = dg(n2[...], wu[0], NN)
    gh = dg(cot[...], wdt, NT)
    sig = jax.nn.sigmoid(gate)
    act = gate * sig
    hidden = (act * up).astype(bf16)
    ggv = (gh * up * sig * (1.0 + gate * (1.0 - sig))).astype(bf16)
    guv = (gh * act).astype(bf16)
    y[...] += dg(hidden, wdt, NN)
    gdt = dg(hidden, cot[...], TN).astype(bf16)
    gd[0] = gdt[:, :half]
    gd[1] = gdt[:, half:]
    gg[0] = dg(n2t[...], ggv, NN).astype(bf16)
    gu[0] = dg(n2t[...], guv, NN).astype(bf16)
    gn[...] += dg(ggv, wg[0], NT) + dg(guv, wu[0], NT)

    @pl.when(t == pl.num_programs(0) - 1)
    def _():
        out[...] = y[...].astype(bf16)


def mlp(n2, n2t, cot, res, wg, wu, wd):
    rows = n2.shape[0]
    cols = wg.shape[2]
    per = cols // FT
    whole = lambda a: pl.BlockSpec(a.shape, lambda t: (0, 0), pipeline_mode=pl.Buffered(1))
    col = pl.BlockSpec((1, D, FT), lambda t: (t // per, 0, t % per))
    row = pl.BlockSpec((2, FT, D // 2), lambda t: (0, t, 0))
    one = lambda: pl.BlockSpec((rows, D), lambda t: (0, 0), pipeline_mode=pl.Buffered(1))
    return pl.pallas_call(
        mlp_body,
        grid=(FF // FT,),
        in_specs=[whole(n2), whole(n2t), whole(cot), whole(res), col, col, row],
        out_specs=[one(), one(), col, col, row],
        out_shape=[
            jax.ShapeDtypeStruct((rows, D), bf16),
            jax.ShapeDtypeStruct((rows, D), f32),
            jax.ShapeDtypeStruct(wg.shape, bf16),
            jax.ShapeDtypeStruct(wu.shape, bf16),
            jax.ShapeDtypeStruct(wd.shape, bf16),
        ],
        scratch_shapes=[pltpu.VMEM((rows, D), f32)],
        compiler_params=pltpu.CompilerParams(vmem_limit_bytes=VMEM_BYTES),
        cost_estimate=pl.CostEstimate(flops=65 * 10**9, bytes_accessed=60 * 10**6, transcendentals=3 * 10**6),
        name="mlp",
    )(n2, n2t, cot, res, wg, wu, wd)


def turn(u, shift, heads, inverse):
    tokens = u.shape[1]
    h = HEAD_SIZE // 2
    places = (shift + jnp.arange(tokens)).astype(f32)
    frequency = 10000.0 ** (-2.0 * jnp.arange(h).astype(f32) / HEAD_SIZE)
    angles = places[:, None] * frequency[None, :]
    cosine, sine = jnp.cos(angles)[:, None, :], jnp.sin(angles)[:, None, :]
    if inverse:
        sine = -sine
    a, b = u[..., :heads, :h], u[..., :heads, h:]
    turned = jnp.concatenate([a * cosine - b * sine, b * cosine + a * sine], -1)
    return jnp.concatenate([turned, u[..., heads:, :]], -2)


def norm_back(grad_norm, rows_in, scale_rows, gain_rows):
    weighted = grad_norm * gain_rows
    cube_rows = scale_rows * scale_rows * scale_rows
    return scale_rows * weighted - rows_in * cube_rows * jnp.mean(
        weighted * rows_in, -1, keepdims=True
    )


def swap(a):
    return lax.ppermute(a, "seq", [(0, 1), (1, 0)])


def in_order(me, mine, theirs, axis):
    return jnp.where(
        me == 0,
        jnp.concatenate([mine, theirs], axis),
        jnp.concatenate([theirs, mine], axis),
    )


BOTH = ("dp", "seq")


def fetch(shards):
    out = []
    for w in shards:
        g = lax.all_gather(w, BOTH, axis=0, tiled=True)
        g = g.reshape(lax.axis_size("dp"), 2, *w.shape)
        out.append(jnp.swapaxes(g, 0, 1).reshape(2, -1, w.shape[1]))
    return out


def reduce_all(grads):
    out = []
    for g in grads:
        n = lax.axis_size("dp")
        t = jnp.swapaxes(g.reshape(2, n, -1, g.shape[2]), 0, 1).reshape(-1, g.shape[2])
        out.append(lax.psum_scatter(t, BOTH, scatter_dimension=0, tiled=True))
    return out


def local(
    layer_input,
    w_query,
    w_key,
    w_value,
    w_out,
    gain_attn,
    w_gate,
    w_up,
    w_down,
    gain_mlp,
    cotangent,
):
    batch, _, piece, _ = layer_input.shape
    tokens = batch * piece
    me = lax.axis_index("seq")
    shift = me * piece
    me_arr = jnp.full((1,), me, jnp.int32)
    gains = jnp.pad(jnp.stack([gain_attn, gain_mlp], 1), ((0, 0), (0, 126)))
    pack = jnp.concatenate([w_query, w_key, w_value, w_out, gains], 1)
    (full,) = fetch([pack])
    full_gate, full_up, full_down = fetch([w_gate, w_up, w_down])
    gain_one = full[0, :, QKV + D // 2].astype(f32)
    gain_two = full[0, :, QKV + D // 2 + 1].astype(f32)
    w_mine = lax.dynamic_index_in_dim(full, me, 0, keepdims=False)[:, :QKV]
    w_theirs = lax.dynamic_index_in_dim(full, 1 - me, 0, keepdims=False)[:, :QKV]
    full_out = jnp.concatenate([full[0, :, QKV : QKV + D // 2], full[1, :, QKV : QKV + D // 2]], 1)

    floats = layer_input.reshape(tokens, D).astype(f32)
    cot = cotangent.reshape(tokens, D)
    scale_attn = lax.rsqrt(jnp.mean(floats * floats, -1, keepdims=True) + epsilon)
    n1 = (floats * scale_attn * gain_one).astype(bf16)

    def heads_of(w):
        u = jnp.dot(n1, w, preferred_element_type=f32).reshape(batch, piece, HALL, HEAD_SIZE)
        return jnp.transpose(turn(u, shift, HQ + HK, False).astype(bf16), (0, 2, 1, 3))

    theirs = swap(heads_of(w_theirs))
    heads = jnp.stack([heads_of(w_mine), theirs])
    mixed, lse = attend(me_arr, heads)
    mixed_back = swap(mixed[1])
    rows_of = lambda a: jnp.transpose(a, (0, 2, 1, 3)).reshape(tokens, -1)
    merged = in_order(me, rows_of(mixed[0]), rows_of(mixed_back), 1)
    residual = floats + jnp.dot(merged, full_out, preferred_element_type=f32)
    scale_mlp = lax.rsqrt(jnp.mean(residual * residual, -1, keepdims=True) + epsilon)
    n2 = (residual * scale_mlp * gain_two).astype(bf16)
    layer_out, grad_n2, grad_gate, grad_up, grad_down = mlp(
        n2, n2.T, cot, residual, full_gate, full_up, full_down
    )
    sum_gain_mlp = jnp.sum(grad_n2 * residual * scale_mlp, 0)
    grad_residual = cot.astype(f32) + norm_back(grad_n2, residual, scale_mlp, gain_two)
    grad_low = grad_residual.astype(bf16)
    grad_out = jnp.einsum("tq,td->qd", merged, grad_low, preferred_element_type=f32)
    grad_merged = jnp.einsum("td,qd->tq", grad_low, full_out, preferred_element_type=f32).astype(bf16)
    by_head = lambda a: jnp.transpose(a.reshape(batch, piece, HQ, HEAD_SIZE), (0, 2, 1, 3))
    part = lambda i: by_head(lax.dynamic_slice_in_dim(grad_merged, i * (QD // 2), QD // 2, 1))
    grad_mixed = jnp.stack([part(me), swap(part(1 - me))])
    d_query, d_key, d_value = attend_back(me_arr, heads, mixed, grad_mixed, lse)
    d_heads = jnp.concatenate([d_query, d_key, d_value], 2)

    def linear_of(a):
        u = jnp.transpose(a.astype(f32), (0, 2, 1, 3))
        return turn(u, shift, HQ + HK, True).astype(bf16).reshape(tokens, QKV)

    lin_theirs = linear_of(swap(d_heads[1]))
    lin_mine = linear_of(d_heads[0])
    weight_grad = lambda lin: jnp.einsum("td,tq->dq", n1, lin, preferred_element_type=f32).astype(bf16)
    grad_n1 = jnp.einsum("tq,dq->td", lin_mine, w_mine, preferred_element_type=f32) + jnp.einsum(
        "tq,dq->td", lin_theirs, w_theirs, preferred_element_type=f32
    )
    sum_gain_attn = jnp.sum(grad_n1 * floats * scale_attn, 0)
    grad_input = (grad_residual + norm_back(grad_n1, floats, scale_attn, gain_one)).astype(bf16)
    grad_qkv = in_order(me, weight_grad(lin_mine)[None], weight_grad(lin_theirs)[None], 0)
    sums = jnp.pad(jnp.stack([sum_gain_attn, sum_gain_mlp], 1), ((0, 0), (0, 126))).astype(bf16)
    go = grad_out.astype(bf16)
    grad_pack = jnp.concatenate(
        [
            grad_qkv,
            jnp.stack([go[:, : D // 2], go[:, D // 2 :]]),
            jnp.stack([sums, sums]),
        ],
        2,
    )
    r_gate, r_up, r_down = reduce_all([grad_gate, grad_up, grad_down])
    (r_pack,) = reduce_all([grad_pack])
    r_pack = r_pack.astype(f32)
    a, b, c, d = HQ * HEAD_SIZE, (HQ + HK) * HEAD_SIZE, QKV, QKV + D // 2
    shape = layer_input.shape
    return (
        layer_out.reshape(shape),
        grad_input.reshape(shape),
        r_pack[:, :a],
        r_pack[:, a:b],
        r_pack[:, b:c],
        r_pack[:, c:d],
        r_pack[:, d],
        r_gate.astype(f32),
        r_up.astype(f32),
        r_down.astype(f32),
        r_pack[:, d + 1],
    )


def solution(mesh):
    tokens, matrix, vector = P(None, "dp", "seq", None), P("dp", "seq"), P("dp")
    placed = (tokens, *[matrix] * 4, vector, *[matrix] * 3, vector, tokens)
    return jax.shard_map(
        local,
        mesh=mesh,
        in_specs=placed,
        out_specs=(tokens, tokens, *[matrix] * 4, vector, *[matrix] * 3, vector),
        check_vma=False,
    )
```

time: 3840 us -> 948 us (0.25)
  blocking collectives: 2670 us -> 0 us
  matrix products: 448 us -> 44.7 us
  Pallas kernels: 0 us -> 161 us
  local copies, waits for them, and re-layouts: 138 us -> 217 us
  waiting for transfers between devices: 478 us -> 400 us
    unnamed x1 -> x0, blocking collectives: 2360 us -> none
    dot_general x126 -> x9, matrix products: 448 us -> 44.7 us  [the longest x2 13.7 us: local(): jnp.einsum('td,tq->dq', n1, lin, preferred_element_type=f32).astype(bf16)]
    all_gather x10 -> x4, waiting for transfers between devices: 404 us -> 144 us  [fetch(): g = lax.all_gather(w, BOTH, axis=0, tiled=True)]
    all_gather x22 -> x0, blocking collectives: 223 us -> none  [the longest x2 98.8 us: fetch_attention(): lax.all_gather(columns[2], 'dp', axis=0, tiled=True)]
    pallas_call x0 -> x3, Pallas kernels: none -> 161 us  [the longest x1 86.3 us: mlp(): pl.pallas_call(mlp_body, grid=(FF // FT,), in_specs=[whole(n2), whole(n2t...]
    reduce_scatter x6 -> x3, waiting for transfers between devices: 19.2 us -> 136 us  [reduce_all(): out.append(lax.psum_scatter(t, BOTH, scatter_dimension=0, tiled=True))]
    while x2 -> x0, blocking collectives: 85.3 us -> none
    unnamed x12 -> x9, waiting for transfers between devices: 54.6 us -> 119 us
  transfers between devices with their start and end apart: 21 -> 12, of which waited for: 13 -> 6; matrix products, arithmetic and copies ran while one was open for 8% -> 34% of each run, Pallas kernels for 0% -> 8%
where the time goes in v1:
time: 948 us; the launch traced here: 936 us
  waiting for transfers between devices  400 us (42%)
  local copies, waits for them, and re-layouts  217 us (23%)
  Pallas kernels  161 us (17%)
  other arithmetic  98.3 us (10%)
  matrix products  44.7 us (5%)
  between operations  15 us (2%)
    all_gather x4, waiting for transfers between devices, fetch(): g = lax.all_gather(w, BOTH, axis=0, tiled=True)  144 us
    reduce_scatter x3, waiting for transfers between devices, reduce_all(): out.append(lax.psum_scatter(t, BOTH, scatter_dimension=0, tiled=True))  136 us
    unnamed x9, waiting for transfers between devices  119 us
    pallas_call x1, Pallas kernels, mlp(): pl.pallas_call(mlp_body, grid=(FF // FT,), in_specs=[whole(n2), whole(n2t...  86.3 us
    pallas_call x1, Pallas kernels, attend_back(): pl.pallas_call(bwd_body, grid_spec=pltpu.PrefetchScalarGridSpec(num_scala...  39.2 us
    unnamed x89, local copies, waits for them, and re-layouts  37.5 us
    pallas_call x1, Pallas kernels, attend(): pl.pallas_call(fwd_body, grid_spec=pltpu.PrefetchScalarGridSpec(num_scala...  35.3 us
    transpose x4, local copies, waits for them, and re-layouts, reduce_all(): jnp.swapaxes(g.reshape(2, n, -1, g.shape[2]), 0, 1).reshape(-1, g.shape[2])  27.9 us
  transfers between devices with their start and end apart: 12, of which 6 were waited for; matrix products, arithmetic and copies ran while one was open for 34% of the time, Pallas kernels for 8%

profile of v1, /device:TPU:0, one launch (start us, length us, event | category | flops | bytes accessed | tf_op | source)
XLA Modules:
  0.0 936.2 jit_solution(11207199831146708715)
XLA Ops:
  16.6 71.9 %all-gather.5.cloned.1.call-done = bf16[2304,1664]{1,0:T(8,128)(2,1)} async-done(((bf16[72,1664]{1,0:T(8,128)(2,1)}), bf16[2304,1664]{1,0:T(8,128)(2,1)}) %all-gather.5.cloned.1.call-update) | async-done | bytes 7667728 | tf_op jit(solution)/shard_map/all_gather | solution.py:253
  88.5 3.7 copy.140
  92.3 3.0 dynamic-slice_bitcast_fusion.1
  96.6 5.9 slice_bitcast_fusion.4
  102.4 4.4 copy.141
  109.1 2.7 fusion.12
  115.3 4.0 copy.179
  119.3 5.2 copy.180
  126.9 5.1 fusion.10
  133.0 4.0 copy.182
  137.1 3.9 copy.183
  142.1 12.2 %subtract_convert_fusion.1 = (bf16[2,512,12,32]{3,1,2,0:T(8,128)(2,1)S(1)}, bf16[2,512,12,32]{3,1,2,0:T(8,128)(2,1)}, bf16[2,512,12,32]{3,1,2,0:T(8,128)(2,1)S(1)}, bf16[2,512,12,32]{3,1,2,0:T(8,128)(2,1)S(1)}) fusion(f32[2,512,12,32]{3,1,2,0:T(8,128)} %copy.180, f32[2,512,12,32]{3,1,2,0:T(8,128)} %copy.179, f32[512,32]{1,0:T(8,128)} %get-tuple-element.131, ...), kind=kLoop, calls=%fused_computation.12 | loop fusion | flops 6291456 | bytes 9568256 | tf_op jit(solution)/shard_map/convert.20
  154.3 3.4 maximum_bitcast_fusion.1
  157.7 4.8 copy.149
  165.0 4.8 maximum_bitcast_fusion
  169.7 4.7 copy.150
  174.4 8.4 pad_maximum_fusion.q.k.v
  182.8 35.3 %attend.1 = (bf16[2,2,9,512,64]{4,3,2,1,0:T(8,128)(2,1)}, f32[2,9,1024,128]{3,2,1,0:T(8,128)}) custom-call(s32[1]{0:T(128)} %bitcast.1.me, bf16[2,2,15,512,64]{4,3,2,1,0:T(8,128)(2,1)} %pad_maximum_fusion.q.k.v, bf16[2,2,15,512,64]{4,3,2,1,0:T(8,128)(2,1)} %pad_maximum_fusion.q.k.v, bf16[2,2,15,512,64]{4,3,2,1,0:T(8,128)(2,1)} %pad_maximum_fusion.q.k.v), custom_call_target="tpu_custom_call" | custom-call | flops 24000000000 | bytes 20000000 | tf_op jit(solution)/shard_map/attend/pallas_call | solution.py:100
  218.1 4.2 slice_bitcast_fusion.3
  222.3 3.8 copy.152
  226.4 7.2 copy.156
  233.6 5.4 all-gather.7.cloned.1.call-done
  239.0 6.4 copy.154
  245.4 66.9 %all-gather.9.cloned.1.call-done = bf16[2304,1536]{1,0:T(8,128)(2,1)} async-done(((bf16[72,1536]{1,0:T(8,128)(2,1)}), bf16[2304,1536]{1,0:T(8,128)(2,1)}) %all-gather.9.cloned.1.call-update) | async-done | bytes 7077904 | tf_op jit(solution)/shard_map/all_gather | solution.py:253
  312.3 6.5 copy.155
  318.8 5.3 slice_bitcast_fusion.7
  326.8 3.1 copy.153
  330.2 4.5 multiply_reduce_fusion.2
  341.3 86.3 %mlp.1 = (bf16[1024,1152]{1,0:T(8,128)(2,1)}, f32[1024,1152]{1,0:T(8,128)}, bf16[2,1152,1536]{2,1,0:T(8,128)(2,1)}, bf16[2,1152,1536]{2,1,0:T(8,128)(2,1)}, bf16[2,3072,576]{2,1,0:T(8,128)(2,1)}) custom-call(bf16[1024,1152]{1,0:T(8,128)(2,1)} %multiply_convert_fusion.n2, bf16[1152,1024]{1,0:T(8,128)(2,1)} %copy.157.n2t, bf16[1024,1152]{1,0:T(8,128)(2,1)} %bitcast.195, ...), custom_call_target="tpu_custom_call" | custom-call | flops 65000001536 | bytes 60000000 | tf_op jit(solution)/shard_map/mlp/pallas_call | solution.py:194
  427.6 7.2 copy.175
  434.9 6.8 copy.173
  441.8 5.4 multiply_reduce_fusion
  448.3 3.6 subtract_add_fusion
  451.9 4.1 convolution_convert_fusion.1
  458.8 3.3 reshape.370
  465.1 3.3 reshape.369
  470.5 7.1 copy.174
  477.6 4.1 copy.162
  481.7 5.1 pad_maximum_fusion.1.do
  486.9 39.2 %attend_back.1 = (bf16[2,2,9,512,64]{4,3,2,1,0:T(8,128)(2,1)}, bf16[2,2,3,512,64]{4,3,2,1,0:T(8,128)(2,1)}, bf16[2,2,3,512,64]{4,3,2,1,0:T(8,128)(2,1)}) custom-call(s32[1]{0:T(128)} %bitcast.1.me, bf16[2,2,15,512,64]{4,3,2,1,0:T(8,128)(2,1)} %pad_maximum_fusion.q.k.v, bf16[2,2,15,512,64]{4,3,2,1,0:T(8,128)(2,1)} %pad_maximum_fusion.q.k.v, ...), custom_call_target="tpu_custom_call" | custom-call | flops 27000000512 | bytes 40000000 | tf_op jit(solution)/shard_map/attend_back/pallas_call | solution.py:127
  526.0 2.8 constant_dynamic-update-slice_fusion.2
  530.5 5.3 slice_bitcast_fusion
  535.8 4.8 copy.164
  541.1 5.8 convolution_convert_fusion
  556.0 5.6 copy.165
  563.1 13.1 %multiply_subtract_fusion = (bf16[2,512,12,32]{3,1,2,0:T(8,128)(2,1)S(1)}, bf16[2,512,12,32]{3,1,2,0:T(8,128)(2,1)S(1)}, bf16[2,512,12,32]{3,1,2,0:T(8,128)(2,1)S(1)}, bf16[2,512,12,32]{3,1,2,0:T(8,128)(2,1)}) fusion(f32[2,512,15,64]{3,1,2,0:T(8,128)} %bitcast.161, f32[512,32]{1,0:T(8,128)} %get-tuple-element.130, f32[512,32]{1,0:T(8,128)S(1)} %copy-done.15, ...), kind=kLoop, calls=%fused_computation.6 | loop fusion | flops 6291456 | bytes 9568256 | tf_op jit(solution)/shard_map/sub | solution.py:223
  576.2 3.2 maximum_convert_fusion.1
  579.4 6.8 copy.166
  586.2 3.6 copy.191
  589.8 3.2 maximum_convert_fusion
  593.0 5.7 copy.163
  601.6 3.0 fusion.15
  605.1 5.9 fusion.9
  611.3 7.3 convolution_convert_fusion.2
  618.6 4.2 copy.168
  622.8 6.4 convolution_convert_fusion.3
  629.2 4.3 copy.167
  633.5 6.9 maximum_select_fusion
  640.4 12.7 %concatenate.78 = bf16[2,16,72,1664]{3,2,1,0:T(8,128)(2,1)} concatenate(bf16[2,16,72,960]{3,2,1,0:T(8,128)(2,1)} %maximum_select_fusion, bf16[2,16,72,576]{3,2,1,0:T(8,128)(2,1)} %pad_maximum_fusion.2, bf16[2,16,72,128]{3,2,1,0:T(8,128)(2,1)S(1)} %pad_maximum_fusion.6), dimensions={3} | concatenate | bytes 15335424 | tf_op jit(solution)/shard_map/concatenate | solution.py:343
  653.1 6.9 copy.172
  660.0 5.5 fusion.6
  667.3 13.4 %reduce-scatter.7.cloned.1.call-done = bf16[72,1536]{1,0:T(8,128)(2,1)} async-done(((bf16[2304,1536]{1,0:T(8,128)(2,1)}), bf16[72,1536]{1,0:T(8,128)(2,1)}) %reduce-scatter.7.cloned.1.call-update) | async-done | bytes 221200 | tf_op jit(solution)/shard_map/reduce_scatter | solution.py:264
  682.4 122.5 %reduce-scatter.9.cloned.1.call-done = bf16[72,1536]{1,0:T(8,128)(2,1)} async-done(((bf16[2304,1536]{1,0:T(8,128)(2,1)}), bf16[72,1536]{1,0:T(8,128)(2,1)}) %reduce-scatter.9.cloned.1.call-update) | async-done | bytes 221200 | tf_op jit(solution)/shard_map/reduce_scatter | solution.py:264
  806.6 117.5 %reduce-scatter.13.cloned.1.call-done = bf16[72,1664]{1,0:T(8,128)(2,1)} async-done(((bf16[2304,1664]{1,0:T(8,128)(2,1)}), bf16[72,1664]{1,0:T(8,128)(2,1)}) %reduce-scatter.13.cloned.1.call-update) | async-done | bytes 239632
  (157 shorter events, 68.8 us)
Async XLA Ops:
  7.2 81.3 %all-gather.5.cloned.1.call-start = ((), (), s32[]{:S(2)}) async-start(), calls=%async_computation.4 | async-start | bytes 7907328 | tf_op jit(solution)/shard_map/all_gather | solution.py:253
  9.9 216.6 %all-gather.11.cloned.1.call-start = ((), (), s32[]{:S(2)}) async-start(), calls=%async_computation.7 | async-start | bytes 8110080 | tf_op jit(solution)/shard_map/all_gather | solution.py:253
  10.6 228.4 %all-gather.7.cloned.1.call-start = ((), (), s32[]{:S(2)}) async-start(), calls=%async_computation.5 | async-start | bytes 7299072 | tf_op jit(solution)/shard_map/all_gather | solution.py:253
  11.4 300.9 %all-gather.9.cloned.1.call-start = ((), (), s32[]{:S(2)}) async-start(), calls=%async_computation.6 | async-start | bytes 7299072 | tf_op jit(solution)/shard_map/all_gather | solution.py:253
  11.9 653.6 %reduce-scatter.11.cloned.1.call-start = ((), (), s32[]{:S(2)}) async-start(), calls=%async_computation.10 | async-start | bytes 8110080 | tf_op jit(solution)/shard_map/reduce_scatter | solution.py:264
  16.6 125.5 %copy-start.14 = (f32[512,32]{1,0:T(8,128)}, f32[512,32]{1,0:T(8,128)S(1)}, u32[]{:S(2)}) copy-start(f32[512,32]{1,0:T(8,128)S(1)} %get-tuple-element.132) | copy-start | bytes 196612
  92.2 4.3 copy-start.1
  96.6 5.9 copy-start.7
  102.4 6.0 copy-start.2
  106.9 2.2 copy-start.18
  108.4 3.4 copy-start.32
  109.1 2.8 copy-start.16
  111.8 2.0 copy-start.11
  119.3 5.2 copy-start.10
  137.1 3.9 copy-start.23
  142.1 12.2 %copy-start.13 = (bf16[2,512,3,64]{3,1,2,0:T(8,128)(2,1)S(1)}, bf16[2,512,3,64]{3,1,2,0:T(8,128)(2,1)}, u32[]{:S(2)}) copy-start(bf16[2,512,3,64]{3,1,2,0:T(8,128)(2,1)} %copy.184) | copy-start | bytes 1179652
  162.5 7.3 collective-permute-start
  226.1 100.7 %collective-permute-start.1 = (bf16[2,9,512,64]{2,3,1,0:T(8,128)(2,1)}, bf16[2,9,512,64]{2,3,1,0:T(8,128)(2,1)}, u32[]{:S(2)}, u32[]{:S(2)}) collective-permute-start(bf16[2,9,512,64]{2,3,1,0:T(8,128)(2,1)} %copy.152), channel_id=1, source_target_pairs={{0,1},{1,0},{2,3},{3,2},{4,5},{5,4},{6,7},{7,6},{8,9},{9,8},{10,11... | collective-permute-start | bytes 3538952 | tf_op jit(solution)/shard_map/ppermute | solution.py:236
  326.5 3.7 copy-start.3
  326.5 3.7 copy-start.24
  326.5 3.7 copy-start.26
  326.8 7.9 copy-start.28
  330.2 4.5 copy-start.30
  334.7 2.2 copy-start
  434.9 245.8 %reduce-scatter.7.cloned.1.call-start = ((), (), s32[]{:S(2)}) async-start(), calls=%async_computation.8 | async-start | bytes 7299072 | tf_op jit(solution)/shard_map/reduce_scatter | solution.py:264
  441.7 5.5 slice-start
  441.7 363.2 %reduce-scatter.9.cloned.1.call-start = ((), (), s32[]{:S(2)}) async-start(), calls=%async_computation.9 | async-start | bytes 7299072 | tf_op jit(solution)/shard_map/reduce_scatter | solution.py:264
  441.8 5.6 slice-start.1
  441.8 6.5 copy-start.17
  448.3 3.6 copy-start.25
  448.3 3.6 copy-start.27
  451.9 4.1 copy-start.5
  463.4 14.2 %collective-permute-start.2 = (bf16[2,9,512,64]{2,3,1,0:T(8,128)(2,1)}, bf16[2,9,512,64]{2,3,1,0:T(8,128)(2,1)}, u32[]{:S(2)}, u32[]{:S(2)}) collective-permute-start(bf16[2,9,512,64]{2,3,1,0:T(8,128)(2,1)} %copy.161), channel_id=1, source_target_pairs={{0,1},{1,0},{2,3},{3,2},{4,5},{5,4},{6,7},{7,6},{8,9},{9,8},{10,11... | collective-permute-start | bytes 3538952 | tf_op jit(solution)/shard_map/ppermute | solution.py:236
  477.5 446.6 %reduce-scatter.13.cloned.1.call-start = ((), (), s32[]{:S(2)}) async-start(), calls=%async_computation.11 | async-start | bytes 7907328
  526.0 2.9 copy-start.22
  528.8 1.4 copy-start.21
  535.8 5.2 copy-start.34
  535.8 5.2 copy-start.29
  535.8 5.2 copy-start.31
  540.7 15.3 %collective-permute-start.3 = (bf16[2,15,512,64]{2,3,1,0:T(8,128)(2,1)}, bf16[2,15,512,64]{2,3,1,0:T(8,128)(2,1)}, u32[]{:S(2)}, u32[]{:S(2)}) collective-permute-start(bf16[2,15,512,64]{2,3,1,0:T(8,128)(2,1)} %copy.164), channel_id=1, source_target_pairs={{0,1},{1,0},{2,3},{3,2},{4,5},{5,4},{6,7},{7,6},{8,9},{9,8},{10,11... | collective-permute-start | bytes 5898248 | tf_op jit(solution)/shard_map/ppermute | solution.py:236
  556.0 7.1 copy-start.15
  586.2 3.6 copy-start.6
  586.2 3.6 copy-start.12
  598.7 2.9 copy-start.9
  599.2 5.4 copy-start.20
  601.6 3.0 copy-start.4
  601.6 3.0 copy-start.8
  601.6 3.4 copy-start.19
  601.6 3.4 copy-start.33
Sparse Core Ops, SparseCore 0:
  11.5 76.9 all-gather.4
  91.4 73.9 all-gather.10
  168.3 70.6 all-gather.6
  241.8 70.5 all-gather.8
  435.0 121.7 reduce-scatter.10
  562.3 118.4 reduce-scatter.6
  686.4 118.4 reduce-scatter.8
  810.8 113.3 reduce-scatter.12

commit v2 on v1

--- a/solution.py
+++ b/solution.py
@@ -152,7 +152,7 @@
     )(me, heads, heads, heads, mixed, grads, lse)
 
 
-def mlp_body(n2, n2t, cot, res, wg, wu, wd, out, gn, gg, gu, gd, y):
+def mlp_body(n2, n2t, cot, res, wg, wu, wd, out, gn, ggu, gd, y):
     t = pl.program_id(0)
 
     @pl.when(t == 0)
@@ -174,8 +174,8 @@
     gdt = dg(hidden, cot[...], TN).astype(bf16)
     gd[0] = gdt[:, :half]
     gd[1] = gdt[:, half:]
-    gg[0] = dg(n2t[...], ggv, NN).astype(bf16)
-    gu[0] = dg(n2t[...], guv, NN).astype(bf16)
+    ggu[0, :, :FT] = dg(n2t[...], ggv, NN).astype(bf16)
+    ggu[0, :, FT:] = dg(n2t[...], guv, NN).astype(bf16)
     gn[...] += dg(ggv, wg[0], NT) + dg(guv, wu[0], NT)
 
     @pl.when(t == pl.num_programs(0) - 1)
@@ -183,31 +183,30 @@
         out[...] = y[...].astype(bf16)
 
 
-def mlp(n2, n2t, cot, res, wg, wu, wd):
+def mlp(n2, n2t, cot, res, wide, wd):
     rows = n2.shape[0]
-    cols = wg.shape[2]
+    cols = FF // 2
     per = cols // FT
     whole = lambda a: pl.BlockSpec(a.shape, lambda t: (0, 0), pipeline_mode=pl.Buffered(1))
-    col = pl.BlockSpec((1, D, FT), lambda t: (t // per, 0, t % per))
+    col = lambda first, width: pl.BlockSpec((1, D, width), lambda t: (t // per, 0, first + t % per))
     row = pl.BlockSpec((2, FT, D // 2), lambda t: (0, t, 0))
     one = lambda: pl.BlockSpec((rows, D), lambda t: (0, 0), pipeline_mode=pl.Buffered(1))
     return pl.pallas_call(
         mlp_body,
         grid=(FF // FT,),
-        in_specs=[whole(n2), whole(n2t), whole(cot), whole(res), col, col, row],
-        out_specs=[one(), one(), col, col, row],
+        in_specs=[whole(n2), whole(n2t), whole(cot), whole(res), col(0, FT), col(per, FT), row],
+        out_specs=[one(), one(), col(0, 2 * FT), row],
         out_shape=[
             jax.ShapeDtypeStruct((rows, D), bf16),
             jax.ShapeDtypeStruct((rows, D), f32),
-            jax.ShapeDtypeStruct(wg.shape, bf16),
-            jax.ShapeDtypeStruct(wu.shape, bf16),
+            jax.ShapeDtypeStruct((2, D, 2 * cols), bf16),
             jax.ShapeDtypeStruct(wd.shape, bf16),
         ],
         scratch_shapes=[pltpu.VMEM((rows, D), f32)],
         compiler_params=pltpu.CompilerParams(vmem_limit_bytes=VMEM_BYTES),
         cost_estimate=pl.CostEstimate(flops=65 * 10**9, bytes_accessed=60 * 10**6, transcendentals=3 * 10**6),
         name="mlp",
-    )(n2, n2t, cot, res, wg, wu, wd)
+    )(n2, n2t, cot, res, wide, wide, wd)
 
 
 def turn(u, shift, heads, inverse):
@@ -247,22 +246,47 @@
 BOTH = ("dp", "seq")
 
 
-def fetch(shards):
+def fetch(w):
+    g = lax.all_gather(w, BOTH, axis=0, tiled=True)
+    g = g.reshape(lax.axis_size("dp"), 2, *w.shape)
+    return jnp.swapaxes(g, 0, 1).reshape(2, -1, w.shape[1])
+
+
+def reduce_all(g):
+    n = lax.axis_size("dp")
+    t = jnp.swapaxes(g.reshape(2, n, -1, g.shape[2]), 0, 1).reshape(-1, g.shape[2])
+    return lax.psum_scatter(t, BOTH, scatter_dimension=0, tiled=True)
+
+
+def add(a, b):
+    return a.astype(f32) + b.astype(f32)
+
+
+def reduce_halving(g, me):
+    n = lax.axis_size("dp")
+    bits = n.bit_length() - 1
+    dp = lax.axis_index("dp")
+    mine = lax.dynamic_index_in_dim(g, me, 0, keepdims=False)
+    theirs = lax.dynamic_index_in_dim(g, 1 - me, 0, keepdims=False)
+    both = add(mine, swap(theirs)).astype(bf16)
+    cols = g.shape[2]
+    cut = cols // 256 * 128
     out = []
-    for w in shards:
-        g = lax.all_gather(w, BOTH, axis=0, tiled=True)
-        g = g.reshape(lax.axis_size("dp"), 2, *w.shape)
-        out.append(jnp.swapaxes(g, 0, 1).reshape(2, -1, w.shape[1]))
-    return out
-
-
-def reduce_all(grads):
-    out = []
-    for g in grads:
-        n = lax.axis_size("dp")
-        t = jnp.swapaxes(g.reshape(2, n, -1, g.shape[2]), 0, 1).reshape(-1, g.shape[2])
-        out.append(lax.psum_scatter(t, BOTH, scatter_dimension=0, tiled=True))
-    return out
+    for part, order in ((both[:, :cut], [0, 1]), (both[:, cut:], [1, 0])):
+        left = list(range(bits))[::-1]
+        a = part.reshape(*[2] * bits, -1, part.shape[1])
+        for bit in order + list(range(2, bits)):
+            axis = left.index(bit)
+            left.remove(bit)
+            mybit = (dp >> bit) & 1
+            keep = lax.dynamic_index_in_dim(a, mybit, axis, keepdims=False)
+            send = lax.dynamic_index_in_dim(a, 1 - mybit, axis, keepdims=False)
+            got = lax.ppermute(send, "dp", [(i, i ^ (1 << bit)) for i in range(n)])
+            a = add(keep, got)
+            if left:
+                a = a.astype(bf16)
+        out.append(a)
+    return jnp.concatenate(out, 1)
 
 
 def local(
@@ -283,15 +307,15 @@
     me = lax.axis_index("seq")
     shift = me * piece
     me_arr = jnp.full((1,), me, jnp.int32)
-    gains = jnp.pad(jnp.stack([gain_attn, gain_mlp], 1), ((0, 0), (0, 126)))
-    pack = jnp.concatenate([w_query, w_key, w_value, w_out, gains], 1)
-    (full,) = fetch([pack])
-    full_gate, full_up, full_down = fetch([w_gate, w_up, w_down])
-    gain_one = full[0, :, QKV + D // 2].astype(f32)
-    gain_two = full[0, :, QKV + D // 2 + 1].astype(f32)
+    gains = jnp.pad(jnp.stack([gain_attn, gain_mlp], 1), ((0, 0), (0, 62)))
+    full = fetch(jnp.concatenate([w_query, w_key, w_value, gains], 1))
+    wide = fetch(jnp.concatenate([w_gate, w_up, w_out], 1))
+    full_down = fetch(w_down)
+    gain_one = full[0, :, QKV].astype(f32)
+    gain_two = full[0, :, QKV + 1].astype(f32)
     w_mine = lax.dynamic_index_in_dim(full, me, 0, keepdims=False)[:, :QKV]
     w_theirs = lax.dynamic_index_in_dim(full, 1 - me, 0, keepdims=False)[:, :QKV]
-    full_out = jnp.concatenate([full[0, :, QKV : QKV + D // 2], full[1, :, QKV : QKV + D // 2]], 1)
+    full_out = jnp.concatenate([wide[0, :, FF:], wide[1, :, FF:]], 1)
 
     floats = layer_input.reshape(tokens, D).astype(f32)
     cot = cotangent.reshape(tokens, D)
@@ -311,9 +335,9 @@
     residual = floats + jnp.dot(merged, full_out, preferred_element_type=f32)
     scale_mlp = lax.rsqrt(jnp.mean(residual * residual, -1, keepdims=True) + epsilon)
     n2 = (residual * scale_mlp * gain_two).astype(bf16)
-    layer_out, grad_n2, grad_gate, grad_up, grad_down = mlp(
-        n2, n2.T, cot, residual, full_gate, full_up, full_down
-    )
+    layer_out, grad_n2, grad_wide, grad_down = mlp(n2, n2.T, cot, residual, wide, full_down)
+    r_wide = reduce_all(grad_wide)
+    r_down = reduce_halving(grad_down, me)
     sum_gain_mlp = jnp.sum(grad_n2 * residual * scale_mlp, 0)
     grad_residual = cot.astype(f32) + norm_back(grad_n2, residual, scale_mlp, gain_two)
     grad_low = grad_residual.astype(bf16)
@@ -338,20 +362,16 @@
     sum_gain_attn = jnp.sum(grad_n1 * floats * scale_attn, 0)
     grad_input = (grad_residual + norm_back(grad_n1, floats, scale_attn, gain_one)).astype(bf16)
     grad_qkv = in_order(me, weight_grad(lin_mine)[None], weight_grad(lin_theirs)[None], 0)
-    sums = jnp.pad(jnp.stack([sum_gain_attn, sum_gain_mlp], 1), ((0, 0), (0, 126))).astype(bf16)
+    sums = jnp.pad(jnp.stack([sum_gain_attn, sum_gain_mlp], 1), ((0, 0), (0, 62))).astype(bf16)
+    grad_pack = jnp.concatenate([grad_qkv, jnp.stack([sums, sums])], 2)
+    r_pack = reduce_halving(grad_pack, me)
     go = grad_out.astype(bf16)
-    grad_pack = jnp.concatenate(
-        [
-            grad_qkv,
-            jnp.stack([go[:, : D // 2], go[:, D // 2 :]]),
-            jnp.stack([sums, sums]),
-        ],
-        2,
-    )
-    r_gate, r_up, r_down = reduce_all([grad_gate, grad_up, grad_down])
-    (r_pack,) = reduce_all([grad_pack])
-    r_pack = r_pack.astype(f32)
-    a, b, c, d = HQ * HEAD_SIZE, (HQ + HK) * HEAD_SIZE, QKV, QKV + D // 2
+    r_out = reduce_halving(jnp.stack([go[:, : D // 2], go[:, D // 2 :]]), me)
+    r_gate, r_up = [
+        a.reshape(a.shape[0], -1).astype(f32)
+        for a in jnp.split(r_wide.reshape(-1, FF // 2 // FT, 2, FT), 2, 2)
+    ]
+    a, b, c = HQ * HEAD_SIZE, (HQ + HK) * HEAD_SIZE, QKV
     shape = layer_input.shape
     return (
         layer_out.reshape(shape),
@@ -359,12 +379,12 @@
         r_pack[:, :a],
         r_pack[:, a:b],
         r_pack[:, b:c],
-        r_pack[:, c:d],
-        r_pack[:, d],
-        r_gate.astype(f32),
-        r_up.astype(f32),
-        r_down.astype(f32),
-        r_pack[:, d + 1],
+        r_out,
+        r_pack[:, c],
+        r_gate,
+        r_up,
+        r_down,
+        r_pack[:, c + 1],
     )
 
 

time: 948 us -> 746 us (0.79)
  waiting for transfers between devices: 400 us -> 168 us
  starting transfers between devices: 1.34 us -> 36.4 us
  other arithmetic: 98.3 us -> 124 us
  local copies, waits for them, and re-layouts: 217 us -> 195 us
    reduce_scatter x3 -> x1, waiting for transfers between devices: 136 us -> 0.01 us  [reduce_all(): return lax.psum_scatter(t, BOTH, scatter_dimension=0, tiled=True)]
    unnamed x9 -> x4, waiting for transfers between devices: 119 us -> 0.74 us
    ppermute x0 -> x24, waiting for transfers between devices: none -> 67.8 us  [reduce_halving(): got = lax.ppermute(send, 'dp', [(i, i ^ 1 << bit) for i in range(n)])]
    all_gather x4 -> x3, waiting for transfers between devices: 144 us -> 99.3 us  [fetch(): g = lax.all_gather(w, BOTH, axis=0, tiled=True)]
    ppermute x0 -> x24, starting transfers between devices: none -> 35 us  [reduce_halving(): got = lax.ppermute(send, 'dp', [(i, i ^ 1 << bit) for i in range(n)])]
    transpose x6 -> x2, local copies, waits for them, and re-layouts: 34.2 us -> 5.45 us  [the longest x1 2.86 us: fetch(): return jnp.swapaxes(g, 0, 1).reshape(2, -1, w.shape[1])]
    concatenate x2 -> x0, local copies, waits for them, and re-layouts: 14.5 us -> none  [the longest x1 12.7 us: local(): jnp.concatenate([grad_qkv, jnp.stack([go[:, :D // 2], go[:, D // 2:]]), j...]
    dynamic_slice x0 -> x8, local copies, waits for them, and re-layouts: none -> 13.7 us  [the longest x2 10.3 us: reduce_halving(): theirs = lax.dynamic_index_in_dim(g, 1 - me, 0, keepdims=False)]
  transfers between devices with their start and end apart: 12 -> 35, of which waited for: 6 -> 22; matrix products, arithmetic and copies ran while one was open for 34% -> 39% of each run, Pallas kernels for 8% -> 10%
where the time goes in v2:
time: 746 us; the launch traced here: 735 us
  local copies, waits for them, and re-layouts  195 us (26%)
  waiting for transfers between devices  168 us (23%)
  Pallas kernels  162 us (22%)
  other arithmetic  124 us (17%)
  starting transfers between devices  36.4 us (5%)
  matrix products  36.1 us (5%)
  between operations  15 us (2%)
    all_gather x3, waiting for transfers between devices, fetch(): g = lax.all_gather(w, BOTH, axis=0, tiled=True)  99.3 us
    pallas_call x1, Pallas kernels, mlp(): pl.pallas_call(mlp_body, grid=(FF // FT,), in_specs=[whole(n2), whole(n2t...  86.9 us
    ppermute x24, waiting for transfers between devices, reduce_halving(): got = lax.ppermute(send, 'dp', [(i, i ^ 1 << bit) for i in range(n)])  67.8 us
    unnamed x118, local copies, waits for them, and re-layouts  50.1 us
    pallas_call x1, Pallas kernels, attend_back(): pl.pallas_call(bwd_body, grid_spec=pltpu.PrefetchScalarGridSpec(num_scala...  39.5 us
    pallas_call x1, Pallas kernels, attend(): pl.pallas_call(fwd_body, grid_spec=pltpu.PrefetchScalarGridSpec(num_scala...  35.2 us
    ppermute x24, starting transfers between devices, reduce_halving(): got = lax.ppermute(send, 'dp', [(i, i ^ 1 << bit) for i in range(n)])  35 us
    reshape x2, local copies, waits for them, and re-layouts, fetch(): g = g.reshape(lax.axis_size('dp'), 2, *w.shape)  15.4 us
  transfers between devices with their start and end apart: 35, of which 22 were waited for; matrix products, arithmetic and copies ran while one was open for 39% of the time, Pallas kernels for 10%

profile of v2, /device:TPU:0, one launch (start us, length us, event | category | flops | bytes accessed | tf_op | source)
XLA Modules:
  0.0 735.4 jit_solution(15826199528845449796)
XLA Ops:
  15.1 62.7 %all-gather.4.cloned.1.call-done = bf16[2304,1024]{1,0:T(8,128)(2,1)} async-done(((bf16[72,1024]{1,0:T(8,128)(2,1)}), bf16[2304,1024]{1,0:T(8,128)(2,1)}) %all-gather.4.cloned.1.call-update) | async-done | bytes 4718608 | tf_op jit(solution)/shard_map/all_gather | solution.py:250
  77.8 2.9 copy.195
  82.9 3.0 slice_bitcast_fusion.4
  86.5 4.3 copy.196
  93.2 2.7 fusion.18
  98.3 4.0 copy.237
  102.3 5.2 copy.238
  109.9 5.1 fusion.16
  116.1 4.0 copy.240
  120.0 4.0 copy.241
  125.2 12.9 %subtract_convert_fusion.1 = (bf16[2,512,12,32]{3,1,2,0:T(8,128)(2,1)S(1)}, bf16[2,512,12,32]{3,1,2,0:T(8,128)(2,1)}, bf16[2,512,12,32]{3,1,2,0:T(8,128)(2,1)S(1)}, bf16[2,512,12,32]{3,1,2,0:T(8,128)(2,1)S(1)}) fusion(f32[2,512,12,32]{3,1,2,0:T(8,128)} %copy.238, f32[2,512,12,32]{3,1,2,0:T(8,128)} %copy.237, f32[512,32]{1,0:T(8,128)} %get-tuple-element.148, ...), kind=kLoop, calls=%fused_computation.14 | loop fusion | flops 6291456 | bytes 9568256 | tf_op jit(solution)/shard_map/convert.49
  138.1 14.3 %maximum_bitcast_fusion.1 = bf16[2,15,512,64]{3,2,1,0:T(8,128)(2,1)} fusion(bf16[2,512,3,64]{3,1,2,0:T(8,128)(2,1)S(1)} %copy-done.19, bf16[2,512,12,32]{3,1,2,0:T(8,128)(2,1)S(1)} %get-tuple-element.139, bf16[2,512,12,32]{3,1,2,0:T(8,128)(2,1)S(1)} %get-tuple-element.140), kind=kLoop, calls=%fused_computation.45 | loop fusion | flops 5898240 | bytes 3932160 | tf_op jit(solution)/shard_map/transpose | solution.py:327
  152.3 4.8 copy.204
  159.7 4.7 maximum_bitcast_fusion
  164.5 4.8 copy.205
  169.2 8.2 %pad_maximum_fusion.q.k.v = bf16[2,2,15,512,64]{4,3,2,1,0:T(8,128)(2,1)} fusion(bf16[1,2,15,512,64]{4,3,2,1,0:T(8,128)(2,1)} %bitcast.320, bf16[1,2,15,512,64]{4,3,2,1,0:T(8,128)(2,1)} %maximum_bitcast_fusion), kind=kLoop, calls=%fused_computation | loop fusion | flops 1966080 | bytes 7864320 | tf_op jit(solution)/shard_map/stack | solution.py:330
  177.4 35.2 %attend.1 = (bf16[2,2,9,512,64]{4,3,2,1,0:T(8,128)(2,1)}, f32[2,9,1024,128]{3,2,1,0:T(8,128)}) custom-call(s32[1]{0:T(128)} %bitcast.1.me, bf16[2,2,15,512,64]{4,3,2,1,0:T(8,128)(2,1)} %pad_maximum_fusion.q.k.v, bf16[2,2,15,512,64]{4,3,2,1,0:T(8,128)(2,1)} %pad_maximum_fusion.q.k.v, bf16[2,2,15,512,64]{4,3,2,1,0:T(8,128)(2,1)} %pad_maximum_fusion.q.k.v), custom_call_target="tpu_custom_call" | custom-call | flops 24000000000 | bytes 20000000 | tf_op jit(solution)/shard_map/attend/pallas_call | solution.py:100
  212.6 4.2 slice_bitcast_fusion.3
  216.8 4.3 copy.207
  224.6 2.6 copy.208
  227.5 7.3 copy.210
  234.8 36.6 %all-gather.6.cloned.1.call-done = bf16[2304,3648]{1,0:T(8,128)(2,1)} async-done(((bf16[72,3648]{1,0:T(8,128)(2,1)}), bf16[2304,3648]{1,0:T(8,128)(2,1)}) %all-gather.6.cloned.1.call-update) | async-done | bytes 16810000 | tf_op jit(solution)/shard_map/all_gather | solution.py:250
  271.3 8.1 %copy.209 = bf16[16,2,72,3648]{3,2,0,1:T(8,128)(2,1)S(1)} copy(bf16[16,2,72,3648]{3,2,1,0:T(8,128)(2,1)} %bitcast.318) | data formatting | bytes 33619968 | tf_op jit(solution)/shard_map/reshape | solution.py:251
  279.7 6.2 copy-done.1
  285.9 4.6 multiply_reduce_fusion.2
  294.5 2.6 copy.211.n2t
  297.1 86.9 %mlp.1 = (bf16[1024,1152]{1,0:T(8,128)(2,1)}, f32[1024,1152]{1,0:T(8,128)}, bf16[2,1152,3072]{2,1,0:T(8,128)(2,1)}, bf16[2,3072,576]{2,1,0:T(8,128)(2,1)}) custom-call(bf16[1024,1152]{1,0:T(8,128)(2,1)} %multiply_convert_fusion.n2, bf16[1152,1024]{1,0:T(8,128)(2,1)} %copy.211.n2t, bf16[1024,1152]{1,0:T(8,128)(2,1)} %bitcast.346, f32[1024,1152]{1,0:T(8,128)} %copy-done, ...), custom_call_target="tpu_custom_call" | custom-call | flops 65000001536 | bytes 60000000 | tf_op jit(solution)/shard_map/mlp/pallas_call | solution.py:194
  384.1 5.0 multiply_reduce_fusion
  390.6 2.8 subtract_add_fusion
  393.4 4.8 convolution_convert_fusion
  398.2 4.1 convolution_convert_fusion.1
  405.2 3.3 reshape.408
  410.0 4.4 constant_dynamic-slice_fusion.4
  414.3 6.0 copy.228
  427.0 3.3 reshape.407
  430.3 3.2 copy.213
  433.5 10.5 %copy.227 = bf16[2,16,72,3072]{3,2,0,1:T(8,128)(2,1)} copy(bf16[2,16,72,3072]{3,2,1,0:T(8,128)(2,1)} %bitcast.321) | data formatting | bytes 28311552 | tf_op jit(solution)/shard_map/reshape | solution.py:257
  444.0 3.7 copy.216
  447.8 5.7 pad_maximum_fusion.1.do
  453.5 39.5 %attend_back.1 = (bf16[2,2,9,512,64]{4,3,2,1,0:T(8,128)(2,1)}, bf16[2,2,3,512,64]{4,3,2,1,0:T(8,128)(2,1)}, bf16[2,2,3,512,64]{4,3,2,1,0:T(8,128)(2,1)}) custom-call(s32[1]{0:T(128)} %bitcast.1.me, bf16[2,2,15,512,64]{4,3,2,1,0:T(8,128)(2,1)} %pad_maximum_fusion.q.k.v, bf16[2,2,15,512,64]{4,3,2,1,0:T(8,128)(2,1)} %pad_maximum_fusion.q.k.v, ...), custom_call_target="tpu_custom_call" | custom-call | flops 27000000512 | bytes 40000000 | tf_op jit(solution)/shard_map/attend_back/pallas_call | solution.py:127
  493.0 6.1 constant_dynamic-update-slice_fusion.2
  508.3 8.9 %slice_bitcast_fusion = (bf16[2,15,512,64]{3,2,1,0:T(8,128)(2,1)}, f32[2,512,15,64]{3,1,2,0:T(8,128)}) fusion(bf16[2,2,15,512,64]{4,3,2,1,0:T(8,128)(2,1)} %constant_dynamic-update-slice_fusion), kind=kLoop, calls=%fused_computation.42 | loop fusion | flops 983040 | bytes 9830400 | tf_op jit(solution)/shard_map/squeeze | solution.py:356
  517.2 4.7 copy.218
  525.9 4.9 collective-permute-done.15
  533.1 6.4 collective-permute-done.16
  539.5 3.9 collective-permute-done.19
  550.8 2.9 collective-permute-done.21
  554.3 5.6 copy.219
  561.5 13.0 %multiply_subtract_fusion = (bf16[2,512,12,32]{3,1,2,0:T(8,128)(2,1)S(1)}, bf16[2,512,12,32]{3,1,2,0:T(8,128)(2,1)S(1)}, bf16[2,512,12,32]{3,1,2,0:T(8,128)(2,1)S(1)}, bf16[2,512,12,32]{3,1,2,0:T(8,128)(2,1)}) fusion(f32[2,512,15,64]{3,1,2,0:T(8,128)} %bitcast.307, f32[512,32]{1,0:T(8,128)} %get-tuple-element.147, f32[512,32]{1,0:T(8,128)S(1)} %copy-done.21, ...), kind=kLoop, calls=%fused_computation.8 | loop fusion | flops 6291456 | bytes 9568256 | tf_op jit(solution)/shard_map/sub | solution.py:222
  574.5 3.1 maximum_convert_fusion.1
  577.7 6.7 copy.220
  584.4 3.5 copy.251
  588.0 3.6 maximum_convert_fusion
  591.5 5.6 copy.217
  598.9 3.0 fusion.21
  602.0 5.9 fusion.11
  607.9 2.9 fusion.13
  610.9 2.9 fusion.12
  616.3 6.1 copy.229
  622.4 4.3 fusion
  637.2 9.9 %collective-permute-done.23 = bf16[2,2,2,192,256]{4,3,0,1,2:T(8,128)(2,1)} collective-permute-done((bf16[2,2,2,192,256]{4,3,0,1,2:T(8,128)(2,1)}, bf16[2,2,2,192,256]{4,3,0,1,2:T(8,128)(2,1)}, u32[]{:S(2)}, u32[]{:S(2)}) %collective-permute-start.23) | collective-permute-done | bytes 786464 | tf_op jit(solution)/shard_map/ppermute | solution.py:284
  650.4 11.6 %collective-permute-done.27 = bf16[2,2,2,192,320]{4,3,0,1,2:T(8,128)(2,1)} collective-permute-done((bf16[2,2,2,192,320]{4,3,0,1,2:T(8,128)(2,1)}, bf16[2,2,2,192,320]{4,3,0,1,2:T(8,128)(2,1)}, u32[]{:S(2)}, u32[]{:S(2)}) %collective-permute-start.27) | collective-permute-done | bytes 983072 | tf_op jit(solution)/shard_map/ppermute | solution.py:284
  668.0 5.9 collective-permute-done.25
  692.0 4.7 collective-permute-done.30
  (289 shorter events, 141.6 us)
Async XLA Ops:
  7.2 5.6 copy-start.3
  7.2 70.7 %all-gather.4.cloned.1.call-start = ((), (), s32[]{:S(2)}) async-start(), calls=%async_computation.1 | async-start | bytes 4866048 | tf_op jit(solution)/shard_map/all_gather | solution.py:250
  9.9 217.5 %all-gather.8.cloned.1.call-start = ((), (), s32[]{:S(2)}) async-start(), calls=%async_computation.3 | async-start | bytes 8110080 | tf_op jit(solution)/shard_map/all_gather | solution.py:250
  10.7 260.7 %all-gather.6.cloned.1.call-start = ((), (), s32[]{:S(2)}) async-start(), calls=%async_computation.2 | async-start | bytes 17639424 | tf_op jit(solution)/shard_map/all_gather | solution.py:250
  12.7 710.5 %reduce-scatter.2.cloned.1.call-start = ((), (), s32[]{:S(2)}) async-start(), calls=%async_computation.4 | async-start | bytes 14598144 | tf_op jit(solution)/shard_map/reduce_scatter | solution.py:258
  15.1 110.0 %copy-start.20 = (f32[512,32]{1,0:T(8,128)}, f32[512,32]{1,0:T(8,128)S(1)}, u32[]{:S(2)}) copy-start(f32[512,32]{1,0:T(8,128)S(1)} %get-tuple-element.149) | copy-start | bytes 196612
  82.9 3.6 copy-start.14
  102.3 5.2 copy-start.16
  120.0 4.0 copy-start.28
  125.2 12.9 %copy-start.19 = (bf16[2,512,3,64]{3,1,2,0:T(8,128)(2,1)S(1)}, bf16[2,512,3,64]{3,1,2,0:T(8,128)(2,1)}, u32[]{:S(2)}) copy-start(bf16[2,512,3,64]{3,1,2,0:T(8,128)(2,1)} %copy.242) | copy-start | bytes 1179652
  157.1 7.3 collective-permute-start
  221.1 3.4 collective-permute-start.1
  224.2 61.7 %copy-start.34 = (bf16[72,8,2,512]{3,1,2,0:T(8,128)(2,1)}, bf16[72,8,2,512]{3,1,2,0:T(8,128)(2,1)S(1)}, u32[]{:S(2)}) copy-start(bf16[72,8,2,512]{3,1,2,0:T(8,128)(2,1)S(1)} %copy.247) | copy-start | bytes 3538948
  279.4 6.5 copy-start.1
  279.4 6.5 copy-start.4
  279.7 10.8 %copy-start.29 = (bf16[1152,576]{1,0:T(8,128)(2,1)}, bf16[1152,576]{1,0:T(8,128)(2,1)S(1)}, u32[]{:S(2)}) copy-start(bf16[1152,576]{1,0:T(8,128)(2,1)S(1)} %get-tuple-element.105) | copy-start | bytes 3981316
  279.7 10.8 %copy-start.31 = (bf16[1152,576]{1,0:T(8,128)(2,1)}, bf16[1152,576]{1,0:T(8,128)(2,1)S(1)}, u32[]{:S(2)}) copy-start(bf16[1152,576]{1,0:T(8,128)(2,1)S(1)} %get-tuple-element.106) | copy-start | bytes 3981316
  384.0 5.1 slice-start
  384.0 5.1 slice-start.1
  384.0 6.5 copy-start.7
  384.0 6.5 copy-start.42
  393.4 4.9 copy-start.6
  393.4 4.8 copy-start.30
  393.4 4.8 copy-start.32
  409.7 34.3 %collective-permute-start.2 = (bf16[2,9,512,64]{2,3,1,0:T(8,128)(2,1)}, bf16[2,9,512,64]{2,3,1,0:T(8,128)(2,1)}, u32[]{:S(2)}, u32[]{:S(2)}) collective-permute-start(bf16[2,9,512,64]{2,3,1,0:T(8,128)(2,1)} %copy.215), channel_id=1, source_target_pairs={{0,1},{1,0},{2,3},{3,2},{4,5},{5,4},{6,7},{7,6},{8,9},{9,8},{10,11... | collective-permute-start | bytes 3538952 | tf_op jit(solution)/shard_map/ppermute | solution.py:235
  420.3 196.0 %collective-permute-start.22 = (bf16[3072,576]{0,1:T(8,128)(2,1)}, bf16[3072,576]{0,1:T(8,128)(2,1)}, u32[]{:S(2)}, u32[]{:S(2)}) collective-permute-start(bf16[3072,576]{0,1:T(8,128)(2,1)} %bitcast.338), channel_id=1, source_target_pairs={{0,1},{1,0},{2,3},{3,2},{4,5},{5,4},{6,7},{7,6},{8,9},{9,8},{10,11... | collective-permute-start | bytes 10616840 | tf_op jit(solution)/shard_map/ppermute | solution.py:235
  425.3 77.5 %collective-permute-start.13 = (bf16[1152,576]{0,1:T(8,128)(2,1)}, bf16[1152,576]{0,1:T(8,128)(2,1)}, u32[]{:S(2)}, u32[]{:S(2)}) collective-permute-start(bf16[1152,576]{0,1:T(8,128)(2,1)} %fusion.25), channel_id=1, source_target_pairs={{0,1},{1,0},{2,3},{3,2},{4,5},{5,4},{6,7},{7,6},{8,9},{9,8},{10,11... | collective-permute-start | bytes 3981320 | tf_op jit(solution)/shard_map/ppermute | solution.py:235
  493.0 6.2 copy-start.27
  505.2 19.2 %collective-permute-start.14 = (bf16[2,2,2,72,256]{4,3,2,1,0:T(8,128)(2,1)S(1)}, bf16[2,2,2,72,256]{4,3,2,1,0:T(8,128)(2,1)S(1)}, u32[]{:S(2)}, u32[]{:S(2)}) collective-permute-start(bf16[2,2,2,72,256]{4,3,2,1,0:T(8,128)(2,1)S(1)} %dynamic-slice_bitcast_fusion.8), channel_id=1, source_target_pairs={{0,2},{2,0},{4,6},{6,4},{8,10},{10,8},{12,14},{14,12},{16,18},{18,... | collective-permute-start | bytes 884744 | tf_op jit(solution)/shard_map/ppermute | solution.py:284
  507.4 18.4 %collective-permute-start.18 = (bf16[2,2,2,72,320]{4,3,2,1,0:T(8,128)(2,1)S(1)}, bf16[2,2,2,72,320]{4,3,2,1,0:T(8,128)(2,1)S(1)}, u32[]{:S(2)}, u32[]{:S(2)}) collective-permute-start(bf16[2,2,2,72,320]{4,3,2,1,0:T(8,128)(2,1)S(1)} %dynamic-slice_bitcast_fusion.5), channel_id=1, source_target_pairs={{0,4},{2,6},{4,0},{6,2},{8,12},{10,14},{12,8},{14,10},{16,20},{18,... | collective-permute-start | bytes 1105928 | tf_op jit(solution)/shard_map/ppermute | solution.py:284
  521.9 32.4 %collective-permute-start.3 = (bf16[2,15,512,64]{2,3,1,0:T(8,128)(2,1)}, bf16[2,15,512,64]{2,3,1,0:T(8,128)(2,1)}, u32[]{:S(2)}, u32[]{:S(2)}) collective-permute-start(bf16[2,15,512,64]{2,3,1,0:T(8,128)(2,1)} %copy.218), channel_id=1, source_target_pairs={{0,1},{1,0},{2,3},{3,2},{4,5},{5,4},{6,7},{7,6},{8,9},{9,8},{10,11... | collective-permute-start | bytes 5898248 | tf_op jit(solution)/shard_map/ppermute | solution.py:235
  524.5 6.3 collective-permute-start.15
  530.8 8.7 %collective-permute-start.16 = (bf16[2,72,256]{2,1,0:T(8,128)(2,1)S(1)}, bf16[2,72,256]{2,1,0:T(8,128)(2,1)S(1)}, u32[]{:S(2)}, u32[]{:S(2)}) collective-permute-start(bf16[2,72,256]{2,1,0:T(8,128)(2,1)S(1)} %dynamic-slice_bitcast_fusion.19), channel_id=1, source_target_pairs={{0,8},{2,10},{4,12},{6,14},{8,0},{10,2},{12,4},{14,6},{16,24},{18,... | collective-permute-start | bytes 221192 | tf_op jit(solution)/shard_map/ppermute | solution.py:284
  531.2 12.2 %collective-permute-start.19 = (bf16[2,2,72,320]{3,2,1,0:T(8,128)(2,1)S(1)}, bf16[2,2,72,320]{3,2,1,0:T(8,128)(2,1)S(1)}, u32[]{:S(2)}, u32[]{:S(2)}) collective-permute-start(bf16[2,2,72,320]{3,2,1,0:T(8,128)(2,1)S(1)} %dynamic-slice_bitcast_fusion.11), channel_id=1, source_target_pairs={{0,2},{2,0},{4,6},{6,4},{8,10},{10,8},{12,14},{14,12},{16,18},{18,... | collective-permute-start | bytes 552968 | tf_op jit(solution)/shard_map/ppermute | solution.py:284
  543.6 4.9 collective-permute-start.20
  545.4 5.4 collective-permute-start.17
  548.5 5.1 collective-permute-start.21
  554.3 7.2 copy-start.21
  601.9 6.0 copy-start.23
  626.8 7.7 %slice-start.4 = ((s8[4423680]{0:T(1024)(128)(4,1)}), s8[4194304]{0:T(1024)(128)(4,1)S(1)}, s32[]{:S(2)}) async-start(s8[4423680]{0:T(1024)(128)(4,1)} %bitcast.316), calls=%async_computation.9 | async-start | bytes 8388608
  628.7 5.8 slice-start.5
  629.7 17.5 %collective-permute-start.23 = (bf16[2,2,2,192,256]{4,3,0,1,2:T(8,128)(2,1)}, bf16[2,2,2,192,256]{4,3,0,1,2:T(8,128)(2,1)}, u32[]{:S(2)}, u32[]{:S(2)}) collective-permute-start(bf16[2,2,2,192,256]{4,3,0,1,2:T(8,128)(2,1)} %bitcast.302), channel_id=1, source_target_pairs={{0,2},{2,0},{4,6},{6,4},{8,10},{10,8},{12,14},{14,12},{16,18},{18,... | collective-permute-start | bytes 2359304 | tf_op jit(solution)/shard_map/ppermute | solution.py:284
  632.9 29.2 %collective-permute-start.27 = (bf16[2,2,2,192,320]{4,3,0,1,2:T(8,128)(2,1)}, bf16[2,2,2,192,320]{4,3,0,1,2:T(8,128)(2,1)}, u32[]{:S(2)}, u32[]{:S(2)}) collective-permute-start(bf16[2,2,2,192,320]{4,3,0,1,2:T(8,128)(2,1)} %bitcast.301), channel_id=1, source_target_pairs={{0,4},{2,6},{4,0},{6,2},{8,12},{10,14},{12,8},{14,10},{16,20},{18,... | collective-permute-start | bytes 2949128 | tf_op jit(solution)/shard_map/ppermute | solution.py:284
  636.9 41.8 %slice-start.7 = ((s8[4718592]{0:T(1024)(128)(4,1)}), s8[4194304]{0:T(1024)(128)(4,1)S(1)}, s32[]{:S(2)}) async-start(s8[4718592]{0:T(1024)(128)(4,1)} %bitcast.329), calls=%async_computation.12 | async-start | bytes 8388608
  637.1 47.1 %collective-permute-start.4 = (bf16[1152,1024]{0,1:T(8,128)(2,1)S(1)}, bf16[1152,1024]{0,1:T(8,128)(2,1)S(1)}, u32[]{:S(2)}, u32[]{:S(2)}) collective-permute-start(bf16[1152,1024]{0,1:T(8,128)(2,1)S(1)} %dynamic-slice_bitcast_fusion), channel_id=1, source_target_pairs={{0,1},{1,0},{2,3},{3,2},{4,5},{5,4},{6,7},{7,6},{8,9},{9,8},{10,11... | collective-permute-start | bytes 7077896 | tf_op jit(solution)/shard_map/ppermute | solution.py:235
  647.1 31.6 %slice-start.2 = ((s8[4718592]{0:T(1024)(128)(4,1)}), s8[4194304]{0:T(1024)(128)(4,1)S(1)}, s32[]{:S(2)}) async-start(s8[4718592]{0:T(1024)(128)(4,1)} %bitcast.314), calls=%async_computation.7 | async-start | bytes 8388608
  648.7 18.4 %collective-permute-start.24 = (bf16[2,2,192,256]{3,2,0,1:T(8,128)(2,1)S(1)}, bf16[2,2,192,256]{3,2,0,1:T(8,128)(2,1)S(1)}, u32[]{:S(2)}, u32[]{:S(2)}) collective-permute-start(bf16[2,2,192,256]{3,2,0,1:T(8,128)(2,1)S(1)} %dynamic-slice_bitcast_fusion.6), channel_id=1, source_target_pairs={{0,4},{2,6},{4,0},{6,2},{8,12},{10,14},{12,8},{14,10},{16,20},{18,... | collective-permute-start | bytes 1179656 | tf_op jit(solution)/shard_map/ppermute | solution.py:284
  662.0 16.7 %slice-start.3 = ((s8[4718592]{0:T(1024)(128)(4,1)}), s8[524288]{0:T(1024)(128)(4,1)S(1)}, s32[]{:S(2)}) async-start(s8[4718592]{0:T(1024)(128)(4,1)} %bitcast.314), calls=%async_computation.8 | async-start | bytes 1048576
  662.0 16.7 %slice-start.8 = ((s8[4718592]{0:T(1024)(128)(4,1)}), s8[524288]{0:T(1024)(128)(4,1)S(1)}, s32[]{:S(2)}) async-start(s8[4718592]{0:T(1024)(128)(4,1)} %bitcast.329), calls=%async_computation.13 | async-start | bytes 1048576
  663.7 15.1 %copy-start.41 = (f32[1024]{0:T(1024)S(1)}, f32[1024]{0:T(1024)}, u32[]{:S(2)}) copy-start(f32[1024]{0:T(1024)} %multiply_multiply_fusion) | copy-start | bytes 12292
  663.8 12.2 %collective-permute-start.28 = (bf16[2,2,192,320]{3,2,0,1:T(8,128)(2,1)S(1)}, bf16[2,2,192,320]{3,2,0,1:T(8,128)(2,1)S(1)}, u32[]{:S(2)}, u32[]{:S(2)}) collective-permute-start(bf16[2,2,192,320]{3,2,0,1:T(8,128)(2,1)S(1)} %dynamic-slice_bitcast_fusion.3), channel_id=1, source_target_pairs={{0,2},{2,0},{4,6},{6,4},{8,10},{10,8},{12,14},{14,12},{16,18},{18,... | collective-permute-start | bytes 1474568 | tf_op jit(solution)/shard_map/ppermute | solution.py:284
  667.2 6.7 collective-permute-start.25
  674.0 7.3 collective-permute-start.26
  676.2 7.3 collective-permute-start.29
  685.8 11.8 %copy-start.36 = (f32[192,256]{1,0:T(8,128)S(1)}, f32[192,256]{1,0:T(8,128)}, u32[]{:S(2)}) copy-start(f32[192,256]{1,0:T(8,128)} %convert_add_fusion.21) | copy-start | bytes 589828
  686.7 11.8 %collective-permute-start.9 = (bf16[2,2,2,72,512]{4,3,0,1,2:T(8,128)(2,1)}, bf16[2,2,2,72,512]{4,3,0,1,2:T(8,128)(2,1)}, u32[]{:S(2)}, u32[]{:S(2)}) collective-permute-start(bf16[2,2,2,72,512]{4,3,0,1,2:T(8,128)(2,1)} %bitcast.303), channel_id=1, source_target_pairs={{0,4},{2,6},{4,0},{6,2},{8,12},{10,14},{12,8},{14,10},{16,20},{18,... | collective-permute-start | bytes 1769480 | tf_op jit(solution)/shard_map/ppermute | solution.py:284
  688.8 7.9 %collective-permute-start.30 = (bf16[192,320]{1,0:T(8,128)(2,1)}, bf16[192,320]{1,0:T(8,128)(2,1)}, u32[]{:S(2)}, u32[]{:S(2)}) collective-permute-start(bf16[192,320]{1,0:T(8,128)(2,1)} %dynamic-slice_bitcast_fusion.13), channel_id=1, source_target_pairs={{0,16},{2,18},{4,20},{6,22},{8,24},{10,26},{12,28},{14,30},{16,0},... | collective-permute-start | bytes 368648 | tf_op jit(solution)/shard_map/ppermute | solution.py:284
  690.1 13.1 %collective-permute-start.5 = (bf16[2,2,2,72,512]{4,3,2,1,0:T(8,128)(2,1)S(1)}, bf16[2,2,2,72,512]{4,3,2,1,0:T(8,128)(2,1)S(1)}, u32[]{:S(2)}, u32[]{:S(2)}) collective-permute-start(bf16[2,2,2,72,512]{4,3,2,1,0:T(8,128)(2,1)S(1)} %dynamic-slice_bitcast_fusion.4), channel_id=1, source_target_pairs={{0,2},{2,0},{4,6},{6,4},{8,10},{10,8},{12,14},{14,12},{16,18},{18,... | collective-permute-start | bytes 1769480 | tf_op jit(solution)/shard_map/ppermute | solution.py:284
  699.7 6.8 collective-permute-start.10
  703.4 6.8 collective-permute-start.6
  706.6 6.1 collective-permute-start.11
  710.4 5.2 collective-permute-start.7
  712.8 6.1 collective-permute-start.12
  715.6 6.1 collective-permute-start.8
  (23 other events, 59.6 us)
Sparse Core Ops, SparseCore 0:
  11.5 66.3 all-gather.3
  80.7 73.1 all-gather.7
  156.9 114.4 all-gather.5
  444.2 165.7 reduce-scatter.1

commit v3 on v2

v3 whole, which is shorter than its diff:
```python
import functools

import jax
import jax.numpy as jnp
from jax import lax
from jax.experimental import pallas as pl
from jax.experimental.pallas import tpu as pltpu
from jax.sharding import PartitionSpec as P

D = 1152
QUERY_HEADS = 18
KEY_VALUE_HEADS = 6
HEAD_SIZE = 64
FF = 3072
BLOCK = 256
QD = 1152
KVD = 384
HQ, HK = QUERY_HEADS // 2, KEY_VALUE_HEADS // 2
HALL = HQ + 2 * HK
QKV = HALL * HEAD_SIZE
FT = 256
WIDE = 1024

epsilon = 1e-05
bf16, f32 = jnp.bfloat16, jnp.float32
NT = (((1,), (1,)), ((), ()))
NN = (((1,), (0,)), ((), ()))
TN = (((0,), (0,)), ((), ()))
VMEM_BYTES = 62 << 20


def dg(a, b, dims):
    return lax.dot_general(a, b, dims, preferred_element_type=f32)


def assemble(w):
    if w.shape[0] == 1:
        return w[0, 0]
    return jnp.concatenate([w[i, 0].astype(f32) for i in range(w.shape[0])], 0).astype(bf16)


def scatter_rows(out, cols, u):
    rows = out.shape[2]
    for i in range(out.shape[0]):
        out[i, 0, :, cols] = u[rows * i : rows * (i + 1)].astype(bf16)


def turned(u, cosine, sine):
    lane = lax.broadcasted_iota(jnp.int32, u.shape, 1)
    h = HEAD_SIZE // 2
    other = jnp.where(lane % HEAD_SIZE < h, pltpu.roll(u, 128 - h, 1), pltpu.roll(u, h, 1))
    return u * cosine + other * sine


def project_body(me, n1, w, cosine, sine, out, flat):
    @pl.when(pl.program_id(0) == 0)
    def _():
        flat[...] = assemble(w)

    u = dg(n1[...], flat[...], NN)
    turns = (HQ + HK) * HEAD_SIZE
    for c in range(0, turns, 128):
        out[:, c : c + 128] = turned(u[:, c : c + 128], cosine[...], sine[...]).astype(bf16)
    out[:, turns:] = u[:, turns:].astype(bf16)


def project(half, me, n1, w, cosine, sine, piece):
    n, _, rows, width = w.shape
    batch = n1.shape[0] // piece
    return pl.pallas_call(
        project_body,
        grid_spec=pltpu.PrefetchScalarGridSpec(
            num_scalar_prefetch=1,
            grid=(batch,),
            in_specs=[
                pl.BlockSpec((piece, D), lambda b, m: (b, 0)),
                pl.BlockSpec((n, 1, rows, width), lambda b, m: (0, m[0] ^ half, 0, 0)),
                pl.BlockSpec((piece, 128), lambda b, m: (m[0], 0)),
                pl.BlockSpec((piece, 128), lambda b, m: (m[0], 0)),
            ],
            out_specs=[
                pl.BlockSpec((piece, width), lambda b, m: (b, 0)),
                pl.BlockSpec((D, width), lambda b, m: (0, 0)),
            ],
        ),
        out_shape=[
            jax.ShapeDtypeStruct((n1.shape[0], width), bf16),
            jax.ShapeDtypeStruct((D, width), bf16),
        ],
        compiler_params=pltpu.CompilerParams(vmem_limit_bytes=VMEM_BYTES),
        cost_estimate=pl.CostEstimate(flops=3 * 10**9, bytes_accessed=12 * 10**6, transcendentals=0),
        name="project",
    )(me, n1, w, cosine, sine)


def head_cols(j):
    return slice(j * HEAD_SIZE, (j + 1) * HEAD_SIZE)


def lane_of(j, shape):
    return lax.broadcasted_iota(jnp.int32, shape, 1) == j


def place(me, mine, got, q, k, v):
    piece = mine.shape[0]
    at = [pl.ds(pl.multiple_of((me[0] ^ a) * piece, piece), piece) for a in range(2)]
    for src, rows in zip((mine, got), at):
        for j in range(HQ):
            q[j, rows, :] = src[:, head_cols(j)] * jnp.asarray(0.125, bf16)
        for j in range(HK):
            k[j, rows, :] = src[:, head_cols(HQ + j)]
            v[j, rows, :] = src[:, head_cols(HQ + HK + j)]
    return at


def fwd_body(me, mine, got, o_mine, o_theirs, lse, q, k, v, o):
    at = place(me, mine, got, q, k, v)
    lse[...] = jnp.zeros_like(lse)

    def head(j, _):
        g = j // (HQ // HK)
        for i in range(lse.shape[0] // BLOCK):
            r = pl.ds(i * BLOCK, BLOCK)
            kw = (i + 1) * BLOCK
            s = dg(q[j, r, :], k[g, :kw, :], NT)
            m = jnp.max(s, axis=1, keepdims=True)
            p = jnp.exp(s - m)
            l = jnp.sum(p, axis=1, keepdims=True)
            mix = dg(p.astype(bf16), v[g, :kw, :], NN)
            o[j, r, :] = (mix / l).astype(bf16)
            lse[r, :] = jnp.where(lane_of(j, (BLOCK, 128)), m + jnp.log(l), lse[r, :])
        return 0

    lax.fori_loop(0, HQ, head, 0)
    for dst, rows in zip((o_mine, o_theirs), at):
        for j in range(HQ):
            dst[:, head_cols(j)] = o[j, rows, :]


def bwd_body(
    me, mine, got, o_mine, o_theirs, do_mine, do_got, lse, cosine, sine,
    lin_mine, lin_theirs, q, k, v, do, d, dka, dva, inner,
):
    at = place(me, mine, got, q, k, v)
    inner[...] = jnp.zeros_like(inner)
    for dsrc, osrc, rows in zip((do_mine, do_got), (o_mine, o_theirs), at):
        for j in range(HQ):
            dj = dsrc[:, head_cols(j)]
            do[j, rows, :] = dj
            part = jnp.sum(dj.astype(f32) * osrc[:, head_cols(j)].astype(f32), axis=1, keepdims=True)
            inner[rows, :] = jnp.where(lane_of(j, (dj.shape[0], 128)), part, inner[rows, :])

    def group(g, _):
        dka[...] = jnp.zeros_like(dka)
        dva[...] = jnp.zeros_like(dva)
        for jj in range(HQ // HK):
            j = g * (HQ // HK) + jj
            for i in range(lse.shape[0] // BLOCK):
                r = pl.ds(i * BLOCK, BLOCK)
                kw = (i + 1) * BLOCK
                mark = lane_of(j, (BLOCK, 128))
                column = lambda a: jnp.sum(jnp.where(mark, a[r, :], 0.0), axis=1, keepdims=True)
                qs = q[j, r, :]
                dO = do[j, r, :]
                kk = k[g, :kw, :]
                p = jnp.exp(dg(qs, kk, NT) - column(lse))
                dp = dg(dO, v[g, :kw, :], NT)
                ds = (p * (dp - column(inner))).astype(bf16)
                d[j, r, :] = dg(ds, kk, NN) * 0.125
                dka[:, :kw] += dg(qs.T, ds, NN)
                dva[:, :kw] += dg(dO.T, p.astype(bf16), NN)
        d[HQ + g] = dka[...].T
        d[HQ + HK + g] = dva[...].T
        return 0

    lax.fori_loop(0, HK, group, 0)
    turns = HQ + HK
    for dst, rows in zip((lin_mine, lin_theirs), at):
        for j in range(0, HALL + 1, 2):
            a = d[j, rows, :]
            b = d[j + 1, rows, :] if j + 1 < HALL else jnp.zeros_like(a)
            u = jnp.concatenate([a, b], 1)
            if j < turns:
                u = turned(u, cosine[rows, :], -sine[rows, :])
            dst[:, j * HEAD_SIZE : (j + 2) * HEAD_SIZE] = u.astype(bf16)


def attend(me, mine, got, piece):
    tokens, width = mine.shape
    batch = tokens // piece
    row = lambda a, c: pl.BlockSpec((a, c), lambda b, m: (b, 0))
    cols = HQ * HEAD_SIZE
    heads = lambda n: pltpu.VMEM((n, 2 * piece, HEAD_SIZE), bf16)
    return pl.pallas_call(
        fwd_body,
        grid_spec=pltpu.PrefetchScalarGridSpec(
            num_scalar_prefetch=1,
            grid=(batch,),
            in_specs=[row(piece, width)] * 2,
            out_specs=[row(piece, cols), row(piece, cols), row(2 * piece, 128)],
            scratch_shapes=[heads(HQ), heads(HK), heads(HK), heads(HQ)],
        ),
        out_shape=[
            jax.ShapeDtypeStruct((tokens, cols), bf16),
            jax.ShapeDtypeStruct((tokens, cols), bf16),
            jax.ShapeDtypeStruct((2 * tokens, 128), f32),
        ],
        compiler_params=pltpu.CompilerParams(vmem_limit_bytes=VMEM_BYTES),
        cost_estimate=pl.CostEstimate(flops=24 * 10**9, bytes_accessed=20 * 10**6, transcendentals=12 * 10**6),
        name="attend",
    )(me, mine, got)


def attend_back(me, mine, got, o_mine, o_theirs, do_mine, do_got, lse, cosine, sine, piece):
    tokens, width = mine.shape
    batch = tokens // piece
    row = lambda a, c: pl.BlockSpec((a, c), lambda b, m: (b, 0))
    cols = HQ * HEAD_SIZE
    table = pl.BlockSpec((2 * piece, 128), lambda b, m: (0, 0))
    heads = lambda n, t: pltpu.VMEM((n, 2 * piece, HEAD_SIZE), t)
    return pl.pallas_call(
        bwd_body,
        grid_spec=pltpu.PrefetchScalarGridSpec(
            num_scalar_prefetch=1,
            grid=(batch,),
            in_specs=[row(piece, width)] * 2 + [row(piece, cols)] * 4 + [row(2 * piece, 128), table, table],
            out_specs=[row(piece, width)] * 2,
            scratch_shapes=[heads(HQ, bf16), heads(HK, bf16), heads(HK, bf16), heads(HQ, bf16)]
            + [heads(HALL, f32)]
            + [pltpu.VMEM((HEAD_SIZE, 2 * piece), f32)] * 2
            + [pltpu.VMEM((2 * piece, 128), f32)],
        ),
        out_shape=[jax.ShapeDtypeStruct((tokens, width), bf16)] * 2,
        compiler_params=pltpu.CompilerParams(vmem_limit_bytes=VMEM_BYTES),
        cost_estimate=pl.CostEstimate(flops=27 * 10**9, bytes_accessed=40 * 10**6, transcendentals=12 * 10**6),
        name="attend_back",
    )(me, mine, got, o_mine, o_theirs, do_mine, do_got, lse, cosine, sine)


def mlp_body(me, n2, n2t, cot, res, wg, wu, wd, out, gn, ggu, gd_mine, gd_theirs, y):
    t = pl.program_id(0)

    @pl.when(t == 0)
    def _():
        y[...] = res[...]
        gn[...] = jnp.zeros_like(gn)

    half = wd.shape[2]
    wdt = jnp.concatenate([wd[0], wd[1]], axis=1)
    wgt, wut = assemble(wg), assemble(wu)
    gate = dg(n2[...], wgt, NN)
    up = dg(n2[...], wut, NN)
    gh = dg(cot[...], wdt, NT)
    sig = jax.nn.sigmoid(gate)
    act = gate * sig
    hidden = (act * up).astype(bf16)
    ggv = (gh * up * sig * (1.0 + gate * (1.0 - sig))).astype(bf16)
    guv = (gh * act).astype(bf16)
    y[...] += dg(hidden, wdt, NN)
    gdt = dg(hidden, cot[...], TN)
    first = me[0] == 0
    gd_mine[...] = jnp.where(first, gdt[:, :half], gdt[:, half:]).astype(bf16)
    gd_theirs[...] = jnp.where(first, gdt[:, half:], gdt[:, :half]).astype(bf16)
    scatter_rows(ggu, slice(0, FT), dg(n2t[...], ggv, NN))
    scatter_rows(ggu, slice(FT, 2 * FT), dg(n2t[...], guv, NN))
    gn[...] += dg(ggv, wgt, NT) + dg(guv, wut, NT)

    @pl.when(t == pl.num_programs(0) - 1)
    def _():
        out[...] = y[...].astype(bf16)


def mlp(me, n2, n2t, cot, res, wide, wd):
    tokens = n2.shape[0]
    n, _, rows, _ = wide.shape
    cols = FF // 2
    per = cols // FT
    whole = lambda a: pl.BlockSpec(a.shape, lambda t, m: (0, 0), pipeline_mode=pl.Buffered(1))
    col = lambda first, width: pl.BlockSpec(
        (n, 1, rows, width), lambda t, m: (0, t // per, 0, first + t % per)
    )
    row = pl.BlockSpec((2, FT, D // 2), lambda t, m: (0, t, 0))
    part = pl.BlockSpec((FT, D // 2), lambda t, m: (t, 0))
    one = lambda: pl.BlockSpec((tokens, D), lambda t, m: (0, 0), pipeline_mode=pl.Buffered(1))
    return pl.pallas_call(
        mlp_body,
        grid_spec=pltpu.PrefetchScalarGridSpec(
            num_scalar_prefetch=1,
            grid=(FF // FT,),
            in_specs=[whole(n2), whole(n2t), whole(cot), whole(res), col(0, FT), col(per, FT), row],
            out_specs=[one(), one(), col(0, 2 * FT), part, part],
            scratch_shapes=[pltpu.VMEM((tokens, D), f32)],
        ),
        out_shape=[
            jax.ShapeDtypeStruct((tokens, D), bf16),
            jax.ShapeDtypeStruct((tokens, D), f32),
            jax.ShapeDtypeStruct((n, 2, rows, 2 * cols), bf16),
            jax.ShapeDtypeStruct((FF, D // 2), bf16),
            jax.ShapeDtypeStruct((FF, D // 2), bf16),
        ],
        compiler_params=pltpu.CompilerParams(vmem_limit_bytes=VMEM_BYTES),
        cost_estimate=pl.CostEstimate(flops=65 * 10**9, bytes_accessed=60 * 10**6, transcendentals=3 * 10**6),
        name="mlp",
    )(me, n2, n2t, cot, res, wide, wide, wd)


def norm_back(grad_norm, rows_in, scale_rows, gain_rows):
    weighted = grad_norm * gain_rows
    cube_rows = scale_rows * scale_rows * scale_rows
    return scale_rows * weighted - rows_in * cube_rows * jnp.mean(
        weighted * rows_in, -1, keepdims=True
    )


def swap(a):
    return lax.ppermute(a, "seq", [(0, 1), (1, 0)])


BOTH = ("dp", "seq")


def whole_halves(g):
    return jnp.swapaxes(g, 0, 1).reshape(1, 2, -1, g.shape[3])


def fetch(w):
    g = lax.all_gather(w, BOTH, axis=0, tiled=True).reshape(lax.axis_size("dp"), 2, *w.shape)
    return g if w.shape[0] % 8 == 0 else whole_halves(g)


def reduce_all(g):
    n = lax.axis_size("dp")
    if g.shape[0] != n:
        g = jnp.swapaxes(g.reshape(2, n, -1, g.shape[3]), 0, 1)
    return lax.psum_scatter(g.reshape(-1, g.shape[3]), BOTH, scatter_dimension=0, tiled=True)


def add(a, b):
    return a.astype(f32) + b.astype(f32)


def reduce_halving(mine, theirs, kind=bf16):
    n = lax.axis_size("dp")
    bits = n.bit_length() - 1
    dp = lax.axis_index("dp")
    both = add(mine, swap(theirs)).astype(kind)
    cut = mine.shape[1] // 256 * 128
    out = []
    for part, order in ((both[:, :cut], [0, 1]), (both[:, cut:], [1, 0])):
        if not part.shape[1]:
            continue
        left = list(range(bits))[::-1]
        a = part.reshape(*[2] * bits, -1, part.shape[1])
        for bit in order + list(range(2, bits)):
            axis = left.index(bit)
            left.remove(bit)
            mybit = (dp >> bit) & 1
            keep = lax.dynamic_index_in_dim(a, mybit, axis, keepdims=False)
            send = lax.dynamic_index_in_dim(a, 1 - mybit, axis, keepdims=False)
            a = add(keep, lax.ppermute(send, "dp", [(i, i ^ (1 << bit)) for i in range(n)]))
            if left:
                a = a.astype(kind)
        out.append(a)
    return jnp.concatenate(out, 1)


def local(
    layer_input,
    w_query,
    w_key,
    w_value,
    w_out,
    gain_attn,
    w_gate,
    w_up,
    w_down,
    gain_mlp,
    cotangent,
):
    batch, _, piece, _ = layer_input.shape
    tokens = batch * piece
    me = lax.axis_index("seq")
    me_arr = jnp.full((1,), me, jnp.int32)
    pick = lambda a, b: jnp.where(me == 0, a, b)
    h = HEAD_SIZE // 2
    frequency = 10000.0 ** (-2.0 * jnp.arange(h).astype(f32) / HEAD_SIZE)
    angles = jnp.arange(2 * piece).astype(f32)[:, None] * jnp.tile(frequency, 128 // h)[None, :]
    cosine = jnp.cos(angles)
    sine = jnp.sin(angles) * jnp.where(jnp.arange(128) % HEAD_SIZE < h, -1.0, 1.0)[None, :]

    gains = jnp.pad(jnp.stack([gain_attn, gain_mlp], 1), ((0, 0), (0, WIDE - QKV - 2)))
    full = fetch(jnp.concatenate([w_query, w_key, w_value, gains], 1))
    wide = fetch(jnp.concatenate([w_gate, w_up, w_out], 1))
    down = lax.all_gather(w_down, BOTH, axis=0, tiled=True)
    full_down = whole_halves(down.reshape(-1, 2, *w_down.shape))[0]
    gain_one = full[:, 0, :, QKV].reshape(D).astype(f32)
    gain_two = full[:, 0, :, QKV + 1].reshape(D).astype(f32)
    out_halves = whole_halves(wide[..., FF:])[0].reshape(2, 2, D // 2, D // 2)
    out_rows = lambda c: jnp.concatenate(
        [lax.dynamic_index_in_dim(out_halves[i], c, 0, keepdims=False) for i in range(2)], 1
    )
    out_mine, out_theirs = out_rows(me), out_rows(1 - me)

    floats = layer_input.reshape(tokens, D).astype(f32)
    cot = cotangent.reshape(tokens, D)
    scale_attn = lax.rsqrt(jnp.mean(floats * floats, -1, keepdims=True) + epsilon)
    n1 = (floats * scale_attn * gain_one).astype(bf16)
    dot = lambda a, b: lax.dot_general(a, b, NN, preferred_element_type=f32)

    heads_out, w_theirs = project(1, me_arr, n1, full, cosine, sine, piece)
    got = swap(heads_out)
    mine, w_mine = project(0, me_arr, n1, full, cosine, sine, piece)
    mixed, mixed_out, lse = attend(me_arr, mine, got, piece)
    mixed_got = swap(mixed_out)
    residual = floats + (dot(mixed, out_mine) + dot(mixed_got, out_theirs))
    scale_mlp = lax.rsqrt(jnp.mean(residual * residual, -1, keepdims=True) + epsilon)
    n2 = (residual * scale_mlp * gain_two).astype(bf16)
    layer_out, grad_n2, grad_wide, grad_down_mine, grad_down_theirs = mlp(
        me_arr, n2, n2.T, cot, residual, wide, full_down
    )
    r_wide = reduce_all(grad_wide)
    sum_gain_mlp = jnp.sum(grad_n2 * residual * scale_mlp, 0)
    grad_residual = cot.astype(f32) + norm_back(grad_n2, residual, scale_mlp, gain_two)
    grad_low = grad_residual.astype(bf16)
    d_out = lax.dot_general(grad_low, out_theirs, NT, preferred_element_type=f32).astype(bf16)
    d_got = swap(d_out)
    d_mine = lax.dot_general(grad_low, out_mine, NT, preferred_element_type=f32).astype(bf16)
    r_down = reduce_halving(grad_down_mine, grad_down_theirs)
    low = grad_low[:, : D // 2], grad_low[:, D // 2 :]

    def grad_out(columns):
        a = lax.dot_general(mixed, columns, TN, preferred_element_type=f32).astype(bf16)
        b = lax.dot_general(mixed_got, columns, TN, preferred_element_type=f32).astype(bf16)
        return pick(jnp.concatenate([a, b], 0), jnp.concatenate([b, a], 0))

    r_out = reduce_halving(grad_out(pick(*low)), grad_out(pick(*low[::-1])))
    lin_mine, lin_out = attend_back(
        me_arr, mine, got, mixed, mixed_out, d_mine, d_got, lse, cosine, sine, piece
    )
    lin_got = swap(lin_out)
    weight_grad = lambda lin: lax.dot_general(n1, lin, TN, preferred_element_type=f32).astype(bf16)
    lin_got, r_out, r_down = lax.optimization_barrier((lin_got, r_out, r_down))
    r_pack = reduce_halving(weight_grad(lin_mine), weight_grad(lin_got))
    grad_n1 = lax.dot_general(lin_mine, w_mine, NT, preferred_element_type=f32) + lax.dot_general(
        lin_got, w_theirs, NT, preferred_element_type=f32
    )
    sum_gain_attn = jnp.sum(grad_n1 * floats * scale_attn, 0)
    grad_input = (grad_residual + norm_back(grad_n1, floats, scale_attn, gain_one)).astype(bf16)
    sums = jnp.pad(jnp.stack([sum_gain_attn, sum_gain_mlp], 1), ((0, 0), (0, 126)))
    r_sums = reduce_halving(sums, sums, f32)
    r_gate, r_up = [
        a.reshape(a.shape[0], -1).astype(f32)
        for a in jnp.split(r_wide.reshape(-1, FF // 2 // FT, 2, FT), 2, 2)
    ]
    a, b, c = HQ * HEAD_SIZE, (HQ + HK) * HEAD_SIZE, QKV
    shape = layer_input.shape
    return (
        layer_out.reshape(shape),
        grad_input.reshape(shape),
        r_pack[:, :a],
        r_pack[:, a:b],
        r_pack[:, b:c],
        r_out,
        r_sums[:, 0],
        r_gate,
        r_up,
        r_down,
        r_sums[:, 1],
    )


def solution(mesh):
    tokens, matrix, vector = P(None, "dp", "seq", None), P("dp", "seq"), P("dp")
    placed = (tokens, *[matrix] * 4, vector, *[matrix] * 3, vector, tokens)
    return jax.shard_map(
        local,
        mesh=mesh,
        in_specs=placed,
        out_specs=(tokens, tokens, *[matrix] * 4, vector, *[matrix] * 3, vector),
        check_vma=False,
    )
```

time: 746 us -> 693 us (0.929)
  local copies, waits for them, and re-layouts: 195 us -> 47.9 us
  waiting for transfers between devices: 168 us -> 308 us
  other arithmetic: 124 us -> 46.5 us
  Pallas kernels: 162 us -> 190 us
    all_gather x3, waiting for transfers between devices: 99.3 us -> 190 us  [the longest x2 172 us: fetch(): lax.all_gather(w, BOTH, axis=0, tiled=True)]
    ppermute x24 -> x28, waiting for transfers between devices: 67.8 us -> 117 us  [reduce_halving(): lax.ppermute(send, 'dp', [(i, i ^ 1 << bit) for i in range(n)])]
    unnamed x118 -> x74, local copies, waits for them, and re-layouts: 50.1 us -> 8.59 us
    another operation x6 -> x2, other arithmetic: 32.4 us -> 0.87 us  [the longest x1 0.83 us: local(): jnp.stack([gain_attn, gain_mlp], 1)]
    reshape x6 -> x1, local copies, waits for them, and re-layouts: 35.7 us -> 7.07 us  [local(): full_down = whole_halves(down.reshape(-1, 2, *w_down.shape))[0]]
    transpose x8 -> x2, local copies, waits for them, and re-layouts: 25.9 us -> 4.59 us  [the longest x1 2.51 us: local(): layer_out, grad_n2, grad_wide, grad_down_mine, grad_down_theirs = mlp(me_...]
    dynamic_slice x5 -> x0, local copies, waits for them, and re-layouts: 14.6 us -> none  [the longest x2 10.3 us: reduce_halving(): theirs = lax.dynamic_index_in_dim(g, 1 - me, 0, keepdims=False)]
    transpose x2 -> x1, other arithmetic: 14.7 us -> 0.49 us  [local(): layer_out, grad_n2, grad_wide, grad_down_mine, grad_down_theirs = mlp(me_...]
  transfers between devices with their start and end apart: 35 -> 40, of which waited for: 22 -> 24; matrix products, arithmetic and copies ran while one was open for 39% -> 14% of each run, Pallas kernels for 10% -> 15%
where the time goes in v3:
time: 693 us; the launch traced here: 685 us
  waiting for transfers between devices  308 us (44%)
  Pallas kernels  190 us (27%)
  local copies, waits for them, and re-layouts  47.9 us (7%)
  other arithmetic  46.5 us (7%)
  matrix products  42.3 us (6%)
  starting transfers between devices  35.6 us (5%)
  between operations  15.1 us (2%)
    all_gather x2, waiting for transfers between devices, fetch(): lax.all_gather(w, BOTH, axis=0, tiled=True)  172 us
    ppermute x28, waiting for transfers between devices, reduce_halving(): lax.ppermute(send, 'dp', [(i, i ^ 1 << bit) for i in range(n)])  117 us
    pallas_call x1, Pallas kernels, mlp(): pl.pallas_call(mlp_body, grid_spec=pltpu.PrefetchScalarGridSpec(num_scala...  87.2 us
    pallas_call x1, Pallas kernels, attend_back(): pl.pallas_call(bwd_body, grid_spec=pltpu.PrefetchScalarGridSpec(num_scala...  51.1 us
    pallas_call x1, Pallas kernels, attend(): pl.pallas_call(fwd_body, grid_spec=pltpu.PrefetchScalarGridSpec(num_scala...  38.6 us
    ppermute x28, starting transfers between devices, reduce_halving(): lax.ppermute(send, 'dp', [(i, i ^ 1 << bit) for i in range(n)])  33.9 us
    all_gather x1, waiting for transfers between devices, local(): down = lax.all_gather(w_down, BOTH, axis=0, tiled=True)  17.9 us
  transfers between devices with their start and end apart: 40, of which 24 were waited for; matrix products, arithmetic and copies ran while one was open for 14% of the time, Pallas kernels for 15%

profile of v3, /device:TPU:0, one launch (start us, length us, event | category | flops | bytes accessed | tf_op | source)
XLA Modules:
  0.0 685.5 jit_solution(17875182421575133227)
XLA Ops:
  8.2 1.7 fusion.32
  10.7 1.9 pad_maximum_fusion.6
  13.4 3.1 fusion.22
  16.5 61.4 %all-gather.4.cloned.1.call-done = bf16[2304,1024]{1,0:T(8,128)(2,1)} async-done(((bf16[72,1024]{1,0:T(8,128)(2,1)}), bf16[2304,1024]{1,0:T(8,128)(2,1)}) %all-gather.4.cloned.1.call-update) | async-done | bytes 4718608 | tf_op jit(solution)/shard_map/all_gather | solution.py:327
  77.8 1.6 convert_reduce_fusion
  79.6 2.0 fusion.2.n1
  81.6 6.7 project.3
  88.6 6.8 project.2
  95.3 38.6 %attend.1 = (bf16[1024,576]{1,0:T(8,128)(2,1)}, bf16[1024,576]{1,0:T(8,128)(2,1)}, f32[2048,128]{1,0:T(8,128)}) custom-call(s32[1]{0:T(128)} %bitcast.me, bf16[1024,1024]{1,0:T(8,128)(2,1)} %get-tuple-element.28.mine, bf16[1024,1024]{1,0:T(8,128)(2,1)} %collective-permute-done.got), custom_call_target="tpu_custom_call" | custom-call | flops 24000000000 | bytes 20000000 | tf_op jit(solution)/shard_map/attend/pallas_call | solution.py:194
  133.9 1.9 copy.125
  136.2 17.9 %all-gather.8.cloned.1.call-done = bf16[6144,576]{1,0:T(8,128)(2,1)} async-done(((bf16[192,576]{1,0:T(8,128)(2,1)}), bf16[6144,576]{1,0:T(8,128)(2,1)}) %all-gather.8.cloned.1.call-update) | async-done | bytes 7077904 | tf_op jit(solution)/shard_map/all_gather | solution.py:394
  154.1 7.1 %copy.126 = bf16[16,2,192,576]{3,2,0,1:T(8,128)(2,1)} copy(bf16[16,2,192,576]{3,2,1,0:T(8,128)(2,1)} %bitcast.244) | data formatting | bytes 14155776 | tf_op jit(solution)/shard_map/reshape | solution.py:395
  161.2 110.3 %all-gather.6.cloned.1.call-done = bf16[2304,3648]{1,0:T(8,128)(2,1)} async-done(((bf16[72,3648]{1,0:T(8,128)(2,1)}), bf16[2304,3648]{1,0:T(8,128)(2,1)}) %all-gather.6.cloned.1.call-update) | async-done | bytes 16810000 | tf_op jit(solution)/shard_map/all_gather | solution.py:327
  271.5 2.1 slice_bitcast_fusion
  274.2 2.3 fusion.17
  277.7 2.5 multiply_reduce_fusion.2
  280.7 1.6 copy-done
  282.3 1.9 multiply_convert_fusion.n2
  284.3 2.5 copy.127.n2t
  286.8 87.2 %mlp.1 = (bf16[1024,1152]{1,0:T(8,128)(2,1)}, f32[1024,1152]{1,0:T(8,128)}, bf16[16,2,72,3072]{3,2,1,0:T(8,128)(2,1)}, bf16[3072,576]{1,0:T(8,128)(2,1)}, bf16[3072,576]{1,0:T(8,128)(2,1)}) custom-call(s32[1]{0:T(128)} %bitcast.me, bf16[1024,1152]{1,0:T(8,128)(2,1)} %multiply_convert_fusion.n2, bf16[1152,1024]{1,0:T(8,128)(2,1)} %copy.127.n2t, ...), custom_call_target="tpu_custom_call" | custom-call | flops 65000001536 | bytes 60000000 | tf_op jit(solution)/shard_map/mlp/pallas_call | solution.py:285
  374.0 5.0 multiply_reduce_fusion
  380.5 4.5 fusion.39
  387.2 1.7 convolution_convert_fusion.4
  388.9 2.0 maximum_select_fusion.1
  391.2 2.8 convolution_convert_fusion.2
  394.3 6.3 copy.132
  400.8 4.4 convolution_convert_fusion.3
  405.2 2.4 copy.128.do_mine
  407.7 3.9 convolution_convert_fusion.6
  413.2 2.4 copy.129.do_got
  415.7 2.6 add_convert_fusion.2
  423.0 51.1 %attend_back.1 = (bf16[1024,1024]{1,0:T(8,128)(2,1)}, bf16[1024,1024]{1,0:T(8,128)(2,1)}) custom-call(s32[1]{0:T(128)} %bitcast.me, bf16[1024,1024]{1,0:T(8,128)(2,1)} %get-tuple-element.28.mine, bf16[1024,1024]{1,0:T(8,128)(2,1)} %collective-permute-done.got, bf16[1024,576]{1,0:T(8,128)(2,1)} %get-tuple-element.30.o_mine, ...), custom_call_target="tpu_custom_call" | custom-call | flops 27000000512 | bytes 40000000 | tf_op jit(solution)/shard_map/attend_back/pallas_call | solution.py:221
  476.8 4.7 collective-permute-done.6
  483.9 9.2 %collective-permute-done.7 = bf16[2,72,256]{2,1,0:T(8,128)(2,1)S(1)} collective-permute-done((bf16[2,72,256]{2,1,0:T(8,128)(2,1)S(1)}, bf16[2,72,256]{2,1,0:T(8,128)(2,1)S(1)}, u32[]{:S(2)}, u32[]{:S(2)}) %collective-permute-start.7) | collective-permute-done | bytes 73760 | tf_op jit(solution)/shard_map/ppermute | solution.py:360
  493.3 6.5 copy.133
  499.8 4.6 add_convert_fusion
  504.5 1.8 copy-done.5
  509.9 1.8 collective-permute-start.11
  511.8 3.0 collective-permute-done.11
  514.8 2.8 collective-permute-start.12
  517.6 11.5 %collective-permute-done.14 = bf16[2,2,2,192,256]{4,3,0,1,2:T(8,128)(2,1)S(1)} collective-permute-done((bf16[2,2,2,192,256]{4,3,0,1,2:T(8,128)(2,1)S(1)}, bf16[2,2,2,192,256]{4,3,0,1,2:T(8,128)(2,1)S(1)}, u32[]{:S(2)}, u32[]{:S(2)}) %collective-permute-start.14) | collective-permute-done | bytes 786464 | tf_op jit(solution)/shard_map/ppermute | solution.py:360
  530.7 13.7 %collective-permute-done.18 = bf16[2,2,2,192,320]{4,3,0,1,2:T(8,128)(2,1)S(1)} collective-permute-done((bf16[2,2,2,192,320]{4,3,0,1,2:T(8,128)(2,1)S(1)}, bf16[2,2,2,192,320]{4,3,0,1,2:T(8,128)(2,1)S(1)}, u32[]{:S(2)}, u32[]{:S(2)}) %collective-permute-start.18) | collective-permute-done | bytes 983072 | tf_op jit(solution)/shard_map/ppermute | solution.py:360
  546.7 11.9 %collective-permute-done.15 = bf16[2,2,192,256]{3,2,0,1:T(8,128)(2,1)S(1)} collective-permute-done((bf16[2,2,192,256]{3,2,0,1:T(8,128)(2,1)S(1)}, bf16[2,2,192,256]{3,2,0,1:T(8,128)(2,1)S(1)}, u32[]{:S(2)}, u32[]{:S(2)}) %collective-permute-start.15) | collective-permute-done | bytes 393248 | tf_op jit(solution)/shard_map/ppermute | solution.py:360
  559.0 2.1 collective-permute-start.20
  561.1 10.4 %collective-permute-done.16 = bf16[2,192,256]{2,1,0:T(8,128)(2,1)S(1)} collective-permute-done((bf16[2,192,256]{2,1,0:T(8,128)(2,1)S(1)}, bf16[2,192,256]{2,1,0:T(8,128)(2,1)S(1)}, u32[]{:S(2)}, u32[]{:S(2)}) %collective-permute-start.16) | collective-permute-done | bytes 196640 | tf_op jit(solution)/shard_map/ppermute | solution.py:360
  572.5 7.2 %collective-permute-done.20 = bf16[2,192,320]{2,1,0:T(8,128)(2,1)S(1)} collective-permute-done((bf16[2,192,320]{2,1,0:T(8,128)(2,1)S(1)}, bf16[2,192,320]{2,1,0:T(8,128)(2,1)S(1)}, u32[]{:S(2)}, u32[]{:S(2)}) %collective-permute-start.20) | collective-permute-done | bytes 245792 | tf_op jit(solution)/shard_map/ppermute | solution.py:360
  579.9 1.6 collective-permute-start.21
  581.5 14.7 %collective-permute-done.21 = bf16[192,320]{1,0:T(8,128)(2,1)S(1)} collective-permute-done((bf16[192,320]{1,0:T(8,128)(2,1)S(1)}, bf16[192,320]{1,0:T(8,128)(2,1)S(1)}, u32[]{:S(2)}, u32[]{:S(2)}) %collective-permute-start.21) | collective-permute-done | bytes 122912 | tf_op jit(solution)/shard_map/ppermute | solution.py:360
  597.1 4.7 fusion.43
  601.8 6.1 fusion.9
  608.1 4.1 convolution_convert_fusion.1
  613.0 6.6 convolution_convert_fusion
  619.6 2.3 collective-permute-done.32
  623.2 4.3 collective-permute-done.33
  627.7 2.4 fusion.6
  630.1 1.8 collective-permute-done.34
  632.3 3.5 add_convert_fusion.1
  639.4 9.9 %collective-permute-done.23 = bf16[2,2,2,72,512]{4,3,0,1,2:T(8,128)(2,1)S(1)} collective-permute-done((bf16[2,2,2,72,512]{4,3,0,1,2:T(8,128)(2,1)S(1)}, bf16[2,2,2,72,512]{4,3,0,1,2:T(8,128)(2,1)S(1)}, u32[]{:S(2)}, u32[]{:S(2)}) %collective-permute-start.23) | collective-permute-done | bytes 589856 | tf_op jit(solution)/shard_map/ppermute | solution.py:360
  652.6 4.4 collective-permute-done.24
  659.0 1.8 collective-permute-start.29
  662.3 2.8 collective-permute-start.26
  665.7 1.9 collective-permute-start.30
  668.5 3.3 collective-permute-done.30
  674.6 2.4 fusion.23
  (234 shorter events, 50.2 us)
Async XLA Ops:
  7.2 5.5 copy-start.1
  7.2 70.7 %all-gather.4.cloned.1.call-start = ((), (), s32[]{:S(2)}) async-start(), calls=%async_computation.1 | async-start | bytes 4866048 | tf_op jit(solution)/shard_map/all_gather | solution.py:327
  9.9 144.2 %all-gather.8.cloned.1.call-start = ((), (), s32[]{:S(2)}) async-start(), calls=%async_computation.3 | async-start | bytes 8110080 | tf_op jit(solution)/shard_map/all_gather | solution.py:394
  10.7 260.9 %all-gather.6.cloned.1.call-start = ((), (), s32[]{:S(2)}) async-start(), calls=%async_computation.2 | async-start | bytes 17639424 | tf_op jit(solution)/shard_map/all_gather | solution.py:327
  12.7 660.6 %reduce-scatter.2.cloned.1.call-start = ((), (), s32[]{:S(2)}) async-start(), calls=%async_computation.4 | async-start | bytes 14598144 | tf_op jit(solution)/shard_map/reduce_scatter | solution.py:335
  88.3 7.0 %collective-permute-start = (bf16[1024,1024]{1,0:T(8,128)(2,1)}, bf16[1024,1024]{1,0:T(8,128)(2,1)}, u32[]{:S(2)}, u32[]{:S(2)}) collective-permute-start(bf16[1024,1024]{1,0:T(8,128)(2,1)} %get-tuple-element.29), channel_id=1, source_target_pairs={{0,1},{1,0},{2,3},{3,2},{4,5},{5,4},{6,7},{7,6},{8,9},{9,8},{10,11... | collective-permute-start | bytes 6291464 | tf_op jit(solution)/shard_map/ppermute | solution.py:316
  135.8 138.4 %collective-permute-start.1 = (bf16[1024,576]{0,1:T(8,128)(2,1)S(1)}, bf16[1024,576]{0,1:T(8,128)(2,1)S(1)}, u32[]{:S(2)}, u32[]{:S(2)}) collective-permute-start(bf16[1024,576]{0,1:T(8,128)(2,1)S(1)} %copy.125), channel_id=1, source_target_pairs={{0,1},{1,0},{2,3},{3,2},{4,5},{5,4},{6,7},{7,6},{8,9},{9,8},{10,11... | collective-permute-start | bytes 3538952 | tf_op jit(solution)/shard_map/ppermute | solution.py:316
  274.2 3.1 copy-start.2
  274.2 3.5 copy-start.6
  373.9 5.0 slice-start
  373.9 5.1 slice-start.1
  374.0 6.5 copy-start.4
  380.5 4.5 copy-start.7
  385.0 6.2 copy-start.12
  390.9 24.8 %collective-permute-start.4 = (bf16[1152,576]{0,1:T(8,128)(2,1)}, bf16[1152,576]{0,1:T(8,128)(2,1)}, u32[]{:S(2)}, u32[]{:S(2)}) collective-permute-start(bf16[1152,576]{0,1:T(8,128)(2,1)} %maximum_select_fusion.1), channel_id=1, source_target_pairs={{0,1},{1,0},{2,3},{3,2},{4,5},{5,4},{6,7},{7,6},{8,9},{9,8},{10,11... | collective-permute-start | bytes 3981320 | tf_op jit(solution)/shard_map/ppermute | solution.py:316
  394.0 19.2 %collective-permute-start.2 = (bf16[1024,576]{0,1:T(8,128)(2,1)}, bf16[1024,576]{0,1:T(8,128)(2,1)}, u32[]{:S(2)}, u32[]{:S(2)}) collective-permute-start(bf16[1024,576]{0,1:T(8,128)(2,1)} %convolution_convert_fusion.2), channel_id=1, source_target_pairs={{0,1},{1,0},{2,3},{3,2},{4,5},{5,4},{6,7},{7,6},{8,9},{9,8},{10,11... | collective-permute-start | bytes 3538952 | tf_op jit(solution)/shard_map/ppermute | solution.py:316
  394.3 6.5 copy-start.9
  394.3 6.5 copy-start.11
  400.5 92.7 %collective-permute-start.13 = (bf16[3072,576]{0,1:T(8,128)(2,1)}, bf16[3072,576]{0,1:T(8,128)(2,1)}, u32[]{:S(2)}, u32[]{:S(2)}) collective-permute-start(bf16[3072,576]{0,1:T(8,128)(2,1)} %copy.132), channel_id=1, source_target_pairs={{0,1},{1,0},{2,3},{3,2},{4,5},{5,4},{6,7},{7,6},{8,9},{9,8},{10,11... | collective-permute-start | bytes 10616840 | tf_op jit(solution)/shard_map/ppermute | solution.py:316
  407.7 200.3 %copy-start.21 = (f32[1152,1]{0,1:T(1,128)}, f32[1152,1]{0,1:T(1,128)S(1)}, u32[]{:S(2)}) copy-start(f32[1152,1]{0,1:T(1,128)S(1)} %stack.22) | copy-start | bytes 13828
  407.7 3.9 copy-start.13
  419.4 54.7 %collective-permute-start.5 = (bf16[2,2,2,72,256]{4,3,2,1,0:T(8,128)(2,1)}, bf16[2,2,2,72,256]{4,3,2,1,0:T(8,128)(2,1)}, u32[]{:S(2)}, u32[]{:S(2)}) collective-permute-start(bf16[2,2,2,72,256]{4,3,2,1,0:T(8,128)(2,1)} %dynamic-slice_bitcast_fusion.11), channel_id=1, source_target_pairs={{0,2},{2,0},{4,6},{6,4},{8,10},{10,8},{12,14},{14,12},{16,18},{18,... | collective-permute-start | bytes 884744 | tf_op jit(solution)/shard_map/ppermute | solution.py:360
  422.4 54.3 %collective-permute-start.9 = (bf16[2,2,2,72,320]{4,3,2,1,0:T(8,128)(2,1)}, bf16[2,2,2,72,320]{4,3,2,1,0:T(8,128)(2,1)S(1)}, u32[]{:S(2)}, u32[]{:S(2)}) collective-permute-start(bf16[2,2,2,72,320]{4,3,2,1,0:T(8,128)(2,1)} %dynamic-slice_bitcast_fusion.5), channel_id=1, source_target_pairs={{0,4},{2,6},{4,0},{6,2},{8,12},{10,14},{12,8},{14,10},{16,20},{18,... | collective-permute-start | bytes 1105928 | tf_op jit(solution)/shard_map/ppermute | solution.py:360
  474.1 123.0 %collective-permute-start.3 = (bf16[1024,1024]{1,0:T(8,128)(2,1)}, bf16[1024,1024]{1,0:T(8,128)(2,1)}, u32[]{:S(2)}, u32[]{:S(2)}) collective-permute-start(bf16[1024,1024]{1,0:T(8,128)(2,1)} %get-tuple-element.37), channel_id=1, source_target_pairs={{0,1},{1,0},{2,3},{3,2},{4,5},{5,4},{6,7},{7,6},{8,9},{9,8},{10,11... | collective-permute-start | bytes 6291464 | tf_op jit(solution)/shard_map/ppermute | solution.py:316
  475.2 6.3 collective-permute-start.6
  481.6 11.5 %collective-permute-start.7 = (bf16[2,72,256]{2,1,0:T(8,128)(2,1)S(1)}, bf16[2,72,256]{2,1,0:T(8,128)(2,1)S(1)}, u32[]{:S(2)}, u32[]{:S(2)}) collective-permute-start(bf16[2,72,256]{2,1,0:T(8,128)(2,1)S(1)} %dynamic-slice_bitcast_fusion.24), channel_id=1, source_target_pairs={{0,8},{2,10},{4,12},{6,14},{8,0},{10,2},{12,4},{14,6},{16,24},{18,... | collective-permute-start | bytes 221192 | tf_op jit(solution)/shard_map/ppermute | solution.py:360
  482.4 10.8 %collective-permute-start.10 = (bf16[2,2,72,320]{3,2,1,0:T(8,128)(2,1)S(1)}, bf16[2,2,72,320]{3,2,1,0:T(8,128)(2,1)S(1)}, u32[]{:S(2)}, u32[]{:S(2)}) collective-permute-start(bf16[2,2,72,320]{3,2,1,0:T(8,128)(2,1)S(1)} %dynamic-slice_bitcast_fusion.12), channel_id=1, source_target_pairs={{0,2},{2,0},{4,6},{6,4},{8,10},{10,8},{12,14},{14,12},{16,18},{18,... | collective-permute-start | bytes 552968 | tf_op jit(solution)/shard_map/ppermute | solution.py:360
  493.1 18.6 %collective-permute-start.8 = (bf16[72,256]{1,0:T(8,128)(2,1)S(1)}, bf16[72,256]{1,0:T(8,128)(2,1)S(1)}, u32[]{:S(2)}, u32[]{:S(2)}) collective-permute-start(bf16[72,256]{1,0:T(8,128)(2,1)S(1)} %dynamic-slice_bitcast_fusion.26), channel_id=1, source_target_pairs={{0,16},{2,18},{4,20},{6,22},{8,24},{10,26},{12,28},{14,30},{16,0},... | collective-permute-start | bytes 110600 | tf_op jit(solution)/shard_map/ppermute | solution.py:360
  506.5 22.6 %collective-permute-start.14 = (bf16[2,2,2,192,256]{4,3,0,1,2:T(8,128)(2,1)S(1)}, bf16[2,2,2,192,256]{4,3,0,1,2:T(8,128)(2,1)S(1)}, u32[]{:S(2)}, u32[]{:S(2)}) collective-permute-start(bf16[2,2,2,192,256]{4,3,0,1,2:T(8,128)(2,1)S(1)} %bitcast.264), channel_id=1, source_target_pairs={{0,2},{2,0},{4,6},{6,4},{8,10},{10,8},{12,14},{14,12},{16,18},{18,... | collective-permute-start | bytes 2359304 | tf_op jit(solution)/shard_map/ppermute | solution.py:360
  508.4 35.9 %collective-permute-start.18 = (bf16[2,2,2,192,320]{4,3,0,1,2:T(8,128)(2,1)S(1)}, bf16[2,2,2,192,320]{4,3,0,1,2:T(8,128)(2,1)S(1)}, u32[]{:S(2)}, u32[]{:S(2)}) collective-permute-start(bf16[2,2,2,192,320]{4,3,0,1,2:T(8,128)(2,1)S(1)} %bitcast.263), channel_id=1, source_target_pairs={{0,4},{2,6},{4,0},{6,2},{8,12},{10,14},{12,8},{14,10},{16,20},{18,... | collective-permute-start | bytes 2949128 | tf_op jit(solution)/shard_map/ppermute | solution.py:360
  509.9 4.8 collective-permute-start.11
  514.8 31.2 %collective-permute-start.12 = (bf16[72,320]{1,0:T(8,128)(2,1)S(1)}, bf16[72,320]{1,0:T(8,128)(2,1)S(1)}, u32[]{:S(2)}, u32[]{:S(2)}) collective-permute-start(bf16[72,320]{1,0:T(8,128)(2,1)S(1)} %dynamic-slice_bitcast_fusion.25), channel_id=1, source_target_pairs={{0,16},{2,18},{4,20},{6,22},{8,24},{10,26},{12,28},{14,30},{16,0},... | collective-permute-start | bytes 138248 | tf_op jit(solution)/shard_map/ppermute | solution.py:360
  529.4 29.2 %collective-permute-start.15 = (bf16[2,2,192,256]{3,2,0,1:T(8,128)(2,1)S(1)}, bf16[2,2,192,256]{3,2,0,1:T(8,128)(2,1)S(1)}, u32[]{:S(2)}, u32[]{:S(2)}) collective-permute-start(bf16[2,2,192,256]{3,2,0,1:T(8,128)(2,1)S(1)} %dynamic-slice_bitcast_fusion.6), channel_id=1, source_target_pairs={{0,4},{2,6},{4,0},{6,2},{8,12},{10,14},{12,8},{14,10},{16,20},{18,... | collective-permute-start | bytes 1179656 | tf_op jit(solution)/shard_map/ppermute | solution.py:360
  544.8 14.0 %collective-permute-start.19 = (bf16[2,2,192,320]{3,2,0,1:T(8,128)(2,1)S(1)}, bf16[2,2,192,320]{3,2,0,1:T(8,128)(2,1)S(1)}, u32[]{:S(2)}, u32[]{:S(2)}) collective-permute-start(bf16[2,2,192,320]{3,2,0,1:T(8,128)(2,1)S(1)} %dynamic-slice_bitcast_fusion.4), channel_id=1, source_target_pairs={{0,2},{2,0},{4,6},{6,4},{8,10},{10,8},{12,14},{14,12},{16,18},{18,... | collective-permute-start | bytes 1474568 | tf_op jit(solution)/shard_map/ppermute | solution.py:360
  558.7 12.8 %collective-permute-start.16 = (bf16[2,192,256]{2,1,0:T(8,128)(2,1)S(1)}, bf16[2,192,256]{2,1,0:T(8,128)(2,1)S(1)}, u32[]{:S(2)}, u32[]{:S(2)}) collective-permute-start(bf16[2,192,256]{2,1,0:T(8,128)(2,1)S(1)} %dynamic-slice_bitcast_fusion.13), channel_id=1, source_target_pairs={{0,8},{2,10},{4,12},{6,14},{8,0},{10,2},{12,4},{14,6},{16,24},{18,... | collective-permute-start | bytes 589832 | tf_op jit(solution)/shard_map/ppermute | solution.py:360
  559.0 38.1 %copy-start.26 = (bf16[1152,1024]{1,0:T(8,128)(2,1)S(1)}, bf16[1152,1024]{1,0:T(8,128)(2,1)}, u32[]{:S(2)}) copy-start(bf16[1152,1024]{1,0:T(8,128)(2,1)} %get-tuple-element.41) | copy-start | bytes 7077892
  559.0 20.8 %collective-permute-start.20 = (bf16[2,192,320]{2,1,0:T(8,128)(2,1)S(1)}, bf16[2,192,320]{2,1,0:T(8,128)(2,1)S(1)}, u32[]{:S(2)}, u32[]{:S(2)}) collective-permute-start(bf16[2,192,320]{2,1,0:T(8,128)(2,1)S(1)} %dynamic-slice_bitcast_fusion.10), channel_id=1, source_target_pairs={{0,8},{2,10},{4,12},{6,14},{8,0},{10,2},{12,4},{14,6},{16,24},{18,... | collective-permute-start | bytes 737288 | tf_op jit(solution)/shard_map/ppermute | solution.py:360
  571.6 9.9 %collective-permute-start.17 = (bf16[192,256]{1,0:T(8,128)(2,1)S(1)}, bf16[192,256]{1,0:T(8,128)(2,1)S(1)}, u32[]{:S(2)}, u32[]{:S(2)}) collective-permute-start(bf16[192,256]{1,0:T(8,128)(2,1)S(1)} %dynamic-slice_bitcast_fusion.20), channel_id=1, source_target_pairs={{0,16},{2,18},{4,20},{6,22},{8,24},{10,26},{12,28},{14,30},{16,0},... | collective-permute-start | bytes 294920 | tf_op jit(solution)/shard_map/ppermute | solution.py:360
  579.9 16.3 %collective-permute-start.21 = (bf16[192,320]{1,0:T(8,128)(2,1)S(1)}, bf16[192,320]{1,0:T(8,128)(2,1)S(1)}, u32[]{:S(2)}, u32[]{:S(2)}) collective-permute-start(bf16[192,320]{1,0:T(8,128)(2,1)S(1)} %dynamic-slice_bitcast_fusion.17), channel_id=1, source_target_pairs={{0,16},{2,18},{4,20},{6,22},{8,24},{10,26},{12,28},{14,30},{16,0},... | collective-permute-start | bytes 368648 | tf_op jit(solution)/shard_map/ppermute | solution.py:360
  597.1 4.7 copy-start.3
  597.1 4.7 copy-start.20
  597.1 4.7 copy-start.27
  597.1 4.7 copy-start.28
  601.8 6.2 copy-start.14
  608.0 4.2 copy-start.22
  608.0 4.2 collective-permute-start.31
  612.4 15.2 %slice-start.2 = ((s8[4718592]{0:T(1024)(128)(4,1)}), s8[4194304]{0:T(1024)(128)(4,1)S(1)}, s32[]{:S(2)}) async-start(s8[4718592]{0:T(1024)(128)(4,1)} %bitcast.240), calls=%async_computation.7 | async-start | bytes 8388608
  612.4 15.2 %slice-start.5 = ((s8[4718592]{0:T(1024)(128)(4,1)}), s8[4194304]{0:T(1024)(128)(4,1)S(1)}, s32[]{:S(2)}) async-start(s8[4718592]{0:T(1024)(128)(4,1)} %bitcast.249), calls=%async_computation.10 | async-start | bytes 8388608
  612.5 10.7 %copy-start.23 = (f32[1024]{0:T(1024)S(1)}, f32[1024]{0:T(1024)}, u32[]{:S(2)}) copy-start(f32[1024]{0:T(1024)} %get-tuple-element.114) | copy-start | bytes 12292
  612.5 15.1 %slice-start.3 = ((s8[4718592]{0:T(1024)(128)(4,1)}), s8[524288]{0:T(1024)(128)(4,1)S(1)}, s32[]{:S(2)}) async-start(s8[4718592]{0:T(1024)(128)(4,1)} %bitcast.240), calls=%async_computation.8 | async-start | bytes 1048576
  612.5 15.1 %slice-start.6 = ((s8[4718592]{0:T(1024)(128)(4,1)}), s8[524288]{0:T(1024)(128)(4,1)S(1)}, s32[]{:S(2)}) async-start(s8[4718592]{0:T(1024)(128)(4,1)} %bitcast.249), calls=%async_computation.11 | async-start | bytes 1048576
  612.5 9.4 %collective-permute-start.32 = (f32[2,2,2,72,128]{4,3,2,1,0:T(8,128)S(1)}, f32[2,2,2,72,128]{4,3,2,1,0:T(8,128)S(1)}, u32[]{:S(2)}, u32[]{:S(2)}) collective-permute-start(f32[2,2,2,72,128]{4,3,2,1,0:T(8,128)S(1)} %dynamic-slice_bitcast_fusion.7), channel_id=1, source_target_pairs={{0,4},{2,6},{4,0},{6,2},{8,12},{10,14},{12,8},{14,10},{16,20},{18,... | collective-permute-start | bytes 884744 | tf_op jit(solution)/shard_map/ppermute | solution.py:360
  619.6 12.7 %collective-permute-start.22 = (bf16[1152,1024]{1,0:T(8,128)(2,1)}, bf16[1152,1024]{1,0:T(8,128)(2,1)}, u32[]{:S(2)}, u32[]{:S(2)}) collective-permute-start(bf16[1152,1024]{1,0:T(8,128)(2,1)} %convolution_convert_fusion), channel_id=1, source_target_pairs={{0,1},{1,0},{2,3},{3,2},{4,5},{5,4},{6,7},{7,6},{8,9},{9,8},{10,11... | collective-permute-start | bytes 7077896 | tf_op jit(solution)/shard_map/ppermute | solution.py:316
  622.0 5.4 collective-permute-start.33
  627.5 4.4 collective-permute-start.34
  632.1 5.5 collective-permute-start.35
  636.1 13.2 %collective-permute-start.23 = (bf16[2,2,2,72,512]{4,3,0,1,2:T(8,128)(2,1)S(1)}, bf16[2,2,2,72,512]{4,3,0,1,2:T(8,128)(2,1)S(1)}, u32[]{:S(2)}, u32[]{:S(2)}) collective-permute-start(bf16[2,2,2,72,512]{4,3,0,1,2:T(8,128)(2,1)S(1)} %bitcast.265), channel_id=1, source_target_pairs={{0,2},{2,0},{4,6},{6,4},{8,10},{10,8},{12,14},{14,12},{16,18},{18,... | collective-permute-start | bytes 1769480 | tf_op jit(solution)/shard_map/ppermute | solution.py:360
  637.8 14.1 %collective-permute-start.27 = (bf16[2,2,2,72,512]{4,3,0,1,2:T(8,128)(2,1)S(1)}, bf16[2,2,2,72,512]{4,3,0,1,2:T(8,128)(2,1)S(1)}, u32[]{:S(2)}, u32[]{:S(2)}) collective-permute-start(bf16[2,2,2,72,512]{4,3,0,1,2:T(8,128)(2,1)S(1)} %bitcast.266), channel_id=1, source_target_pairs={{0,4},{2,6},{4,0},{6,2},{8,12},{10,14},{12,8},{14,10},{16,20},{18,... | collective-permute-start | bytes 1769480 | tf_op jit(solution)/shard_map/ppermute | solution.py:360
  649.5 7.4 %collective-permute-start.24 = (bf16[2,2,72,512]{3,2,0,1:T(8,128)(2,1)S(1)}, bf16[2,2,72,512]{3,2,0,1:T(8,128)(2,1)S(1)}, u32[]{:S(2)}, u32[]{:S(2)}) collective-permute-start(bf16[2,2,72,512]{3,2,0,1:T(8,128)(2,1)S(1)} %dynamic-slice_bitcast_fusion.9), channel_id=1, source_target_pairs={{0,4},{2,6},{4,0},{6,2},{8,12},{10,14},{12,8},{14,10},{16,20},{18,... | collective-permute-start | bytes 884744 | tf_op jit(solution)/shard_map/ppermute | solution.py:360
  652.1 6.8 collective-permute-start.28
  657.1 5.2 collective-permute-start.25
  659.0 6.6 collective-permute-start.29
  662.3 6.1 collective-permute-start.26
  665.7 6.1 collective-permute-start.30
  (12 other events, 26.6 us)
Sparse Core Ops, SparseCore 0:
  11.5 66.3 all-gather.3
  80.7 73.3 all-gather.7
  157.1 114.4 all-gather.5
  407.8 192.5 reduce-scatter.1

commit v4 on v3

--- a/solution.py
+++ b/solution.py
@@ -39,12 +39,6 @@
     return jnp.concatenate([w[i, 0].astype(f32) for i in range(w.shape[0])], 0).astype(bf16)
 
 
-def scatter_rows(out, cols, u):
-    rows = out.shape[2]
-    for i in range(out.shape[0]):
-        out[i, 0, :, cols] = u[rows * i : rows * (i + 1)].astype(bf16)
-
-
 def turned(u, cosine, sine):
     lane = lax.broadcasted_iota(jnp.int32, u.shape, 1)
     h = HEAD_SIZE // 2
@@ -65,7 +59,8 @@
 
 
 def project(half, me, n1, w, cosine, sine, piece):
-    n, _, rows, width = w.shape
+    n, _, rows, _ = w.shape
+    width = WIDE
     batch = n1.shape[0] // piece
     return pl.pallas_call(
         project_body,
@@ -138,9 +133,9 @@
 
 
 def bwd_body(
-    me, mine, got, o_mine, o_theirs, do_mine, do_got, lse, cosine, sine,
-    lin_mine, lin_theirs, q, k, v, do, d, dka, dva, inner,
+    me, mine, got, o_mine, o_theirs, do_mine, do_got, lse, cosine, sine, *rest
 ):
+    lin_mine, lin_theirs, q, k, v, do, d, dka, dva, inner = rest[-10:]
     at = place(me, mine, got, q, k, v)
     inner[...] = jnp.zeros_like(inner)
     for dsrc, osrc, rows in zip((do_mine, do_got), (o_mine, o_theirs), at):
@@ -211,19 +206,21 @@
     )(me, mine, got)
 
 
-def attend_back(me, mine, got, o_mine, o_theirs, do_mine, do_got, lse, cosine, sine, piece):
+def attend_back(b, before, me, mine, got, o_mine, o_theirs, do_mine, do_got, lse, cosine, sine, piece):
     tokens, width = mine.shape
-    batch = tokens // piece
-    row = lambda a, c: pl.BlockSpec((a, c), lambda b, m: (b, 0))
+    row = lambda a, c: pl.BlockSpec((a, c), lambda _, m: (b, 0))
     cols = HQ * HEAD_SIZE
-    table = pl.BlockSpec((2 * piece, 128), lambda b, m: (0, 0))
+    table = pl.BlockSpec((2 * piece, 128), lambda _, m: (0, 0))
     heads = lambda n, t: pltpu.VMEM((n, 2 * piece, HEAD_SIZE), t)
     return pl.pallas_call(
         bwd_body,
         grid_spec=pltpu.PrefetchScalarGridSpec(
             num_scalar_prefetch=1,
-            grid=(batch,),
-            in_specs=[row(piece, width)] * 2 + [row(piece, cols)] * 4 + [row(2 * piece, 128), table, table],
+            grid=(1,),
+            in_specs=[row(piece, width)] * 2
+            + [row(piece, cols)] * 4
+            + [row(2 * piece, 128), table, table]
+            + [pl.BlockSpec(memory_space=pl.ANY)] * len(before),
             out_specs=[row(piece, width)] * 2,
             scratch_shapes=[heads(HQ, bf16), heads(HK, bf16), heads(HK, bf16), heads(HQ, bf16)]
             + [heads(HALL, f32)]
@@ -231,38 +228,61 @@
             + [pltpu.VMEM((2 * piece, 128), f32)],
         ),
         out_shape=[jax.ShapeDtypeStruct((tokens, width), bf16)] * 2,
+        input_output_aliases={10 + i: i for i in range(len(before))},
         compiler_params=pltpu.CompilerParams(vmem_limit_bytes=VMEM_BYTES),
-        cost_estimate=pl.CostEstimate(flops=27 * 10**9, bytes_accessed=40 * 10**6, transcendentals=12 * 10**6),
+        cost_estimate=pl.CostEstimate(flops=13 * 10**9, bytes_accessed=20 * 10**6, transcendentals=6 * 10**6),
         name="attend_back",
-    )(me, mine, got, o_mine, o_theirs, do_mine, do_got, lse, cosine, sine)
-
-
-def mlp_body(me, n2, n2t, cot, res, wg, wu, wd, out, gn, ggu, gd_mine, gd_theirs, y):
+    )(me, mine, got, o_mine, o_theirs, do_mine, do_got, lse, cosine, sine, *before)
+
+
+def mlp_body(me, n2, n2t, cot, res, wg, wu, wd_mine, wd_theirs, out, gn, g_mine, g_theirs, gd_mine, gd_theirs, y, wd):
     t = pl.program_id(0)
+    per = pl.num_programs(0) // 2
 
     @pl.when(t == 0)
     def _():
         y[...] = res[...]
         gn[...] = jnp.zeros_like(gn)
 
-    half = wd.shape[2]
-    wdt = jnp.concatenate([wd[0], wd[1]], axis=1)
+    half = wd_mine.shape[1]
+    first = me[0] == 0
+
+    @pl.when(first)
+    def _():
+        wd[:, :half] = wd_mine[...]
+        wd[:, half:] = wd_theirs[...]
+
+    @pl.when(jnp.logical_not(first))
+    def _():
+        wd[:, :half] = wd_theirs[...]
+        wd[:, half:] = wd_mine[...]
+
     wgt, wut = assemble(wg), assemble(wu)
     gate = dg(n2[...], wgt, NN)
     up = dg(n2[...], wut, NN)
-    gh = dg(cot[...], wdt, NT)
+    gh = dg(cot[...], wd[...], NT)
     sig = jax.nn.sigmoid(gate)
     act = gate * sig
     hidden = (act * up).astype(bf16)
     ggv = (gh * up * sig * (1.0 + gate * (1.0 - sig))).astype(bf16)
     guv = (gh * act).astype(bf16)
-    y[...] += dg(hidden, wdt, NN)
+    y[...] += dg(hidden, wd[...], NN)
     gdt = dg(hidden, cot[...], TN)
-    first = me[0] == 0
     gd_mine[...] = jnp.where(first, gdt[:, :half], gdt[:, half:]).astype(bf16)
     gd_theirs[...] = jnp.where(first, gdt[:, half:], gdt[:, :half]).astype(bf16)
-    scatter_rows(ggu, slice(0, FT), dg(n2t[...], ggv, NN))
-    scatter_rows(ggu, slice(FT, 2 * FT), dg(n2t[...], guv, NN))
+    gg = dg(n2t[...], ggv, NN).astype(bf16)
+    gu = dg(n2t[...], guv, NN).astype(bf16)
+
+    @pl.when(t < per)
+    def _():
+        g_theirs[:, :FT] = gg
+        g_theirs[:, FT:] = gu
+
+    @pl.when(t >= per)
+    def _():
+        g_mine[:, :FT] = gg
+        g_mine[:, FT:] = gu
+
     gn[...] += dg(ggv, wgt, NT) + dg(guv, wut, NT)
 
     @pl.when(t == pl.num_programs(0) - 1)
@@ -270,38 +290,46 @@
         out[...] = y[...].astype(bf16)
 
 
-def mlp(me, n2, n2t, cot, res, wide, wd):
+def mlp(me, n2, n2t, cot, res, wide, wd_mine, wd_theirs):
     tokens = n2.shape[0]
     n, _, rows, _ = wide.shape
     cols = FF // 2
     per = cols // FT
+    half = lambda t, m: 1 - m[0] ^ t // per
     whole = lambda a: pl.BlockSpec(a.shape, lambda t, m: (0, 0), pipeline_mode=pl.Buffered(1))
-    col = lambda first, width: pl.BlockSpec(
-        (n, 1, rows, width), lambda t, m: (0, t // per, 0, first + t % per)
-    )
-    row = pl.BlockSpec((2, FT, D // 2), lambda t, m: (0, t, 0))
-    part = pl.BlockSpec((FT, D // 2), lambda t, m: (t, 0))
+    col = lambda first: pl.BlockSpec(
+        (n, 1, rows, FT), lambda t, m: (0, half(t, m), 0, first + t % per)
+    )
+    part = pl.BlockSpec((FT, D // 2), lambda t, m: (half(t, m) * per + t % per, 0))
     one = lambda: pl.BlockSpec((tokens, D), lambda t, m: (0, 0), pipeline_mode=pl.Buffered(1))
     return pl.pallas_call(
         mlp_body,
         grid_spec=pltpu.PrefetchScalarGridSpec(
             num_scalar_prefetch=1,
             grid=(FF // FT,),
-            in_specs=[whole(n2), whole(n2t), whole(cot), whole(res), col(0, FT), col(per, FT), row],
-            out_specs=[one(), one(), col(0, 2 * FT), part, part],
-            scratch_shapes=[pltpu.VMEM((tokens, D), f32)],
+            in_specs=[whole(n2), whole(n2t), whole(cot), whole(res), col(0), col(per), part, part],
+            out_specs=[
+                one(),
+                one(),
+                pl.BlockSpec((D, 2 * FT), lambda t, m: (0, jnp.maximum(t - per, 0))),
+                pl.BlockSpec((D, 2 * FT), lambda t, m: (0, jnp.minimum(t, per - 1))),
+                part,
+                part,
+            ],
+            scratch_shapes=[pltpu.VMEM((tokens, D), f32), pltpu.VMEM((FT, D), bf16)],
         ),
         out_shape=[
             jax.ShapeDtypeStruct((tokens, D), bf16),
             jax.ShapeDtypeStruct((tokens, D), f32),
-            jax.ShapeDtypeStruct((n, 2, rows, 2 * cols), bf16),
+            jax.ShapeDtypeStruct((D, 2 * cols), bf16),
+            jax.ShapeDtypeStruct((D, 2 * cols), bf16),
             jax.ShapeDtypeStruct((FF, D // 2), bf16),
             jax.ShapeDtypeStruct((FF, D // 2), bf16),
         ],
         compiler_params=pltpu.CompilerParams(vmem_limit_bytes=VMEM_BYTES),
         cost_estimate=pl.CostEstimate(flops=65 * 10**9, bytes_accessed=60 * 10**6, transcendentals=3 * 10**6),
         name="mlp",
-    )(me, n2, n2t, cot, res, wide, wide, wd)
+    )(me, n2, n2t, cot, res, wide, wide, wd_mine, wd_theirs)
 
 
 def norm_back(grad_norm, rows_in, scale_rows, gain_rows):
@@ -328,40 +356,64 @@
     return g if w.shape[0] % 8 == 0 else whole_halves(g)
 
 
-def reduce_all(g):
-    n = lax.axis_size("dp")
-    if g.shape[0] != n:
-        g = jnp.swapaxes(g.reshape(2, n, -1, g.shape[3]), 0, 1)
-    return lax.psum_scatter(g.reshape(-1, g.shape[3]), BOTH, scatter_dimension=0, tiled=True)
+def exchange(a, bit):
+    return lax.ppermute(a, "dp", [(i, i ^ (1 << bit)) for i in range(lax.axis_size("dp"))])
+
+
+def column_parts(cols):
+    cut = cols // 256 * 128
+    parts = (slice(0, cut), (0, 1)), (slice(cut, cols), (1, 0))
+    return parts if cut else parts[1:]
+
+
+def gather_doubling(w):
+    bits = lax.axis_size("dp").bit_length() - 1
+    dp = lax.axis_index("dp")
+    out = []
+    for part, order in column_parts(w.shape[1]):
+        a, have = w[:, part], []
+        for bit in list(range(bits))[:1:-1] + list(order[::-1]):
+            got = exchange(a, bit)
+            axis = sum(b > bit for b in have)
+            have.append(bit)
+            a = jnp.where((dp >> bit) & 1 == 0, jnp.stack([a, got], axis), jnp.stack([got, a], axis))
+        out.append(a.reshape(-1, a.shape[-1]))
+    mine = jnp.concatenate(out, 1)
+    return mine, swap(mine)
 
 
 def add(a, b):
     return a.astype(f32) + b.astype(f32)
 
 
-def reduce_halving(mine, theirs, kind=bf16):
-    n = lax.axis_size("dp")
-    bits = n.bit_length() - 1
-    dp = lax.axis_index("dp")
-    both = add(mine, swap(theirs)).astype(kind)
-    cut = mine.shape[1] // 256 * 128
-    out = []
-    for part, order in ((both[:, :cut], [0, 1]), (both[:, cut:], [1, 0])):
-        if not part.shape[1]:
-            continue
-        left = list(range(bits))[::-1]
-        a = part.reshape(*[2] * bits, -1, part.shape[1])
-        for bit in order + list(range(2, bits)):
-            axis = left.index(bit)
-            left.remove(bit)
-            mybit = (dp >> bit) & 1
-            keep = lax.dynamic_index_in_dim(a, mybit, axis, keepdims=False)
-            send = lax.dynamic_index_in_dim(a, 1 - mybit, axis, keepdims=False)
-            a = add(keep, lax.ppermute(send, "dp", [(i, i ^ (1 << bit)) for i in range(n)]))
-            if left:
-                a = a.astype(kind)
-        out.append(a)
-    return jnp.concatenate(out, 1)
+class Halving:
+    def __init__(self, mine, theirs, kind=bf16):
+        self.kind = kind
+        self.bits = lax.axis_size("dp").bit_length() - 1
+        both = add(mine, swap(theirs)).astype(kind)
+        self.left = [list(range(self.bits))[::-1] for _ in column_parts(mine.shape[1])]
+        self.sums = []
+        for part, _ in column_parts(mine.shape[1]):
+            self.sums.append(both[:, part].reshape(*[2] * self.bits, -1, both[:, part].shape[1]))
+        for i in range(2):
+            for p, (_, order) in enumerate(column_parts(mine.shape[1])):
+                self.step(p, order[i])
+
+    def step(self, p, bit):
+        axis = self.left[p].index(bit)
+        self.left[p].remove(bit)
+        mybit = (lax.axis_index("dp") >> bit) & 1
+        a = self.sums[p]
+        keep = lax.dynamic_index_in_dim(a, mybit, axis, keepdims=False)
+        send = lax.dynamic_index_in_dim(a, 1 - mybit, axis, keepdims=False)
+        a = add(keep, exchange(send, bit))
+        self.sums[p] = a.astype(self.kind) if self.left[p] else a
+
+    def finish(self):
+        for bit in range(2, self.bits):
+            for p in range(len(self.sums)):
+                self.step(p, bit)
+        return jnp.concatenate(self.sums, 1)
 
 
 def local(
@@ -389,13 +441,12 @@
     sine = jnp.sin(angles) * jnp.where(jnp.arange(128) % HEAD_SIZE < h, -1.0, 1.0)[None, :]
 
     gains = jnp.pad(jnp.stack([gain_attn, gain_mlp], 1), ((0, 0), (0, WIDE - QKV - 2)))
-    full = fetch(jnp.concatenate([w_query, w_key, w_value, gains], 1))
-    wide = fetch(jnp.concatenate([w_gate, w_up, w_out], 1))
-    down = lax.all_gather(w_down, BOTH, axis=0, tiled=True)
-    full_down = whole_halves(down.reshape(-1, 2, *w_down.shape))[0]
+    full = fetch(jnp.concatenate([w_query, w_key, w_value, gains, w_out], 1))
+    wide = fetch(jnp.concatenate([w_gate, w_up], 1))
+    down_mine, down_theirs = gather_doubling(w_down)
     gain_one = full[:, 0, :, QKV].reshape(D).astype(f32)
     gain_two = full[:, 0, :, QKV + 1].reshape(D).astype(f32)
-    out_halves = whole_halves(wide[..., FF:])[0].reshape(2, 2, D // 2, D // 2)
+    out_halves = whole_halves(full[..., WIDE:])[0].reshape(2, 2, D // 2, D // 2)
     out_rows = lambda c: jnp.concatenate(
         [lax.dynamic_index_in_dim(out_halves[i], c, 0, keepdims=False) for i in range(2)], 1
     )
@@ -415,17 +466,17 @@
     residual = floats + (dot(mixed, out_mine) + dot(mixed_got, out_theirs))
     scale_mlp = lax.rsqrt(jnp.mean(residual * residual, -1, keepdims=True) + epsilon)
     n2 = (residual * scale_mlp * gain_two).astype(bf16)
-    layer_out, grad_n2, grad_wide, grad_down_mine, grad_down_theirs = mlp(
-        me_arr, n2, n2.T, cot, residual, wide, full_down
-    )
-    r_wide = reduce_all(grad_wide)
+    layer_out, grad_n2, g_mine, g_theirs, gd_mine, gd_theirs = mlp(
+        me_arr, n2, n2.T, cot, residual, wide, down_mine, down_theirs
+    )
+    r_wide = Halving(g_mine, g_theirs)
+    r_down = Halving(gd_mine, gd_theirs)
     sum_gain_mlp = jnp.sum(grad_n2 * residual * scale_mlp, 0)
     grad_residual = cot.astype(f32) + norm_back(grad_n2, residual, scale_mlp, gain_two)
     grad_low = grad_residual.astype(bf16)
     d_out = lax.dot_general(grad_low, out_theirs, NT, preferred_element_type=f32).astype(bf16)
     d_got = swap(d_out)
     d_mine = lax.dot_general(grad_low, out_mine, NT, preferred_element_type=f32).astype(bf16)
-    r_down = reduce_halving(grad_down_mine, grad_down_theirs)
     low = grad_low[:, : D // 2], grad_low[:, D // 2 :]
 
     def grad_out(columns):
@@ -433,21 +484,27 @@
         b = lax.dot_general(mixed_got, columns, TN, preferred_element_type=f32).astype(bf16)
         return pick(jnp.concatenate([a, b], 0), jnp.concatenate([b, a], 0))
 
-    r_out = reduce_halving(grad_out(pick(*low)), grad_out(pick(*low[::-1])))
-    lin_mine, lin_out = attend_back(
-        me_arr, mine, got, mixed, mixed_out, d_mine, d_got, lse, cosine, sine, piece
-    )
+    r_out = Halving(grad_out(pick(*low)), grad_out(pick(*low[::-1])))
+    lins = ()
+    for b in range(batch):
+        lins = attend_back(
+            b, lins, me_arr, mine, got, mixed, mixed_out, d_mine, d_got, lse, cosine, sine, piece
+        )
+    lin_mine, lin_out = lins
     lin_got = swap(lin_out)
     weight_grad = lambda lin: lax.dot_general(n1, lin, TN, preferred_element_type=f32).astype(bf16)
-    lin_got, r_out, r_down = lax.optimization_barrier((lin_got, r_out, r_down))
-    r_pack = reduce_halving(weight_grad(lin_mine), weight_grad(lin_got))
+    lin_got, r_wide.sums, r_down.sums, r_out.sums = lax.optimization_barrier(
+        (lin_got, r_wide.sums, r_down.sums, r_out.sums)
+    )
+    r_wide, r_down, r_out = r_wide.finish(), r_down.finish(), r_out.finish()
+    r_pack = Halving(weight_grad(lin_mine), weight_grad(lin_got)).finish()
     grad_n1 = lax.dot_general(lin_mine, w_mine, NT, preferred_element_type=f32) + lax.dot_general(
         lin_got, w_theirs, NT, preferred_element_type=f32
     )
     sum_gain_attn = jnp.sum(grad_n1 * floats * scale_attn, 0)
     grad_input = (grad_residual + norm_back(grad_n1, floats, scale_attn, gain_one)).astype(bf16)
     sums = jnp.pad(jnp.stack([sum_gain_attn, sum_gain_mlp], 1), ((0, 0), (0, 126)))
-    r_sums = reduce_halving(sums, sums, f32)
+    r_sums = Halving(sums, sums, f32).finish()
     r_gate, r_up = [
         a.reshape(a.shape[0], -1).astype(f32)
         for a in jnp.split(r_wide.reshape(-1, FF // 2 // FT, 2, FT), 2, 2)

time: 693 us -> 697 us (level)
  waiting for transfers between devices: 308 us -> 244 us
  other arithmetic: 46.5 us -> 69.6 us
  starting transfers between devices: 35.6 us -> 55.3 us
  local copies, waits for them, and re-layouts: 47.9 us -> 60.9 us
  Pallas kernels: 190 us -> 200 us
    all_gather x2, waiting for transfers between devices: 172 us -> 46.4 us  [fetch(): lax.all_gather(w, BOTH, axis=0, tiled=True)]
    ppermute x28 -> x44, waiting for transfers between devices: 117 us -> 198 us  [exchange(): lax.ppermute(a, 'dp', [(i, i ^ 1 << bit) for i in range(lax.axis_size('dp...]
    ppermute x28 -> x44, starting transfers between devices: 33.9 us -> 52.6 us  [exchange(): lax.ppermute(a, 'dp', [(i, i ^ 1 << bit) for i in range(lax.axis_size('dp...]
    all_gather x1 -> x0, waiting for transfers between devices: 17.9 us -> none  [local(): down = lax.all_gather(w_down, BOTH, axis=0, tiled=True)]
    convert_element_type x22 -> x28, other arithmetic: 15.8 us -> 25.9 us  [the longest x4 21.5 us: __init__(): both = add(mine, swap(theirs)).astype(kind)]
    select_n x0 -> x14, other arithmetic: none -> 7.79 us  [gather_doubling(): jnp.where(dp >> bit & 1 == 0, jnp.stack([a, got], axis), jnp.stack([got,...]
    concatenate x0 -> x2, local copies, waits for them, and re-layouts: none -> 7.77 us  [the longest x1 5.99 us: gather_doubling(): mine = jnp.concatenate(out, 1)]
    reshape x1 -> x0, local copies, waits for them, and re-layouts: 7.07 us -> none  [local(): full_down = whole_halves(down.reshape(-1, 2, *w_down.shape))[0]]
  transfers between devices with their start and end apart: 40 -> 56, of which waited for: 24 -> 31; matrix products, arithmetic and copies ran while one was open for 14% -> 21% of each run, Pallas kernels for 15% -> 16%
where the time goes in v4:
time: 697 us; the launch traced here: 688 us
  waiting for transfers between devices  244 us (35%)
  Pallas kernels  200 us (29%)
  other arithmetic  69.6 us (10%)
  local copies, waits for them, and re-layouts  60.9 us (9%)
  starting transfers between devices  55.3 us (8%)
  matrix products  42 us (6%)
  between operations  15.8 us (2%)
    ppermute x44, waiting for transfers between devices, exchange(): lax.ppermute(a, 'dp', [(i, i ^ 1 << bit) for i in range(lax.axis_size('dp...  198 us
    pallas_call x1, Pallas kernels, mlp(): pl.pallas_call(mlp_body, grid_spec=pltpu.PrefetchScalarGridSpec(num_scala...  93.6 us
    pallas_call x2, Pallas kernels, attend_back(): pl.pallas_call(bwd_body, grid_spec=pltpu.PrefetchScalarGridSpec(num_scala...  54.2 us
    ppermute x44, starting transfers between devices, exchange(): lax.ppermute(a, 'dp', [(i, i ^ 1 << bit) for i in range(lax.axis_size('dp...  52.6 us
    all_gather x2, waiting for transfers between devices, fetch(): lax.all_gather(w, BOTH, axis=0, tiled=True)  46.4 us
    pallas_call x1, Pallas kernels, attend(): pl.pallas_call(fwd_body, grid_spec=pltpu.PrefetchScalarGridSpec(num_scala...  38.9 us
    convert_element_type x4, other arithmetic, __init__(): both = add(mine, swap(theirs)).astype(kind)  21.5 us
    ppermute x3, local copies, waits for them, and re-layouts, swap(): return lax.ppermute(a, 'seq', [(0, 1), (1, 0)])  14 us
  transfers between devices with their start and end apart: 56, of which 31 were waited for; matrix products, arithmetic and copies ran while one was open for 21% of the time, Pallas kernels for 16%

profile of v4, /device:TPU:0, one launch (start us, length us, event | category | flops | bytes accessed | tf_op | source)
XLA Modules:
  0.0 688.1 jit_solution(16700628471591868457)
XLA Ops:
  12.9 4.1 collective-permute-start.6
  18.1 3.1 fusion.28
  21.8 8.4 %collective-permute-done.2 = bf16[192,256]{1,0:T(8,128)(2,1)S(1)} collective-permute-done((bf16[192,256]{1,0:T(8,128)(2,1)S(1)}, bf16[192,256]{1,0:T(8,128)(2,1)S(1)}, u32[]{:S(2)}, u32[]{:S(2)}) %collective-permute-start.2) | collective-permute-done | bytes 98336 | tf_op jit(solution)/shard_map/ppermute | solution.py:360
  30.2 2.4 collective-permute-start.3
  33.0 6.2 collective-permute-done.3
  40.9 4.0 collective-permute-done.7
  47.8 4.8 collective-permute-done.4
  55.3 9.9 %collective-permute-done.8 = bf16[2,2,192,320]{3,2,0,1:T(8,128)(2,1)S(1)} collective-permute-done((bf16[2,2,192,320]{3,2,0,1:T(8,128)(2,1)S(1)}, bf16[2,2,192,320]{3,2,0,1:T(8,128)(2,1)S(1)}, u32[]{:S(2)}, u32[]{:S(2)}) %collective-permute-start.8) | collective-permute-done | bytes 491552 | tf_op jit(solution)/shard_map/ppermute | solution.py:360
  68.1 39.5 %all-gather.3.cloned.1.call-done = bf16[2304,1600]{1,0:T(8,128)(2,1)} async-done(((bf16[72,1600]{1,0:T(8,128)(2,1)}), bf16[2304,1600]{1,0:T(8,128)(2,1)}) %all-gather.3.cloned.1.call-update) | async-done | bytes 7372816 | tf_op jit(solution)/shard_map/all_gather | solution.py:355
  107.6 2.2 convert_reduce_fusion
  112.6 6.8 project.3
  122.0 2.5 maximum_select_fusion
  124.8 2.3 pad_maximum_fusion.wd_mine
  127.1 6.0 copy.123
  133.4 6.8 project.2
  140.1 38.9 %attend.1 = (bf16[1024,576]{1,0:T(8,128)(2,1)}, bf16[1024,576]{1,0:T(8,128)(2,1)}, f32[2048,128]{1,0:T(8,128)}) custom-call(s32[1]{0:T(128)} %bitcast.me, bf16[1024,1024]{1,0:T(8,128)(2,1)} %get-tuple-element.35.mine, bf16[1024,1024]{1,0:T(8,128)(2,1)} %collective-permute-done.got), custom_call_target="tpu_custom_call" | custom-call | flops 24000000000 | bytes 20000000 | tf_op jit(solution)/shard_map/attend/pallas_call | solution.py:189
  181.5 6.1 copy.125.wd_theirs
  190.4 2.3 fusion.23
  193.9 2.5 multiply_reduce_fusion.2
  199.0 2.5 copy.124.n2t
  201.5 4.2 multiply_convert_fusion.n2
  205.8 7.0 %all-gather.5.cloned.1.call-done = bf16[2304,3072]{1,0:T(8,128)(2,1)} async-done(((bf16[72,3072]{1,0:T(8,128)(2,1)}), bf16[2304,3072]{1,0:T(8,128)(2,1)}) %all-gather.5.cloned.1.call-update) | async-done | bytes 14155792 | tf_op jit(solution)/shard_map/all_gather | solution.py:355
  212.7 93.6 %mlp.1 = (bf16[1024,1152]{1,0:T(8,128)(2,1)}, f32[1024,1152]{1,0:T(8,128)}, bf16[1152,3072]{1,0:T(8,128)(2,1)}, bf16[1152,3072]{1,0:T(8,128)(2,1)}, bf16[3072,57...) custom-call(s32[1]{0:T(128)} %bitcast.me, bf16[1024,1152]{1,0:T(8,128)(2,1)} %multiply_convert_fusion.n2, ...), custom_call_target="tpu_custom_call" | custom-call | flops 65000001536 | bytes 60000000 | tf_op jit(solution)/shard_map/mlp/pallas_call | solution.py:305
  306.4 5.0 multiply_reduce_fusion
  312.9 4.5 fusion.41
  317.5 2.7 convolution_convert_fusion.3
  326.4 6.1 copy.133
  332.8 4.8 convolution_convert_fusion.6
  337.6 2.5 convolution_convert_fusion.7
  340.1 3.3 convolution_convert_fusion.2.do_mine
  345.0 27.2 %attend_back.2 = (bf16[1024,1024]{1,0:T(8,128)(2,1)}, bf16[1024,1024]{1,0:T(8,128)(2,1)}) custom-call(s32[1]{0:T(128)} %bitcast.me, bf16[1024,1024]{1,0:T(8,128)(2,1)} %get-tuple-element.35.mine, bf16[1024,1024]{1,0:T(8,128)(2,1)} %collective-permute-done.got, bf16[1024,576]{1,0:T(8,128)(2,1)} %get-tuple-element.37.o_mine, ...), custom_call_target="tpu_custom_call" | custom-call | flops 12999999488 | bytes 20000000 | tf_op jit(solution)/shard_map/attend_back/pallas_call | solution.py:215
  372.2 27.0 %attend_back.3 = (bf16[1024,1024]{1,0:T(8,128)(2,1)}, bf16[1024,1024]{1,0:T(8,128)(2,1)}) custom-call(s32[1]{0:T(128)} %bitcast.me, bf16[1024,1024]{1,0:T(8,128)(2,1)} %get-tuple-element.35.mine, bf16[1024,1024]{1,0:T(8,128)(2,1)} %collective-permute-done.got, ...), custom_call_target="tpu_custom_call", output_to_operand_aliasing={{0}: (10, {}), {1}: (11, {})} | custom-call | flops 12999999488 | bytes 20000000 | tf_op jit(solution)/shard_map/attend_back/pallas_call | solution.py:215
  399.5 2.5 add_convert_fusion.3
  405.4 6.4 convolution_convert_fusion.1
  418.2 6.2 copy.134
  424.5 4.3 add_convert_fusion.1
  431.0 11.2 %add_convert_fusion = bf16[1152,3072]{1,0:T(8,128)(2,1)} fusion(bf16[1152,3072]{1,0:T(8,128)(2,1)} %collective-permute-done.13, bf16[1152,3072]{1,0:T(8,128)(2,1)} %get-tuple-element.47), kind=kLoop, calls=%fused_computation | loop fusion | flops 14155776 | bytes 21233664 | tf_op jit(solution)/shard_map/convert_element_type | solution.py:393
  442.2 3.5 fusion.42
  454.4 58.7 %collective-permute-done.21 = bf16[2,2,2,192,320]{4,3,0,1,2:T(8,128)(2,1)S(1)} collective-permute-done((bf16[2,2,2,192,320]{4,3,0,1,2:T(8,128)(2,1)S(1)}, bf16[2,2,2,192,320]{4,3,0,1,2:T(8,128)(2,1)S(1)}, u32[]{:S(2)}, u32[]{:S(2)}) %collective-permute-start.21) | collective-permute-done | bytes 983072 | tf_op jit(solution)/shard_map/ppermute | solution.py:360
  518.8 2.8 collective-permute-done.20
  521.7 8.1 %collective-permute-done.22 = bf16[2,2,192,320]{3,2,0,1:T(8,128)(2,1)S(1)} collective-permute-done((bf16[2,2,192,320]{3,2,0,1:T(8,128)(2,1)S(1)}, bf16[2,2,192,320]{3,2,0,1:T(8,128)(2,1)S(1)}, u32[]{:S(2)}, u32[]{:S(2)}) %collective-permute-start.22) | collective-permute-done | bytes 491552 | tf_op jit(solution)/shard_map/ppermute | solution.py:360
  529.9 13.5 %collective-permute-done.17 = bf16[2,2,72,1536]{3,2,0,1:T(8,128)(2,1)S(1)} collective-permute-done((bf16[2,2,72,1536]{3,2,0,1:T(8,128)(2,1)S(1)}, bf16[2,2,72,1536]{3,2,0,1:T(8,128)(2,1)S(1)}, u32[]{:S(2)}, u32[]{:S(2)}) %collective-permute-start.17) | collective-permute-done | bytes 884768 | tf_op jit(solution)/shard_map/ppermute | solution.py:360
  548.4 5.9 convolution_convert_fusion
  554.4 4.7 fusion.46
  559.1 3.6 fusion.9
  563.6 2.5 fusion.6
  566.1 7.6 %collective-permute-done.37 = bf16[2,72,256]{2,1,0:T(8,128)(2,1)S(1)} collective-permute-done((bf16[2,72,256]{2,1,0:T(8,128)(2,1)S(1)}, bf16[2,72,256]{2,1,0:T(8,128)(2,1)S(1)}, u32[]{:S(2)}, u32[]{:S(2)}) %collective-permute-start.37) | collective-permute-done | bytes 73760 | tf_op jit(solution)/shard_map/ppermute | solution.py:360
  574.1 4.3 collective-permute-done.39
  578.5 2.2 collective-permute-start.38
  580.7 2.8 collective-permute-done.38
  585.5 3.3 collective-permute-done.40
  592.1 5.3 collective-permute-done.51
  597.7 12.4 %collective-permute-done.53 = bf16[192,320]{1,0:T(8,128)(2,1)S(1)} collective-permute-done((bf16[192,320]{1,0:T(8,128)(2,1)S(1)}, bf16[192,320]{1,0:T(8,128)(2,1)S(1)}, u32[]{:S(2)}, u32[]{:S(2)}) %collective-permute-start.53) | collective-permute-done | bytes 122912 | tf_op jit(solution)/shard_map/ppermute | solution.py:360
  611.4 3.0 collective-permute-start.49
  614.7 6.1 collective-permute-done.47
  620.9 4.6 collective-permute-done.49
  627.8 3.8 collective-permute-done.43
  631.6 2.3 slice_reduce_fusion
  638.1 3.5 add_convert_fusion.2
  642.0 3.9 collective-permute-start.33
  647.0 11.0 %collective-permute-done.33 = bf16[2,2,2,72,512]{4,3,0,1,2:T(8,128)(2,1)S(1)} collective-permute-done((bf16[2,2,2,72,512]{4,3,0,1,2:T(8,128)(2,1)S(1)}, bf16[2,2,2,72,512]{4,3,0,1,2:T(8,128)(2,1)S(1)}, u32[]{:S(2)}, u32[]{:S(2)}) %collective-permute-start.33) | collective-permute-done | bytes 589856 | tf_op jit(solution)/shard_map/ppermute | solution.py:360
  660.8 5.2 collective-permute-done.34
  668.5 3.1 collective-permute-done.35
  675.1 2.7 collective-permute-done.36
  (317 shorter events, 101.7 us)
Async XLA Ops:
  7.2 14.0 %copy-start.1 = (bf16[2,1,512,1152]{3,2,1,0:T(8,128)(2,1)S(1)}, bf16[2,1,512,1152]{3,2,1,0:T(8,128)(2,1)}, u32[]{:S(2)}) copy-start(bf16[2,1,512,1152]{3,2,1,0:T(8,128)(2,1)} %param.11) | copy-start | bytes 7077892
  7.2 100.4 %all-gather.3.cloned.1.call-start = ((), (), s32[]{:S(2)}) async-start(), calls=%async_computation | async-start | bytes 7907328 | tf_op jit(solution)/shard_map/all_gather | solution.py:355
  10.0 202.7 %all-gather.5.cloned.1.call-start = ((), (), s32[]{:S(2)}) async-start(), calls=%async_computation.1 | async-start | bytes 14598144 | tf_op jit(solution)/shard_map/all_gather | solution.py:355
  12.9 19.8 %collective-permute-start.6 = (bf16[192,320]{1,0:T(8,128)(2,1)S(1)}, bf16[192,320]{1,0:T(8,128)(2,1)S(1)}, u32[]{:S(2)}, u32[]{:S(2)}) collective-permute-start(bf16[192,320]{1,0:T(8,128)(2,1)S(1)} %get-tuple-element.151), channel_id=1, source_target_pairs={{0,16},{2,18},{4,20},{6,22},{8,24},{10,26},{12,28},{14,30},{16,0},... | collective-permute-start | bytes 368648 | tf_op jit(solution)/shard_map/ppermute | solution.py:360
  17.9 12.3 %collective-permute-start.2 = (bf16[192,256]{1,0:T(8,128)(2,1)S(1)}, bf16[192,256]{1,0:T(8,128)(2,1)S(1)}, u32[]{:S(2)}, u32[]{:S(2)}) collective-permute-start(bf16[192,256]{1,0:T(8,128)(2,1)S(1)} %get-tuple-element.148), channel_id=1, source_target_pairs={{0,16},{2,18},{4,20},{6,22},{8,24},{10,26},{12,28},{14,30},{16,0},... | collective-permute-start | bytes 294920 | tf_op jit(solution)/shard_map/ppermute | solution.py:360
  21.8 159.1 %copy-start.26 = (f32[1,4,2,128]{3,1,2,0:T(4,128)}, f32[1,4,2,128]{3,1,2,0:T(4,128)S(1)}, u32[]{:S(2)}) copy-start(f32[1,4,2,128]{3,1,2,0:T(4,128)S(1)} %copy.158) | copy-start | bytes 12292
  30.2 9.0 %collective-permute-start.3 = (bf16[2,192,256]{2,1,0:T(8,128)(2,1)S(1)}, bf16[2,192,256]{2,1,0:T(8,128)(2,1)S(1)}, u32[]{:S(2)}, u32[]{:S(2)}) collective-permute-start(bf16[2,192,256]{2,1,0:T(8,128)(2,1)S(1)} %maximum_select_fusion.15), channel_id=1, source_target_pairs={{0,8},{2,10},{4,12},{6,14},{8,0},{10,2},{12,4},{14,6},{16,24},{18,... | collective-permute-start | bytes 589832 | tf_op jit(solution)/shard_map/ppermute | solution.py:360
  32.7 12.2 %collective-permute-start.7 = (bf16[2,192,320]{2,1,0:T(8,128)(2,1)S(1)}, bf16[2,192,320]{2,1,0:T(8,128)(2,1)S(1)}, u32[]{:S(2)}, u32[]{:S(2)}) collective-permute-start(bf16[2,192,320]{2,1,0:T(8,128)(2,1)S(1)} %maximum_select_fusion.13), channel_id=1, source_target_pairs={{0,8},{2,10},{4,12},{6,14},{8,0},{10,2},{12,4},{14,6},{16,24},{18,... | collective-permute-start | bytes 737288 | tf_op jit(solution)/shard_map/ppermute | solution.py:360
  39.3 13.3 %collective-permute-start.4 = (bf16[2,2,192,256]{3,2,0,1:T(8,128)(2,1)S(1)}, bf16[2,2,192,256]{3,2,0,1:T(8,128)(2,1)S(1)}, u32[]{:S(2)}, u32[]{:S(2)}) collective-permute-start(bf16[2,2,192,256]{3,2,0,1:T(8,128)(2,1)S(1)} %maximum_select_fusion.11), channel_id=1, source_target_pairs={{0,4},{2,6},{4,0},{6,2},{8,12},{10,14},{12,8},{14,10},{16,20},{18,... | collective-permute-start | bytes 1179656 | tf_op jit(solution)/shard_map/ppermute | solution.py:360
  45.1 20.1 %collective-permute-start.8 = (bf16[2,2,192,320]{3,2,0,1:T(8,128)(2,1)S(1)}, bf16[2,2,192,320]{3,2,0,1:T(8,128)(2,1)S(1)}, u32[]{:S(2)}, u32[]{:S(2)}) collective-permute-start(bf16[2,2,192,320]{3,2,0,1:T(8,128)(2,1)S(1)} %maximum_select_fusion.9), channel_id=1, source_target_pairs={{0,2},{2,0},{4,6},{6,4},{8,10},{10,8},{12,14},{14,12},{16,18},{18,... | collective-permute-start | bytes 1474568 | tf_op jit(solution)/shard_map/ppermute | solution.py:360
  52.6 12.6 %copy-start.15 = (bf16[2,2,192,256]{3,2,0,1:T(8,128)(2,1)}, bf16[2,2,192,256]{3,2,0,1:T(8,128)(2,1)S(1)}, u32[]{:S(2)}) copy-start(bf16[2,2,192,256]{3,2,0,1:T(8,128)(2,1)S(1)} %collective-permute-done.4) | copy-start | bytes 1179652
  53.7 66.5 %collective-permute-start.5 = (bf16[2,2,2,192,256]{4,3,0,1,2:T(8,128)(2,1)}, bf16[2,2,2,192,256]{4,3,0,1,2:T(8,128)(2,1)}, u32[]{:S(2)}, u32[]{:S(2)}) collective-permute-start(bf16[2,2,2,192,256]{4,3,0,1,2:T(8,128)(2,1)} %maximum_select_fusion.7), channel_id=1, source_target_pairs={{0,2},{2,0},{4,6},{6,4},{8,10},{10,8},{12,14},{14,12},{16,18},{18,... | collective-permute-start | bytes 2359304 | tf_op jit(solution)/shard_map/ppermute | solution.py:360
  66.6 55.3 %collective-permute-start.9 = (bf16[2,2,2,192,320]{4,3,0,1,2:T(8,128)(2,1)}, bf16[2,2,2,192,320]{4,3,0,1,2:T(8,128)(2,1)}, u32[]{:S(2)}, u32[]{:S(2)}) collective-permute-start(bf16[2,2,2,192,320]{4,3,0,1,2:T(8,128)(2,1)} %maximum_select_fusion.5), channel_id=1, source_target_pairs={{0,4},{2,6},{4,0},{6,2},{8,12},{10,14},{12,8},{14,10},{16,20},{18,... | collective-permute-start | bytes 2949128 | tf_op jit(solution)/shard_map/ppermute | solution.py:360
  112.6 7.1 %copy-start.16 = (bf16[2,2,192,256]{3,2,0,1:T(8,128)(2,1)S(1)}, bf16[2,2,192,256]{3,2,0,1:T(8,128)(2,1)}, u32[]{:S(2)}) copy-start(bf16[2,2,192,256]{3,2,0,1:T(8,128)(2,1)} %copy-done.15) | copy-start | bytes 1179652
  112.6 7.1 %copy-start.17 = (bf16[2,2,1,1,192,256]{5,4,0,1,2,3:T(8,128)(2,1)S(1)}, bf16[2,2,1,1,192,256]{5,4,0,1,2,3:T(8,128)(2,1)}, u32[]{:S(2)}) copy-start(bf16[2,2,1,1,192,256]{5,4,0,1,2,3:T(8,128)(2,1)} %fusion.63) | copy-start | bytes 1179652
  119.4 20.7 %collective-permute-start = (bf16[1024,1024]{1,0:T(8,128)(2,1)}, bf16[1024,1024]{1,0:T(8,128)(2,1)}, u32[]{:S(2)}, u32[]{:S(2)}) collective-permute-start(bf16[1024,1024]{1,0:T(8,128)(2,1)} %get-tuple-element.36), channel_id=1, source_target_pairs={{0,1},{1,0},{2,3},{3,2},{4,5},{5,4},{6,7},{7,6},{8,9},{9,8},{10,11... | collective-permute-start | bytes 6291464 | tf_op jit(solution)/shard_map/ppermute | solution.py:344
  133.1 48.4 %collective-permute-start.10 = (bf16[3072,576]{0,1:T(8,128)(2,1)}, bf16[3072,576]{0,1:T(8,128)(2,1)}, u32[]{:S(2)}, u32[]{:S(2)}) collective-permute-start(bf16[3072,576]{0,1:T(8,128)(2,1)} %copy.123), channel_id=1, source_target_pairs={{0,1},{1,0},{2,3},{3,2},{4,5},{5,4},{6,7},{7,6},{8,9},{9,8},{10,11... | collective-permute-start | bytes 10616840 | tf_op jit(solution)/shard_map/ppermute | solution.py:344
  180.6 9.8 %collective-permute-start.1 = (bf16[1024,576]{0,1:T(8,128)(2,1)S(1)}, bf16[1024,576]{0,1:T(8,128)(2,1)S(1)}, u32[]{:S(2)}, u32[]{:S(2)}) collective-permute-start(bf16[1024,576]{0,1:T(8,128)(2,1)S(1)} %copy.120), channel_id=1, source_target_pairs={{0,1},{1,0},{2,3},{3,2},{4,5},{5,4},{6,7},{7,6},{8,9},{9,8},{10,11... | collective-permute-start | bytes 3538952 | tf_op jit(solution)/shard_map/ppermute | solution.py:344
  321.8 109.2 %collective-permute-start.13 = (bf16[1152,3072]{1,0:T(8,128)(2,1)}, bf16[1152,3072]{1,0:T(8,128)(2,1)}, u32[]{:S(2)}, u32[]{:S(2)}) collective-permute-start(bf16[1152,3072]{1,0:T(8,128)(2,1)} %get-tuple-element.48), channel_id=1, source_target_pairs={{0,1},{1,0},{2,3},{3,2},{4,5},{5,4},{6,7},{7,6},{8,9},{9,8},{10,11... | collective-permute-start | bytes 21233672 | tf_op jit(solution)/shard_map/ppermute | solution.py:344
  322.1 21.2 %collective-permute-start.11 = (bf16[1024,576]{0,1:T(8,128)(2,1)}, bf16[1024,576]{0,1:T(8,128)(2,1)S(1)}, u32[]{:S(2)}, u32[]{:S(2)}) collective-permute-start(bf16[1024,576]{0,1:T(8,128)(2,1)} %convolution_convert_fusion.3), channel_id=1, source_target_pairs={{0,1},{1,0},{2,3},{3,2},{4,5},{5,4},{6,7},{7,6},{8,9},{9,8},{10,11... | collective-permute-start | bytes 3538952 | tf_op jit(solution)/shard_map/ppermute | solution.py:344
  326.2 73.3 %collective-permute-start.23 = (bf16[1152,576]{0,1:T(8,128)(2,1)}, bf16[1152,576]{0,1:T(8,128)(2,1)}, u32[]{:S(2)}, u32[]{:S(2)}) collective-permute-start(bf16[1152,576]{0,1:T(8,128)(2,1)} %maximum_select_fusion.3), channel_id=1, source_target_pairs={{0,1},{1,0},{2,3},{3,2},{4,5},{5,4},{6,7},{7,6},{8,9},{9,8},{10,11... | collective-permute-start | bytes 3981320 | tf_op jit(solution)/shard_map/ppermute | solution.py:344
  332.6 85.7 %collective-permute-start.18 = (bf16[3072,576]{0,1:T(8,128)(2,1)}, bf16[3072,576]{0,1:T(8,128)(2,1)}, u32[]{:S(2)}, u32[]{:S(2)}) collective-permute-start(bf16[3072,576]{0,1:T(8,128)(2,1)} %copy.133), channel_id=1, source_target_pairs={{0,1},{1,0},{2,3},{3,2},{4,5},{5,4},{6,7},{7,6},{8,9},{9,8},{10,11... | collective-permute-start | bytes 10616840 | tf_op jit(solution)/shard_map/ppermute | solution.py:344
  372.2 27.3 %copy-start.22 = (bf16[576,576]{0,1:T(8,128)(2,1)S(1)}, bf16[576,576]{0,1:T(8,128)(2,1)}, u32[]{:S(2)}) copy-start(bf16[576,576]{0,1:T(8,128)(2,1)} %convolution_convert_fusion.6) | copy-start | bytes 1990660
  372.2 27.3 %copy-start.23 = (bf16[576,576]{0,1:T(8,128)(2,1)S(1)}, bf16[576,576]{0,1:T(8,128)(2,1)}, u32[]{:S(2)}) copy-start(bf16[576,576]{0,1:T(8,128)(2,1)} %convolution_convert_fusion.7) | copy-start | bytes 1990660
  399.2 144.7 %collective-permute-start.12 = (bf16[1024,1024]{1,0:T(8,128)(2,1)}, bf16[1024,1024]{1,0:T(8,128)(2,1)}, u32[]{:S(2)}, u32[]{:S(2)}) collective-permute-start(bf16[1024,1024]{1,0:T(8,128)(2,1)} %get-tuple-element.46), channel_id=1, source_target_pairs={{0,1},{1,0},{2,3},{3,2},{4,5},{5,4},{6,7},{7,6},{8,9},{9,8},{10,11... | collective-permute-start | bytes 6291464 | tf_op jit(solution)/shard_map/ppermute | solution.py:344
  403.1 12.4 %collective-permute-start.26 = (bf16[2,2,2,72,320]{4,3,2,1,0:T(8,128)(2,1)S(1)}, bf16[2,2,2,72,320]{4,3,2,1,0:T(8,128)(2,1)S(1)}, u32[]{:S(2)}, u32[]{:S(2)}) collective-permute-start(bf16[2,2,2,72,320]{4,3,2,1,0:T(8,128)(2,1)S(1)} %dynamic-slice_bitcast_fusion.9), channel_id=1, source_target_pairs={{0,4},{2,6},{4,0},{6,2},{8,12},{10,14},{12,8},{14,10},{16,20},{18,... | collective-permute-start | bytes 1105928 | tf_op jit(solution)/shard_map/ppermute | solution.py:360
  404.8 9.0 %collective-permute-start.24 = (bf16[2,2,2,72,256]{4,3,2,1,0:T(8,128)(2,1)S(1)}, bf16[2,2,2,72,256]{4,3,2,1,0:T(8,128)(2,1)S(1)}, u32[]{:S(2)}, u32[]{:S(2)}) collective-permute-start(bf16[2,2,2,72,256]{4,3,2,1,0:T(8,128)(2,1)S(1)} %dynamic-slice_bitcast_fusion.15), channel_id=1, source_target_pairs={{0,2},{2,0},{4,6},{6,4},{8,10},{10,8},{12,14},{14,12},{16,18},{18,... | collective-permute-start | bytes 884744 | tf_op jit(solution)/shard_map/ppermute | solution.py:360
  413.9 34.5 %collective-permute-start.25 = (bf16[2,2,72,256]{3,2,1,0:T(8,128)(2,1)S(1)}, bf16[2,2,72,256]{3,2,1,0:T(8,128)(2,1)S(1)}, u32[]{:S(2)}, u32[]{:S(2)}) collective-permute-start(bf16[2,2,72,256]{3,2,1,0:T(8,128)(2,1)S(1)} %dynamic-slice_bitcast_fusion.24), channel_id=1, source_target_pairs={{0,4},{2,6},{4,0},{6,2},{8,12},{10,14},{12,8},{14,10},{16,20},{18,... | collective-permute-start | bytes 442376 | tf_op jit(solution)/shard_map/ppermute | solution.py:360
  416.3 34.8 %collective-permute-start.27 = (bf16[2,2,72,320]{3,2,1,0:T(8,128)(2,1)}, bf16[2,2,72,320]{3,2,1,0:T(8,128)(2,1)}, u32[]{:S(2)}, u32[]{:S(2)}) collective-permute-start(bf16[2,2,72,320]{3,2,1,0:T(8,128)(2,1)} %dynamic-slice_bitcast_fusion.18), channel_id=1, source_target_pairs={{0,2},{2,0},{4,6},{6,4},{8,10},{10,8},{12,14},{14,12},{16,18},{18,... | collective-permute-start | bytes 552968 | tf_op jit(solution)/shard_map/ppermute | solution.py:360
  430.9 23.1 %collective-permute-start.19 = (bf16[2,2,2,192,256]{4,3,0,1,2:T(8,128)(2,1)S(1)}, bf16[2,2,2,192,256]{4,3,0,1,2:T(8,128)(2,1)S(1)}, u32[]{:S(2)}, u32[]{:S(2)}) collective-permute-start(bf16[2,2,2,192,256]{4,3,0,1,2:T(8,128)(2,1)S(1)} %bitcast.360), channel_id=1, source_target_pairs={{0,2},{2,0},{4,6},{6,4},{8,10},{10,8},{12,14},{14,12},{16,18},{18,... | collective-permute-start | bytes 2359304 | tf_op jit(solution)/shard_map/ppermute | solution.py:360
  446.2 69.2 %collective-permute-start.16 = (bf16[2,2,2,72,1536]{4,3,0,1,2:T(8,128)(2,1)S(1)}, bf16[2,2,2,72,1536]{4,3,0,1,2:T(8,128)(2,1)S(1)}, u32[]{:S(2)}, u32[]{:S(2)}) collective-permute-start(bf16[2,2,2,72,1536]{4,3,0,1,2:T(8,128)(2,1)S(1)} %bitcast.342), channel_id=1, source_target_pairs={{0,4},{2,6},{4,0},{6,2},{8,12},{10,14},{12,8},{14,10},{16,20},{18,... | collective-permute-start | bytes 5308424 | tf_op jit(solution)/shard_map/ppermute | solution.py:360
  450.5 62.6 %collective-permute-start.21 = (bf16[2,2,2,192,320]{4,3,0,1,2:T(8,128)(2,1)S(1)}, bf16[2,2,2,192,320]{4,3,0,1,2:T(8,128)(2,1)S(1)}, u32[]{:S(2)}, u32[]{:S(2)}) collective-permute-start(bf16[2,2,2,192,320]{4,3,0,1,2:T(8,128)(2,1)S(1)} %bitcast.356), channel_id=1, source_target_pairs={{0,4},{2,6},{4,0},{6,2},{8,12},{10,14},{12,8},{14,10},{16,20},{18,... | collective-permute-start | bytes 2949128 | tf_op jit(solution)/shard_map/ppermute | solution.py:360
  451.0 65.1 %collective-permute-start.14 = (bf16[2,2,2,72,1536]{4,3,0,1,2:T(8,128)(2,1)S(1)}, bf16[2,2,2,72,1536]{4,3,0,1,2:T(8,128)(2,1)S(1)}, u32[]{:S(2)}, u32[]{:S(2)}) collective-permute-start(bf16[2,2,2,72,1536]{4,3,0,1,2:T(8,128)(2,1)S(1)} %bitcast.343), channel_id=1, source_target_pairs={{0,2},{2,0},{4,6},{6,4},{8,10},{10,8},{12,14},{14,12},{16,18},{18,... | collective-permute-start | bytes 5308424 | tf_op jit(solution)/shard_map/ppermute | solution.py:360
  454.2 67.3 %collective-permute-start.20 = (bf16[2,2,192,256]{3,2,0,1:T(8,128)(2,1)S(1)}, bf16[2,2,192,256]{3,2,0,1:T(8,128)(2,1)S(1)}, u32[]{:S(2)}, u32[]{:S(2)}) collective-permute-start(bf16[2,2,192,256]{3,2,0,1:T(8,128)(2,1)S(1)} %dynamic-slice_bitcast_fusion.10), channel_id=1, source_target_pairs={{0,4},{2,6},{4,0},{6,2},{8,12},{10,14},{12,8},{14,10},{16,20},{18,... | collective-permute-start | bytes 1179656 | tf_op jit(solution)/shard_map/ppermute | solution.py:360
  513.5 16.3 %collective-permute-start.22 = (bf16[2,2,192,320]{3,2,0,1:T(8,128)(2,1)S(1)}, bf16[2,2,192,320]{3,2,0,1:T(8,128)(2,1)S(1)}, u32[]{:S(2)}, u32[]{:S(2)}) collective-permute-start(bf16[2,2,192,320]{3,2,0,1:T(8,128)(2,1)S(1)} %dynamic-slice_bitcast_fusion.6), channel_id=1, source_target_pairs={{0,2},{2,0},{4,6},{6,4},{8,10},{10,8},{12,14},{14,12},{16,18},{18,... | collective-permute-start | bytes 1474568 | tf_op jit(solution)/shard_map/ppermute | solution.py:360
  516.0 27.4 %collective-permute-start.17 = (bf16[2,2,72,1536]{3,2,0,1:T(8,128)(2,1)S(1)}, bf16[2,2,72,1536]{3,2,0,1:T(8,128)(2,1)S(1)}, u32[]{:S(2)}, u32[]{:S(2)}) collective-permute-start(bf16[2,2,72,1536]{3,2,0,1:T(8,128)(2,1)S(1)} %dynamic-slice_bitcast_fusion), channel_id=1, source_target_pairs={{0,2},{2,0},{4,6},{6,4},{8,10},{10,8},{12,14},{14,12},{16,18},{18,... | collective-permute-start | bytes 2654216 | tf_op jit(solution)/shard_map/ppermute | solution.py:360
  516.7 27.0 %collective-permute-start.15 = (bf16[2,2,72,1536]{3,2,0,1:T(8,128)(2,1)S(1)}, bf16[2,2,72,1536]{3,2,0,1:T(8,128)(2,1)S(1)}, u32[]{:S(2)}, u32[]{:S(2)}) collective-permute-start(bf16[2,2,72,1536]{3,2,0,1:T(8,128)(2,1)S(1)} %dynamic-slice_bitcast_fusion.1), channel_id=1, source_target_pairs={{0,4},{2,6},{4,0},{6,2},{8,12},{10,14},{12,8},{14,10},{16,20},{18,... | collective-permute-start | bytes 2654216 | tf_op jit(solution)/shard_map/ppermute | solution.py:360
  544.0 45.5 %collective-permute-start.50 = (bf16[2,192,256]{2,1,0:T(8,128)(2,1)S(1)}, bf16[2,192,256]{2,1,0:T(8,128)(2,1)S(1)}, u32[]{:S(2)}, u32[]{:S(2)}) collective-permute-start(bf16[2,192,256]{2,1,0:T(8,128)(2,1)S(1)} %dynamic-slice_bitcast_fusion.19), channel_id=1, source_target_pairs={{0,8},{2,10},{4,12},{6,14},{8,0},{10,2},{12,4},{14,6},{16,24},{18,... | collective-permute-start | bytes 589832 | tf_op jit(solution)/shard_map/ppermute | solution.py:360
  544.8 45.3 %collective-permute-start.52 = (bf16[2,192,320]{2,1,0:T(8,128)(2,1)S(1)}, bf16[2,192,320]{2,1,0:T(8,128)(2,1)S(1)}, u32[]{:S(2)}, u32[]{:S(2)}) collective-permute-start(bf16[2,192,320]{2,1,0:T(8,128)(2,1)S(1)} %dynamic-slice_bitcast_fusion.11), channel_id=1, source_target_pairs={{0,8},{2,10},{4,12},{6,14},{8,0},{10,2},{12,4},{14,6},{16,24},{18,... | collective-permute-start | bytes 737288 | tf_op jit(solution)/shard_map/ppermute | solution.py:360
  546.2 64.8 %collective-permute-start.46 = (bf16[2,72,1536]{2,1,0:T(8,128)(2,1)S(1)}, bf16[2,72,1536]{2,1,0:T(8,128)(2,1)S(1)}, u32[]{:S(2)}, u32[]{:S(2)}) collective-permute-start(bf16[2,72,1536]{2,1,0:T(8,128)(2,1)S(1)} %dynamic-slice_bitcast_fusion.8), channel_id=1, source_target_pairs={{0,8},{2,10},{4,12},{6,14},{8,0},{10,2},{12,4},{14,6},{16,24},{18,... | collective-permute-start | bytes 1327112 | tf_op jit(solution)/shard_map/ppermute | solution.py:360
  547.0 7.3 %copy-start.32 = (bf16[1152,1024]{1,0:T(8,128)(2,1)S(1)}, bf16[1152,1024]{1,0:T(8,128)(2,1)}, u32[]{:S(2)}) copy-start(bf16[1152,1024]{1,0:T(8,128)(2,1)} %get-tuple-element.52) | copy-start | bytes 7077892
  547.0 64.2 %collective-permute-start.48 = (bf16[2,72,1536]{2,1,0:T(8,128)(2,1)S(1)}, bf16[2,72,1536]{2,1,0:T(8,128)(2,1)S(1)}, u32[]{:S(2)}, u32[]{:S(2)}) collective-permute-start(bf16[2,72,1536]{2,1,0:T(8,128)(2,1)S(1)} %dynamic-slice_bitcast_fusion.7), channel_id=1, source_target_pairs={{0,8},{2,10},{4,12},{6,14},{8,0},{10,2},{12,4},{14,6},{16,24},{18,... | collective-permute-start | bytes 1327112 | tf_op jit(solution)/shard_map/ppermute | solution.py:360
  562.7 11.0 %collective-permute-start.37 = (bf16[2,72,256]{2,1,0:T(8,128)(2,1)S(1)}, bf16[2,72,256]{2,1,0:T(8,128)(2,1)S(1)}, u32[]{:S(2)}, u32[]{:S(2)}) collective-permute-start(bf16[2,72,256]{2,1,0:T(8,128)(2,1)S(1)} %dynamic-slice_bitcast_fusion.28), channel_id=1, source_target_pairs={{0,8},{2,10},{4,12},{6,14},{8,0},{10,2},{12,4},{14,6},{16,24},{18,... | collective-permute-start | bytes 221192 | tf_op jit(solution)/shard_map/ppermute | solution.py:360
  573.7 4.7 collective-permute-start.39
  578.5 5.1 collective-permute-start.38
  583.5 5.3 collective-permute-start.40
  588.8 25.5 %collective-permute-start.41 = (f32[1152,128]{0,1:T(8,128)S(1)}, f32[1152,128]{0,1:T(8,128)S(1)}, u32[]{:S(2)}, u32[]{:S(2)}) collective-permute-start(f32[1152,128]{0,1:T(8,128)S(1)} %select_maximum_fusion), channel_id=1, source_target_pairs={{0,1},{1,0},{2,3},{3,2},{4,5},{5,4},{6,7},{7,6},{8,9},{9,8},{10,11... | collective-permute-start | bytes 1769480 | tf_op jit(solution)/shard_map/ppermute | solution.py:344
  589.5 48.6 %collective-permute-start.28 = (bf16[1152,1024]{1,0:T(8,128)(2,1)}, bf16[1152,1024]{1,0:T(8,128)(2,1)}, u32[]{:S(2)}, u32[]{:S(2)}) collective-permute-start(bf16[1152,1024]{1,0:T(8,128)(2,1)} %convolution_convert_fusion), channel_id=1, source_target_pairs={{0,1},{1,0},{2,3},{3,2},{4,5},{5,4},{6,7},{7,6},{8,9},{9,8},{10,11... | collective-permute-start | bytes 7077896 | tf_op jit(solution)/shard_map/ppermute | solution.py:344
  590.1 7.2 %collective-permute-start.51 = (bf16[192,256]{1,0:T(8,128)(2,1)S(1)}, bf16[192,256]{1,0:T(8,128)(2,1)S(1)}, u32[]{:S(2)}, u32[]{:S(2)}) collective-permute-start(bf16[192,256]{1,0:T(8,128)(2,1)S(1)} %dynamic-slice_bitcast_fusion.26), channel_id=1, source_target_pairs={{0,16},{2,18},{4,20},{6,22},{8,24},{10,26},{12,28},{14,30},{16,0},... | collective-permute-start | bytes 294920 | tf_op jit(solution)/shard_map/ppermute | solution.py:360
  597.3 12.8 %collective-permute-start.53 = (bf16[192,320]{1,0:T(8,128)(2,1)S(1)}, bf16[192,320]{1,0:T(8,128)(2,1)S(1)}, u32[]{:S(2)}, u32[]{:S(2)}) collective-permute-start(bf16[192,320]{1,0:T(8,128)(2,1)S(1)} %dynamic-slice_bitcast_fusion.20), channel_id=1, source_target_pairs={{0,16},{2,18},{4,20},{6,22},{8,24},{10,26},{12,28},{14,30},{16,0},... | collective-permute-start | bytes 368648 | tf_op jit(solution)/shard_map/ppermute | solution.py:360
  611.1 9.8 %collective-permute-start.47 = (bf16[72,1536]{1,0:T(8,128)(2,1)S(1)}, bf16[72,1536]{1,0:T(8,128)(2,1)S(1)}, u32[]{:S(2)}, u32[]{:S(2)}) collective-permute-start(bf16[72,1536]{1,0:T(8,128)(2,1)S(1)} %dynamic-slice_bitcast_fusion.17), channel_id=1, source_target_pairs={{0,16},{2,18},{4,20},{6,22},{8,24},{10,26},{12,28},{14,30},{16,0},... | collective-permute-start | bytes 663560 | tf_op jit(solution)/shard_map/ppermute | solution.py:360
  611.4 14.2 %collective-permute-start.49 = (bf16[72,1536]{1,0:T(8,128)(2,1)S(1)}, bf16[72,1536]{1,0:T(8,128)(2,1)S(1)}, u32[]{:S(2)}, u32[]{:S(2)}) collective-permute-start(bf16[72,1536]{1,0:T(8,128)(2,1)S(1)} %dynamic-slice_bitcast_fusion.16), channel_id=1, source_target_pairs={{0,16},{2,18},{4,20},{6,22},{8,24},{10,26},{12,28},{14,30},{16,0},... | collective-permute-start | bytes 663560 | tf_op jit(solution)/shard_map/ppermute | solution.py:360
  614.7 10.9 %collective-permute-start.42 = (f32[2,2,2,72,128]{4,3,2,1,0:T(8,128)S(1)}, f32[2,2,2,72,128]{4,3,2,1,0:T(8,128)S(1)}, u32[]{:S(2)}, u32[]{:S(2)}) collective-permute-start(f32[2,2,2,72,128]{4,3,2,1,0:T(8,128)S(1)} %dynamic-slice_bitcast_fusion.12), channel_id=1, source_target_pairs={{0,4},{2,6},{4,0},{6,2},{8,12},{10,14},{12,8},{14,10},{16,20},{18,... | collective-permute-start | bytes 884744 | tf_op jit(solution)/shard_map/ppermute | solution.py:360
  625.7 5.8 collective-permute-start.43
  631.6 4.4 collective-permute-start.44
  636.1 9.8 %collective-permute-start.45 = (f32[72,128]{0,1:T(8,128)S(1)}, f32[72,128]{0,1:T(8,128)S(1)}, u32[]{:S(2)}, u32[]{:S(2)}) collective-permute-start(f32[72,128]{0,1:T(8,128)S(1)} %bitcast.365), channel_id=1, source_target_pairs={{0,16},{2,18},{4,20},{6,22},{8,24},{10,26},{12,28},{14,30},{16,0},... | collective-permute-start | bytes 110600 | tf_op jit(solution)/shard_map/ppermute | solution.py:360
  642.0 16.0 %collective-permute-start.33 = (bf16[2,2,2,72,512]{4,3,0,1,2:T(8,128)(2,1)S(1)}, bf16[2,2,2,72,512]{4,3,0,1,2:T(8,128)(2,1)S(1)}, u32[]{:S(2)}, u32[]{:S(2)}) collective-permute-start(bf16[2,2,2,72,512]{4,3,0,1,2:T(8,128)(2,1)S(1)} %bitcast.361), channel_id=1, source_target_pairs={{0,4},{2,6},{4,0},{6,2},{8,12},{10,14},{12,8},{14,10},{16,20},{18,... | collective-permute-start | bytes 1769480 | tf_op jit(solution)/shard_map/ppermute | solution.py:360
  646.1 14.5 %collective-permute-start.29 = (bf16[2,2,2,72,512]{4,3,0,1,2:T(8,128)(2,1)S(1)}, bf16[2,2,2,72,512]{4,3,0,1,2:T(8,128)(2,1)S(1)}, u32[]{:S(2)}, u32[]{:S(2)}) collective-permute-start(bf16[2,2,2,72,512]{4,3,0,1,2:T(8,128)(2,1)S(1)} %bitcast.362), channel_id=1, source_target_pairs={{0,2},{2,0},{4,6},{6,4},{8,10},{10,8},{12,14},{14,12},{16,18},{18,... | collective-permute-start | bytes 1769480 | tf_op jit(solution)/shard_map/ppermute | solution.py:360
  658.2 7.9 %collective-permute-start.34 = (bf16[2,2,72,512]{3,2,0,1:T(8,128)(2,1)S(1)}, bf16[2,2,72,512]{3,2,0,1:T(8,128)(2,1)S(1)}, u32[]{:S(2)}, u32[]{:S(2)}) collective-permute-start(bf16[2,2,72,512]{3,2,0,1:T(8,128)(2,1)S(1)} %dynamic-slice_bitcast_fusion.13), channel_id=1, source_target_pairs={{0,2},{2,0},{4,6},{6,4},{8,10},{10,8},{12,14},{14,12},{16,18},{18,... | collective-permute-start | bytes 884744 | tf_op jit(solution)/shard_map/ppermute | solution.py:360
  660.8 6.8 collective-permute-start.30
  666.2 5.4 collective-permute-start.35
  667.7 6.3 collective-permute-start.31
  671.7 6.1 collective-permute-start.36
  674.0 6.1 collective-permute-start.32
  (32 other events, 119.7 us)
Sparse Core Ops, SparseCore 0:
  11.5 96.0 all-gather.2
  111.0 101.6 all-gather.4

commit v5 on v4

--- a/solution.py
+++ b/solution.py
@@ -360,8 +360,8 @@
     return lax.ppermute(a, "dp", [(i, i ^ (1 << bit)) for i in range(lax.axis_size("dp"))])
 
 
-def column_parts(cols):
-    cut = cols // 256 * 128
+def column_parts(cols, split=True):
+    cut = cols // 256 * 128 * split
     parts = (slice(0, cut), (0, 1)), (slice(cut, cols), (1, 0))
     return parts if cut else parts[1:]
 
@@ -387,33 +387,39 @@
 
 
 class Halving:
-    def __init__(self, mine, theirs, kind=bf16):
+    def __init__(self, mine, theirs, kind=bf16, split=True):
         self.kind = kind
-        self.bits = lax.axis_size("dp").bit_length() - 1
-        both = add(mine, swap(theirs)).astype(kind)
-        self.left = [list(range(self.bits))[::-1] for _ in column_parts(mine.shape[1])]
-        self.sums = []
-        for part, _ in column_parts(mine.shape[1]):
-            self.sums.append(both[:, part].reshape(*[2] * self.bits, -1, both[:, part].shape[1]))
-        for i in range(2):
-            for p, (_, order) in enumerate(column_parts(mine.shape[1])):
-                self.step(p, order[i])
-
-    def step(self, p, bit):
-        axis = self.left[p].index(bit)
-        self.left[p].remove(bit)
-        mybit = (lax.axis_index("dp") >> bit) & 1
-        a = self.sums[p]
-        keep = lax.dynamic_index_in_dim(a, mybit, axis, keepdims=False)
-        send = lax.dynamic_index_in_dim(a, 1 - mybit, axis, keepdims=False)
-        a = add(keep, exchange(send, bit))
-        self.sums[p] = a.astype(self.kind) if self.left[p] else a
-
-    def finish(self):
-        for bit in range(2, self.bits):
-            for p in range(len(self.sums)):
-                self.step(p, bit)
-        return jnp.concatenate(self.sums, 1)
+        bits = lax.axis_size("dp").bit_length() - 1
+        self.steps = bits
+        got = swap(theirs)
+        self.orders, self.stay, self.got = [], [], []
+        for part, order in column_parts(mine.shape[1], split):
+            self.orders.append(list(order) + list(range(2, bits)))
+            for to, u in ((self.stay, mine), (self.got, got)):
+                to.append(u[:, part].reshape(*[2] * bits, -1, u[:, part].shape[1]))
+
+    def prepare(self, step):
+        self.send = []
+        for p, order in enumerate(self.orders):
+            bit = order[step]
+            axis = sum(b > bit for b in order[step:])
+            mybit = (lax.axis_index("dp") >> bit) & 1
+            at = lambda u, i: lax.dynamic_index_in_dim(u, i, axis, keepdims=False)
+            total = lambda i: add(at(self.stay[p], i), at(self.got[p], i)).astype(self.kind)
+            self.send.append(total(1 - mybit))
+            self.stay[p] = total(mybit)
+
+    def move(self, step):
+        self.got = [exchange(a, order[step]) for a, order in zip(self.send, self.orders)]
+
+    def advance(self, step):
+        self.prepare(step)
+        self.move(step)
+
+    def finish(self, step=0):
+        for i in range(step, self.steps):
+            self.advance(i)
+        return jnp.concatenate([add(*u) for u in zip(self.stay, self.got)], 1)
 
 
 def local(
@@ -469,8 +475,8 @@
     layer_out, grad_n2, g_mine, g_theirs, gd_mine, gd_theirs = mlp(
         me_arr, n2, n2.T, cot, residual, wide, down_mine, down_theirs
     )
-    r_wide = Halving(g_mine, g_theirs)
-    r_down = Halving(gd_mine, gd_theirs)
+    tie = lax.optimization_barrier
+    wide_sum, down_sum = Halving(g_mine, g_theirs), Halving(gd_mine, gd_theirs)
     sum_gain_mlp = jnp.sum(grad_n2 * residual * scale_mlp, 0)
     grad_residual = cot.astype(f32) + norm_back(grad_n2, residual, scale_mlp, gain_two)
     grad_low = grad_residual.astype(bf16)
@@ -484,26 +490,44 @@
         b = lax.dot_general(mixed_got, columns, TN, preferred_element_type=f32).astype(bf16)
         return pick(jnp.concatenate([a, b], 0), jnp.concatenate([b, a], 0))
 
-    r_out = Halving(grad_out(pick(*low)), grad_out(pick(*low[::-1])))
+    out_sum = Halving(grad_out(pick(*low)), grad_out(pick(*low[::-1])), split=False)
+    early = wide_sum, down_sum, out_sum
+    for u in early:
+        u.prepare(0)
+    (d_mine, d_got), sends = tie(((d_mine, d_got), [u.send for u in early]))
+    for u, send in zip(early, sends):
+        u.send = send
+        u.move(0)
     lins = ()
     for b in range(batch):
         lins = attend_back(
             b, lins, me_arr, mine, got, mixed, mixed_out, d_mine, d_got, lse, cosine, sine, piece
         )
-    lin_mine, lin_out = lins
+    (lin_mine, lin_out), gots = tie((lins, [u.got for u in early]))
+    for u, arrived in zip(early, gots):
+        u.got = arrived
+        u.advance(1)
     lin_got = swap(lin_out)
     weight_grad = lambda lin: lax.dot_general(n1, lin, TN, preferred_element_type=f32).astype(bf16)
-    lin_got, r_wide.sums, r_down.sums, r_out.sums = lax.optimization_barrier(
-        (lin_got, r_wide.sums, r_down.sums, r_out.sums)
-    )
-    r_wide, r_down, r_out = r_wide.finish(), r_down.finish(), r_out.finish()
-    r_pack = Halving(weight_grad(lin_mine), weight_grad(lin_got)).finish()
+    pack_sum = Halving(weight_grad(lin_mine), weight_grad(lin_got))
+    pack_sum.prepare(0)
+    pack_sum.send, gots = tie((pack_sum.send, [u.got for u in early]))
+    pack_sum.move(0)
+    for u, arrived in zip(early, gots):
+        u.got = arrived
+        u.advance(2)
     grad_n1 = lax.dot_general(lin_mine, w_mine, NT, preferred_element_type=f32) + lax.dot_general(
         lin_got, w_theirs, NT, preferred_element_type=f32
     )
+    grad_n1, pack_sum.got, gots = tie((grad_n1, pack_sum.got, [u.got for u in early]))
+    pack_sum.advance(1)
+    for u, arrived in zip(early, gots):
+        u.got = arrived
     sum_gain_attn = jnp.sum(grad_n1 * floats * scale_attn, 0)
     grad_input = (grad_residual + norm_back(grad_n1, floats, scale_attn, gain_one)).astype(bf16)
     sums = jnp.pad(jnp.stack([sum_gain_attn, sum_gain_mlp], 1), ((0, 0), (0, 126)))
+    r_wide, r_down, r_out = [u.finish(3) for u in early]
+    r_pack = pack_sum.finish(2)
     r_sums = Halving(sums, sums, f32).finish()
     r_gate, r_up = [
         a.reshape(a.shape[0], -1).astype(f32)

time: 697 us -> 670 us (0.961)
  waiting for transfers between devices: 244 us -> 180 us
  local copies, waits for them, and re-layouts: 60.9 us -> 85.4 us
  other arithmetic: 69.6 us -> 90.7 us
    ppermute x44 -> x40, waiting for transfers between devices: 198 us -> 133 us  [exchange(): lax.ppermute(a, 'dp', [(i, i ^ 1 << bit) for i in range(lax.axis_size('dp...]
    convert_element_type x28 -> x38, other arithmetic: 25.9 us -> 41.6 us  [prepare(): add(at(self.stay[p], i), at(self.got[p], i)).astype(self.kind)]
    slice x9, local copies, waits for them, and re-layouts: 6.68 us -> 18.6 us  [the longest x8 17.9 us: __init__(): to.append(u[:, part].reshape(*[2] * bits, -1, u[:, part].shape[1]))]
    unnamed x82 -> x138, local copies, waits for them, and re-layouts: 8.45 us -> 14.2 us
    ppermute x44 -> x40, starting transfers between devices: 52.6 us -> 50.4 us  [exchange(): lax.ppermute(a, 'dp', [(i, i ^ 1 << bit) for i in range(lax.axis_size('dp...]
  transfers between devices with their start and end apart: 56 -> 52, of which waited for: 31 -> 19; matrix products, arithmetic and copies ran while one was open for 21% -> 29% of each run, Pallas kernels for 16% -> 16%
where the time goes in v5:
time: 670 us; the launch traced here: 661 us
  Pallas kernels  200 us (30%)
  waiting for transfers between devices  180 us (27%)
  other arithmetic  90.7 us (14%)
  local copies, waits for them, and re-layouts  85.4 us (13%)
  starting transfers between devices  52.8 us (8%)
  matrix products  35.9 us (5%)
  between operations  15.9 us (2%)
    ppermute x40, waiting for transfers between devices, exchange(): lax.ppermute(a, 'dp', [(i, i ^ 1 << bit) for i in range(lax.axis_size('dp...  133 us
    pallas_call x1, Pallas kernels, mlp(): pl.pallas_call(mlp_body, grid_spec=pltpu.PrefetchScalarGridSpec(num_scala...  93.6 us
    pallas_call x2, Pallas kernels, attend_back(): pl.pallas_call(bwd_body, grid_spec=pltpu.PrefetchScalarGridSpec(num_scala...  54 us
    ppermute x40, starting transfers between devices, exchange(): lax.ppermute(a, 'dp', [(i, i ^ 1 << bit) for i in range(lax.axis_size('dp...  50.4 us
    all_gather x2, waiting for transfers between devices, fetch(): lax.all_gather(w, BOTH, axis=0, tiled=True)  47.1 us
    convert_element_type x38, other arithmetic, prepare(): add(at(self.stay[p], i), at(self.got[p], i)).astype(self.kind)  41.6 us
    pallas_call x1, Pallas kernels, attend(): pl.pallas_call(fwd_body, grid_spec=pltpu.PrefetchScalarGridSpec(num_scala...  38.9 us
    slice x8, local copies, waits for them, and re-layouts, __init__(): to.append(u[:, part].reshape(*[2] * bits, -1, u[:, part].shape[1]))  17.9 us
  transfers between devices with their start and end apart: 52, of which 19 were waited for; matrix products, arithmetic and copies ran while one was open for 29% of the time, Pallas kernels for 16%

profile of v5, /device:TPU:0, one launch (start us, length us, event | category | flops | bytes accessed | tf_op | source)
XLA Modules:
  0.0 660.6 jit_solution(5203055562717586113)
XLA Ops:
  12.0 4.1 collective-permute-start.6
  16.9 3.1 fusion.41
  20.6 8.5 %collective-permute-done.2 = bf16[192,256]{1,0:T(8,128)(2,1)S(1)} collective-permute-done((bf16[192,256]{1,0:T(8,128)(2,1)}, bf16[192,256]{1,0:T(8,128)(2,1)S(1)}, u32[]{:S(2)}, u32[]{:S(2)}) %collective-permute-start.2) | collective-permute-done | bytes 98336 | tf_op jit(solution)/shard_map/ppermute | solution.py:360
  31.7 6.6 %collective-permute-done.3 = bf16[2,192,256]{2,1,0:T(8,128)(2,1)S(1)} collective-permute-done((bf16[2,192,256]{2,1,0:T(8,128)(2,1)S(1)}, bf16[2,192,256]{2,1,0:T(8,128)(2,1)S(1)}, u32[]{:S(2)}, u32[]{:S(2)}) %collective-permute-start.3) | collective-permute-done | bytes 196640 | tf_op jit(solution)/shard_map/ppermute | solution.py:360
  40.2 3.7 collective-permute-done.7
  46.8 4.1 collective-permute-done.4
  53.6 12.0 %collective-permute-done.8 = bf16[2,2,192,320]{3,2,0,1:T(8,128)(2,1)S(1)} collective-permute-done((bf16[2,2,192,320]{3,2,0,1:T(8,128)(2,1)S(1)}, bf16[2,2,192,320]{3,2,0,1:T(8,128)(2,1)S(1)}, u32[]{:S(2)}, u32[]{:S(2)}) %collective-permute-start.8) | collective-permute-done | bytes 491552 | tf_op jit(solution)/shard_map/ppermute | solution.py:360
  68.6 41.7 %all-gather.3.cloned.1.call-done = bf16[2304,1600]{1,0:T(8,128)(2,1)} async-done(((bf16[72,1600]{1,0:T(8,128)(2,1)}), bf16[2304,1600]{1,0:T(8,128)(2,1)}) %all-gather.3.cloned.1.call-update) | async-done | bytes 7372816 | tf_op jit(solution)/shard_map/all_gather | solution.py:355
  110.2 2.2 convert_reduce_fusion
  115.3 6.8 %project.3 = (bf16[1024,1024]{1,0:T(8,128)(2,1)}, bf16[1152,1024]{1,0:T(8,128)(2,1)}) custom-call(s32[1]{0:T(128)} %bitcast.me, bf16[1024,1152]{1,0:T(8,128)(2,1)} %fusion.2.n1, bf16[16,2,72,1600]{3,2,1,0:T(8,128)(2,1)} %bitcast.450, f32[1024,128]{1,0:T(8,128)} %get-tuple-element.237.cosine, f32[1024,128]{1,0:T(8,128)} %get-tuple-element.236.sine), custom_call_target="tpu_custom_call" | custom-call | flops 3000000000 | bytes 12000000 | tf_op jit(solution)/shard_map/project/pallas_call | solution.py:65
  124.6 2.5 maximum_select_fusion
  127.4 2.3 pad_maximum_fusion.wd_mine
  129.6 6.0 copy.270
  135.9 6.8 %project.2 = (bf16[1024,1024]{1,0:T(8,128)(2,1)}, bf16[1152,1024]{1,0:T(8,128)(2,1)}) custom-call(s32[1]{0:T(128)} %bitcast.me, bf16[1024,1152]{1,0:T(8,128)(2,1)} %fusion.2.n1, bf16[16,2,72,1600]{3,2,1,0:T(8,128)(2,1)} %bitcast.451, f32[1024,128]{1,0:T(8,128)} %get-tuple-element.237.cosine, f32[1024,128]{1,0:T(8,128)} %get-tuple-element.236.sine), custom_call_target="tpu_custom_call" | custom-call | flops 3000000000 | bytes 12000000 | tf_op jit(solution)/shard_map/project/pallas_call | solution.py:65
  142.7 38.9 %attend.1 = (bf16[1024,576]{1,0:T(8,128)(2,1)}, bf16[1024,576]{1,0:T(8,128)(2,1)}, f32[2048,128]{1,0:T(8,128)}) custom-call(s32[1]{0:T(128)} %bitcast.me, bf16[1024,1024]{1,0:T(8,128)(2,1)} %get-tuple-element.57.mine, bf16[1024,1024]{1,0:T(8,128)(2,1)} %collective-permute-done.got), custom_call_target="tpu_custom_call" | custom-call | flops 24000000000 | bytes 20000000 | tf_op jit(solution)/shard_map/attend/pallas_call | solution.py:189
  184.0 6.1 copy.272.wd_theirs
  193.0 4.4 fusion.28
  197.4 2.5 multiply_reduce_fusion.2
  202.5 2.5 copy.271.n2t
  205.1 4.4 multiply_convert_fusion.n2
  209.5 5.4 all-gather.5.cloned.1.call-done
  214.9 93.6 %mlp.1 = (bf16[1024,1152]{1,0:T(8,128)(2,1)}, f32[1024,1152]{1,0:T(8,128)}, bf16[1152,3072]{1,0:T(8,128)(2,1)}, bf16[1152,3072]{1,0:T(8,128)(2,1)}, bf16[3072,57...) custom-call(s32[1]{0:T(128)} %bitcast.me, bf16[1024,1152]{1,0:T(8,128)(2,1)} %multiply_convert_fusion.n2, ...), custom_call_target="tpu_custom_call" | custom-call | flops 65000001536 | bytes 60000000 | tf_op jit(solution)/shard_map/mlp/pallas_call | solution.py:305
  310.6 2.7 slice.93
  313.3 3.9 multiply_reduce_fusion
  317.8 3.5 fusion.96
  321.3 3.9 convolution_convert_fusion.4
  329.2 6.0 copy.279
  335.4 3.9 convolution_convert_fusion.6
  343.0 2.8 copy.285
  345.8 3.7 fusion.97
  349.9 2.8 convolution_convert_fusion.3
  355.7 2.1 constant_dynamic-slice_fusion.10
  357.8 3.3 convolution_convert_fusion.2.do_mine
  361.2 2.6 copy.287
  363.8 2.5 add_convert_fusion.8
  366.3 2.2 fusion.29
  368.5 2.9 slice.116
  371.4 4.1 copy.340
  375.5 2.7 slice.115
  378.2 2.6 copy.337
  380.8 2.6 fusion.25
  383.4 2.4 add_convert_fusion.6
  388.4 3.5 fusion.98
  398.8 2.8 copy.290.do_got
  407.2 26.9 %attend_back.2 = (bf16[1024,1024]{1,0:T(8,128)(2,1)}, bf16[1024,1024]{1,0:T(8,128)(2,1)}) custom-call(s32[1]{0:T(128)} %bitcast.me, bf16[1024,1024]{1,0:T(8,128)(2,1)} %get-tuple-element.57.mine, bf16[1024,1024]{1,0:T(8,128)(2,1)} %collective-permute-done.got, bf16[1024,576]{1,0:T(8,128)(2,1)} %get-tuple-element.59.o_mine, ...), custom_call_target="tpu_custom_call" | custom-call | flops 12999999488 | bytes 20000000 | tf_op jit(solution)/shard_map/attend_back/pallas_call | solution.py:215
  434.1 27.1 %attend_back.3 = (bf16[1024,1024]{1,0:T(8,128)(2,1)}, bf16[1024,1024]{1,0:T(8,128)(2,1)}) custom-call(s32[1]{0:T(128)} %bitcast.me, bf16[1024,1024]{1,0:T(8,128)(2,1)} %get-tuple-element.57.mine, bf16[1024,1024]{1,0:T(8,128)(2,1)} %collective-permute-done.got, ...), custom_call_target="tpu_custom_call", output_to_operand_aliasing={{0}: (10, {}), {1}: (11, {})} | custom-call | flops 12999999488 | bytes 20000000 | tf_op jit(solution)/shard_map/attend_back/pallas_call | solution.py:215
  463.4 21.5 %collective-permute-done.19 = bf16[2,2,2,72,576]{4,3,0,1,2:T(8,128)(2,1)} collective-permute-done((bf16[2,2,2,72,576]{4,3,0,1,2:T(8,128)(2,1)}, bf16[2,2,2,72,576]{4,3,0,1,2:T(8,128)(2,1)}, u32[]{:S(2)}, u32[]{:S(2)}) %collective-permute-start.19) | collective-permute-done | bytes 663584 | tf_op jit(solution)/shard_map/ppermute | solution.py:360
  499.4 2.9 convolution_convert_fusion.1
  502.4 3.1 convolution_convert_fusion
  509.5 2.9 fusion.103
  512.4 3.0 convolution_add_fusion
  517.1 12.8 %collective-permute-done.23 = bf16[2,2,72,1536]{3,2,1,0:T(8,128)(2,1)S(1)} collective-permute-done((bf16[2,2,72,1536]{3,2,1,0:T(8,128)(2,1)S(1)}, bf16[2,2,72,1536]{3,2,1,0:T(8,128)(2,1)S(1)}, u32[]{:S(2)}, u32[]{:S(2)}) %collective-permute-start.23) | collective-permute-done | bytes 884768 | tf_op jit(solution)/shard_map/ppermute | solution.py:360
  529.9 7.6 %collective-permute-done.22 = bf16[2,2,72,1536]{3,2,1,0:T(8,128)(2,1)S(1)} collective-permute-done((bf16[2,2,72,1536]{3,2,1,0:T(8,128)(2,1)S(1)}, bf16[2,2,72,1536]{3,2,1,0:T(8,128)(2,1)S(1)}, u32[]{:S(2)}, u32[]{:S(2)}) %collective-permute-start.22) | collective-permute-done | bytes 884768 | tf_op jit(solution)/shard_map/ppermute | solution.py:360
  551.1 22.8 %collective-permute-done.32 = bf16[2,192,320]{2,1,0:T(8,128)(2,1)S(1)} collective-permute-done((bf16[2,192,320]{2,1,0:T(8,128)(2,1)S(1)}, bf16[2,192,320]{2,1,0:T(8,128)(2,1)S(1)}, u32[]{:S(2)}, u32[]{:S(2)}) %collective-permute-start.32) | collective-permute-done | bytes 245792 | tf_op jit(solution)/shard_map/ppermute | solution.py:360
  576.5 2.2 copy.323
  592.1 4.4 fusion.6
  596.8 11.0 %collective-permute-done.40 = bf16[72,576]{1,0:T(8,128)(2,1)S(1)} collective-permute-done((bf16[72,576]{1,0:T(8,128)(2,1)S(1)}, bf16[72,576]{1,0:T(8,128)(2,1)S(1)}, u32[]{:S(2)}, u32[]{:S(2)}) %collective-permute-start.40) | collective-permute-done | bytes 82976 | tf_op jit(solution)/shard_map/ppermute | solution.py:360
  612.6 7.1 %collective-permute-done.47 = bf16[72,1536]{1,0:T(8,128)(2,1)S(1)} collective-permute-done((bf16[72,1536]{1,0:T(8,128)(2,1)S(1)}, bf16[72,1536]{1,0:T(8,128)(2,1)S(1)}, u32[]{:S(2)}, u32[]{:S(2)}) %collective-permute-start.47) | collective-permute-done | bytes 221216 | tf_op jit(solution)/shard_map/ppermute | solution.py:360
  621.0 2.3 slice_reduce_fusion
  631.7 2.3 collective-permute-start.36
  634.0 3.6 collective-permute-done.42
  639.4 3.5 collective-permute-done.43
  644.7 3.0 collective-permute-done.44
  650.4 2.1 collective-permute-done.45
  (343 shorter events, 134.9 us)
Async XLA Ops:
  7.2 103.1 %all-gather.3.cloned.1.call-start = ((), (), s32[]{:S(2)}) async-start(), calls=%async_computation | async-start | bytes 7907328 | tf_op jit(solution)/shard_map/all_gather | solution.py:355
  9.9 205.0 %all-gather.5.cloned.1.call-start = ((), (), s32[]{:S(2)}) async-start(), calls=%async_computation.1 | async-start | bytes 14598144 | tf_op jit(solution)/shard_map/all_gather | solution.py:355
  12.0 18.5 %collective-permute-start.6 = (bf16[192,320]{1,0:T(8,128)(2,1)S(1)}, bf16[192,320]{1,0:T(8,128)(2,1)S(1)}, u32[]{:S(2)}, u32[]{:S(2)}) collective-permute-start(bf16[192,320]{1,0:T(8,128)(2,1)S(1)} %get-tuple-element.233), channel_id=1, source_target_pairs={{0,16},{2,18},{4,20},{6,22},{8,24},{10,26},{12,28},{14,30},{16,0},... | collective-permute-start | bytes 368648 | tf_op jit(solution)/shard_map/ppermute | solution.py:360
  16.8 12.3 %collective-permute-start.2 = (bf16[192,256]{1,0:T(8,128)(2,1)}, bf16[192,256]{1,0:T(8,128)(2,1)S(1)}, u32[]{:S(2)}, u32[]{:S(2)}) collective-permute-start(bf16[192,256]{1,0:T(8,128)(2,1)} %get-tuple-element.230), channel_id=1, source_target_pairs={{0,16},{2,18},{4,20},{6,22},{8,24},{10,26},{12,28},{14,30},{16,0},... | collective-permute-start | bytes 294920 | tf_op jit(solution)/shard_map/ppermute | solution.py:360
  20.6 162.9 %copy-start.56 = (f32[1,4,2,128]{3,1,2,0:T(4,128)}, f32[1,4,2,128]{3,1,2,0:T(4,128)S(1)}, u32[]{:S(2)}) copy-start(f32[1,4,2,128]{3,1,2,0:T(4,128)S(1)} %copy.363) | copy-start | bytes 12292
  29.2 9.1 %collective-permute-start.3 = (bf16[2,192,256]{2,1,0:T(8,128)(2,1)S(1)}, bf16[2,192,256]{2,1,0:T(8,128)(2,1)S(1)}, u32[]{:S(2)}, u32[]{:S(2)}) collective-permute-start(bf16[2,192,256]{2,1,0:T(8,128)(2,1)S(1)} %maximum_select_fusion.15), channel_id=1, source_target_pairs={{0,8},{2,10},{4,12},{6,14},{8,0},{10,2},{12,4},{14,6},{16,24},{18,... | collective-permute-start | bytes 589832 | tf_op jit(solution)/shard_map/ppermute | solution.py:360
  30.6 13.3 %collective-permute-start.7 = (bf16[2,192,320]{2,1,0:T(8,128)(2,1)S(1)}, bf16[2,192,320]{2,1,0:T(8,128)(2,1)S(1)}, u32[]{:S(2)}, u32[]{:S(2)}) collective-permute-start(bf16[2,192,320]{2,1,0:T(8,128)(2,1)S(1)} %maximum_select_fusion.13), channel_id=1, source_target_pairs={{0,8},{2,10},{4,12},{6,14},{8,0},{10,2},{12,4},{14,6},{16,24},{18,... | collective-permute-start | bytes 737288 | tf_op jit(solution)/shard_map/ppermute | solution.py:360
  38.3 12.5 %collective-permute-start.4 = (bf16[2,2,192,256]{3,2,0,1:T(8,128)(2,1)S(1)}, bf16[2,2,192,256]{3,2,0,1:T(8,128)(2,1)S(1)}, u32[]{:S(2)}, u32[]{:S(2)}) collective-permute-start(bf16[2,2,192,256]{3,2,0,1:T(8,128)(2,1)S(1)} %maximum_select_fusion.11), channel_id=1, source_target_pairs={{0,4},{2,6},{4,0},{6,2},{8,12},{10,14},{12,8},{14,10},{16,20},{18,... | collective-permute-start | bytes 1179656 | tf_op jit(solution)/shard_map/ppermute | solution.py:360
  44.0 21.6 %collective-permute-start.8 = (bf16[2,2,192,320]{3,2,0,1:T(8,128)(2,1)S(1)}, bf16[2,2,192,320]{3,2,0,1:T(8,128)(2,1)S(1)}, u32[]{:S(2)}, u32[]{:S(2)}) collective-permute-start(bf16[2,2,192,320]{3,2,0,1:T(8,128)(2,1)S(1)} %maximum_select_fusion.9), channel_id=1, source_target_pairs={{0,2},{2,0},{4,6},{6,4},{8,10},{10,8},{12,14},{14,12},{16,18},{18,... | collective-permute-start | bytes 1474568 | tf_op jit(solution)/shard_map/ppermute | solution.py:360
  51.9 71.0 %collective-permute-start.5 = (bf16[2,2,2,192,256]{4,3,0,1,2:T(8,128)(2,1)}, bf16[2,2,2,192,256]{4,3,0,1,2:T(8,128)(2,1)}, u32[]{:S(2)}, u32[]{:S(2)}) collective-permute-start(bf16[2,2,2,192,256]{4,3,0,1,2:T(8,128)(2,1)} %maximum_select_fusion.7), channel_id=1, source_target_pairs={{0,2},{2,0},{4,6},{6,4},{8,10},{10,8},{12,14},{14,12},{16,18},{18,... | collective-permute-start | bytes 2359304 | tf_op jit(solution)/shard_map/ppermute | solution.py:360
  67.1 57.6 %collective-permute-start.9 = (bf16[2,2,2,192,320]{4,3,0,1,2:T(8,128)(2,1)}, bf16[2,2,2,192,320]{4,3,0,1,2:T(8,128)(2,1)}, u32[]{:S(2)}, u32[]{:S(2)}) collective-permute-start(bf16[2,2,2,192,320]{4,3,0,1,2:T(8,128)(2,1)} %maximum_select_fusion.5), channel_id=1, source_target_pairs={{0,4},{2,6},{4,0},{6,2},{8,12},{10,14},{12,8},{14,10},{16,20},{18,... | collective-permute-start | bytes 2949128 | tf_op jit(solution)/shard_map/ppermute | solution.py:360
  122.1 20.6 %collective-permute-start = (bf16[1024,1024]{1,0:T(8,128)(2,1)}, bf16[1024,1024]{1,0:T(8,128)(2,1)}, u32[]{:S(2)}, u32[]{:S(2)}) collective-permute-start(bf16[1024,1024]{1,0:T(8,128)(2,1)} %get-tuple-element.58), channel_id=1, source_target_pairs={{0,1},{1,0},{2,3},{3,2},{4,5},{5,4},{6,7},{7,6},{8,9},{9,8},{10,11... | collective-permute-start | bytes 6291464 | tf_op jit(solution)/shard_map/ppermute | solution.py:344
  135.6 48.4 %collective-permute-start.10 = (bf16[3072,576]{0,1:T(8,128)(2,1)}, bf16[3072,576]{0,1:T(8,128)(2,1)}, u32[]{:S(2)}, u32[]{:S(2)}) collective-permute-start(bf16[3072,576]{0,1:T(8,128)(2,1)} %copy.270), channel_id=1, source_target_pairs={{0,1},{1,0},{2,3},{3,2},{4,5},{5,4},{6,7},{7,6},{8,9},{9,8},{10,11... | collective-permute-start | bytes 10616840 | tf_op jit(solution)/shard_map/ppermute | solution.py:344
  183.2 9.8 %collective-permute-start.1 = (bf16[1024,576]{0,1:T(8,128)(2,1)S(1)}, bf16[1024,576]{0,1:T(8,128)(2,1)}, u32[]{:S(2)}, u32[]{:S(2)}) collective-permute-start(bf16[1024,576]{0,1:T(8,128)(2,1)S(1)} %copy.267), channel_id=1, source_target_pairs={{0,1},{1,0},{2,3},{3,2},{4,5},{5,4},{6,7},{7,6},{8,9},{9,8},{10,11... | collective-permute-start | bytes 3538952 | tf_op jit(solution)/shard_map/ppermute | solution.py:344
  317.2 71.3 %collective-permute-start.12 = (bf16[1152,3072]{1,0:T(8,128)(2,1)}, bf16[1152,3072]{1,0:T(8,128)(2,1)}, u32[]{:S(2)}, u32[]{:S(2)}) collective-permute-start(bf16[1152,3072]{1,0:T(8,128)(2,1)} %get-tuple-element.64), channel_id=1, source_target_pairs={{0,1},{1,0},{2,3},{3,2},{4,5},{5,4},{6,7},{7,6},{8,9},{9,8},{10,11... | collective-permute-start | bytes 21233672 | tf_op jit(solution)/shard_map/ppermute | solution.py:344
  328.9 32.3 %collective-permute-start.14 = (bf16[1152,576]{0,1:T(8,128)(2,1)}, bf16[1152,576]{0,1:T(8,128)(2,1)}, u32[]{:S(2)}, u32[]{:S(2)}) collective-permute-start(bf16[1152,576]{0,1:T(8,128)(2,1)} %maximum_select_fusion.3), channel_id=1, source_target_pairs={{0,1},{1,0},{2,3},{3,2},{4,5},{5,4},{6,7},{7,6},{8,9},{9,8},{10,11... | collective-permute-start | bytes 3981320 | tf_op jit(solution)/shard_map/ppermute | solution.py:344
  335.3 33.2 %collective-permute-start.13 = (bf16[3072,576]{0,1:T(8,128)(2,1)}, bf16[3072,576]{0,1:T(8,128)(2,1)}, u32[]{:S(2)}, u32[]{:S(2)}) collective-permute-start(bf16[3072,576]{0,1:T(8,128)(2,1)} %copy.279), channel_id=1, source_target_pairs={{0,1},{1,0},{2,3},{3,2},{4,5},{5,4},{6,7},{7,6},{8,9},{9,8},{10,11... | collective-permute-start | bytes 10616840 | tf_op jit(solution)/shard_map/ppermute | solution.py:344
  352.6 46.2 %collective-permute-start.11 = (bf16[1024,576]{0,1:T(8,128)(2,1)}, bf16[1024,576]{0,1:T(8,128)(2,1)}, u32[]{:S(2)}, u32[]{:S(2)}) collective-permute-start(bf16[1024,576]{0,1:T(8,128)(2,1)} %convolution_convert_fusion.3), channel_id=1, source_target_pairs={{0,1},{1,0},{2,3},{3,2},{4,5},{5,4},{6,7},{7,6},{8,9},{9,8},{10,11... | collective-permute-start | bytes 3538952 | tf_op jit(solution)/shard_map/ppermute | solution.py:344
  401.6 83.2 %collective-permute-start.15 = (bf16[2,2,2,72,1536]{4,3,0,2,1:T(8,128)(2,1)}, bf16[2,2,2,72,1536]{4,3,0,2,1:T(8,128)(2,1)}, u32[]{:S(2)}, u32[]{:S(2)}) collective-permute-start(bf16[2,2,2,72,1536]{4,3,0,2,1:T(8,128)(2,1)} %fusion.10), channel_id=1, source_target_pairs={{0,2},{2,0},{4,6},{6,4},{8,10},{10,8},{12,14},{14,12},{16,18},{18,... | collective-permute-start | bytes 5308424 | tf_op jit(solution)/shard_map/ppermute | solution.py:360
  403.1 81.7 %collective-permute-start.16 = (bf16[2,2,2,72,1536]{4,3,0,2,1:T(8,128)(2,1)}, bf16[2,2,2,72,1536]{4,3,0,2,1:T(8,128)(2,1)}, u32[]{:S(2)}, u32[]{:S(2)}) collective-permute-start(bf16[2,2,2,72,1536]{4,3,0,2,1:T(8,128)(2,1)} %fusion.11), channel_id=1, source_target_pairs={{0,4},{2,6},{4,0},{6,2},{8,12},{10,14},{12,8},{14,10},{16,20},{18,... | collective-permute-start | bytes 5308424 | tf_op jit(solution)/shard_map/ppermute | solution.py:360
  403.8 81.1 %collective-permute-start.18 = (bf16[2,2,2,192,320]{4,3,0,1,2:T(8,128)(2,1)}, bf16[2,2,2,192,320]{4,3,0,1,2:T(8,128)(2,1)}, u32[]{:S(2)}, u32[]{:S(2)}) collective-permute-start(bf16[2,2,2,192,320]{4,3,0,1,2:T(8,128)(2,1)} %fusion.16), channel_id=1, source_target_pairs={{0,4},{2,6},{4,0},{6,2},{8,12},{10,14},{12,8},{14,10},{16,20},{18,... | collective-permute-start | bytes 2949128 | tf_op jit(solution)/shard_map/ppermute | solution.py:360
  405.2 79.7 %collective-permute-start.17 = (bf16[2,2,2,192,256]{4,3,0,1,2:T(8,128)(2,1)}, bf16[2,2,2,192,256]{4,3,0,1,2:T(8,128)(2,1)}, u32[]{:S(2)}, u32[]{:S(2)}) collective-permute-start(bf16[2,2,2,192,256]{4,3,0,1,2:T(8,128)(2,1)} %fusion.25), channel_id=1, source_target_pairs={{0,2},{2,0},{4,6},{6,4},{8,10},{10,8},{12,14},{14,12},{16,18},{18,... | collective-permute-start | bytes 2359304 | tf_op jit(solution)/shard_map/ppermute | solution.py:360
  405.8 79.1 %collective-permute-start.19 = (bf16[2,2,2,72,576]{4,3,0,1,2:T(8,128)(2,1)}, bf16[2,2,2,72,576]{4,3,0,1,2:T(8,128)(2,1)}, u32[]{:S(2)}, u32[]{:S(2)}) collective-permute-start(bf16[2,2,2,72,576]{4,3,0,1,2:T(8,128)(2,1)} %fusion.29), channel_id=1, source_target_pairs={{0,4},{2,6},{4,0},{6,2},{8,12},{10,14},{12,8},{14,10},{16,20},{18,... | collective-permute-start | bytes 1990664 | tf_op jit(solution)/shard_map/ppermute | solution.py:360
  434.1 27.1 %copy-start.9 = (bf16[2,2,1,2,72,1536]{5,4,3,2,1,0:T(8,128)(2,1)S(1)}, bf16[2,2,1,2,72,1536]{5,4,3,2,1,0:T(8,128)(2,1)}, u32[]{:S(2)}) copy-start(bf16[2,2,1,2,72,1536]{5,4,3,2,1,0:T(8,128)(2,1)} %get-tuple-element.178) | copy-start | bytes 5308420
  461.3 23.7 %copy-start.8 = (bf16[2,2,2,1,72,1536]{5,4,3,2,1,0:T(8,128)(2,1)S(1)}, bf16[2,2,2,1,72,1536]{5,4,3,2,1,0:T(8,128)(2,1)}, u32[]{:S(2)}) copy-start(bf16[2,2,2,1,72,1536]{5,4,3,2,1,0:T(8,128)(2,1)} %get-tuple-element.182) | copy-start | bytes 5308420
  461.3 23.7 %copy-start.10 = (bf16[2,2,2,1,72,1536]{5,4,3,2,1,0:T(8,128)(2,1)S(1)}, bf16[2,2,2,1,72,1536]{5,4,3,2,1,0:T(8,128)(2,1)}, u32[]{:S(2)}) copy-start(bf16[2,2,2,1,72,1536]{5,4,3,2,1,0:T(8,128)(2,1)} %get-tuple-element.184) | copy-start | bytes 5308420
  484.9 17.4 %collective-permute-start.20 = (bf16[1024,1024]{1,0:T(8,128)(2,1)}, bf16[1024,1024]{1,0:T(8,128)(2,1)S(1)}, u32[]{:S(2)}, u32[]{:S(2)}) collective-permute-start(bf16[1024,1024]{1,0:T(8,128)(2,1)} %get-tuple-element.81), channel_id=1, source_target_pairs={{0,1},{1,0},{2,3},{3,2},{4,5},{5,4},{6,7},{7,6},{8,9},{9,8},{10,11... | collective-permute-start | bytes 6291464 | tf_op jit(solution)/shard_map/ppermute | solution.py:344
  487.3 29.8 %collective-permute-start.26 = (bf16[2,2,72,576]{3,2,0,1:T(8,128)(2,1)S(1)}, bf16[2,2,72,576]{3,2,0,1:T(8,128)(2,1)S(1)}, u32[]{:S(2)}, u32[]{:S(2)}) collective-permute-start(bf16[2,2,72,576]{3,2,0,1:T(8,128)(2,1)S(1)} %fusion.51), channel_id=1, source_target_pairs={{0,2},{2,0},{4,6},{6,4},{8,10},{10,8},{12,14},{14,12},{16,18},{18,... | collective-permute-start | bytes 995336 | tf_op jit(solution)/shard_map/ppermute | solution.py:360
  489.2 27.9 %collective-permute-start.25 = (bf16[2,2,192,320]{3,2,0,1:T(8,128)(2,1)S(1)}, bf16[2,2,192,320]{3,2,0,1:T(8,128)(2,1)S(1)}, u32[]{:S(2)}, u32[]{:S(2)}) collective-permute-start(bf16[2,2,192,320]{3,2,0,1:T(8,128)(2,1)S(1)} %fusion.34), channel_id=1, source_target_pairs={{0,2},{2,0},{4,6},{6,4},{8,10},{10,8},{12,14},{14,12},{16,18},{18,... | collective-permute-start | bytes 1474568 | tf_op jit(solution)/shard_map/ppermute | solution.py:360
  491.8 25.3 %collective-permute-start.24 = (bf16[2,2,192,256]{3,2,0,1:T(8,128)(2,1)S(1)}, bf16[2,2,192,256]{3,2,0,1:T(8,128)(2,1)S(1)}, u32[]{:S(2)}, u32[]{:S(2)}) collective-permute-start(bf16[2,2,192,256]{3,2,0,1:T(8,128)(2,1)S(1)} %fusion.48), channel_id=1, source_target_pairs={{0,4},{2,6},{4,0},{6,2},{8,12},{10,14},{12,8},{14,10},{16,20},{18,... | collective-permute-start | bytes 1179656 | tf_op jit(solution)/shard_map/ppermute | solution.py:360
  494.5 35.4 %collective-permute-start.23 = (bf16[2,2,72,1536]{3,2,1,0:T(8,128)(2,1)S(1)}, bf16[2,2,72,1536]{3,2,1,0:T(8,128)(2,1)S(1)}, u32[]{:S(2)}, u32[]{:S(2)}) collective-permute-start(bf16[2,2,72,1536]{3,2,1,0:T(8,128)(2,1)S(1)} %copy.300), channel_id=1, source_target_pairs={{0,2},{2,0},{4,6},{6,4},{8,10},{10,8},{12,14},{14,12},{16,18},{18,... | collective-permute-start | bytes 2654216 | tf_op jit(solution)/shard_map/ppermute | solution.py:360
  505.5 9.9 %collective-permute-start.21 = (bf16[1152,1024]{1,0:T(8,128)(2,1)S(1)}, bf16[1152,1024]{1,0:T(8,128)(2,1)S(1)}, u32[]{:S(2)}, u32[]{:S(2)}) collective-permute-start(bf16[1152,1024]{1,0:T(8,128)(2,1)S(1)} %convolution_convert_fusion), channel_id=1, source_target_pairs={{0,1},{1,0},{2,3},{3,2},{4,5},{5,4},{6,7},{7,6},{8,9},{9,8},{10,11... | collective-permute-start | bytes 7077896 | tf_op jit(solution)/shard_map/ppermute | solution.py:344
  515.4 58.6 %copy-start.4 = (f32[1024,1152]{1,0:T(8,128)}, f32[1024,1152]{1,0:T(8,128)S(1)}, u32[]{:S(2)}) copy-start(f32[1024,1152]{1,0:T(8,128)S(1)} %convolution_add_fusion) | copy-start | bytes 14155780
  515.4 22.1 %collective-permute-start.22 = (bf16[2,2,72,1536]{3,2,1,0:T(8,128)(2,1)S(1)}, bf16[2,2,72,1536]{3,2,1,0:T(8,128)(2,1)S(1)}, u32[]{:S(2)}, u32[]{:S(2)}) collective-permute-start(bf16[2,2,72,1536]{3,2,1,0:T(8,128)(2,1)S(1)} %copy.297), channel_id=1, source_target_pairs={{0,4},{2,6},{4,0},{6,2},{8,12},{10,14},{12,8},{14,10},{16,20},{18,... | collective-permute-start | bytes 2654216 | tf_op jit(solution)/shard_map/ppermute | solution.py:360
  538.3 7.8 %collective-permute-start.33 = (bf16[2,72,576]{2,1,0:T(8,128)(2,1)S(1)}, bf16[2,72,576]{2,1,0:T(8,128)(2,1)}, u32[]{:S(2)}, u32[]{:S(2)}) collective-permute-start(bf16[2,72,576]{2,1,0:T(8,128)(2,1)S(1)} %get-tuple-element.219), channel_id=1, source_target_pairs={{0,8},{2,10},{4,12},{6,14},{8,0},{10,2},{12,4},{14,6},{16,24},{18,... | collective-permute-start | bytes 497672 | tf_op jit(solution)/shard_map/ppermute | solution.py:360
  540.0 10.0 %collective-permute-start.31 = (bf16[2,192,256]{2,1,0:T(8,128)(2,1)S(1)}, bf16[2,192,256]{2,1,0:T(8,128)(2,1)S(1)}, u32[]{:S(2)}, u32[]{:S(2)}) collective-permute-start(bf16[2,192,256]{2,1,0:T(8,128)(2,1)S(1)} %get-tuple-element.217), channel_id=1, source_target_pairs={{0,8},{2,10},{4,12},{6,14},{8,0},{10,2},{12,4},{14,6},{16,24},{18,... | collective-permute-start | bytes 589832 | tf_op jit(solution)/shard_map/ppermute | solution.py:360
  542.1 31.8 %collective-permute-start.30 = (bf16[2,72,1536]{2,1,0:T(8,128)(2,1)S(1)}, bf16[2,72,1536]{2,1,0:T(8,128)(2,1)S(1)}, u32[]{:S(2)}, u32[]{:S(2)}) collective-permute-start(bf16[2,72,1536]{2,1,0:T(8,128)(2,1)S(1)} %get-tuple-element.195), channel_id=1, source_target_pairs={{0,8},{2,10},{4,12},{6,14},{8,0},{10,2},{12,4},{14,6},{16,24},{18,... | collective-permute-start | bytes 1327112 | tf_op jit(solution)/shard_map/ppermute | solution.py:360
  544.1 29.9 %collective-permute-start.29 = (bf16[2,72,1536]{2,1,0:T(8,128)(2,1)S(1)}, bf16[2,72,1536]{2,1,0:T(8,128)(2,1)S(1)}, u32[]{:S(2)}, u32[]{:S(2)}) collective-permute-start(bf16[2,72,1536]{2,1,0:T(8,128)(2,1)S(1)} %get-tuple-element.193), channel_id=1, source_target_pairs={{0,8},{2,10},{4,12},{6,14},{8,0},{10,2},{12,4},{14,6},{16,24},{18,... | collective-permute-start | bytes 1327112 | tf_op jit(solution)/shard_map/ppermute | solution.py:360
  545.1 28.8 %collective-permute-start.27 = (bf16[2,2,2,72,512]{4,3,0,2,1:T(8,128)(2,1)S(1)}, bf16[2,2,2,72,512]{4,3,0,2,1:T(8,128)(2,1)S(1)}, u32[]{:S(2)}, u32[]{:S(2)}) collective-permute-start(bf16[2,2,2,72,512]{4,3,0,2,1:T(8,128)(2,1)S(1)} %fusion.32), channel_id=1, source_target_pairs={{0,2},{2,0},{4,6},{6,4},{8,10},{10,8},{12,14},{14,12},{16,18},{18,... | collective-permute-start | bytes 1769480 | tf_op jit(solution)/shard_map/ppermute | solution.py:360
  546.1 27.9 %collective-permute-start.28 = (bf16[2,2,2,72,512]{4,3,0,2,1:T(8,128)(2,1)S(1)}, bf16[2,2,2,72,512]{4,3,0,2,1:T(8,128)(2,1)S(1)}, u32[]{:S(2)}, u32[]{:S(2)}) collective-permute-start(bf16[2,2,2,72,512]{4,3,0,2,1:T(8,128)(2,1)S(1)} %fusion.33), channel_id=1, source_target_pairs={{0,4},{2,6},{4,0},{6,2},{8,12},{10,14},{12,8},{14,10},{16,20},{18,... | collective-permute-start | bytes 1769480 | tf_op jit(solution)/shard_map/ppermute | solution.py:360
  547.3 26.7 %copy-start.3 = (bf16[2,1,512,1152]{3,2,1,0:T(8,128)(2,1)S(1)}, bf16[2,1,512,1152]{3,2,1,0:T(8,128)(2,1)}, u32[]{:S(2)}) copy-start(bf16[2,1,512,1152]{3,2,1,0:T(8,128)(2,1)} %param.11) | copy-start | bytes 7077892
  547.3 26.7 %copy-start.55 = (f32[1152]{0:T(1024)S(1)}, f32[1152]{0:T(1024)}, u32[]{:S(2)}) copy-start(f32[1152]{0:T(1024)} %copy-done.54) | copy-start | bytes 13828
  547.3 26.7 %copy-start.57 = (f32[1,4,2,128]{3,1,2,0:T(4,128)S(1)}, f32[1,4,2,128]{3,1,2,0:T(4,128)}, u32[]{:S(2)}) copy-start(f32[1,4,2,128]{3,1,2,0:T(4,128)} %copy-done.56) | copy-start | bytes 12292
  550.0 25.6 %copy-start.52 = (bf16[2,192,256]{2,1,0:T(8,128)(2,1)}, bf16[2,192,256]{2,1,0:T(8,128)(2,1)S(1)}, u32[]{:S(2)}) copy-start(bf16[2,192,256]{2,1,0:T(8,128)(2,1)S(1)} %collective-permute-done.31) | copy-start | bytes 589828
  550.0 23.9 %collective-permute-start.32 = (bf16[2,192,320]{2,1,0:T(8,128)(2,1)S(1)}, bf16[2,192,320]{2,1,0:T(8,128)(2,1)S(1)}, u32[]{:S(2)}, u32[]{:S(2)}) collective-permute-start(bf16[2,192,320]{2,1,0:T(8,128)(2,1)S(1)} %get-tuple-element.201), channel_id=1, source_target_pairs={{0,8},{2,10},{4,12},{6,14},{8,0},{10,2},{12,4},{14,6},{16,24},{18,... | collective-permute-start | bytes 737288 | tf_op jit(solution)/shard_map/ppermute | solution.py:360
  551.1 24.6 %copy-start.59 = (f32[1152,1]{0,1:T(1,128)S(1)}, f32[1152,1]{0,1:T(1,128)}, u32[]{:S(2)}) copy-start(f32[1152,1]{0,1:T(1,128)} %stack.220) | copy-start | bytes 13828
  576.5 51.6 %collective-permute-start.41 = (f32[1152,128]{0,1:T(8,128)}, f32[1152,128]{0,1:T(8,128)}, u32[]{:S(2)}, u32[]{:S(2)}) collective-permute-start(f32[1152,128]{0,1:T(8,128)} %select_maximum_fusion), channel_id=1, source_target_pairs={{0,1},{1,0},{2,3},{3,2},{4,5},{5,4},{6,7},{7,6},{8,9},{9,8},{10,11... | collective-permute-start | bytes 1769480 | tf_op jit(solution)/shard_map/ppermute | solution.py:344
  579.8 29.6 %collective-permute-start.48 = (bf16[192,256]{1,0:T(8,128)(2,1)S(1)}, bf16[192,256]{1,0:T(8,128)(2,1)S(1)}, u32[]{:S(2)}, u32[]{:S(2)}) collective-permute-start(bf16[192,256]{1,0:T(8,128)(2,1)S(1)} %fusion.83), channel_id=1, source_target_pairs={{0,16},{2,18},{4,20},{6,22},{8,24},{10,26},{12,28},{14,30},{16,0},... | collective-permute-start | bytes 294920 | tf_op jit(solution)/shard_map/ppermute | solution.py:360
  582.5 28.0 %collective-permute-start.49 = (bf16[192,320]{1,0:T(8,128)(2,1)S(1)}, bf16[192,320]{1,0:T(8,128)(2,1)S(1)}, u32[]{:S(2)}, u32[]{:S(2)}) collective-permute-start(bf16[192,320]{1,0:T(8,128)(2,1)S(1)} %fusion.76), channel_id=1, source_target_pairs={{0,16},{2,18},{4,20},{6,22},{8,24},{10,26},{12,28},{14,30},{16,0},... | collective-permute-start | bytes 368648 | tf_op jit(solution)/shard_map/ppermute | solution.py:360
  585.0 27.5 %collective-permute-start.46 = (bf16[72,1536]{1,0:T(8,128)(2,1)S(1)}, bf16[72,1536]{1,0:T(8,128)(2,1)S(1)}, u32[]{:S(2)}, u32[]{:S(2)}) collective-permute-start(bf16[72,1536]{1,0:T(8,128)(2,1)S(1)} %fusion.64), channel_id=1, source_target_pairs={{0,16},{2,18},{4,20},{6,22},{8,24},{10,26},{12,28},{14,30},{16,0},... | collective-permute-start | bytes 663560 | tf_op jit(solution)/shard_map/ppermute | solution.py:360
  587.7 20.2 %collective-permute-start.40 = (bf16[72,576]{1,0:T(8,128)(2,1)S(1)}, bf16[72,576]{1,0:T(8,128)(2,1)S(1)}, u32[]{:S(2)}, u32[]{:S(2)}) collective-permute-start(bf16[72,576]{1,0:T(8,128)(2,1)S(1)} %fusion.85), channel_id=1, source_target_pairs={{0,16},{2,18},{4,20},{6,22},{8,24},{10,26},{12,28},{14,30},{16,0},... | collective-permute-start | bytes 248840 | tf_op jit(solution)/shard_map/ppermute | solution.py:360
  596.8 15.7 %copy-start.30 = (bf16[2,1,72,1536]{3,2,1,0:T(8,128)(2,1)S(1)}, bf16[2,1,72,1536]{3,2,1,0:T(8,128)(2,1)}, u32[]{:S(2)}) copy-start(bf16[2,1,72,1536]{3,2,1,0:T(8,128)(2,1)} %get-tuple-element.192) | copy-start | bytes 1327108
  596.8 15.7 %copy-start.48 = (bf16[2,72,1536]{2,1,0:T(8,128)(2,1)S(1)}, bf16[2,72,1536]{2,1,0:T(8,128)(2,1)}, u32[]{:S(2)}) copy-start(bf16[2,72,1536]{2,1,0:T(8,128)(2,1)} %copy-done.47) | copy-start | bytes 1327108
  607.9 11.8 %collective-permute-start.47 = (bf16[72,1536]{1,0:T(8,128)(2,1)S(1)}, bf16[72,1536]{1,0:T(8,128)(2,1)S(1)}, u32[]{:S(2)}, u32[]{:S(2)}) collective-permute-start(bf16[72,1536]{1,0:T(8,128)(2,1)S(1)} %fusion.66), channel_id=1, source_target_pairs={{0,16},{2,18},{4,20},{6,22},{8,24},{10,26},{12,28},{14,30},{16,0},... | collective-permute-start | bytes 663560 | tf_op jit(solution)/shard_map/ppermute | solution.py:360
  609.5 15.7 %collective-permute-start.34 = (bf16[2,2,72,512]{3,2,1,0:T(8,128)(2,1)S(1)}, bf16[2,2,72,512]{3,2,1,0:T(8,128)(2,1)S(1)}, u32[]{:S(2)}, u32[]{:S(2)}) collective-permute-start(bf16[2,2,72,512]{3,2,1,0:T(8,128)(2,1)S(1)} %copy.315), channel_id=1, source_target_pairs={{0,4},{2,6},{4,0},{6,2},{8,12},{10,14},{12,8},{14,10},{16,20},{18,... | collective-permute-start | bytes 884744 | tf_op jit(solution)/shard_map/ppermute | solution.py:360
  610.5 10.1 %collective-permute-start.37 = (bf16[2,2,72,512]{3,2,1,0:T(8,128)(2,1)S(1)}, bf16[2,2,72,512]{3,2,1,0:T(8,128)(2,1)S(1)}, u32[]{:S(2)}, u32[]{:S(2)}) collective-permute-start(bf16[2,2,72,512]{3,2,1,0:T(8,128)(2,1)S(1)} %copy.320), channel_id=1, source_target_pairs={{0,2},{2,0},{4,6},{6,4},{8,10},{10,8},{12,14},{14,12},{16,18},{18,... | collective-permute-start | bytes 884744 | tf_op jit(solution)/shard_map/ppermute | solution.py:360
  620.7 6.4 collective-permute-start.38
  625.2 6.5 collective-permute-start.35
  627.2 6.8 %collective-permute-start.39 = (bf16[72,512]{1,0:T(8,128)(2,1)S(1)}, bf16[72,512]{1,0:T(8,128)(2,1)S(1)}, u32[]{:S(2)}, u32[]{:S(2)}) collective-permute-start(bf16[72,512]{1,0:T(8,128)(2,1)S(1)} %fusion.89), channel_id=1, source_target_pairs={{0,16},{2,18},{4,20},{6,22},{8,24},{10,26},{12,28},{14,30},{16,0},... | collective-permute-start | bytes 221192 | tf_op jit(solution)/shard_map/ppermute | solution.py:360
  629.6 8.0 %collective-permute-start.42 = (f32[2,2,2,72,128]{4,3,2,1,0:T(8,128)S(1)}, f32[2,2,2,72,128]{4,3,2,1,0:T(8,128)S(1)}, u32[]{:S(2)}, u32[]{:S(2)}) collective-permute-start(f32[2,2,2,72,128]{4,3,2,1,0:T(8,128)S(1)} %get-tuple-element.203), channel_id=1, source_target_pairs={{0,4},{2,6},{4,0},{6,2},{8,12},{10,14},{12,8},{14,10},{16,20},{18,... | collective-permute-start | bytes 884744 | tf_op jit(solution)/shard_map/ppermute | solution.py:360
  631.7 12.9 %collective-permute-start.36 = (bf16[72,512]{1,0:T(8,128)(2,1)S(1)}, bf16[72,512]{1,0:T(8,128)(2,1)S(1)}, u32[]{:S(2)}, u32[]{:S(2)}) collective-permute-start(bf16[72,512]{1,0:T(8,128)(2,1)S(1)} %fusion.87), channel_id=1, source_target_pairs={{0,16},{2,18},{4,20},{6,22},{8,24},{10,26},{12,28},{14,30},{16,0},... | collective-permute-start | bytes 221192 | tf_op jit(solution)/shard_map/ppermute | solution.py:360
  637.6 5.2 collective-permute-start.43
  642.9 4.8 collective-permute-start.44
  647.7 4.9 collective-permute-start.45
  (54 other events, 291.1 us)
Sparse Core Ops, SparseCore 0:
  11.5 98.7 all-gather.2
  113.7 101.1 all-gather.4

commit v6 on v5

--- a/solution.py
+++ b/solution.py
@@ -19,6 +19,7 @@
 HALL = HQ + 2 * HK
 QKV = HALL * HEAD_SIZE
 FT = 256
+HALF = 640
 WIDE = 1024
 
 epsilon = 1e-05
@@ -130,6 +131,7 @@
     for dst, rows in zip((o_mine, o_theirs), at):
         for j in range(HQ):
             dst[:, head_cols(j)] = o[j, rows, :]
+        dst[:, HQ * HEAD_SIZE :] = jnp.zeros_like(dst[:, HQ * HEAD_SIZE :])
 
 
 def bwd_body(
@@ -184,7 +186,7 @@
     tokens, width = mine.shape
     batch = tokens // piece
     row = lambda a, c: pl.BlockSpec((a, c), lambda b, m: (b, 0))
-    cols = HQ * HEAD_SIZE
+    cols = HALF
     heads = lambda n: pltpu.VMEM((n, 2 * piece, HEAD_SIZE), bf16)
     return pl.pallas_call(
         fwd_body,
@@ -209,7 +211,7 @@
 def attend_back(b, before, me, mine, got, o_mine, o_theirs, do_mine, do_got, lse, cosine, sine, piece):
     tokens, width = mine.shape
     row = lambda a, c: pl.BlockSpec((a, c), lambda _, m: (b, 0))
-    cols = HQ * HEAD_SIZE
+    cols = HALF
     table = pl.BlockSpec((2 * piece, 128), lambda _, m: (0, 0))
     heads = lambda n, t: pltpu.VMEM((n, 2 * piece, HEAD_SIZE), t)
     return pl.pallas_call(
@@ -235,7 +237,7 @@
     )(me, mine, got, o_mine, o_theirs, do_mine, do_got, lse, cosine, sine, *before)
 
 
-def mlp_body(me, n2, n2t, cot, res, wg, wu, wd_mine, wd_theirs, out, gn, g_mine, g_theirs, gd_mine, gd_theirs, y, wd):
+def mlp_body(me, n2, n2t, cot, res, wg, wu, wd_mine, wd_theirs, out, gn, gg_mine, gu_mine, gg_theirs, gu_theirs, gd_mine, gd_theirs, y, wd):
     t = pl.program_id(0)
     per = pl.num_programs(0) // 2
 
@@ -244,18 +246,18 @@
         y[...] = res[...]
         gn[...] = jnp.zeros_like(gn)
 
-    half = wd_mine.shape[1]
+    half = D // 2
     first = me[0] == 0
 
     @pl.when(first)
     def _():
-        wd[:, :half] = wd_mine[...]
-        wd[:, half:] = wd_theirs[...]
+        wd[:, :half] = wd_mine[:, :half]
+        wd[:, half:] = wd_theirs[:, :half]
 
     @pl.when(jnp.logical_not(first))
     def _():
-        wd[:, :half] = wd_theirs[...]
-        wd[:, half:] = wd_mine[...]
+        wd[:, :half] = wd_theirs[:, :half]
+        wd[:, half:] = wd_mine[:, :half]
 
     wgt, wut = assemble(wg), assemble(wu)
     gate = dg(n2[...], wgt, NN)
@@ -268,20 +270,24 @@
     guv = (gh * act).astype(bf16)
     y[...] += dg(hidden, wd[...], NN)
     gdt = dg(hidden, cot[...], TN)
-    gd_mine[...] = jnp.where(first, gdt[:, :half], gdt[:, half:]).astype(bf16)
-    gd_theirs[...] = jnp.where(first, gdt[:, half:], gdt[:, :half]).astype(bf16)
+    for dst, u in (
+        (gd_mine, jnp.where(first, gdt[:, :half], gdt[:, half:])),
+        (gd_theirs, jnp.where(first, gdt[:, half:], gdt[:, :half])),
+    ):
+        dst[:, :half] = u.astype(bf16)
+        dst[:, half:] = jnp.zeros((FT, HALF - half), bf16)
     gg = dg(n2t[...], ggv, NN).astype(bf16)
     gu = dg(n2t[...], guv, NN).astype(bf16)
 
     @pl.when(t < per)
     def _():
-        g_theirs[:, :FT] = gg
-        g_theirs[:, FT:] = gu
+        gg_theirs[...] = gg
+        gu_theirs[...] = gu
 
     @pl.when(t >= per)
     def _():
-        g_mine[:, :FT] = gg
-        g_mine[:, FT:] = gu
+        gg_mine[...] = gg
+        gu_mine[...] = gu
 
     gn[...] += dg(ggv, wgt, NT) + dg(guv, wut, NT)
 
@@ -300,7 +306,7 @@
     col = lambda first: pl.BlockSpec(
         (n, 1, rows, FT), lambda t, m: (0, half(t, m), 0, first + t % per)
     )
-    part = pl.BlockSpec((FT, D // 2), lambda t, m: (half(t, m) * per + t % per, 0))
+    part = pl.BlockSpec((FT, HALF), lambda t, m: (half(t, m) * per + t % per, 0))
     one = lambda: pl.BlockSpec((tokens, D), lambda t, m: (0, 0), pipeline_mode=pl.Buffered(1))
     return pl.pallas_call(
         mlp_body,
@@ -311,8 +317,8 @@
             out_specs=[
                 one(),
                 one(),
-                pl.BlockSpec((D, 2 * FT), lambda t, m: (0, jnp.maximum(t - per, 0))),
-                pl.BlockSpec((D, 2 * FT), lambda t, m: (0, jnp.minimum(t, per - 1))),
+                *[pl.BlockSpec((D, FT), lambda t, m: (0, jnp.maximum(t - per, 0)))] * 2,
+                *[pl.BlockSpec((D, FT), lambda t, m: (0, jnp.minimum(t, per - 1)))] * 2,
                 part,
                 part,
             ],
@@ -321,10 +327,9 @@
         out_shape=[
             jax.ShapeDtypeStruct((tokens, D), bf16),
             jax.ShapeDtypeStruct((tokens, D), f32),
-            jax.ShapeDtypeStruct((D, 2 * cols), bf16),
-            jax.ShapeDtypeStruct((D, 2 * cols), bf16),
-            jax.ShapeDtypeStruct((FF, D // 2), bf16),
-            jax.ShapeDtypeStruct((FF, D // 2), bf16),
+            *[jax.ShapeDtypeStruct((D, cols), bf16)] * 4,
+            jax.ShapeDtypeStruct((FF, HALF), bf16),
+            jax.ShapeDtypeStruct((FF, HALF), bf16),
         ],
         compiler_params=pltpu.CompilerParams(vmem_limit_bytes=VMEM_BYTES),
         cost_estimate=pl.CostEstimate(flops=65 * 10**9, bytes_accessed=60 * 10**6, transcendentals=3 * 10**6),
@@ -360,18 +365,16 @@
     return lax.ppermute(a, "dp", [(i, i ^ (1 << bit)) for i in range(lax.axis_size("dp"))])
 
 
-def column_parts(cols, split=True):
-    cut = cols // 256 * 128 * split
-    parts = (slice(0, cut), (0, 1)), (slice(cut, cols), (1, 0))
-    return parts if cut else parts[1:]
+ORDERS = (0, 1), (1, 0)
 
 
 def gather_doubling(w):
     bits = lax.axis_size("dp").bit_length() - 1
     dp = lax.axis_index("dp")
+    cut = w.shape[1] // 256 * 128
     out = []
-    for part, order in column_parts(w.shape[1]):
-        a, have = w[:, part], []
+    for part, order in ((w[:, :cut], ORDERS[0]), (w[:, cut:], ORDERS[1])):
+        a, have = part, []
         for bit in list(range(bits))[:1:-1] + list(order[::-1]):
             got = exchange(a, bit)
             axis = sum(b > bit for b in have)
@@ -387,16 +390,14 @@
 
 
 class Halving:
-    def __init__(self, mine, theirs, kind=bf16, split=True):
+    def __init__(self, parts, kind=bf16):
         self.kind = kind
         bits = lax.axis_size("dp").bit_length() - 1
         self.steps = bits
-        got = swap(theirs)
-        self.orders, self.stay, self.got = [], [], []
-        for part, order in column_parts(mine.shape[1], split):
-            self.orders.append(list(order) + list(range(2, bits)))
-            for to, u in ((self.stay, mine), (self.got, got)):
-                to.append(u[:, part].reshape(*[2] * bits, -1, u[:, part].shape[1]))
+        self.orders = [[*order, *range(2, bits)] for _, _, order in parts]
+        shape = lambda u: u.reshape(*[2] * bits, -1, u.shape[-1])
+        self.stay = [shape(u) for u, _, _ in parts]
+        self.got = [shape(v) for _, v, _ in parts]
 
     def prepare(self, step):
         self.send = []
@@ -419,7 +420,7 @@
     def finish(self, step=0):
         for i in range(step, self.steps):
             self.advance(i)
-        return jnp.concatenate([add(*u) for u in zip(self.stay, self.got)], 1)
+        return [add(*u) for u in zip(self.stay, self.got)]
 
 
 def local(
@@ -449,14 +450,15 @@
     gains = jnp.pad(jnp.stack([gain_attn, gain_mlp], 1), ((0, 0), (0, WIDE - QKV - 2)))
     full = fetch(jnp.concatenate([w_query, w_key, w_value, gains, w_out], 1))
     wide = fetch(jnp.concatenate([w_gate, w_up], 1))
-    down_mine, down_theirs = gather_doubling(w_down)
+    widen = lambda a: jnp.pad(a, ((0, 0), (0, HALF - D // 2)))
+    down_mine, down_theirs = gather_doubling(widen(w_down))
     gain_one = full[:, 0, :, QKV].reshape(D).astype(f32)
     gain_two = full[:, 0, :, QKV + 1].reshape(D).astype(f32)
     out_halves = whole_halves(full[..., WIDE:])[0].reshape(2, 2, D // 2, D // 2)
     out_rows = lambda c: jnp.concatenate(
         [lax.dynamic_index_in_dim(out_halves[i], c, 0, keepdims=False) for i in range(2)], 1
     )
-    out_mine, out_theirs = out_rows(me), out_rows(1 - me)
+    out_mine, out_theirs = [jnp.pad(out_rows(c), ((0, HALF - D // 2), (0, 0))) for c in (me, 1 - me)]
 
     floats = layer_input.reshape(tokens, D).astype(f32)
     cot = cotangent.reshape(tokens, D)
@@ -472,67 +474,86 @@
     residual = floats + (dot(mixed, out_mine) + dot(mixed_got, out_theirs))
     scale_mlp = lax.rsqrt(jnp.mean(residual * residual, -1, keepdims=True) + epsilon)
     n2 = (residual * scale_mlp * gain_two).astype(bf16)
-    layer_out, grad_n2, g_mine, g_theirs, gd_mine, gd_theirs = mlp(
+    layer_out, grad_n2, gg_mine, gu_mine, gg_theirs, gu_theirs, gd_mine, gd_theirs = mlp(
         me_arr, n2, n2.T, cot, residual, wide, down_mine, down_theirs
     )
     tie = lax.optimization_barrier
-    wide_sum, down_sum = Halving(g_mine, g_theirs), Halving(gd_mine, gd_theirs)
+    wide_sum = Halving([(gg_mine, swap(gg_theirs), ORDERS[0]), (gu_mine, swap(gu_theirs), ORDERS[1])])
+    wide_sum.prepare(0)
     sum_gain_mlp = jnp.sum(grad_n2 * residual * scale_mlp, 0)
     grad_residual = cot.astype(f32) + norm_back(grad_n2, residual, scale_mlp, gain_two)
+    grad_residual, wide_sum.send = tie((grad_residual, wide_sum.send))
+    wide_sum.move(0)
     grad_low = grad_residual.astype(bf16)
     d_out = lax.dot_general(grad_low, out_theirs, NT, preferred_element_type=f32).astype(bf16)
     d_got = swap(d_out)
     d_mine = lax.dot_general(grad_low, out_mine, NT, preferred_element_type=f32).astype(bf16)
-    low = grad_low[:, : D // 2], grad_low[:, D // 2 :]
+    down_sum = Halving([(gd_mine, swap(gd_theirs), ORDERS[1])])
+    down_sum.prepare(0)
+    d_mine, d_got, down_sum.send = tie((d_mine, d_got, down_sum.send))
+    down_sum.move(0)
+    back = lambda b, before: attend_back(
+        b, before, me_arr, mine, got, mixed, mixed_out, d_mine, d_got, lse, cosine, sine, piece
+    )
+    lins = back(0, ())
+
+    lins, grad_low, wide_sum.got = tie((lins, grad_low, wide_sum.got))
+    low = widen(grad_low[:, : D // 2]), widen(grad_low[:, D // 2 :])
 
     def grad_out(columns):
-        a = lax.dot_general(mixed, columns, TN, preferred_element_type=f32).astype(bf16)
-        b = lax.dot_general(mixed_got, columns, TN, preferred_element_type=f32).astype(bf16)
+        a, b = [
+            lax.dot_general(u, columns, TN, preferred_element_type=f32).astype(bf16)[: QD // 2]
+            for u in (mixed, mixed_got)
+        ]
         return pick(jnp.concatenate([a, b], 0), jnp.concatenate([b, a], 0))
 
-    out_sum = Halving(grad_out(pick(*low)), grad_out(pick(*low[::-1])), split=False)
-    early = wide_sum, down_sum, out_sum
-    for u in early:
-        u.prepare(0)
-    (d_mine, d_got), sends = tie(((d_mine, d_got), [u.send for u in early]))
-    for u, send in zip(early, sends):
-        u.send = send
-        u.move(0)
-    lins = ()
-    for b in range(batch):
-        lins = attend_back(
-            b, lins, me_arr, mine, got, mixed, mixed_out, d_mine, d_got, lse, cosine, sine, piece
-        )
-    (lin_mine, lin_out), gots = tie((lins, [u.got for u in early]))
-    for u, arrived in zip(early, gots):
-        u.got = arrived
-        u.advance(1)
+    wide_sum.prepare(1)
+    out_sum = Halving([(grad_out(pick(*low)), swap(grad_out(pick(*low[::-1]))), ORDERS[0])])
+    out_sum.prepare(0)
+    lins, wide_sum.send, out_sum.send = tie((lins, wide_sum.send, out_sum.send))
+    wide_sum.move(1)
+    out_sum.move(0)
+    for b in range(1, batch):
+        lins = back(b, lins)
+    (lin_mine, lin_out), wide_sum.got, down_sum.got, out_sum.got = tie(
+        (lins, wide_sum.got, down_sum.got, out_sum.got)
+    )
     lin_got = swap(lin_out)
-    weight_grad = lambda lin: lax.dot_general(n1, lin, TN, preferred_element_type=f32).astype(bf16)
-    pack_sum = Halving(weight_grad(lin_mine), weight_grad(lin_got))
-    pack_sum.prepare(0)
-    pack_sum.send, gots = tie((pack_sum.send, [u.got for u in early]))
-    pack_sum.move(0)
-    for u, arrived in zip(early, gots):
-        u.got = arrived
-        u.advance(2)
+    down_sum.advance(1)
+    out_sum.advance(1)
+    wide_sum.advance(2)
     grad_n1 = lax.dot_general(lin_mine, w_mine, NT, preferred_element_type=f32) + lax.dot_general(
         lin_got, w_theirs, NT, preferred_element_type=f32
     )
-    grad_n1, pack_sum.got, gots = tie((grad_n1, pack_sum.got, [u.got for u in early]))
+    sum_gain_attn = jnp.sum(grad_n1 * floats * scale_attn, 0)
+    column = lax.broadcasted_iota(jnp.int32, (1, WIDE), 1)
+    sums = jnp.where(column == QKV, sum_gain_attn[:, None], 0.0) + jnp.where(
+        column == QKV + 1, sum_gain_mlp[:, None], 0.0
+    )
+    weight_grad = lambda lin: (
+        lax.dot_general(n1, lin, TN, preferred_element_type=f32) + sums
+    ).astype(bf16)
+    half = WIDE // 2
+    grad_mine, grad_theirs = weight_grad(lin_mine), weight_grad(lin_got)
+    grad_got = swap(grad_theirs)
+    pack_sum = Halving(
+        [
+            (grad_mine[:, :half], grad_got[:, :half], ORDERS[0]),
+            (grad_mine[:, half:], grad_got[:, half:], ORDERS[1]),
+        ]
+    )
+    pack_sum.prepare(0)
+    pack_sum.send, down_sum.got, out_sum.got = tie((pack_sum.send, down_sum.got, out_sum.got))
+    pack_sum.move(0)
+    down_sum.advance(2)
+    out_sum.advance(2)
+    grad_input = (grad_residual + norm_back(grad_n1, floats, scale_attn, gain_one)).astype(bf16)
+    pack_sum.got, wide_sum.got = tie((pack_sum.got, wide_sum.got))
     pack_sum.advance(1)
-    for u, arrived in zip(early, gots):
-        u.got = arrived
-    sum_gain_attn = jnp.sum(grad_n1 * floats * scale_attn, 0)
-    grad_input = (grad_residual + norm_back(grad_n1, floats, scale_attn, gain_one)).astype(bf16)
-    sums = jnp.pad(jnp.stack([sum_gain_attn, sum_gain_mlp], 1), ((0, 0), (0, 126)))
-    r_wide, r_down, r_out = [u.finish(3) for u in early]
-    r_pack = pack_sum.finish(2)
-    r_sums = Halving(sums, sums, f32).finish()
-    r_gate, r_up = [
-        a.reshape(a.shape[0], -1).astype(f32)
-        for a in jnp.split(r_wide.reshape(-1, FF // 2 // FT, 2, FT), 2, 2)
-    ]
+    r_gate, r_up = wide_sum.finish(3)
+    r_down = down_sum.finish(3)[0][:, : D // 2]
+    r_out = out_sum.finish(3)[0][:, : D // 2]
+    r_pack = jnp.concatenate(pack_sum.finish(2), 1)
     a, b, c = HQ * HEAD_SIZE, (HQ + HK) * HEAD_SIZE, QKV
     shape = layer_input.shape
     return (
@@ -542,11 +563,11 @@
         r_pack[:, a:b],
         r_pack[:, b:c],
         r_out,
-        r_sums[:, 0],
+        r_pack[:, c],
         r_gate,
         r_up,
         r_down,
-        r_sums[:, 1],
+        r_pack[:, c + 1],
     )
 
 

time: 670 us -> 566 us (0.84)
  local copies, waits for them, and re-layouts: 85.4 us -> 40.9 us
  other arithmetic: 90.7 us -> 64.8 us
  waiting for transfers between devices: 180 us -> 160 us
  starting transfers between devices: 52.8 us -> 44.6 us
    ppermute x40 -> x32, waiting for transfers between devices: 133 us -> 114 us  [exchange(): lax.ppermute(a, 'dp', [(i, i ^ 1 << bit) for i in range(lax.axis_size('dp...]
    convert_element_type x38 -> x30, other arithmetic: 41.6 us -> 26 us  [prepare(): add(at(self.stay[p], i), at(self.got[p], i)).astype(self.kind)]
    slice x9, local copies, waits for them, and re-layouts: 18.6 us -> 3.15 us  [the longest x1 1.92 us: local(): low = (widen(grad_low[:, :D // 2]), widen(grad_low[:, D // 2:]))]
    ppermute x3 -> x0, local copies, waits for them, and re-layouts: 10.1 us -> none  [swap(): return lax.ppermute(a, 'seq', [(0, 1), (1, 0)])]
    ppermute x40 -> x32, starting transfers between devices: 50.4 us -> 42.2 us  [exchange(): lax.ppermute(a, 'dp', [(i, i ^ 1 << bit) for i in range(lax.axis_size('dp...]
    pallas_call x2 -> x0, local copies, waits for them, and re-layouts: 7.62 us -> none  [the longest x1 6.05 us: mlp(): pl.pallas_call(mlp_body, grid_spec=pltpu.PrefetchScalarGridSpec(num_scala...]
    dynamic_slice x8 -> x12, local copies, waits for them, and re-layouts: 7.63 us -> 13.8 us  [prepare(): at = lambda u, i: lax.dynamic_index_in_dim(u, i, axis, keepdims=False)]
    unnamed x138 -> x100, local copies, waits for them, and re-layouts: 14.2 us -> 11.3 us
  transfers between devices with their start and end apart: 52 -> 44, of which waited for: 19 -> 18; matrix products, arithmetic and copies ran while one was open for 29% -> 22% of each run, Pallas kernels for 16% -> 19%
where the time goes in v6:
time: 566 us; the launch traced here: 558 us
  Pallas kernels  200 us (35%)
  waiting for transfers between devices  160 us (28%)
  other arithmetic  64.8 us (11%)
  starting transfers between devices  44.6 us (8%)
  local copies, waits for them, and re-layouts  40.9 us (7%)
  matrix products  32.5 us (6%)
  between operations  15.4 us (3%)
    ppermute x32, waiting for transfers between devices, exchange(): lax.ppermute(a, 'dp', [(i, i ^ 1 << bit) for i in range(lax.axis_size('dp...  114 us
    pallas_call x1, Pallas kernels, mlp(): pl.pallas_call(mlp_body, grid_spec=pltpu.PrefetchScalarGridSpec(num_scala...  93.6 us
    pallas_call x2, Pallas kernels, attend_back(): pl.pallas_call(bwd_body, grid_spec=pltpu.PrefetchScalarGridSpec(num_scala...  54.3 us
    all_gather x2, waiting for transfers between devices, fetch(): lax.all_gather(w, BOTH, axis=0, tiled=True)  46.4 us
    ppermute x32, starting transfers between devices, exchange(): lax.ppermute(a, 'dp', [(i, i ^ 1 << bit) for i in range(lax.axis_size('dp...  42.2 us
    pallas_call x1, Pallas kernels, attend(): pl.pallas_call(fwd_body, grid_spec=pltpu.PrefetchScalarGridSpec(num_scala...  38.9 us
    convert_element_type x30, other arithmetic, prepare(): add(at(self.stay[p], i), at(self.got[p], i)).astype(self.kind)  26 us
    dynamic_slice x12, local copies, waits for them, and re-layouts, prepare(): at = lambda u, i: lax.dynamic_index_in_dim(u, i, axis, keepdims=False)  13.8 us
  transfers between devices with their start and end apart: 44, of which 18 were waited for; matrix products, arithmetic and copies ran while one was open for 22% of the time, Pallas kernels for 19%

profile of v6, /device:TPU:0, one launch (start us, length us, event | category | flops | bytes accessed | tf_op | source)
XLA Modules:
  0.0 558.4 jit_solution(9022851293860526529)
XLA Ops:
  8.1 1.8 concatenate.186
  10.0 2.0 pad_maximum_fusion.1
  12.7 4.1 collective-permute-start.6
  17.0 3.1 fusion.43
  20.7 9.5 %collective-permute-done.2 = bf16[192,256]{1,0:T(8,128)(2,1)S(1)} collective-permute-done((bf16[192,256]{1,0:T(8,128)(2,1)S(1)}, bf16[192,256]{1,0:T(8,128)(2,1)S(1)}, u32[]{:S(2)}, u32[]{:S(2)}) %collective-permute-start.2) | collective-permute-done | bytes 98336 | tf_op jit(solution)/shard_map/ppermute | solution.py:365
  30.2 2.3 collective-permute-start.3
  33.4 5.8 %collective-permute-done.3 = bf16[2,192,256]{2,1,0:T(8,128)(2,1)S(1)} collective-permute-done((bf16[2,192,256]{2,1,0:T(8,128)(2,1)S(1)}, bf16[2,192,256]{2,1,0:T(8,128)(2,1)S(1)}, u32[]{:S(2)}, u32[]{:S(2)}) %collective-permute-start.3) | collective-permute-done | bytes 196640 | tf_op jit(solution)/shard_map/ppermute | solution.py:365
  41.5 3.3 collective-permute-done.7
  47.3 46.4 %all-gather.3.cloned.1.call-done = bf16[2304,1600]{1,0:T(8,128)(2,1)} async-done(((bf16[72,1600]{1,0:T(8,128)(2,1)}), bf16[2304,1600]{1,0:T(8,128)(2,1)}) %all-gather.3.cloned.1.call-update) | async-done | bytes 7372816 | tf_op jit(solution)/shard_map/all_gather | solution.py:360
  95.5 2.0 fusion.2.n1
  97.5 6.8 %project.3 = (bf16[1024,1024]{1,0:T(8,128)(2,1)}, bf16[1152,1024]{1,0:T(8,128)(2,1)}) custom-call(s32[1]{0:T(128)} %bitcast.me, bf16[1024,1152]{1,0:T(8,128)(2,1)} %fusion.2.n1, bf16[16,2,72,1600]{3,2,1,0:T(8,128)(2,1)} %bitcast.360, f32[1024,128]{1,0:T(8,128)} %get-tuple-element.210.cosine, f32[1024,128]{1,0:T(8,128)} %get-tuple-element.209.sine), custom_call_target="tpu_custom_call" | custom-call | flops 3000000000 | bytes 12000000 | tf_op jit(solution)/shard_map/project/pallas_call | solution.py:66
  110.1 17.2 %collective-permute-done.5 = bf16[2,2,2,192,256]{4,3,0,1,2:T(8,128)(2,1)S(1)} collective-permute-done((bf16[2,2,2,192,256]{4,3,0,1,2:T(8,128)(2,1)S(1)}, bf16[2,2,2,192,256]{4,3,0,1,2:T(8,128)(2,1)S(1)}, u32[]{:S(2)}, u32[]{:S(2)}) %collective-permute-start.5) | collective-permute-done | bytes 786464 | tf_op jit(solution)/shard_map/ppermute | solution.py:365
  127.7 14.3 %collective-permute-done.9 = bf16[2,2,2,192,384]{4,3,0,1,2:T(8,128)(2,1)S(1)} collective-permute-done((bf16[2,2,2,192,384]{4,3,0,1,2:T(8,128)(2,1)S(1)}, bf16[2,2,2,192,384]{4,3,0,1,2:T(8,128)(2,1)S(1)}, u32[]{:S(2)}, u32[]{:S(2)}) %collective-permute-start.9) | collective-permute-done | bytes 1179680 | tf_op jit(solution)/shard_map/ppermute | solution.py:365
  142.4 1.7 copy.74
  144.1 6.8 %project.2 = (bf16[1024,1024]{1,0:T(8,128)(2,1)}, bf16[1152,1024]{1,0:T(8,128)(2,1)}) custom-call(s32[1]{0:T(128)} %bitcast.me, bf16[1024,1152]{1,0:T(8,128)(2,1)} %fusion.2.n1, bf16[16,2,72,1600]{3,2,1,0:T(8,128)(2,1)} %bitcast.361, f32[1024,128]{1,0:T(8,128)} %get-tuple-element.210.cosine, f32[1024,128]{1,0:T(8,128)} %get-tuple-element.209.sine), custom_call_target="tpu_custom_call" | custom-call | flops 3000000000 | bytes 12000000 | tf_op jit(solution)/shard_map/project/pallas_call | solution.py:66
  150.8 38.9 %attend.1 = (bf16[1024,640]{1,0:T(8,128)(2,1)}, bf16[1024,640]{1,0:T(8,128)(2,1)}, f32[2048,128]{1,0:T(8,128)}) custom-call(s32[1]{0:T(128)} %bitcast.me, bf16[1024,1024]{1,0:T(8,128)(2,1)} %get-tuple-element.60.mine, bf16[1024,1024]{1,0:T(8,128)(2,1)} %collective-permute-done.got), custom_call_target="tpu_custom_call" | custom-call | flops 24000000000 | bytes 20000000 | tf_op jit(solution)/shard_map/attend/pallas_call | solution.py:191
  189.7 3.9 pad_maximum_fusion.wd_mine
  194.2 2.1 slice_bitcast_fusion
  196.9 2.1 fusion.62
  200.7 2.5 multiply_reduce_fusion.2
  203.2 2.1 copy-done
  205.7 2.5 copy.75.n2t
  208.3 4.2 multiply_convert_fusion.n2
  212.4 93.6 %mlp.1 = (bf16[1024,1152]{1,0:T(8,128)(2,1)}, f32[1024,1152]{1,0:T(8,128)}, bf16[1152,1536]{1,0:T(8,128)(2,1)}, bf16[1152,1536]{1,0:T(8,128)(2,1)}, bf16[1152,15...) custom-call(s32[1]{0:T(128)} %bitcast.me, ...), custom_call_target="tpu_custom_call" | custom-call | flops 65000001536 | bytes 60000000 | tf_op jit(solution)/shard_map/mlp/pallas_call | solution.py:311
  306.7 2.7 constant_dynamic-slice_fusion.5
  310.2 3.9 multiply_reduce_fusion
  314.4 1.7 copy-done.10
  318.3 1.9 subtract_add_fusion
  320.2 4.0 constant_dynamic-slice_fusion.14
  324.3 2.3 constant_dynamic-slice_fusion.16
  328.3 1.7 fusion.17
  331.4 2.2 convolution_convert_fusion
  336.1 1.7 add_convert_fusion.4
  337.8 3.3 convolution_convert_fusion.1.do_mine
  341.1 1.7 add_convert_fusion.5
  342.8 1.7 constant_dynamic-slice_fusion.4
  344.5 1.8 fusion.14
  347.7 26.9 %attend_back.2 = (bf16[1024,1024]{1,0:T(8,128)(2,1)}, bf16[1024,1024]{1,0:T(8,128)(2,1)}) custom-call(s32[1]{0:T(128)} %bitcast.me, bf16[1024,1024]{1,0:T(8,128)(2,1)} %get-tuple-element.60.mine, bf16[1024,1024]{1,0:T(8,128)(2,1)} %collective-permute-done.got, bf16[1024,640]{1,0:T(8,128)(2,1)} %get-tuple-element.62.o_mine, ...), custom_call_target="tpu_custom_call" | custom-call | flops 12999999488 | bytes 20000000 | tf_op jit(solution)/shard_map/attend_back/pallas_call | solution.py:217
  375.0 2.2 collective-permute-done.16
  377.2 1.9 slice.86
  379.1 2.7 fusion.91
  387.5 2.9 fusion.19
  392.8 2.8 fusion.20
  400.5 1.9 collective-permute-start.21
  402.4 27.4 %attend_back.3 = (bf16[1024,1024]{1,0:T(8,128)(2,1)}, bf16[1024,1024]{1,0:T(8,128)(2,1)}) custom-call(s32[1]{0:T(128)} %bitcast.me, bf16[1024,1024]{1,0:T(8,128)(2,1)} %get-tuple-element.60.mine, bf16[1024,1024]{1,0:T(8,128)(2,1)} %collective-permute-done.got, ...), custom_call_target="tpu_custom_call", output_to_operand_aliasing={{0}: (10, {}), {1}: (11, {})} | custom-call | flops 12999999488 | bytes 20000000 | tf_op jit(solution)/shard_map/attend_back/pallas_call | solution.py:217
  429.8 8.0 %collective-permute-done.21 = bf16[2,2,2,72,640]{4,3,0,2,1:T(8,128)(2,1)} collective-permute-done((bf16[2,2,2,72,640]{4,3,0,2,1:T(8,128)(2,1)}, bf16[2,2,2,72,640]{4,3,0,2,1:T(8,128)(2,1)}, u32[]{:S(2)}, u32[]{:S(2)}) %collective-permute-start.21) | collective-permute-done | bytes 737312 | tf_op jit(solution)/shard_map/ppermute | solution.py:365
  437.9 2.1 add_convert_fusion.2
  443.2 4.6 fusion.114
  447.9 3.7 fusion.9
  451.6 4.6 add_convert_fusion
  456.4 2.0 fusion.15
  464.8 3.0 add_convert_fusion.1
  469.0 13.6 %collective-permute-done.24 = bf16[2,2,192,640]{3,2,1,0:T(8,128)(2,1)S(1)} collective-permute-done((bf16[2,2,192,640]{3,2,1,0:T(8,128)(2,1)S(1)}, bf16[2,2,192,640]{3,2,1,0:T(8,128)(2,1)S(1)}, u32[]{:S(2)}, u32[]{:S(2)}) %collective-permute-start.24) | collective-permute-done | bytes 983072 | tf_op jit(solution)/shard_map/ppermute | solution.py:365
  484.2 2.5 fusion.6
  488.8 3.2 collective-permute-start.37
  492.1 8.1 %collective-permute-done.37 = bf16[72,640]{1,0:T(8,128)(2,1)S(1)} collective-permute-done((bf16[72,640]{1,0:T(8,128)(2,1)S(1)}, bf16[72,640]{1,0:T(8,128)(2,1)S(1)}, u32[]{:S(2)}, u32[]{:S(2)}) %collective-permute-start.37) | collective-permute-done | bytes 92192 | tf_op jit(solution)/shard_map/ppermute | solution.py:365
  501.7 3.4 collective-permute-start.41
  505.2 9.4 %collective-permute-done.27 = bf16[2,2,2,72,512]{4,3,0,2,1:T(8,128)(2,1)S(1)} collective-permute-done((bf16[2,2,2,72,512]{4,3,0,2,1:T(8,128)(2,1)S(1)}, bf16[2,2,2,72,512]{4,3,0,2,1:T(8,128)(2,1)S(1)}, u32[]{:S(2)}, u32[]{:S(2)}) %collective-permute-start.27) | collective-permute-done | bytes 589856 | tf_op jit(solution)/shard_map/ppermute | solution.py:365
  514.6 3.4 collective-permute-start.39
  520.8 11.9 %collective-permute-done.39 = bf16[72,1536]{1,0:T(8,128)(2,1)S(1)} collective-permute-done((bf16[72,1536]{1,0:T(8,128)(2,1)S(1)}, bf16[72,1536]{1,0:T(8,128)(2,1)S(1)}, u32[]{:S(2)}, u32[]{:S(2)}) %collective-permute-start.39) | collective-permute-done | bytes 221216 | tf_op jit(solution)/shard_map/ppermute | solution.py:365
  533.8 2.1 collective-permute-start.34
  537.1 5.4 collective-permute-done.34
  542.6 3.0 collective-permute-start.32
  545.6 3.0 collective-permute-done.35
  (267 shorter events, 67.9 us)
Async XLA Ops:
  7.2 4.8 copy-start.32
  7.2 86.6 %all-gather.3.cloned.1.call-start = ((), (), s32[]{:S(2)}) async-start(), calls=%async_computation | async-start | bytes 7907328 | tf_op jit(solution)/shard_map/all_gather | solution.py:360
  9.9 10.2 %copy-start.2 = (bf16[2,1,512,1152]{3,2,1,0:T(8,128)(2,1)S(1)}, bf16[2,1,512,1152]{3,2,1,0:T(8,128)(2,1)}, u32[]{:S(2)}) copy-start(bf16[2,1,512,1152]{3,2,1,0:T(8,128)(2,1)} %param.11) | copy-start | bytes 7077892
  9.9 202.5 %all-gather.5.cloned.1.call-start = ((), (), s32[]{:S(2)}) async-start(), calls=%async_computation.1 | async-start | bytes 14598144 | tf_op jit(solution)/shard_map/all_gather | solution.py:360
  12.7 20.7 %copy-start.20 = (bf16[1,1,192,384]{3,2,0,1:T(8,128)(2,1)}, bf16[1,1,192,384]{3,2,0,1:T(8,128)(2,1)S(1)}, u32[]{:S(2)}) copy-start(bf16[1,1,192,384]{3,2,0,1:T(8,128)(2,1)S(1)} %get-tuple-element.204) | copy-start | bytes 442372
  12.7 20.5 %collective-permute-start.6 = (bf16[192,384]{1,0:T(8,128)(2,1)}, bf16[192,384]{1,0:T(8,128)(2,1)S(1)}, u32[]{:S(2)}, u32[]{:S(2)}) collective-permute-start(bf16[192,384]{1,0:T(8,128)(2,1)} %get-tuple-element.206), channel_id=1, source_target_pairs={{0,16},{2,18},{4,20},{6,22},{8,24},{10,26},{12,28},{14,30},{16,0},... | collective-permute-start | bytes 442376 | tf_op jit(solution)/shard_map/ppermute | solution.py:365
  16.8 13.4 %collective-permute-start.2 = (bf16[192,256]{1,0:T(8,128)(2,1)S(1)}, bf16[192,256]{1,0:T(8,128)(2,1)S(1)}, u32[]{:S(2)}, u32[]{:S(2)}) collective-permute-start(bf16[192,256]{1,0:T(8,128)(2,1)S(1)} %get-tuple-element.203), channel_id=1, source_target_pairs={{0,16},{2,18},{4,20},{6,22},{8,24},{10,26},{12,28},{14,30},{16,0},... | collective-permute-start | bytes 294920 | tf_op jit(solution)/shard_map/ppermute | solution.py:365
  20.7 74.8 %copy-start.35 = (f32[1,4,2,128]{3,1,2,0:T(4,128)}, f32[1,4,2,128]{3,1,2,0:T(4,128)S(1)}, u32[]{:S(2)}) copy-start(f32[1,4,2,128]{3,1,2,0:T(4,128)S(1)} %copy.145) | copy-start | bytes 12292
  30.2 9.1 %collective-permute-start.3 = (bf16[2,192,256]{2,1,0:T(8,128)(2,1)S(1)}, bf16[2,192,256]{2,1,0:T(8,128)(2,1)S(1)}, u32[]{:S(2)}, u32[]{:S(2)}) collective-permute-start(bf16[2,192,256]{2,1,0:T(8,128)(2,1)S(1)} %maximum_select_fusion.15), channel_id=1, source_target_pairs={{0,8},{2,10},{4,12},{6,14},{8,0},{10,2},{12,4},{14,6},{16,24},{18,... | collective-permute-start | bytes 589832 | tf_op jit(solution)/shard_map/ppermute | solution.py:365
  33.2 11.7 %copy-start.22 = (bf16[192,384]{1,0:T(8,128)(2,1)}, bf16[192,384]{1,0:T(8,128)(2,1)S(1)}, u32[]{:S(2)}) copy-start(bf16[192,384]{1,0:T(8,128)(2,1)S(1)} %collective-permute-done.6) | copy-start | bytes 442372
  33.3 11.6 %collective-permute-start.7 = (bf16[2,192,384]{2,1,0:T(8,128)(2,1)S(1)}, bf16[2,192,384]{2,1,0:T(8,128)(2,1)S(1)}, u32[]{:S(2)}, u32[]{:S(2)}) collective-permute-start(bf16[2,192,384]{2,1,0:T(8,128)(2,1)S(1)} %maximum_select_fusion.13), channel_id=1, source_target_pairs={{0,8},{2,10},{4,12},{6,14},{8,0},{10,2},{12,4},{14,6},{16,24},{18,... | collective-permute-start | bytes 884744 | tf_op jit(solution)/shard_map/ppermute | solution.py:365
  40.0 66.5 %collective-permute-start.4 = (bf16[2,2,192,256]{3,2,0,1:T(8,128)(2,1)}, bf16[2,2,192,256]{3,2,0,1:T(8,128)(2,1)}, u32[]{:S(2)}, u32[]{:S(2)}) collective-permute-start(bf16[2,2,192,256]{3,2,0,1:T(8,128)(2,1)} %maximum_select_fusion.11), channel_id=1, source_target_pairs={{0,4},{2,6},{4,0},{6,2},{8,12},{10,14},{12,8},{14,10},{16,20},{18,... | collective-permute-start | bytes 1179656 | tf_op jit(solution)/shard_map/ppermute | solution.py:365
  45.8 58.9 %collective-permute-start.8 = (bf16[2,2,192,384]{3,2,0,1:T(8,128)(2,1)}, bf16[2,2,192,384]{3,2,0,1:T(8,128)(2,1)S(1)}, u32[]{:S(2)}, u32[]{:S(2)}) collective-permute-start(bf16[2,2,192,384]{3,2,0,1:T(8,128)(2,1)} %maximum_select_fusion.9), channel_id=1, source_target_pairs={{0,2},{2,0},{4,6},{6,4},{8,10},{10,8},{12,14},{14,12},{16,18},{18,... | collective-permute-start | bytes 1769480 | tf_op jit(solution)/shard_map/ppermute | solution.py:365
  97.5 7.1 %copy-start.21 = (bf16[1,1,192,384]{3,2,0,1:T(8,128)(2,1)S(1)}, bf16[1,1,192,384]{3,2,0,1:T(8,128)(2,1)}, u32[]{:S(2)}) copy-start(bf16[1,1,192,384]{3,2,0,1:T(8,128)(2,1)} %copy-done.20) | copy-start | bytes 442372
  97.5 7.1 %copy-start.23 = (bf16[192,384]{1,0:T(8,128)(2,1)S(1)}, bf16[192,384]{1,0:T(8,128)(2,1)}, u32[]{:S(2)}) copy-start(bf16[192,384]{1,0:T(8,128)(2,1)} %copy-done.22) | copy-start | bytes 442372
  104.3 46.5 %collective-permute-start = (bf16[1024,1024]{1,0:T(8,128)(2,1)}, bf16[1024,1024]{1,0:T(8,128)(2,1)}, u32[]{:S(2)}, u32[]{:S(2)}) collective-permute-start(bf16[1024,1024]{1,0:T(8,128)(2,1)} %get-tuple-element.61), channel_id=1, source_target_pairs={{0,1},{1,0},{2,3},{3,2},{4,5},{5,4},{6,7},{7,6},{8,9},{9,8},{10,11... | collective-permute-start | bytes 6291464 | tf_op jit(solution)/shard_map/ppermute | solution.py:349
  105.0 37.0 %collective-permute-start.9 = (bf16[2,2,2,192,384]{4,3,0,1,2:T(8,128)(2,1)S(1)}, bf16[2,2,2,192,384]{4,3,0,1,2:T(8,128)(2,1)S(1)}, u32[]{:S(2)}, u32[]{:S(2)}) collective-permute-start(bf16[2,2,2,192,384]{4,3,0,1,2:T(8,128)(2,1)S(1)} %maximum_select_fusion.5), channel_id=1, source_target_pairs={{0,4},{2,6},{4,0},{6,2},{8,12},{10,14},{12,8},{14,10},{16,20},{18,... | collective-permute-start | bytes 3538952 | tf_op jit(solution)/shard_map/ppermute | solution.py:365
  107.8 19.5 %collective-permute-start.5 = (bf16[2,2,2,192,256]{4,3,0,1,2:T(8,128)(2,1)S(1)}, bf16[2,2,2,192,256]{4,3,0,1,2:T(8,128)(2,1)S(1)}, u32[]{:S(2)}, u32[]{:S(2)}) collective-permute-start(bf16[2,2,2,192,256]{4,3,0,1,2:T(8,128)(2,1)S(1)} %maximum_select_fusion.7), channel_id=1, source_target_pairs={{0,2},{2,0},{4,6},{6,4},{8,10},{10,8},{12,14},{14,12},{16,18},{18,... | collective-permute-start | bytes 2359304 | tf_op jit(solution)/shard_map/ppermute | solution.py:365
  189.7 7.2 %collective-permute-start.1 = (bf16[1024,640]{1,0:T(8,128)(2,1)}, bf16[1024,640]{1,0:T(8,128)(2,1)S(1)}, u32[]{:S(2)}, u32[]{:S(2)}) collective-permute-start(bf16[1024,640]{1,0:T(8,128)(2,1)} %get-tuple-element.63.o_theirs), channel_id=1, source_target_pairs={{0,1},{1,0},{2,3},{3,2},{4,5},{5,4},{6,7},{7,6},{8,9},{9,8},{10,11... | collective-permute-start | bytes 3932168 | tf_op jit(solution)/shard_map/ppermute | solution.py:349
  193.6 18.9 %collective-permute-start.10 = (bf16[3072,640]{1,0:T(8,128)(2,1)}, bf16[3072,640]{1,0:T(8,128)(2,1)}, u32[]{:S(2)}, u32[]{:S(2)}) collective-permute-start(bf16[3072,640]{1,0:T(8,128)(2,1)} %pad_maximum_fusion.wd_mine), channel_id=1, source_target_pairs={{0,1},{1,0},{2,3},{3,2},{4,5},{5,4},{6,7},{7,6},{8,9},{9,8},{10,11... | collective-permute-start | bytes 11796488 | tf_op jit(solution)/shard_map/ppermute | solution.py:349
  306.0 14.2 %collective-permute-start.12 = (bf16[1152,1536]{1,0:T(8,128)(2,1)}, bf16[1152,1536]{1,0:T(8,128)(2,1)}, u32[]{:S(2)}, u32[]{:S(2)}) collective-permute-start(bf16[1152,1536]{1,0:T(8,128)(2,1)} %get-tuple-element.69), channel_id=1, source_target_pairs={{0,1},{1,0},{2,3},{3,2},{4,5},{5,4},{6,7},{7,6},{8,9},{9,8},{10,11... | collective-permute-start | bytes 10616840 | tf_op jit(solution)/shard_map/ppermute | solution.py:349
  306.1 18.2 %collective-permute-start.11 = (bf16[1152,1536]{1,0:T(8,128)(2,1)}, bf16[1152,1536]{1,0:T(8,128)(2,1)}, u32[]{:S(2)}, u32[]{:S(2)}) collective-permute-start(bf16[1152,1536]{1,0:T(8,128)(2,1)} %get-tuple-element.67), channel_id=1, source_target_pairs={{0,1},{1,0},{2,3},{3,2},{4,5},{5,4},{6,7},{7,6},{8,9},{9,8},{10,11... | collective-permute-start | bytes 10616840 | tf_op jit(solution)/shard_map/ppermute | solution.py:349
  306.6 36.2 %collective-permute-start.14 = (bf16[3072,640]{1,0:T(8,128)(2,1)}, bf16[3072,640]{1,0:T(8,128)(2,1)S(1)}, u32[]{:S(2)}, u32[]{:S(2)}) collective-permute-start(bf16[3072,640]{1,0:T(8,128)(2,1)} %get-tuple-element.72), channel_id=1, source_target_pairs={{0,1},{1,0},{2,3},{3,2},{4,5},{5,4},{6,7},{7,6},{8,9},{9,8},{10,11... | collective-permute-start | bytes 11796488 | tf_op jit(solution)/shard_map/ppermute | solution.py:349
  310.2 6.2 %slice-start = ((s8[4718592]{0:T(1024)(128)(4,1)}), s8[524288]{0:T(1024)(128)(4,1)S(1)}, s32[]{:S(2)}) async-start(s8[4718592]{0:T(1024)(128)(4,1)} %bitcast.332), calls=%async_computation.2 | async-start | bytes 1048576
  320.2 9.8 %copy-start.1 = (f32[1024,1152]{1,0:T(8,128)}, f32[1024,1152]{1,0:T(8,128)S(1)}, u32[]{:S(2)}) copy-start(f32[1024,1152]{1,0:T(8,128)S(1)} %subtract_add_fusion) | copy-start | bytes 14155780
  331.3 6.4 %copy-start.8 = (bf16[1024,1152]{1,0:T(8,128)(2,1)}, bf16[1024,1152]{1,0:T(8,128)(2,1)S(1)}, u32[]{:S(2)}) copy-start(bf16[1024,1152]{1,0:T(8,128)(2,1)S(1)} %convert_element_type.926) | copy-start | bytes 7077892
  333.6 12.7 %collective-permute-start.13 = (bf16[1024,640]{1,0:T(8,128)(2,1)S(1)}, bf16[1024,640]{1,0:T(8,128)(2,1)}, u32[]{:S(2)}, u32[]{:S(2)}) collective-permute-start(bf16[1024,640]{1,0:T(8,128)(2,1)S(1)} %convolution_convert_fusion), channel_id=1, source_target_pairs={{0,1},{1,0},{2,3},{3,2},{4,5},{5,4},{6,7},{7,6},{8,9},{9,8},{10,11... | collective-permute-start | bytes 3932168 | tf_op jit(solution)/shard_map/ppermute | solution.py:349
  334.1 40.9 %collective-permute-start.15 = (bf16[2,2,2,72,1536]{4,3,0,2,1:T(8,128)(2,1)}, bf16[2,2,2,72,1536]{4,3,0,2,1:T(8,128)(2,1)}, u32[]{:S(2)}, u32[]{:S(2)}) collective-permute-start(bf16[2,2,2,72,1536]{4,3,0,2,1:T(8,128)(2,1)} %fusion.17), channel_id=1, source_target_pairs={{0,2},{2,0},{4,6},{6,4},{8,10},{10,8},{12,14},{14,12},{16,18},{18,... | collective-permute-start | bytes 5308424 | tf_op jit(solution)/shard_map/ppermute | solution.py:365
  335.4 41.8 %collective-permute-start.16 = (bf16[2,2,2,72,1536]{4,3,0,2,1:T(8,128)(2,1)}, bf16[2,2,2,72,1536]{4,3,0,2,1:T(8,128)(2,1)}, u32[]{:S(2)}, u32[]{:S(2)}) collective-permute-start(bf16[2,2,2,72,1536]{4,3,0,2,1:T(8,128)(2,1)} %fusion.18), channel_id=1, source_target_pairs={{0,4},{2,6},{4,0},{6,2},{8,12},{10,14},{12,8},{14,10},{16,20},{18,... | collective-permute-start | bytes 5308424 | tf_op jit(solution)/shard_map/ppermute | solution.py:365
  346.3 83.5 %collective-permute-start.20 = (bf16[2,2,2,192,640]{4,3,0,2,1:T(8,128)(2,1)}, bf16[2,2,2,192,640]{4,3,0,2,1:T(8,128)(2,1)}, u32[]{:S(2)}, u32[]{:S(2)}) collective-permute-start(bf16[2,2,2,192,640]{4,3,0,2,1:T(8,128)(2,1)} %fusion.14), channel_id=1, source_target_pairs={{0,4},{2,6},{4,0},{6,2},{8,12},{10,14},{12,8},{14,10},{16,20},{18,... | collective-permute-start | bytes 5898248 | tf_op jit(solution)/shard_map/ppermute | solution.py:365
  374.6 4.5 copy-start.9
  374.6 4.5 copy-start.41
  383.9 11.7 %collective-permute-start.17 = (bf16[1152,640]{1,0:T(8,128)(2,1)S(1)}, bf16[1152,640]{1,0:T(8,128)(2,1)S(1)}, u32[]{:S(2)}, u32[]{:S(2)}) collective-permute-start(bf16[1152,640]{1,0:T(8,128)(2,1)S(1)} %maximum_select_fusion.3), channel_id=1, source_target_pairs={{0,1},{1,0},{2,3},{3,2},{4,5},{5,4},{6,7},{7,6},{8,9},{9,8},{10,11... | collective-permute-start | bytes 4423688 | tf_op jit(solution)/shard_map/ppermute | solution.py:349
  398.7 39.1 %collective-permute-start.18 = (bf16[2,2,72,1536]{3,2,1,0:T(8,128)(2,1)}, bf16[2,2,72,1536]{3,2,1,0:T(8,128)(2,1)}, u32[]{:S(2)}, u32[]{:S(2)}) collective-permute-start(bf16[2,2,72,1536]{3,2,1,0:T(8,128)(2,1)} %copy.88), channel_id=1, source_target_pairs={{0,4},{2,6},{4,0},{6,2},{8,12},{10,14},{12,8},{14,10},{16,20},{18,... | collective-permute-start | bytes 2654216 | tf_op jit(solution)/shard_map/ppermute | solution.py:365
  400.4 37.4 %copy-start.36 = (f32[1,4,2,128]{3,1,2,0:T(4,128)S(1)}, f32[1,4,2,128]{3,1,2,0:T(4,128)}, u32[]{:S(2)}) copy-start(f32[1,4,2,128]{3,1,2,0:T(4,128)} %copy-done.35) | copy-start | bytes 12292
  400.4 37.4 %collective-permute-start.19 = (bf16[2,2,72,1536]{3,2,1,0:T(8,128)(2,1)}, bf16[2,2,72,1536]{3,2,1,0:T(8,128)(2,1)}, u32[]{:S(2)}, u32[]{:S(2)}) collective-permute-start(bf16[2,2,72,1536]{3,2,1,0:T(8,128)(2,1)} %copy.89), channel_id=1, source_target_pairs={{0,2},{2,0},{4,6},{6,4},{8,10},{10,8},{12,14},{14,12},{16,18},{18,... | collective-permute-start | bytes 2654216 | tf_op jit(solution)/shard_map/ppermute | solution.py:365
  400.5 37.3 %collective-permute-start.21 = (bf16[2,2,2,72,640]{4,3,0,2,1:T(8,128)(2,1)}, bf16[2,2,2,72,640]{4,3,0,2,1:T(8,128)(2,1)}, u32[]{:S(2)}, u32[]{:S(2)}) collective-permute-start(bf16[2,2,2,72,640]{4,3,0,2,1:T(8,128)(2,1)} %fusion.34), channel_id=1, source_target_pairs={{0,2},{2,0},{4,6},{6,4},{8,10},{10,8},{12,14},{14,12},{16,18},{18,... | collective-permute-start | bytes 2211848 | tf_op jit(solution)/shard_map/ppermute | solution.py:365
  437.8 5.4 collective-permute-start.22
  441.7 27.2 %collective-permute-start.25 = (bf16[2,2,72,640]{3,2,1,0:T(8,128)(2,1)S(1)}, bf16[2,2,72,640]{3,2,1,0:T(8,128)(2,1)S(1)}, u32[]{:S(2)}, u32[]{:S(2)}) collective-permute-start(bf16[2,2,72,640]{3,2,1,0:T(8,128)(2,1)S(1)} %copy.101), channel_id=1, source_target_pairs={{0,4},{2,6},{4,0},{6,2},{8,12},{10,14},{12,8},{14,10},{16,20},{18,... | collective-permute-start | bytes 1105928 | tf_op jit(solution)/shard_map/ppermute | solution.py:365
  443.1 4.7 copy-start.4
  443.2 4.7 copy-start.34
  443.2 4.7 copy-start.40
  443.2 4.7 copy-start.44
  456.1 12.1 %collective-permute-start.23 = (bf16[1152,1024]{1,0:T(8,128)(2,1)S(1)}, bf16[1152,1024]{1,0:T(8,128)(2,1)S(1)}, u32[]{:S(2)}, u32[]{:S(2)}) collective-permute-start(bf16[1152,1024]{1,0:T(8,128)(2,1)S(1)} %add_convert_fusion), channel_id=1, source_target_pairs={{0,1},{1,0},{2,3},{3,2},{4,5},{5,4},{6,7},{7,6},{8,9},{9,8},{10,11... | collective-permute-start | bytes 7077896 | tf_op jit(solution)/shard_map/ppermute | solution.py:349
  458.4 4.3 copy-start.13
  458.5 24.0 %collective-permute-start.24 = (bf16[2,2,192,640]{3,2,1,0:T(8,128)(2,1)S(1)}, bf16[2,2,192,640]{3,2,1,0:T(8,128)(2,1)S(1)}, u32[]{:S(2)}, u32[]{:S(2)}) collective-permute-start(bf16[2,2,192,640]{3,2,1,0:T(8,128)(2,1)S(1)} %copy.98), channel_id=1, source_target_pairs={{0,2},{2,0},{4,6},{6,4},{8,10},{10,8},{12,14},{14,12},{16,18},{18,... | collective-permute-start | bytes 2949128 | tf_op jit(solution)/shard_map/ppermute | solution.py:365
  461.2 44.0 %collective-permute-start.29 = (bf16[2,72,1536]{2,1,0:T(8,128)(2,1)S(1)}, bf16[2,72,1536]{2,1,0:T(8,128)(2,1)S(1)}, u32[]{:S(2)}, u32[]{:S(2)}) collective-permute-start(bf16[2,72,1536]{2,1,0:T(8,128)(2,1)S(1)} %get-tuple-element.166), channel_id=1, source_target_pairs={{0,8},{2,10},{4,12},{6,14},{8,0},{10,2},{12,4},{14,6},{16,24},{18,... | collective-permute-start | bytes 1327112 | tf_op jit(solution)/shard_map/ppermute | solution.py:365
  464.1 41.0 %collective-permute-start.28 = (bf16[2,72,1536]{2,1,0:T(8,128)(2,1)S(1)}, bf16[2,72,1536]{2,1,0:T(8,128)(2,1)S(1)}, u32[]{:S(2)}, u32[]{:S(2)}) collective-permute-start(bf16[2,72,1536]{2,1,0:T(8,128)(2,1)S(1)} %get-tuple-element.168), channel_id=1, source_target_pairs={{0,8},{2,10},{4,12},{6,14},{8,0},{10,2},{12,4},{14,6},{16,24},{18,... | collective-permute-start | bytes 1327112 | tf_op jit(solution)/shard_map/ppermute | solution.py:365
  468.2 15.9 %slice-start.2 = ((s8[4718592]{0:T(1024)(128)(4,1)}), s8[4194304]{0:T(1024)(128)(4,1)S(1)}, s32[]{:S(2)}) async-start(s8[4718592]{0:T(1024)(128)(4,1)} %bitcast.334), calls=%async_computation.4 | async-start | bytes 8388608
  468.4 15.7 %slice-start.3 = ((s8[4718592]{0:T(1024)(128)(4,1)}), s8[524288]{0:T(1024)(128)(4,1)S(1)}, s32[]{:S(2)}) async-start(s8[4718592]{0:T(1024)(128)(4,1)} %bitcast.334), calls=%async_computation.5 | async-start | bytes 1048576
  482.7 6.1 %collective-permute-start.36 = (bf16[2,72,640]{2,1,0:T(8,128)(2,1)S(1)}, bf16[2,72,640]{2,1,0:T(8,128)(2,1)S(1)}, u32[]{:S(2)}, u32[]{:S(2)}) collective-permute-start(bf16[2,72,640]{2,1,0:T(8,128)(2,1)S(1)} %get-tuple-element.194), channel_id=1, source_target_pairs={{0,8},{2,10},{4,12},{6,14},{8,0},{10,2},{12,4},{14,6},{16,24},{18,... | collective-permute-start | bytes 552968 | tf_op jit(solution)/shard_map/ppermute | solution.py:365
  486.9 14.7 %collective-permute-start.40 = (bf16[2,192,640]{2,1,0:T(8,128)(2,1)S(1)}, bf16[2,192,640]{2,1,0:T(8,128)(2,1)S(1)}, u32[]{:S(2)}, u32[]{:S(2)}) collective-permute-start(bf16[2,192,640]{2,1,0:T(8,128)(2,1)S(1)} %get-tuple-element.164), channel_id=1, source_target_pairs={{0,8},{2,10},{4,12},{6,14},{8,0},{10,2},{12,4},{14,6},{16,24},{18,... | collective-permute-start | bytes 1474568 | tf_op jit(solution)/shard_map/ppermute | solution.py:365
  487.6 17.6 %collective-permute-start.26 = (bf16[2,2,2,72,512]{4,3,0,2,1:T(8,128)(2,1)S(1)}, bf16[2,2,2,72,512]{4,3,0,2,1:T(8,128)(2,1)S(1)}, u32[]{:S(2)}, u32[]{:S(2)}) collective-permute-start(bf16[2,2,2,72,512]{4,3,0,2,1:T(8,128)(2,1)S(1)} %fusion.37), channel_id=1, source_target_pairs={{0,2},{2,0},{4,6},{6,4},{8,10},{10,8},{12,14},{14,12},{16,18},{18,... | collective-permute-start | bytes 1769480 | tf_op jit(solution)/shard_map/ppermute | solution.py:365
  488.8 11.4 %collective-permute-start.37 = (bf16[72,640]{1,0:T(8,128)(2,1)S(1)}, bf16[72,640]{1,0:T(8,128)(2,1)S(1)}, u32[]{:S(2)}, u32[]{:S(2)}) collective-permute-start(bf16[72,640]{1,0:T(8,128)(2,1)S(1)} %get-tuple-element.199), channel_id=1, source_target_pairs={{0,16},{2,18},{4,20},{6,22},{8,24},{10,26},{12,28},{14,30},{16,0},... | collective-permute-start | bytes 276488 | tf_op jit(solution)/shard_map/ppermute | solution.py:365
  500.2 14.4 %collective-permute-start.27 = (bf16[2,2,2,72,512]{4,3,0,2,1:T(8,128)(2,1)S(1)}, bf16[2,2,2,72,512]{4,3,0,2,1:T(8,128)(2,1)S(1)}, u32[]{:S(2)}, u32[]{:S(2)}) collective-permute-start(bf16[2,2,2,72,512]{4,3,0,2,1:T(8,128)(2,1)S(1)} %fusion.38), channel_id=1, source_target_pairs={{0,4},{2,6},{4,0},{6,2},{8,12},{10,14},{12,8},{14,10},{16,20},{18,... | collective-permute-start | bytes 1769480 | tf_op jit(solution)/shard_map/ppermute | solution.py:365
  501.7 18.2 %collective-permute-start.41 = (bf16[192,640]{1,0:T(8,128)(2,1)S(1)}, bf16[192,640]{1,0:T(8,128)(2,1)S(1)}, u32[]{:S(2)}, u32[]{:S(2)}) collective-permute-start(bf16[192,640]{1,0:T(8,128)(2,1)S(1)} %get-tuple-element.191), channel_id=1, source_target_pairs={{0,16},{2,18},{4,20},{6,22},{8,24},{10,26},{12,28},{14,30},{16,0},... | collective-permute-start | bytes 737288 | tf_op jit(solution)/shard_map/ppermute | solution.py:365
  514.6 18.0 %collective-permute-start.39 = (bf16[72,1536]{1,0:T(8,128)(2,1)S(1)}, bf16[72,1536]{1,0:T(8,128)(2,1)S(1)}, u32[]{:S(2)}, u32[]{:S(2)}) collective-permute-start(bf16[72,1536]{1,0:T(8,128)(2,1)S(1)} %fusion.72), channel_id=1, source_target_pairs={{0,16},{2,18},{4,20},{6,22},{8,24},{10,26},{12,28},{14,30},{16,0},... | collective-permute-start | bytes 663560 | tf_op jit(solution)/shard_map/ppermute | solution.py:365
  518.1 18.1 %collective-permute-start.38 = (bf16[72,1536]{1,0:T(8,128)(2,1)S(1)}, bf16[72,1536]{1,0:T(8,128)(2,1)S(1)}, u32[]{:S(2)}, u32[]{:S(2)}) collective-permute-start(bf16[72,1536]{1,0:T(8,128)(2,1)S(1)} %fusion.70), channel_id=1, source_target_pairs={{0,16},{2,18},{4,20},{6,22},{8,24},{10,26},{12,28},{14,30},{16,0},... | collective-permute-start | bytes 663560 | tf_op jit(solution)/shard_map/ppermute | solution.py:365
  518.4 15.1 %collective-permute-start.30 = (bf16[2,2,72,512]{3,2,1,0:T(8,128)(2,1)S(1)}, bf16[2,2,72,512]{3,2,1,0:T(8,128)(2,1)S(1)}, u32[]{:S(2)}, u32[]{:S(2)}) collective-permute-start(bf16[2,2,72,512]{3,2,1,0:T(8,128)(2,1)S(1)} %copy.105), channel_id=1, source_target_pairs={{0,4},{2,6},{4,0},{6,2},{8,12},{10,14},{12,8},{14,10},{16,20},{18,... | collective-permute-start | bytes 884744 | tf_op jit(solution)/shard_map/ppermute | solution.py:365
  518.9 14.7 %collective-permute-start.33 = (bf16[2,2,72,512]{3,2,1,0:T(8,128)(2,1)S(1)}, bf16[2,2,72,512]{3,2,1,0:T(8,128)(2,1)S(1)}, u32[]{:S(2)}, u32[]{:S(2)}) collective-permute-start(bf16[2,2,72,512]{3,2,1,0:T(8,128)(2,1)S(1)} %copy.110), channel_id=1, source_target_pairs={{0,2},{2,0},{4,6},{6,4},{8,10},{10,8},{12,14},{14,12},{16,18},{18,... | collective-permute-start | bytes 884744 | tf_op jit(solution)/shard_map/ppermute | solution.py:365
  533.6 9.0 %collective-permute-start.31 = (bf16[2,72,512]{2,1,0:T(8,128)(2,1)S(1)}, bf16[2,72,512]{2,1,0:T(8,128)(2,1)S(1)}, u32[]{:S(2)}, u32[]{:S(2)}) collective-permute-start(bf16[2,72,512]{2,1,0:T(8,128)(2,1)S(1)} %get-tuple-element.196), channel_id=1, source_target_pairs={{0,8},{2,10},{4,12},{6,14},{8,0},{10,2},{12,4},{14,6},{16,24},{18,... | collective-permute-start | bytes 442376 | tf_op jit(solution)/shard_map/ppermute | solution.py:365
  533.8 8.7 %collective-permute-start.34 = (bf16[2,72,512]{2,1,0:T(8,128)(2,1)S(1)}, bf16[2,72,512]{2,1,0:T(8,128)(2,1)S(1)}, u32[]{:S(2)}, u32[]{:S(2)}) collective-permute-start(bf16[2,72,512]{2,1,0:T(8,128)(2,1)S(1)} %get-tuple-element.198), channel_id=1, source_target_pairs={{0,8},{2,10},{4,12},{6,14},{8,0},{10,2},{12,4},{14,6},{16,24},{18,... | collective-permute-start | bytes 442376 | tf_op jit(solution)/shard_map/ppermute | solution.py:365
  542.5 6.1 %collective-permute-start.35 = (bf16[72,512]{1,0:T(8,128)(2,1)S(1)}, bf16[72,512]{1,0:T(8,128)(2,1)S(1)}, u32[]{:S(2)}, u32[]{:S(2)}) collective-permute-start(bf16[72,512]{1,0:T(8,128)(2,1)S(1)} %fusion.87), channel_id=1, source_target_pairs={{0,16},{2,18},{4,20},{6,22},{8,24},{10,26},{12,28},{14,30},{16,0},... | collective-permute-start | bytes 221192 | tf_op jit(solution)/shard_map/ppermute | solution.py:365
  542.6 8.0 %collective-permute-start.32 = (bf16[72,512]{1,0:T(8,128)(2,1)S(1)}, bf16[72,512]{1,0:T(8,128)(2,1)S(1)}, u32[]{:S(2)}, u32[]{:S(2)}) collective-permute-start(bf16[72,512]{1,0:T(8,128)(2,1)S(1)} %fusion.85), channel_id=1, source_target_pairs={{0,16},{2,18},{4,20},{6,22},{8,24},{10,26},{12,28},{14,30},{16,0},... | collective-permute-start | bytes 221192 | tf_op jit(solution)/shard_map/ppermute | solution.py:365
  (30 other events, 69.1 us)
Sparse Core Ops, SparseCore 0:
  11.5 82.2 all-gather.2
  97.2 106.9 all-gather.4

commit v7 on v6

--- a/solution.py
+++ b/solution.py
@@ -147,30 +147,39 @@
             part = jnp.sum(dj.astype(f32) * osrc[:, head_cols(j)].astype(f32), axis=1, keepdims=True)
             inner[rows, :] = jnp.where(lane_of(j, (dj.shape[0], 128)), part, inner[rows, :])
 
-    def group(g, _):
-        dka[...] = jnp.zeros_like(dka)
-        dva[...] = jnp.zeros_like(dva)
-        for jj in range(HQ // HK):
-            j = g * (HQ // HK) + jj
-            for i in range(lse.shape[0] // BLOCK):
-                r = pl.ds(i * BLOCK, BLOCK)
-                kw = (i + 1) * BLOCK
-                mark = lane_of(j, (BLOCK, 128))
-                column = lambda a: jnp.sum(jnp.where(mark, a[r, :], 0.0), axis=1, keepdims=True)
-                qs = q[j, r, :]
-                dO = do[j, r, :]
-                kk = k[g, :kw, :]
-                p = jnp.exp(dg(qs, kk, NT) - column(lse))
-                dp = dg(dO, v[g, :kw, :], NT)
-                ds = (p * (dp - column(inner))).astype(bf16)
-                d[j, r, :] = dg(ds, kk, NN) * 0.125
-                dka[:, :kw] += dg(qs.T, ds, NN)
-                dva[:, :kw] += dg(dO.T, p.astype(bf16), NN)
-        d[HQ + g] = dka[...].T
-        d[HQ + HK + g] = dva[...].T
+    per = HQ // HK
+
+    def head(j, _):
+        g = j // per
+
+        @pl.when(j % per == 0)
+        def _():
+            dka[...] = jnp.zeros_like(dka)
+            dva[...] = jnp.zeros_like(dva)
+
+        for i in range(lse.shape[0] // BLOCK):
+            r = pl.ds(i * BLOCK, BLOCK)
+            kw = (i + 1) * BLOCK
+            mark = lane_of(j, (BLOCK, 128))
+            column = lambda a: jnp.sum(jnp.where(mark, a[r, :], 0.0), axis=1, keepdims=True)
+            qs = q[j, r, :]
+            dO = do[j, r, :]
+            kk = k[g, :kw, :]
+            p = jnp.exp(dg(qs, kk, NT) - column(lse))
+            dp = dg(dO, v[g, :kw, :], NT)
+            ds = (p * (dp - column(inner))).astype(bf16)
+            d[j, r, :] = dg(ds, kk, NN) * 0.125
+            dka[:, :kw] += dg(qs.T, ds, NN)
+            dva[:, :kw] += dg(dO.T, p.astype(bf16), NN)
+
+        @pl.when(j % per == per - 1)
+        def _():
+            d[HQ + g] = dka[...].T
+            d[HQ + HK + g] = dva[...].T
+
         return 0
 
-    lax.fori_loop(0, HK, group, 0)
+    lax.fori_loop(0, HQ, head, 0)
     turns = HQ + HK
     for dst, rows in zip((lin_mine, lin_theirs), at):
         for j in range(0, HALL + 1, 2):
@@ -237,7 +246,7 @@
     )(me, mine, got, o_mine, o_theirs, do_mine, do_got, lse, cosine, sine, *before)
 
 
-def mlp_body(me, n2, n2t, cot, res, wg, wu, wd_mine, wd_theirs, out, gn, gg_mine, gu_mine, gg_theirs, gu_theirs, gd_mine, gd_theirs, y, wd):
+def mlp_body(me, n2, n2t, cot, res, wg, wu, wd_mine, wd_theirs, out, gn, gg_mine, gu_mine, gg_theirs, gu_theirs, gd_mine, gd_theirs, y):
     t = pl.program_id(0)
     per = pl.num_programs(0) // 2
 
@@ -249,26 +258,18 @@
     half = D // 2
     first = me[0] == 0
 
-    @pl.when(first)
-    def _():
-        wd[:, :half] = wd_mine[:, :half]
-        wd[:, half:] = wd_theirs[:, :half]
-
-    @pl.when(jnp.logical_not(first))
-    def _():
-        wd[:, :half] = wd_theirs[:, :half]
-        wd[:, half:] = wd_mine[:, :half]
-
+    da, db = wd_mine[:, :half], wd_theirs[:, :half]
+    wd = jnp.concatenate([jnp.where(first, da, db), jnp.where(first, db, da)], axis=1)
     wgt, wut = assemble(wg), assemble(wu)
     gate = dg(n2[...], wgt, NN)
     up = dg(n2[...], wut, NN)
-    gh = dg(cot[...], wd[...], NT)
+    gh = dg(cot[...], wd, NT)
     sig = jax.nn.sigmoid(gate)
     act = gate * sig
     hidden = (act * up).astype(bf16)
     ggv = (gh * up * sig * (1.0 + gate * (1.0 - sig))).astype(bf16)
     guv = (gh * act).astype(bf16)
-    y[...] += dg(hidden, wd[...], NN)
+    y[...] += dg(hidden, wd, NN)
     gdt = dg(hidden, cot[...], TN)
     for dst, u in (
         (gd_mine, jnp.where(first, gdt[:, :half], gdt[:, half:])),
@@ -322,7 +323,7 @@
                 part,
                 part,
             ],
-            scratch_shapes=[pltpu.VMEM((tokens, D), f32), pltpu.VMEM((FT, D), bf16)],
+            scratch_shapes=[pltpu.VMEM((tokens, D), f32)],
         ),
         out_shape=[
             jax.ShapeDtypeStruct((tokens, D), bf16),
@@ -368,20 +369,28 @@
 ORDERS = (0, 1), (1, 0)
 
 
+def doubled(a, got, bit, axis):
+    low = (lax.axis_index("dp") >> bit) & 1 == 0
+    return jnp.where(low, jnp.stack([a, got], axis), jnp.stack([got, a], axis))
+
+
 def gather_doubling(w):
     bits = lax.axis_size("dp").bit_length() - 1
-    dp = lax.axis_index("dp")
     cut = w.shape[1] // 256 * 128
     out = []
     for part, order in ((w[:, :cut], ORDERS[0]), (w[:, cut:], ORDERS[1])):
-        a, have = part, []
+        last, have = None, []
         for bit in list(range(bits))[:1:-1] + list(order[::-1]):
-            got = exchange(a, bit)
-            axis = sum(b > bit for b in have)
+            a = part if last is None else doubled(*last)
+            last = a, exchange(a, bit), bit, sum(b > bit for b in have)
             have.append(bit)
-            a = jnp.where((dp >> bit) & 1 == 0, jnp.stack([a, got], axis), jnp.stack([got, a], axis))
-        out.append(a.reshape(-1, a.shape[-1]))
-    mine = jnp.concatenate(out, 1)
+        out.append(last)
+    return out
+
+
+def gather_finish(lasts):
+    out = [doubled(*last) for last in lasts]
+    mine = jnp.concatenate([a.reshape(-1, a.shape[-1]) for a in out], 1)
     return mine, swap(mine)
 
 
@@ -441,6 +450,7 @@
     me = lax.axis_index("seq")
     me_arr = jnp.full((1,), me, jnp.int32)
     pick = lambda a, b: jnp.where(me == 0, a, b)
+    tie = lax.optimization_barrier
     h = HEAD_SIZE // 2
     frequency = 10000.0 ** (-2.0 * jnp.arange(h).astype(f32) / HEAD_SIZE)
     angles = jnp.arange(2 * piece).astype(f32)[:, None] * jnp.tile(frequency, 128 // h)[None, :]
@@ -451,7 +461,8 @@
     full = fetch(jnp.concatenate([w_query, w_key, w_value, gains, w_out], 1))
     wide = fetch(jnp.concatenate([w_gate, w_up], 1))
     widen = lambda a: jnp.pad(a, ((0, 0), (0, HALF - D // 2)))
-    down_mine, down_theirs = gather_doubling(widen(w_down))
+    down_last = gather_doubling(widen(w_down))
+    full, _ = tie((full, [last[0] for last in down_last]))
     gain_one = full[:, 0, :, QKV].reshape(D).astype(f32)
     gain_two = full[:, 0, :, QKV + 1].reshape(D).astype(f32)
     out_halves = whole_halves(full[..., WIDE:])[0].reshape(2, 2, D // 2, D // 2)
@@ -470,6 +481,10 @@
     got = swap(heads_out)
     mine, w_mine = project(0, me_arr, n1, full, cosine, sine, piece)
     mixed, mixed_out, lse = attend(me_arr, mine, got, piece)
+    mixed_out, arrived = tie((mixed_out, [last[1] for last in down_last]))
+    down_mine, down_theirs = gather_finish(
+        [(a, b, bit, axis) for (a, _, bit, axis), b in zip(down_last, arrived)]
+    )
     mixed_got = swap(mixed_out)
     residual = floats + (dot(mixed, out_mine) + dot(mixed_got, out_theirs))
     scale_mlp = lax.rsqrt(jnp.mean(residual * residual, -1, keepdims=True) + epsilon)
@@ -477,7 +492,6 @@
     layer_out, grad_n2, gg_mine, gu_mine, gg_theirs, gu_theirs, gd_mine, gd_theirs = mlp(
         me_arr, n2, n2.T, cot, residual, wide, down_mine, down_theirs
     )
-    tie = lax.optimization_barrier
     wide_sum = Halving([(gg_mine, swap(gg_theirs), ORDERS[0]), (gu_mine, swap(gu_theirs), ORDERS[1])])
     wide_sum.prepare(0)
     sum_gain_mlp = jnp.sum(grad_n2 * residual * scale_mlp, 0)
@@ -543,12 +557,13 @@
         ]
     )
     pack_sum.prepare(0)
-    pack_sum.send, down_sum.got, out_sum.got = tie((pack_sum.send, down_sum.got, out_sum.got))
+    _, down_sum.got, out_sum.got, wide_sum.got = tie(
+        (pack_sum.send, down_sum.got, out_sum.got, wide_sum.got)
+    )
     pack_sum.move(0)
     down_sum.advance(2)
     out_sum.advance(2)
     grad_input = (grad_residual + norm_back(grad_n1, floats, scale_attn, gain_one)).astype(bf16)
-    pack_sum.got, wide_sum.got = tie((pack_sum.got, wide_sum.got))
     pack_sum.advance(1)
     r_gate, r_up = wide_sum.finish(3)
     r_down = down_sum.finish(3)[0][:, : D // 2]

time: 566 us -> 546 us (0.965)
  waiting for transfers between devices: 160 us -> 139 us
    ppermute x32, waiting for transfers between devices: 114 us -> 87.3 us  [exchange(): lax.ppermute(a, 'dp', [(i, i ^ 1 << bit) for i in range(lax.axis_size('dp...]
    unnamed x100 -> x110, local copies, waits for them, and re-layouts: 11.3 us -> 14.2 us
  transfers between devices with their start and end apart: 44 -> 44, of which waited for: 18 -> 16; matrix products, arithmetic and copies ran while one was open for 22% -> 23% of each run, Pallas kernels for 19% -> 20%
where the time goes in v7:
time: 546 us; the launch traced here: 537 us
  Pallas kernels  201 us (37%)
  waiting for transfers between devices  139 us (25%)
  other arithmetic  64.2 us (12%)
  local copies, waits for them, and re-layouts  42.3 us (8%)
  starting transfers between devices  41.9 us (8%)
  matrix products  32.8 us (6%)
  between operations  15.5 us (3%)
    pallas_call x1, Pallas kernels, mlp(): pl.pallas_call(mlp_body, grid_spec=pltpu.PrefetchScalarGridSpec(num_scala...  91.8 us
    ppermute x32, waiting for transfers between devices, exchange(): lax.ppermute(a, 'dp', [(i, i ^ 1 << bit) for i in range(lax.axis_size('dp...  87.3 us
    pallas_call x2, Pallas kernels, attend_back(): pl.pallas_call(bwd_body, grid_spec=pltpu.PrefetchScalarGridSpec(num_scala...  57.1 us
    all_gather x2, waiting for transfers between devices, fetch(): lax.all_gather(w, BOTH, axis=0, tiled=True)  51.3 us
    ppermute x32, starting transfers between devices, exchange(): lax.ppermute(a, 'dp', [(i, i ^ 1 << bit) for i in range(lax.axis_size('dp...  39.8 us
    pallas_call x1, Pallas kernels, attend(): pl.pallas_call(fwd_body, grid_spec=pltpu.PrefetchScalarGridSpec(num_scala...  38.9 us
    convert_element_type x30, other arithmetic, prepare(): add(at(self.stay[p], i), at(self.got[p], i)).astype(self.kind)  25.7 us
    unnamed x110, local copies, waits for them, and re-layouts  14.2 us
  transfers between devices with their start and end apart: 44, of which 16 were waited for; matrix products, arithmetic and copies ran while one was open for 23% of the time, Pallas kernels for 20%

profile of v7, /device:TPU:0, one launch (start us, length us, event | category | flops | bytes accessed | tf_op | source)
XLA Modules:
  0.0 536.7 jit_solution(15543004193332303515)
XLA Ops:
  8.1 1.8 concatenate.186
  10.0 2.0 pad_maximum_fusion.1
  12.7 4.1 collective-permute-start.3
  17.0 3.1 fusion.43
  20.7 9.5 %collective-permute-done = bf16[192,256]{1,0:T(8,128)(2,1)S(1)} collective-permute-done((bf16[192,256]{1,0:T(8,128)(2,1)S(1)}, bf16[192,256]{1,0:T(8,128)(2,1)S(1)}, u32[]{:S(2)}, u32[]{:S(2)}) %collective-permute-start) | collective-permute-done | bytes 98336 | tf_op jit(solution)/shard_map/ppermute | solution.py:366
  30.2 2.3 collective-permute-start.1
  32.8 6.5 %collective-permute-done.1 = bf16[2,192,256]{2,1,0:T(8,128)(2,1)S(1)} collective-permute-done((bf16[2,192,256]{2,1,0:T(8,128)(2,1)S(1)}, bf16[2,192,256]{2,1,0:T(8,128)(2,1)S(1)}, u32[]{:S(2)}, u32[]{:S(2)}) %collective-permute-start.1) | collective-permute-done | bytes 196640 | tf_op jit(solution)/shard_map/ppermute | solution.py:366
  40.9 4.0 collective-permute-done.4
  47.8 4.6 collective-permute-done.2
  53.4 11.4 %collective-permute-done.5 = bf16[2,2,192,384]{3,2,0,1:T(8,128)(2,1)S(1)} collective-permute-done((bf16[2,2,192,384]{3,2,0,1:T(8,128)(2,1)S(1)}, bf16[2,2,192,384]{3,2,0,1:T(8,128)(2,1)S(1)}, u32[]{:S(2)}, u32[]{:S(2)}) %collective-permute-start.5) | collective-permute-done | bytes 589856 | tf_op jit(solution)/shard_map/ppermute | solution.py:366
  66.9 27.8 %all-gather.3.cloned.1.call-done = bf16[2304,1600]{1,0:T(8,128)(2,1)} async-done(((bf16[72,1600]{1,0:T(8,128)(2,1)}), bf16[2304,1600]{1,0:T(8,128)(2,1)}) %all-gather.3.cloned.1.call-update) | async-done | bytes 7372816 | tf_op jit(solution)/shard_map/all_gather | solution.py:361
  96.4 2.0 fusion.2.n1
  98.4 6.7 %project.3 = (bf16[1024,1024]{1,0:T(8,128)(2,1)}, bf16[1152,1024]{1,0:T(8,128)(2,1)}) custom-call(s32[1]{0:T(128)} %bitcast.me, bf16[1024,1152]{1,0:T(8,128)(2,1)} %fusion.2.n1, bf16[16,2,72,1600]{3,2,1,0:T(8,128)(2,1)} %bitcast.360, f32[1024,128]{1,0:T(8,128)} %get-tuple-element.210.cosine, f32[1024,128]{1,0:T(8,128)} %get-tuple-element.209.sine), custom_call_target="tpu_custom_call" | custom-call | flops 3000000000 | bytes 12000000 | tf_op jit(solution)/shard_map/project/pallas_call | solution.py:66
  108.1 6.8 %project.2 = (bf16[1024,1024]{1,0:T(8,128)(2,1)}, bf16[1152,1024]{1,0:T(8,128)(2,1)}) custom-call(s32[1]{0:T(128)} %bitcast.me, bf16[1024,1152]{1,0:T(8,128)(2,1)} %fusion.2.n1, bf16[16,2,72,1600]{3,2,1,0:T(8,128)(2,1)} %bitcast.361, f32[1024,128]{1,0:T(8,128)} %get-tuple-element.210.cosine, f32[1024,128]{1,0:T(8,128)} %get-tuple-element.209.sine), custom_call_target="tpu_custom_call" | custom-call | flops 3000000000 | bytes 12000000 | tf_op jit(solution)/shard_map/project/pallas_call | solution.py:66
  114.9 38.9 %attend.1 = (bf16[1024,640]{1,0:T(8,128)(2,1)}, bf16[1024,640]{1,0:T(8,128)(2,1)}, f32[2048,128]{1,0:T(8,128)}) custom-call(s32[1]{0:T(128)} %bitcast.me, bf16[1024,1024]{1,0:T(8,128)(2,1)} %get-tuple-element.61.mine, bf16[1024,1024]{1,0:T(8,128)(2,1)} %collective-permute-done.6.got), custom_call_target="tpu_custom_call" | custom-call | flops 24000000000 | bytes 20000000 | tf_op jit(solution)/shard_map/attend/pallas_call | solution.py:200
  153.8 2.0 maximum_select_fusion
  156.1 1.6 maximum_select_fusion.1
  159.5 2.2 pad_maximum_fusion.wd_mine
  162.3 2.1 slice_bitcast_fusion
  165.0 2.1 fusion.62
  168.5 2.4 multiply_reduce_fusion.2
  170.9 2.1 copy-done
  173.5 2.5 copy.75.n2t
  176.0 4.2 multiply_convert_fusion.n2
  180.2 23.5 %all-gather.5.cloned.1.call-done = bf16[2304,3072]{1,0:T(8,128)(2,1)} async-done(((bf16[72,3072]{1,0:T(8,128)(2,1)}), bf16[2304,3072]{1,0:T(8,128)(2,1)}) %all-gather.5.cloned.1.call-update) | async-done | bytes 14155792 | tf_op jit(solution)/shard_map/all_gather | solution.py:361
  203.7 91.8 %mlp.1 = (bf16[1024,1152]{1,0:T(8,128)(2,1)}, f32[1024,1152]{1,0:T(8,128)}, bf16[1152,1536]{1,0:T(8,128)(2,1)}, bf16[1152,1536]{1,0:T(8,128)(2,1)}, bf16[1152,15...) custom-call(s32[1]{0:T(128)} %bitcast.me, ...), custom_call_target="tpu_custom_call" | custom-call | flops 65000001536 | bytes 60000000 | tf_op jit(solution)/shard_map/mlp/pallas_call | solution.py:312
  296.4 2.7 constant_dynamic-slice_fusion.1
  299.9 3.9 multiply_reduce_fusion
  304.1 1.7 copy-done.10
  308.0 1.9 subtract_add_fusion
  309.9 4.0 constant_dynamic-slice_fusion.14
  314.0 2.3 constant_dynamic-slice_fusion.16
  316.3 1.7 fusion.18
  318.0 1.7 fusion.17
  321.0 2.2 convolution_convert_fusion
  325.6 1.8 add_convert_fusion.4
  327.3 3.3 convolution_convert_fusion.1.do_mine
  330.6 1.7 add_convert_fusion.5
  332.3 1.7 constant_dynamic-slice_fusion
  334.0 1.8 fusion.14
  337.2 28.6 %attend_back.2 = (bf16[1024,1024]{1,0:T(8,128)(2,1)}, bf16[1024,1024]{1,0:T(8,128)(2,1)}) custom-call(s32[1]{0:T(128)} %bitcast.me, bf16[1024,1024]{1,0:T(8,128)(2,1)} %get-tuple-element.61.mine, bf16[1024,1024]{1,0:T(8,128)(2,1)} %collective-permute-done.6.got, bf16[1024,640]{1,0:T(8,128)(2,1)} %get-tuple-element.63.o_mine, ...), custom_call_target="tpu_custom_call" | custom-call | flops 12999999488 | bytes 20000000 | tf_op jit(solution)/shard_map/attend_back/pallas_call | solution.py:226
  366.8 1.9 slice.86
  368.7 2.7 fusion.91
  377.1 2.9 fusion.19
  382.4 2.8 fusion.20
  392.0 28.5 %attend_back.3 = (bf16[1024,1024]{1,0:T(8,128)(2,1)}, bf16[1024,1024]{1,0:T(8,128)(2,1)}) custom-call(s32[1]{0:T(128)} %bitcast.me, bf16[1024,1024]{1,0:T(8,128)(2,1)} %get-tuple-element.61.mine, bf16[1024,1024]{1,0:T(8,128)(2,1)} %collective-permute-done.6.got, ...), custom_call_target="tpu_custom_call", output_to_operand_aliasing={{0}: (10, {}), {1}: (11, {})} | custom-call | flops 12999999488 | bytes 20000000 | tf_op jit(solution)/shard_map/attend_back/pallas_call | solution.py:226
  420.5 6.8 %collective-permute-done.21 = bf16[2,2,2,72,640]{4,3,0,2,1:T(8,128)(2,1)} collective-permute-done((bf16[2,2,2,72,640]{4,3,0,2,1:T(8,128)(2,1)}, bf16[2,2,2,72,640]{4,3,0,2,1:T(8,128)(2,1)}, u32[]{:S(2)}, u32[]{:S(2)}) %collective-permute-start.21) | collective-permute-done | bytes 737312 | tf_op jit(solution)/shard_map/ppermute | solution.py:366
  427.4 2.1 add_convert_fusion.2
  438.4 2.2 fusion.15
  441.4 4.7 fusion.114
  446.1 3.7 fusion.9
  449.8 5.0 add_convert_fusion
  454.8 3.0 add_convert_fusion.1
  458.3 2.5 fusion.6
  468.7 17.1 %collective-permute-done.36 = bf16[2,72,640]{2,1,0:T(8,128)(2,1)S(1)} collective-permute-done((bf16[2,72,640]{2,1,0:T(8,128)(2,1)S(1)}, bf16[2,72,640]{2,1,0:T(8,128)(2,1)S(1)}, u32[]{:S(2)}, u32[]{:S(2)}) %collective-permute-start.36) | collective-permute-done | bytes 184352 | tf_op jit(solution)/shard_map/ppermute | solution.py:366
  485.8 1.7 collective-permute-start.38
  489.7 10.3 %collective-permute-done.38 = bf16[72,1536]{1,0:T(8,128)(2,1)S(1)} collective-permute-done((bf16[72,1536]{1,0:T(8,128)(2,1)S(1)}, bf16[72,1536]{1,0:T(8,128)(2,1)S(1)}, u32[]{:S(2)}, u32[]{:S(2)}) %collective-permute-start.38) | collective-permute-done | bytes 221216 | tf_op jit(solution)/shard_map/ppermute | solution.py:366
  501.3 1.8 collective-permute-start.25
  504.2 5.1 collective-permute-done.25
  509.4 1.6 collective-permute-start.26
  511.2 1.7 collective-permute-start.30
  513.8 5.4 %collective-permute-done.30 = bf16[2,72,512]{2,1,0:T(8,128)(2,1)S(1)} collective-permute-done((bf16[2,72,512]{2,1,0:T(8,128)(2,1)S(1)}, bf16[2,72,512]{2,1,0:T(8,128)(2,1)S(1)}, u32[]{:S(2)}, u32[]{:S(2)}) %collective-permute-start.30) | collective-permute-done | bytes 147488 | tf_op jit(solution)/shard_map/ppermute | solution.py:366
  519.9 2.4 collective-permute-start.27
  522.3 5.2 collective-permute-done.31
  (277 shorter events, 71.5 us)
Async XLA Ops:
  7.2 4.8 copy-start.36
  7.2 87.5 %all-gather.3.cloned.1.call-start = ((), (), s32[]{:S(2)}) async-start(), calls=%async_computation | async-start | bytes 7907328 | tf_op jit(solution)/shard_map/all_gather | solution.py:361
  9.9 10.2 %copy-start.2 = (bf16[2,1,512,1152]{3,2,1,0:T(8,128)(2,1)S(1)}, bf16[2,1,512,1152]{3,2,1,0:T(8,128)(2,1)}, u32[]{:S(2)}) copy-start(bf16[2,1,512,1152]{3,2,1,0:T(8,128)(2,1)} %param.11) | copy-start | bytes 7077892
  9.9 193.8 %all-gather.5.cloned.1.call-start = ((), (), s32[]{:S(2)}) async-start(), calls=%async_computation.1 | async-start | bytes 14598144 | tf_op jit(solution)/shard_map/all_gather | solution.py:361
  12.7 19.8 %collective-permute-start.3 = (bf16[192,384]{1,0:T(8,128)(2,1)}, bf16[192,384]{1,0:T(8,128)(2,1)S(1)}, u32[]{:S(2)}, u32[]{:S(2)}) collective-permute-start(bf16[192,384]{1,0:T(8,128)(2,1)} %get-tuple-element.203), channel_id=1, source_target_pairs={{0,16},{2,18},{4,20},{6,22},{8,24},{10,26},{12,28},{14,30},{16,0},... | collective-permute-start | bytes 442376 | tf_op jit(solution)/shard_map/ppermute | solution.py:366
  16.8 15.9 %copy-start.24 = (bf16[1,1,192,256]{3,2,0,1:T(8,128)(2,1)}, bf16[1,1,192,256]{3,2,0,1:T(8,128)(2,1)S(1)}, u32[]{:S(2)}) copy-start(bf16[1,1,192,256]{3,2,0,1:T(8,128)(2,1)S(1)} %get-tuple-element.204) | copy-start | bytes 294916
  16.8 13.4 %collective-permute-start = (bf16[192,256]{1,0:T(8,128)(2,1)S(1)}, bf16[192,256]{1,0:T(8,128)(2,1)S(1)}, u32[]{:S(2)}, u32[]{:S(2)}) collective-permute-start(bf16[192,256]{1,0:T(8,128)(2,1)S(1)} %get-tuple-element.206), channel_id=1, source_target_pairs={{0,16},{2,18},{4,20},{6,22},{8,24},{10,26},{12,28},{14,30},{16,0},... | collective-permute-start | bytes 294920 | tf_op jit(solution)/shard_map/ppermute | solution.py:366
  20.6 75.7 %copy-start.39 = (f32[1,4,2,128]{3,1,2,0:T(4,128)}, f32[1,4,2,128]{3,1,2,0:T(4,128)S(1)}, u32[]{:S(2)}) copy-start(f32[1,4,2,128]{3,1,2,0:T(4,128)S(1)} %copy.145) | copy-start | bytes 12292
  30.2 9.1 %collective-permute-start.1 = (bf16[2,192,256]{2,1,0:T(8,128)(2,1)S(1)}, bf16[2,192,256]{2,1,0:T(8,128)(2,1)S(1)}, u32[]{:S(2)}, u32[]{:S(2)}) collective-permute-start(bf16[2,192,256]{2,1,0:T(8,128)(2,1)S(1)} %maximum_select_fusion.15), channel_id=1, source_target_pairs={{0,8},{2,10},{4,12},{6,14},{8,0},{10,2},{12,4},{14,6},{16,24},{18,... | collective-permute-start | bytes 589832 | tf_op jit(solution)/shard_map/ppermute | solution.py:366
  32.5 12.5 %copy-start.23 = (bf16[192,384]{1,0:T(8,128)(2,1)}, bf16[192,384]{1,0:T(8,128)(2,1)S(1)}, u32[]{:S(2)}) copy-start(bf16[192,384]{1,0:T(8,128)(2,1)S(1)} %collective-permute-done.3) | copy-start | bytes 442372
  32.5 12.3 %collective-permute-start.4 = (bf16[2,192,384]{2,1,0:T(8,128)(2,1)S(1)}, bf16[2,192,384]{2,1,0:T(8,128)(2,1)S(1)}, u32[]{:S(2)}, u32[]{:S(2)}) collective-permute-start(bf16[2,192,384]{2,1,0:T(8,128)(2,1)S(1)} %maximum_select_fusion.13), channel_id=1, source_target_pairs={{0,8},{2,10},{4,12},{6,14},{8,0},{10,2},{12,4},{14,6},{16,24},{18,... | collective-permute-start | bytes 884744 | tf_op jit(solution)/shard_map/ppermute | solution.py:366
  32.7 13.9 %copy-start.25 = (bf16[1,1,192,256]{3,2,0,1:T(8,128)(2,1)S(1)}, bf16[1,1,192,256]{3,2,0,1:T(8,128)(2,1)}, u32[]{:S(2)}) copy-start(bf16[1,1,192,256]{3,2,0,1:T(8,128)(2,1)} %copy-done.24) | copy-start | bytes 294916
  32.7 13.9 %copy-start.27 = (bf16[192,256]{1,0:T(8,128)(2,1)S(1)}, bf16[192,256]{1,0:T(8,128)(2,1)}, u32[]{:S(2)}) copy-start(bf16[192,256]{1,0:T(8,128)(2,1)} %copy-done.26) | copy-start | bytes 294916
  39.3 13.1 %collective-permute-start.2 = (bf16[2,2,192,256]{3,2,0,1:T(8,128)(2,1)S(1)}, bf16[2,2,192,256]{3,2,0,1:T(8,128)(2,1)S(1)}, u32[]{:S(2)}, u32[]{:S(2)}) collective-permute-start(bf16[2,2,192,256]{3,2,0,1:T(8,128)(2,1)S(1)} %maximum_select_fusion.11), channel_id=1, source_target_pairs={{0,4},{2,6},{4,0},{6,2},{8,12},{10,14},{12,8},{14,10},{16,20},{18,... | collective-permute-start | bytes 1179656 | tf_op jit(solution)/shard_map/ppermute | solution.py:366
  45.0 19.8 %collective-permute-start.5 = (bf16[2,2,192,384]{3,2,0,1:T(8,128)(2,1)S(1)}, bf16[2,2,192,384]{3,2,0,1:T(8,128)(2,1)S(1)}, u32[]{:S(2)}, u32[]{:S(2)}) collective-permute-start(bf16[2,2,192,384]{3,2,0,1:T(8,128)(2,1)S(1)} %maximum_select_fusion.9), channel_id=1, source_target_pairs={{0,2},{2,0},{4,6},{6,4},{8,10},{10,8},{12,14},{14,12},{16,18},{18,... | collective-permute-start | bytes 1769480 | tf_op jit(solution)/shard_map/ppermute | solution.py:366
  52.4 12.4 %copy-start.21 = (bf16[2,2,192,256]{3,2,0,1:T(8,128)(2,1)}, bf16[2,2,192,256]{3,2,0,1:T(8,128)(2,1)S(1)}, u32[]{:S(2)}) copy-start(bf16[2,2,192,256]{3,2,0,1:T(8,128)(2,1)S(1)} %collective-permute-done.2) | copy-start | bytes 1179652
  105.2 9.7 %collective-permute-start.6 = (bf16[1024,1024]{1,0:T(8,128)(2,1)}, bf16[1024,1024]{1,0:T(8,128)(2,1)}, u32[]{:S(2)}, u32[]{:S(2)}) collective-permute-start(bf16[1024,1024]{1,0:T(8,128)(2,1)} %get-tuple-element.62), channel_id=1, source_target_pairs={{0,1},{1,0},{2,3},{3,2},{4,5},{5,4},{6,7},{7,6},{8,9},{9,8},{10,11... | collective-permute-start | bytes 6291464 | tf_op jit(solution)/shard_map/ppermute | solution.py:350
  105.6 48.2 %collective-permute-start.7 = (bf16[2,2,2,192,256]{4,3,0,1,2:T(8,128)(2,1)}, bf16[2,2,2,192,256]{4,3,0,1,2:T(8,128)(2,1)}, u32[]{:S(2)}, u32[]{:S(2)}) collective-permute-start(bf16[2,2,2,192,256]{4,3,0,1,2:T(8,128)(2,1)} %maximum_select_fusion.6), channel_id=1, source_target_pairs={{0,2},{2,0},{4,6},{6,4},{8,10},{10,8},{12,14},{14,12},{16,18},{18,... | collective-permute-start | bytes 2359304 | tf_op jit(solution)/shard_map/ppermute | solution.py:366
  107.2 46.6 %collective-permute-start.8 = (bf16[2,2,2,192,384]{4,3,0,1,2:T(8,128)(2,1)}, bf16[2,2,2,192,384]{4,3,0,1,2:T(8,128)(2,1)}, u32[]{:S(2)}, u32[]{:S(2)}) collective-permute-start(bf16[2,2,2,192,384]{4,3,0,1,2:T(8,128)(2,1)} %maximum_select_fusion.4), channel_id=1, source_target_pairs={{0,4},{2,6},{4,0},{6,2},{8,12},{10,14},{12,8},{14,10},{16,20},{18,... | collective-permute-start | bytes 3538952 | tf_op jit(solution)/shard_map/ppermute | solution.py:366
  159.4 5.5 %collective-permute-start.9 = (bf16[1024,640]{1,0:T(8,128)(2,1)S(1)}, bf16[1024,640]{1,0:T(8,128)(2,1)S(1)}, u32[]{:S(2)}, u32[]{:S(2)}) collective-permute-start(bf16[1024,640]{1,0:T(8,128)(2,1)S(1)} %copy-done.41), channel_id=1, source_target_pairs={{0,1},{1,0},{2,3},{3,2},{4,5},{5,4},{6,7},{7,6},{8,9},{9,8},{10,11... | collective-permute-start | bytes 3932168 | tf_op jit(solution)/shard_map/ppermute | solution.py:350
  161.7 18.6 %collective-permute-start.10 = (bf16[3072,640]{1,0:T(8,128)(2,1)}, bf16[3072,640]{1,0:T(8,128)(2,1)}, u32[]{:S(2)}, u32[]{:S(2)}) collective-permute-start(bf16[3072,640]{1,0:T(8,128)(2,1)} %pad_maximum_fusion.wd_mine), channel_id=1, source_target_pairs={{0,1},{1,0},{2,3},{3,2},{4,5},{5,4},{6,7},{7,6},{8,9},{9,8},{10,11... | collective-permute-start | bytes 11796488 | tf_op jit(solution)/shard_map/ppermute | solution.py:350
  165.0 3.6 copy-start.47
  295.6 14.3 %collective-permute-start.12 = (bf16[1152,1536]{1,0:T(8,128)(2,1)}, bf16[1152,1536]{1,0:T(8,128)(2,1)}, u32[]{:S(2)}, u32[]{:S(2)}) collective-permute-start(bf16[1152,1536]{1,0:T(8,128)(2,1)} %get-tuple-element.73), channel_id=1, source_target_pairs={{0,1},{1,0},{2,3},{3,2},{4,5},{5,4},{6,7},{7,6},{8,9},{9,8},{10,11... | collective-permute-start | bytes 10616840 | tf_op jit(solution)/shard_map/ppermute | solution.py:350
  295.8 18.1 %collective-permute-start.11 = (bf16[1152,1536]{1,0:T(8,128)(2,1)}, bf16[1152,1536]{1,0:T(8,128)(2,1)}, u32[]{:S(2)}, u32[]{:S(2)}) collective-permute-start(bf16[1152,1536]{1,0:T(8,128)(2,1)} %get-tuple-element.71), channel_id=1, source_target_pairs={{0,1},{1,0},{2,3},{3,2},{4,5},{5,4},{6,7},{7,6},{8,9},{9,8},{10,11... | collective-permute-start | bytes 10616840 | tf_op jit(solution)/shard_map/ppermute | solution.py:350
  296.1 36.2 %collective-permute-start.14 = (bf16[3072,640]{1,0:T(8,128)(2,1)}, bf16[3072,640]{1,0:T(8,128)(2,1)S(1)}, u32[]{:S(2)}, u32[]{:S(2)}) collective-permute-start(bf16[3072,640]{1,0:T(8,128)(2,1)} %get-tuple-element.76), channel_id=1, source_target_pairs={{0,1},{1,0},{2,3},{3,2},{4,5},{5,4},{6,7},{7,6},{8,9},{9,8},{10,11... | collective-permute-start | bytes 11796488 | tf_op jit(solution)/shard_map/ppermute | solution.py:350
  299.9 3.9 copy-start.11
  299.9 6.2 %slice-start = ((s8[4718592]{0:T(1024)(128)(4,1)}), s8[524288]{0:T(1024)(128)(4,1)S(1)}, s32[]{:S(2)}) async-start(s8[4718592]{0:T(1024)(128)(4,1)} %bitcast.332), calls=%async_computation.2 | async-start | bytes 1048576
  309.9 9.8 %copy-start.1 = (f32[1024,1152]{1,0:T(8,128)}, f32[1024,1152]{1,0:T(8,128)S(1)}, u32[]{:S(2)}) copy-start(f32[1024,1152]{1,0:T(8,128)S(1)} %subtract_add_fusion) | copy-start | bytes 14155780
  321.0 6.4 %copy-start.8 = (bf16[1024,1152]{1,0:T(8,128)(2,1)}, bf16[1024,1152]{1,0:T(8,128)(2,1)S(1)}, u32[]{:S(2)}) copy-start(bf16[1024,1152]{1,0:T(8,128)(2,1)S(1)} %convert_element_type.926) | copy-start | bytes 7077892
  323.2 12.6 %collective-permute-start.13 = (bf16[1024,640]{1,0:T(8,128)(2,1)S(1)}, bf16[1024,640]{1,0:T(8,128)(2,1)}, u32[]{:S(2)}, u32[]{:S(2)}) collective-permute-start(bf16[1024,640]{1,0:T(8,128)(2,1)S(1)} %convolution_convert_fusion), channel_id=1, source_target_pairs={{0,1},{1,0},{2,3},{3,2},{4,5},{5,4},{6,7},{7,6},{8,9},{9,8},{10,11... | collective-permute-start | bytes 3932168 | tf_op jit(solution)/shard_map/ppermute | solution.py:350
  323.6 42.3 %collective-permute-start.15 = (bf16[2,2,2,72,1536]{4,3,0,2,1:T(8,128)(2,1)}, bf16[2,2,2,72,1536]{4,3,0,2,1:T(8,128)(2,1)}, u32[]{:S(2)}, u32[]{:S(2)}) collective-permute-start(bf16[2,2,2,72,1536]{4,3,0,2,1:T(8,128)(2,1)} %fusion.17), channel_id=1, source_target_pairs={{0,2},{2,0},{4,6},{6,4},{8,10},{10,8},{12,14},{14,12},{16,18},{18,... | collective-permute-start | bytes 5308424 | tf_op jit(solution)/shard_map/ppermute | solution.py:366
  325.0 41.8 %collective-permute-start.16 = (bf16[2,2,2,72,1536]{4,3,0,2,1:T(8,128)(2,1)}, bf16[2,2,2,72,1536]{4,3,0,2,1:T(8,128)(2,1)}, u32[]{:S(2)}, u32[]{:S(2)}) collective-permute-start(bf16[2,2,2,72,1536]{4,3,0,2,1:T(8,128)(2,1)} %fusion.18), channel_id=1, source_target_pairs={{0,4},{2,6},{4,0},{6,2},{8,12},{10,14},{12,8},{14,10},{16,20},{18,... | collective-permute-start | bytes 5308424 | tf_op jit(solution)/shard_map/ppermute | solution.py:366
  335.8 84.7 %collective-permute-start.20 = (bf16[2,2,2,192,640]{4,3,0,2,1:T(8,128)(2,1)}, bf16[2,2,2,192,640]{4,3,0,2,1:T(8,128)(2,1)}, u32[]{:S(2)}, u32[]{:S(2)}) collective-permute-start(bf16[2,2,2,192,640]{4,3,0,2,1:T(8,128)(2,1)} %fusion.14), channel_id=1, source_target_pairs={{0,4},{2,6},{4,0},{6,2},{8,12},{10,14},{12,8},{14,10},{16,20},{18,... | collective-permute-start | bytes 5898248 | tf_op jit(solution)/shard_map/ppermute | solution.py:366
  373.5 11.7 %collective-permute-start.17 = (bf16[1152,640]{1,0:T(8,128)(2,1)S(1)}, bf16[1152,640]{1,0:T(8,128)(2,1)S(1)}, u32[]{:S(2)}, u32[]{:S(2)}) collective-permute-start(bf16[1152,640]{1,0:T(8,128)(2,1)S(1)} %maximum_select_fusion.3), channel_id=1, source_target_pairs={{0,1},{1,0},{2,3},{3,2},{4,5},{5,4},{6,7},{7,6},{8,9},{9,8},{10,11... | collective-permute-start | bytes 4423688 | tf_op jit(solution)/shard_map/ppermute | solution.py:350
  388.3 39.0 %collective-permute-start.18 = (bf16[2,2,72,1536]{3,2,1,0:T(8,128)(2,1)}, bf16[2,2,72,1536]{3,2,1,0:T(8,128)(2,1)}, u32[]{:S(2)}, u32[]{:S(2)}) collective-permute-start(bf16[2,2,72,1536]{3,2,1,0:T(8,128)(2,1)} %copy.88), channel_id=1, source_target_pairs={{0,4},{2,6},{4,0},{6,2},{8,12},{10,14},{12,8},{14,10},{16,20},{18,... | collective-permute-start | bytes 2654216 | tf_op jit(solution)/shard_map/ppermute | solution.py:366
  389.9 37.4 %copy-start.40 = (f32[1,4,2,128]{3,1,2,0:T(4,128)S(1)}, f32[1,4,2,128]{3,1,2,0:T(4,128)}, u32[]{:S(2)}) copy-start(f32[1,4,2,128]{3,1,2,0:T(4,128)} %copy-done.39) | copy-start | bytes 12292
  389.9 37.4 %collective-permute-start.19 = (bf16[2,2,72,1536]{3,2,1,0:T(8,128)(2,1)}, bf16[2,2,72,1536]{3,2,1,0:T(8,128)(2,1)}, u32[]{:S(2)}, u32[]{:S(2)}) collective-permute-start(bf16[2,2,72,1536]{3,2,1,0:T(8,128)(2,1)} %copy.89), channel_id=1, source_target_pairs={{0,2},{2,0},{4,6},{6,4},{8,10},{10,8},{12,14},{14,12},{16,18},{18,... | collective-permute-start | bytes 2654216 | tf_op jit(solution)/shard_map/ppermute | solution.py:366
  391.4 35.9 %collective-permute-start.21 = (bf16[2,2,2,72,640]{4,3,0,2,1:T(8,128)(2,1)}, bf16[2,2,2,72,640]{4,3,0,2,1:T(8,128)(2,1)}, u32[]{:S(2)}, u32[]{:S(2)}) collective-permute-start(bf16[2,2,2,72,640]{4,3,0,2,1:T(8,128)(2,1)} %fusion.34), channel_id=1, source_target_pairs={{0,2},{2,0},{4,6},{6,4},{8,10},{10,8},{12,14},{14,12},{16,18},{18,... | collective-permute-start | bytes 2211848 | tf_op jit(solution)/shard_map/ppermute | solution.py:366
  427.3 14.0 %collective-permute-start.22 = (bf16[1024,1024]{1,0:T(8,128)(2,1)}, bf16[1024,1024]{1,0:T(8,128)(2,1)}, u32[]{:S(2)}, u32[]{:S(2)}) collective-permute-start(bf16[1024,1024]{1,0:T(8,128)(2,1)} %get-tuple-element.99), channel_id=1, source_target_pairs={{0,1},{1,0},{2,3},{3,2},{4,5},{5,4},{6,7},{7,6},{8,9},{9,8},{10,11... | collective-permute-start | bytes 6291464 | tf_op jit(solution)/shard_map/ppermute | solution.py:350
  432.1 31.6 %collective-permute-start.35 = (bf16[2,72,1536]{2,1,0:T(8,128)(2,1)S(1)}, bf16[2,72,1536]{2,1,0:T(8,128)(2,1)S(1)}, u32[]{:S(2)}, u32[]{:S(2)}) collective-permute-start(bf16[2,72,1536]{2,1,0:T(8,128)(2,1)S(1)} %get-tuple-element.166), channel_id=1, source_target_pairs={{0,8},{2,10},{4,12},{6,14},{8,0},{10,2},{12,4},{14,6},{16,24},{18,... | collective-permute-start | bytes 1327112 | tf_op jit(solution)/shard_map/ppermute | solution.py:366
  434.5 29.2 %collective-permute-start.34 = (bf16[2,72,1536]{2,1,0:T(8,128)(2,1)S(1)}, bf16[2,72,1536]{2,1,0:T(8,128)(2,1)S(1)}, u32[]{:S(2)}, u32[]{:S(2)}) collective-permute-start(bf16[2,72,1536]{2,1,0:T(8,128)(2,1)S(1)} %get-tuple-element.168), channel_id=1, source_target_pairs={{0,8},{2,10},{4,12},{6,14},{8,0},{10,2},{12,4},{14,6},{16,24},{18,... | collective-permute-start | bytes 1327112 | tf_op jit(solution)/shard_map/ppermute | solution.py:366
  436.9 26.1 %collective-permute-start.33 = (bf16[2,2,72,640]{3,2,1,0:T(8,128)(2,1)S(1)}, bf16[2,2,72,640]{3,2,1,0:T(8,128)(2,1)S(1)}, u32[]{:S(2)}, u32[]{:S(2)}) collective-permute-start(bf16[2,2,72,640]{3,2,1,0:T(8,128)(2,1)S(1)} %copy.110), channel_id=1, source_target_pairs={{0,4},{2,6},{4,0},{6,2},{8,12},{10,14},{12,8},{14,10},{16,20},{18,... | collective-permute-start | bytes 1105928 | tf_op jit(solution)/shard_map/ppermute | solution.py:366
  440.7 23.4 %collective-permute-start.32 = (bf16[2,2,192,640]{3,2,1,0:T(8,128)(2,1)S(1)}, bf16[2,2,192,640]{3,2,1,0:T(8,128)(2,1)S(1)}, u32[]{:S(2)}, u32[]{:S(2)}) collective-permute-start(bf16[2,2,192,640]{3,2,1,0:T(8,128)(2,1)S(1)} %copy.109), channel_id=1, source_target_pairs={{0,2},{2,0},{4,6},{6,4},{8,10},{10,8},{12,14},{14,12},{16,18},{18,... | collective-permute-start | bytes 2949128 | tf_op jit(solution)/shard_map/ppermute | solution.py:366
  441.4 4.7 copy-start.4
  441.4 4.7 copy-start.38
  441.4 4.7 copy-start.45
  441.4 4.7 copy-start.49
  446.1 3.7 copy-start.19
  449.8 8.5 %slice-start.2 = ((s8[4718592]{0:T(1024)(128)(4,1)}), s8[4194304]{0:T(1024)(128)(4,1)S(1)}, s32[]{:S(2)}) async-start(s8[4718592]{0:T(1024)(128)(4,1)} %bitcast.334), calls=%async_computation.4 | async-start | bytes 8388608
  454.8 6.0 %collective-permute-start.23 = (bf16[1152,1024]{1,0:T(8,128)(2,1)S(1)}, bf16[1152,1024]{1,0:T(8,128)(2,1)S(1)}, u32[]{:S(2)}, u32[]{:S(2)}) collective-permute-start(bf16[1152,1024]{1,0:T(8,128)(2,1)S(1)} %add_convert_fusion), channel_id=1, source_target_pairs={{0,1},{1,0},{2,3},{3,2},{4,5},{5,4},{6,7},{7,6},{8,9},{9,8},{10,11... | collective-permute-start | bytes 7077896 | tf_op jit(solution)/shard_map/ppermute | solution.py:350
  461.3 39.8 %collective-permute-start.24 = (bf16[2,2,2,72,512]{4,3,0,2,1:T(8,128)(2,1)S(1)}, bf16[2,2,2,72,512]{4,3,0,2,1:T(8,128)(2,1)S(1)}, u32[]{:S(2)}, u32[]{:S(2)}) collective-permute-start(bf16[2,2,2,72,512]{4,3,0,2,1:T(8,128)(2,1)S(1)} %fusion.37), channel_id=1, source_target_pairs={{0,2},{2,0},{4,6},{6,4},{8,10},{10,8},{12,14},{14,12},{16,18},{18,... | collective-permute-start | bytes 1769480 | tf_op jit(solution)/shard_map/ppermute | solution.py:366
  463.0 40.0 %collective-permute-start.28 = (bf16[2,2,2,72,512]{4,3,0,2,1:T(8,128)(2,1)S(1)}, bf16[2,2,2,72,512]{4,3,0,2,1:T(8,128)(2,1)S(1)}, u32[]{:S(2)}, u32[]{:S(2)}) collective-permute-start(bf16[2,2,2,72,512]{4,3,0,2,1:T(8,128)(2,1)S(1)} %fusion.38), channel_id=1, source_target_pairs={{0,4},{2,6},{4,0},{6,2},{8,12},{10,14},{12,8},{14,10},{16,20},{18,... | collective-permute-start | bytes 1769480 | tf_op jit(solution)/shard_map/ppermute | solution.py:366
  464.3 36.6 %collective-permute-start.40 = (bf16[2,192,640]{2,1,0:T(8,128)(2,1)S(1)}, bf16[2,192,640]{2,1,0:T(8,128)(2,1)S(1)}, u32[]{:S(2)}, u32[]{:S(2)}) collective-permute-start(bf16[2,192,640]{2,1,0:T(8,128)(2,1)S(1)} %get-tuple-element.164), channel_id=1, source_target_pairs={{0,8},{2,10},{4,12},{6,14},{8,0},{10,2},{12,4},{14,6},{16,24},{18,... | collective-permute-start | bytes 1474568 | tf_op jit(solution)/shard_map/ppermute | solution.py:366
  465.4 22.1 %collective-permute-start.39 = (bf16[72,1536]{1,0:T(8,128)(2,1)S(1)}, bf16[72,1536]{1,0:T(8,128)(2,1)S(1)}, u32[]{:S(2)}, u32[]{:S(2)}) collective-permute-start(bf16[72,1536]{1,0:T(8,128)(2,1)S(1)} %fusion.72), channel_id=1, source_target_pairs={{0,16},{2,18},{4,20},{6,22},{8,24},{10,26},{12,28},{14,30},{16,0},... | collective-permute-start | bytes 663560 | tf_op jit(solution)/shard_map/ppermute | solution.py:366
  466.9 18.9 %collective-permute-start.36 = (bf16[2,72,640]{2,1,0:T(8,128)(2,1)S(1)}, bf16[2,72,640]{2,1,0:T(8,128)(2,1)S(1)}, u32[]{:S(2)}, u32[]{:S(2)}) collective-permute-start(bf16[2,72,640]{2,1,0:T(8,128)(2,1)S(1)} %get-tuple-element.194), channel_id=1, source_target_pairs={{0,8},{2,10},{4,12},{6,14},{8,0},{10,2},{12,4},{14,6},{16,24},{18,... | collective-permute-start | bytes 552968 | tf_op jit(solution)/shard_map/ppermute | solution.py:366
  485.8 14.2 %collective-permute-start.38 = (bf16[72,1536]{1,0:T(8,128)(2,1)S(1)}, bf16[72,1536]{1,0:T(8,128)(2,1)S(1)}, u32[]{:S(2)}, u32[]{:S(2)}) collective-permute-start(bf16[72,1536]{1,0:T(8,128)(2,1)S(1)} %fusion.70), channel_id=1, source_target_pairs={{0,16},{2,18},{4,20},{6,22},{8,24},{10,26},{12,28},{14,30},{16,0},... | collective-permute-start | bytes 663560 | tf_op jit(solution)/shard_map/ppermute | solution.py:366
  487.5 16.0 %collective-permute-start.37 = (bf16[72,640]{1,0:T(8,128)(2,1)S(1)}, bf16[72,640]{1,0:T(8,128)(2,1)S(1)}, u32[]{:S(2)}, u32[]{:S(2)}) collective-permute-start(bf16[72,640]{1,0:T(8,128)(2,1)S(1)} %get-tuple-element.199), channel_id=1, source_target_pairs={{0,16},{2,18},{4,20},{6,22},{8,24},{10,26},{12,28},{14,30},{16,0},... | collective-permute-start | bytes 276488 | tf_op jit(solution)/shard_map/ppermute | solution.py:366
  501.0 12.0 %collective-permute-start.41 = (bf16[192,640]{1,0:T(8,128)(2,1)S(1)}, bf16[192,640]{1,0:T(8,128)(2,1)S(1)}, u32[]{:S(2)}, u32[]{:S(2)}) collective-permute-start(bf16[192,640]{1,0:T(8,128)(2,1)S(1)} %get-tuple-element.191), channel_id=1, source_target_pairs={{0,16},{2,18},{4,20},{6,22},{8,24},{10,26},{12,28},{14,30},{16,0},... | collective-permute-start | bytes 737288 | tf_op jit(solution)/shard_map/ppermute | solution.py:366
  501.3 8.1 %collective-permute-start.25 = (bf16[2,2,72,512]{3,2,1,0:T(8,128)(2,1)S(1)}, bf16[2,2,72,512]{3,2,1,0:T(8,128)(2,1)S(1)}, u32[]{:S(2)}, u32[]{:S(2)}) collective-permute-start(bf16[2,2,72,512]{3,2,1,0:T(8,128)(2,1)S(1)} %copy.95), channel_id=1, source_target_pairs={{0,4},{2,6},{4,0},{6,2},{8,12},{10,14},{12,8},{14,10},{16,20},{18,... | collective-permute-start | bytes 884744 | tf_op jit(solution)/shard_map/ppermute | solution.py:366
  503.2 7.9 %collective-permute-start.29 = (bf16[2,2,72,512]{3,2,1,0:T(8,128)(2,1)S(1)}, bf16[2,2,72,512]{3,2,1,0:T(8,128)(2,1)S(1)}, u32[]{:S(2)}, u32[]{:S(2)}) collective-permute-start(bf16[2,2,72,512]{3,2,1,0:T(8,128)(2,1)S(1)} %copy.102), channel_id=1, source_target_pairs={{0,2},{2,0},{4,6},{6,4},{8,10},{10,8},{12,14},{14,12},{16,18},{18,... | collective-permute-start | bytes 884744 | tf_op jit(solution)/shard_map/ppermute | solution.py:366
  509.4 10.4 %collective-permute-start.26 = (bf16[2,72,512]{2,1,0:T(8,128)(2,1)S(1)}, bf16[2,72,512]{2,1,0:T(8,128)(2,1)S(1)}, u32[]{:S(2)}, u32[]{:S(2)}) collective-permute-start(bf16[2,72,512]{2,1,0:T(8,128)(2,1)S(1)} %get-tuple-element.196), channel_id=1, source_target_pairs={{0,8},{2,10},{4,12},{6,14},{8,0},{10,2},{12,4},{14,6},{16,24},{18,... | collective-permute-start | bytes 442376 | tf_op jit(solution)/shard_map/ppermute | solution.py:366
  511.2 8.0 %collective-permute-start.30 = (bf16[2,72,512]{2,1,0:T(8,128)(2,1)S(1)}, bf16[2,72,512]{2,1,0:T(8,128)(2,1)S(1)}, u32[]{:S(2)}, u32[]{:S(2)}) collective-permute-start(bf16[2,72,512]{2,1,0:T(8,128)(2,1)S(1)} %get-tuple-element.198), channel_id=1, source_target_pairs={{0,8},{2,10},{4,12},{6,14},{8,0},{10,2},{12,4},{14,6},{16,24},{18,... | collective-permute-start | bytes 442376 | tf_op jit(solution)/shard_map/ppermute | solution.py:366
  519.2 8.3 %collective-permute-start.31 = (bf16[72,512]{1,0:T(8,128)(2,1)S(1)}, bf16[72,512]{1,0:T(8,128)(2,1)S(1)}, u32[]{:S(2)}, u32[]{:S(2)}) collective-permute-start(bf16[72,512]{1,0:T(8,128)(2,1)S(1)} %fusion.87), channel_id=1, source_target_pairs={{0,16},{2,18},{4,20},{6,22},{8,24},{10,26},{12,28},{14,30},{16,0},... | collective-permute-start | bytes 221192 | tf_op jit(solution)/shard_map/ppermute | solution.py:366
  519.9 9.1 %collective-permute-start.27 = (bf16[72,512]{1,0:T(8,128)(2,1)S(1)}, bf16[72,512]{1,0:T(8,128)(2,1)S(1)}, u32[]{:S(2)}, u32[]{:S(2)}) collective-permute-start(bf16[72,512]{1,0:T(8,128)(2,1)S(1)} %fusion.85), channel_id=1, source_target_pairs={{0,16},{2,18},{4,20},{6,22},{8,24},{10,26},{12,28},{14,30},{16,0},... | collective-permute-start | bytes 221192 | tf_op jit(solution)/shard_map/ppermute | solution.py:366
  (35 other events, 78.2 us)
Sparse Core Ops, SparseCore 0:
  11.5 83.1 all-gather.2
  98.1 105.5 all-gather.4

commit v8 on v7

--- a/solution.py
+++ b/solution.py
@@ -367,6 +367,7 @@
 
 
 ORDERS = (0, 1), (1, 0)
+HIGH, LAST = (), (0, 1)
 
 
 def doubled(a, got, bit, axis):
@@ -403,7 +404,9 @@
         self.kind = kind
         bits = lax.axis_size("dp").bit_length() - 1
         self.steps = bits
-        self.orders = [[*order, *range(2, bits)] for _, _, order in parts]
+        rest = list(range(2, bits))
+        ways = {ORDERS[0]: [*ORDERS[0], *rest], ORDERS[1]: [*ORDERS[1], *rest[::-1]], HIGH: [*rest, *LAST]}
+        self.orders = [ways[order] for _, _, order in parts]
         shape = lambda u: u.reshape(*[2] * bits, -1, u.shape[-1])
         self.stay = [shape(u) for u, _, _ in parts]
         self.got = [shape(v) for _, v, _ in parts]
@@ -502,7 +505,7 @@
     d_out = lax.dot_general(grad_low, out_theirs, NT, preferred_element_type=f32).astype(bf16)
     d_got = swap(d_out)
     d_mine = lax.dot_general(grad_low, out_mine, NT, preferred_element_type=f32).astype(bf16)
-    down_sum = Halving([(gd_mine, swap(gd_theirs), ORDERS[1])])
+    down_sum = Halving([(gd_mine, swap(gd_theirs), HIGH)])
     down_sum.prepare(0)
     d_mine, d_got, down_sum.send = tie((d_mine, d_got, down_sum.send))
     down_sum.move(0)
@@ -511,7 +514,7 @@
     )
     lins = back(0, ())
 
-    lins, grad_low, wide_sum.got = tie((lins, grad_low, wide_sum.got))
+    lins, grad_low, wide_sum.got, down_sum.got = tie((lins, grad_low, wide_sum.got, down_sum.got))
     low = widen(grad_low[:, : D // 2]), widen(grad_low[:, D // 2 :])
 
     def grad_out(columns):
@@ -522,10 +525,14 @@
         return pick(jnp.concatenate([a, b], 0), jnp.concatenate([b, a], 0))
 
     wide_sum.prepare(1)
+    down_sum.prepare(1)
     out_sum = Halving([(grad_out(pick(*low)), swap(grad_out(pick(*low[::-1]))), ORDERS[0])])
     out_sum.prepare(0)
-    lins, wide_sum.send, out_sum.send = tie((lins, wide_sum.send, out_sum.send))
+    lins, wide_sum.send, down_sum.send, out_sum.send = tie(
+        (lins, wide_sum.send, down_sum.send, out_sum.send)
+    )
     wide_sum.move(1)
+    down_sum.move(1)
     out_sum.move(0)
     for b in range(1, batch):
         lins = back(b, lins)
@@ -533,7 +540,7 @@
         (lins, wide_sum.got, down_sum.got, out_sum.got)
     )
     lin_got = swap(lin_out)
-    down_sum.advance(1)
+    down_sum.advance(2)
     out_sum.advance(1)
     wide_sum.advance(2)
     grad_n1 = lax.dot_general(lin_mine, w_mine, NT, preferred_element_type=f32) + lax.dot_general(
@@ -561,14 +568,21 @@
         (pack_sum.send, down_sum.got, out_sum.got, wide_sum.got)
     )
     pack_sum.move(0)
-    down_sum.advance(2)
+    wide_sum.advance(3)
+    down_sum.advance(3)
     out_sum.advance(2)
     grad_input = (grad_residual + norm_back(grad_n1, floats, scale_attn, gain_one)).astype(bf16)
     pack_sum.advance(1)
-    r_gate, r_up = wide_sum.finish(3)
-    r_down = down_sum.finish(3)[0][:, : D // 2]
-    r_out = out_sum.finish(3)[0][:, : D // 2]
-    r_pack = jnp.concatenate(pack_sum.finish(2), 1)
+    _, down_sum.got, out_sum.got, wide_sum.got = tie(
+        (pack_sum.send, down_sum.got, out_sum.got, wide_sum.got)
+    )
+    out_sum.advance(3)
+    pack_sum.advance(2)
+    _, down_sum.got, out_sum.got = tie((pack_sum.send, down_sum.got, out_sum.got))
+    r_gate, r_up = wide_sum.finish(4)
+    r_down = down_sum.finish(4)[0][:, : D // 2]
+    r_out = out_sum.finish(4)[0][:, : D // 2]
+    r_pack = jnp.concatenate(pack_sum.finish(3), 1)
     a, b, c = HQ * HEAD_SIZE, (HQ + HK) * HEAD_SIZE, QKV
     shape = layer_input.shape
     return (

time: 546 us -> 541 us (level)
  local copies, waits for them, and re-layouts: 42.3 us -> 34.9 us
  other arithmetic: 64.2 us -> 71 us
    dynamic_slice x12, local copies, waits for them, and re-layouts: 13.8 us -> 6.5 us  [prepare(): at = lambda u, i: lax.dynamic_index_in_dim(u, i, axis, keepdims=False)]
    convert_element_type x30 -> x29, other arithmetic: 25.7 us -> 26.7 us  [prepare(): add(at(self.stay[p], i), at(self.got[p], i)).astype(self.kind)]
    unnamed x110 -> x118, local copies, waits for them, and re-layouts: 14.2 us -> 14.1 us
  transfers between devices with their start and end apart: 44 -> 44, of which waited for: 16 -> 19; matrix products, arithmetic and copies ran while one was open for 23% -> 20% of each run, Pallas kernels for 20% -> 21%
where the time goes in v8:
time: 541 us; the launch traced here: 531 us
  Pallas kernels  201 us (37%)
  waiting for transfers between devices  139 us (26%)
  other arithmetic  71 us (13%)
  starting transfers between devices  40.7 us (8%)
  local copies, waits for them, and re-layouts  34.9 us (6%)
  matrix products  28.9 us (5%)
  between operations  15.4 us (3%)
    pallas_call x1, Pallas kernels, mlp(): pl.pallas_call(mlp_body, grid_spec=pltpu.PrefetchScalarGridSpec(num_scala...  91.8 us
    ppermute x32, waiting for transfers between devices, exchange(): lax.ppermute(a, 'dp', [(i, i ^ 1 << bit) for i in range(lax.axis_size('dp...  87.3 us
    pallas_call x2, Pallas kernels, attend_back(): pl.pallas_call(bwd_body, grid_spec=pltpu.PrefetchScalarGridSpec(num_scala...  57.1 us
    all_gather x2, waiting for transfers between devices, fetch(): lax.all_gather(w, BOTH, axis=0, tiled=True)  51.6 us
    pallas_call x1, Pallas kernels, attend(): pl.pallas_call(fwd_body, grid_spec=pltpu.PrefetchScalarGridSpec(num_scala...  38.9 us
    ppermute x32, starting transfers between devices, exchange(): lax.ppermute(a, 'dp', [(i, i ^ 1 << bit) for i in range(lax.axis_size('dp...  38.6 us
    convert_element_type x29, other arithmetic, prepare(): add(at(self.stay[p], i), at(self.got[p], i)).astype(self.kind)  26.7 us
    unnamed x118, local copies, waits for them, and re-layouts  14.1 us
  transfers between devices with their start and end apart: 44, of which 19 were waited for; matrix products, arithmetic and copies ran while one was open for 20% of the time, Pallas kernels for 21%

profile of v8, /device:TPU:0, one launch (start us, length us, event | category | flops | bytes accessed | tf_op | source)
XLA Modules:
  0.0 531.4 jit_solution(4635264245927688826)
XLA Ops:
  8.1 1.8 concatenate.186
  10.0 2.0 pad_maximum_fusion.1
  12.0 4.1 collective-permute-start.3
  16.4 3.1 fusion.43
  20.1 9.1 %collective-permute-done = bf16[192,256]{1,0:T(8,128)(2,1)S(1)} collective-permute-done((bf16[192,256]{1,0:T(8,128)(2,1)S(1)}, bf16[192,256]{1,0:T(8,128)(2,1)S(1)}, u32[]{:S(2)}, u32[]{:S(2)}) %collective-permute-start) | collective-permute-done | bytes 98336 | tf_op jit(solution)/shard_map/ppermute | solution.py:366
  31.5 6.8 %collective-permute-done.1 = bf16[2,192,256]{2,1,0:T(8,128)(2,1)S(1)} collective-permute-done((bf16[2,192,256]{2,1,0:T(8,128)(2,1)S(1)}, bf16[2,192,256]{2,1,0:T(8,128)(2,1)S(1)}, u32[]{:S(2)}, u32[]{:S(2)}) %collective-permute-start.1) | collective-permute-done | bytes 196640 | tf_op jit(solution)/shard_map/ppermute | solution.py:366
  38.3 1.8 collective-permute-start.2
  40.2 3.7 collective-permute-done.4
  47.8 3.0 collective-permute-done.2
  51.8 13.2 %collective-permute-done.5 = bf16[2,2,192,384]{3,2,0,1:T(8,128)(2,1)S(1)} collective-permute-done((bf16[2,2,192,384]{3,2,0,1:T(8,128)(2,1)S(1)}, bf16[2,2,192,384]{3,2,0,1:T(8,128)(2,1)S(1)}, u32[]{:S(2)}, u32[]{:S(2)}) %collective-permute-start.5) | collective-permute-done | bytes 589856 | tf_op jit(solution)/shard_map/ppermute | solution.py:366
  66.3 30.0 %all-gather.3.cloned.1.call-done = bf16[2304,1600]{1,0:T(8,128)(2,1)} async-done(((bf16[72,1600]{1,0:T(8,128)(2,1)}), bf16[2304,1600]{1,0:T(8,128)(2,1)}) %all-gather.3.cloned.1.call-update) | async-done | bytes 7372816 | tf_op jit(solution)/shard_map/all_gather | solution.py:361
  96.3 2.2 convert_reduce_fusion
  99.4 2.0 fusion.2.n1
  101.4 6.8 %project.3 = (bf16[1024,1024]{1,0:T(8,128)(2,1)}, bf16[1152,1024]{1,0:T(8,128)(2,1)}) custom-call(s32[1]{0:T(128)} %bitcast.me, bf16[1024,1152]{1,0:T(8,128)(2,1)} %fusion.2.n1, bf16[16,2,72,1600]{3,2,1,0:T(8,128)(2,1)} %bitcast.350, f32[1024,128]{1,0:T(8,128)} %get-tuple-element.226.cosine, f32[1024,128]{1,0:T(8,128)} %get-tuple-element.225.sine), custom_call_target="tpu_custom_call" | custom-call | flops 3000000000 | bytes 12000000 | tf_op jit(solution)/shard_map/project/pallas_call | solution.py:66
  111.2 6.8 %project.2 = (bf16[1024,1024]{1,0:T(8,128)(2,1)}, bf16[1152,1024]{1,0:T(8,128)(2,1)}) custom-call(s32[1]{0:T(128)} %bitcast.me, bf16[1024,1152]{1,0:T(8,128)(2,1)} %fusion.2.n1, bf16[16,2,72,1600]{3,2,1,0:T(8,128)(2,1)} %bitcast.351, f32[1024,128]{1,0:T(8,128)} %get-tuple-element.226.cosine, f32[1024,128]{1,0:T(8,128)} %get-tuple-element.225.sine), custom_call_target="tpu_custom_call" | custom-call | flops 3000000000 | bytes 12000000 | tf_op jit(solution)/shard_map/project/pallas_call | solution.py:66
  118.0 38.9 %attend.1 = (bf16[1024,640]{1,0:T(8,128)(2,1)}, bf16[1024,640]{1,0:T(8,128)(2,1)}, f32[2048,128]{1,0:T(8,128)}) custom-call(s32[1]{0:T(128)} %bitcast.me, bf16[1024,1024]{1,0:T(8,128)(2,1)} %get-tuple-element.69.mine, bf16[1024,1024]{1,0:T(8,128)(2,1)} %collective-permute-done.6.got), custom_call_target="tpu_custom_call" | custom-call | flops 24000000000 | bytes 20000000 | tf_op jit(solution)/shard_map/attend/pallas_call | solution.py:200
  156.9 2.0 maximum_select_fusion
  159.2 2.1 maximum_select_fusion.1
  162.6 2.2 pad_maximum_fusion.wd_mine
  165.4 2.1 slice_bitcast_fusion
  168.2 2.1 fusion.62
  171.7 2.4 multiply_reduce_fusion.2
  174.1 2.1 copy-done
  176.6 2.5 copy.70.n2t
  179.2 4.2 multiply_convert_fusion.n2
  183.4 21.6 %all-gather.5.cloned.1.call-done = bf16[2304,3072]{1,0:T(8,128)(2,1)} async-done(((bf16[72,3072]{1,0:T(8,128)(2,1)}), bf16[2304,3072]{1,0:T(8,128)(2,1)}) %all-gather.5.cloned.1.call-update) | async-done | bytes 14155792 | tf_op jit(solution)/shard_map/all_gather | solution.py:361
  205.0 91.8 %mlp.1 = (bf16[1024,1152]{1,0:T(8,128)(2,1)}, f32[1024,1152]{1,0:T(8,128)}, bf16[1152,1536]{1,0:T(8,128)(2,1)}, bf16[1152,1536]{1,0:T(8,128)(2,1)}, bf16[1152,15...) custom-call(s32[1]{0:T(128)} %bitcast.me, ...), custom_call_target="tpu_custom_call" | custom-call | flops 65000001536 | bytes 60000000 | tf_op jit(solution)/shard_map/mlp/pallas_call | solution.py:312
  297.6 5.6 %multiply_reduce_fusion = (f32[1152]{0:T(1024)}, f32[1024]{0:T(1024)S(1)}) fusion(f32[1024,1152]{1,0:T(8,128)} %get-tuple-element.77, f32[1024,1152]{1,0:T(8,128)} %copy-done, f32[1024]{0:T(1024)S(1)} %get-tuple-element.228, f32[1152]{0:T(1024)S(1)} %reshape.1105), kind=kLoop, calls=%fused_computation.19 | loop fusion | flops 7075712 | bytes 9454592 | tf_op jit(solution)/shard_map/reduce_sum | solution.py:500
  303.5 2.0 copy-done.5
  306.3 3.4 subtract_add_fusion
  310.2 3.2 copy-done.12
  313.7 2.3 constant_dynamic-slice_fusion.14
  316.4 1.7 fusion.18
  318.1 1.7 fusion.17
  321.1 2.2 convolution_convert_fusion
  323.7 3.3 convolution_convert_fusion.1.do_mine
  331.0 1.9 fusion.14
  333.8 1.8 add_convert_fusion.5
  336.1 28.6 %attend_back.2 = (bf16[1024,1024]{1,0:T(8,128)(2,1)}, bf16[1024,1024]{1,0:T(8,128)(2,1)}) custom-call(s32[1]{0:T(128)} %bitcast.me, bf16[1024,1024]{1,0:T(8,128)(2,1)} %get-tuple-element.69.mine, bf16[1024,1024]{1,0:T(8,128)(2,1)} %collective-permute-done.6.got, bf16[1024,640]{1,0:T(8,128)(2,1)} %get-tuple-element.71.o_mine, ...), custom_call_target="tpu_custom_call" | custom-call | flops 12999999488 | bytes 20000000 | tf_op jit(solution)/shard_map/attend_back/pallas_call | solution.py:226
  364.8 3.2 collective-permute-done.15
  369.1 8.4 %collective-permute-done.17 = bf16[2,2,2,192,640]{4,3,1,2,0:T(8,128)(2,1)} collective-permute-done((bf16[2,2,2,192,640]{4,3,1,2,0:T(8,128)(2,1)}, bf16[2,2,2,192,640]{4,3,1,2,0:T(8,128)(2,1)}, u32[]{:S(2)}, u32[]{:S(2)}) %collective-permute-start.17) | collective-permute-done | bytes 1966112 | tf_op jit(solution)/shard_map/ppermute | solution.py:366
  377.6 1.9 slice.86
  379.5 2.7 fusion.89
  388.2 3.0 fusion.15
  393.6 3.0 fusion.19
  396.7 1.9 fusion.20
  408.0 28.5 %attend_back.3 = (bf16[1024,1024]{1,0:T(8,128)(2,1)}, bf16[1024,1024]{1,0:T(8,128)(2,1)}) custom-call(s32[1]{0:T(128)} %bitcast.me, bf16[1024,1024]{1,0:T(8,128)(2,1)} %get-tuple-element.69.mine, bf16[1024,1024]{1,0:T(8,128)(2,1)} %collective-permute-done.6.got, ...), custom_call_target="tpu_custom_call", output_to_operand_aliasing={{0}: (10, {}), {1}: (11, {})} | custom-call | flops 12999999488 | bytes 20000000 | tf_op jit(solution)/shard_map/attend_back/pallas_call | solution.py:226
  436.5 7.1 %collective-permute-done.22 = bf16[2,2,2,72,640]{4,3,0,2,1:T(8,128)(2,1)} collective-permute-done((bf16[2,2,2,72,640]{4,3,0,2,1:T(8,128)(2,1)}, bf16[2,2,2,72,640]{4,3,0,2,1:T(8,128)(2,1)}, u32[]{:S(2)}, u32[]{:S(2)}) %collective-permute-start.22) | collective-permute-done | bytes 737312 | tf_op jit(solution)/shard_map/ppermute | solution.py:366
  443.6 4.8 collective-permute-done.21
  452.7 2.3 collective-permute-start.35
  460.1 2.9 fusion.114
  463.1 3.5 fusion.9
  466.7 3.0 add_convert_fusion
  469.8 3.0 add_convert_fusion.1
  473.2 2.7 fusion.6
  479.1 2.6 collective-permute-start.39
  483.7 8.4 %collective-permute-done.25 = bf16[2,2,2,72,512]{4,3,0,2,1:T(8,128)(2,1)S(1)} collective-permute-done((bf16[2,2,2,72,512]{4,3,0,2,1:T(8,128)(2,1)S(1)}, bf16[2,2,2,72,512]{4,3,0,2,1:T(8,128)(2,1)S(1)}, u32[]{:S(2)}, u32[]{:S(2)}) %collective-permute-start.25) | collective-permute-done | bytes 589856 | tf_op jit(solution)/shard_map/ppermute | solution.py:366
  492.5 1.9 collective-permute-done.29
  495.3 3.1 collective-permute-done.38
  502.5 5.1 collective-permute-done.26
  507.8 2.0 collective-permute-start.27
  511.8 5.9 %collective-permute-done.31 = bf16[2,72,512]{2,1,0:T(8,128)(2,1)S(1)} collective-permute-done((bf16[2,72,512]{2,1,0:T(8,128)(2,1)S(1)}, bf16[2,72,512]{2,1,0:T(8,128)(2,1)S(1)}, u32[]{:S(2)}, u32[]{:S(2)}) %collective-permute-start.31) | collective-permute-done | bytes 147488 | tf_op jit(solution)/shard_map/ppermute | solution.py:366
  517.8 2.3 collective-permute-start.28
  520.1 2.0 collective-permute-done.32
  (282 shorter events, 72.3 us)
Async XLA Ops:
  7.2 89.2 %all-gather.3.cloned.1.call-start = ((), (), s32[]{:S(2)}) async-start(), calls=%async_computation | async-start | bytes 7907328 | tf_op jit(solution)/shard_map/all_gather | solution.py:361
  9.9 9.6 %copy-start.2 = (bf16[2,1,512,1152]{3,2,1,0:T(8,128)(2,1)S(1)}, bf16[2,1,512,1152]{3,2,1,0:T(8,128)(2,1)}, u32[]{:S(2)}) copy-start(bf16[2,1,512,1152]{3,2,1,0:T(8,128)(2,1)} %param.11) | copy-start | bytes 7077892
  9.9 195.1 %all-gather.5.cloned.1.call-start = ((), (), s32[]{:S(2)}) async-start(), calls=%async_computation.1 | async-start | bytes 14598144 | tf_op jit(solution)/shard_map/all_gather | solution.py:361
  12.0 19.4 %copy-start.25 = (bf16[1,1,192,384]{3,2,0,1:T(8,128)(2,1)}, bf16[1,1,192,384]{3,2,0,1:T(8,128)(2,1)S(1)}, u32[]{:S(2)}) copy-start(bf16[1,1,192,384]{3,2,0,1:T(8,128)(2,1)S(1)} %get-tuple-element.217) | copy-start | bytes 442372
  12.0 18.3 %collective-permute-start.3 = (bf16[192,384]{1,0:T(8,128)(2,1)S(1)}, bf16[192,384]{1,0:T(8,128)(2,1)S(1)}, u32[]{:S(2)}, u32[]{:S(2)}) collective-permute-start(bf16[192,384]{1,0:T(8,128)(2,1)S(1)} %get-tuple-element.219), channel_id=1, source_target_pairs={{0,16},{2,18},{4,20},{6,22},{8,24},{10,26},{12,28},{14,30},{16,0},... | collective-permute-start | bytes 442376 | tf_op jit(solution)/shard_map/ppermute | solution.py:366
  16.2 15.2 %copy-start.28 = (bf16[1,1,192,256]{3,2,0,1:T(8,128)(2,1)}, bf16[1,1,192,256]{3,2,0,1:T(8,128)(2,1)S(1)}, u32[]{:S(2)}) copy-start(bf16[1,1,192,256]{3,2,0,1:T(8,128)(2,1)S(1)} %get-tuple-element.220) | copy-start | bytes 294916
  16.2 12.9 %collective-permute-start = (bf16[192,256]{1,0:T(8,128)(2,1)S(1)}, bf16[192,256]{1,0:T(8,128)(2,1)S(1)}, u32[]{:S(2)}, u32[]{:S(2)}) collective-permute-start(bf16[192,256]{1,0:T(8,128)(2,1)S(1)} %get-tuple-element.222), channel_id=1, source_target_pairs={{0,16},{2,18},{4,20},{6,22},{8,24},{10,26},{12,28},{14,30},{16,0},... | collective-permute-start | bytes 294920 | tf_op jit(solution)/shard_map/ppermute | solution.py:366
  20.1 79.3 %copy-start.42 = (f32[1,4,2,128]{3,1,2,0:T(4,128)}, f32[1,4,2,128]{3,1,2,0:T(4,128)S(1)}, u32[]{:S(2)}) copy-start(f32[1,4,2,128]{3,1,2,0:T(4,128)S(1)} %copy.135) | copy-start | bytes 12292
  29.1 14.7 %copy-start.30 = (bf16[192,256]{1,0:T(8,128)(2,1)}, bf16[192,256]{1,0:T(8,128)(2,1)S(1)}, u32[]{:S(2)}) copy-start(bf16[192,256]{1,0:T(8,128)(2,1)S(1)} %collective-permute-done) | copy-start | bytes 294916
  29.2 9.1 %collective-permute-start.1 = (bf16[2,192,256]{2,1,0:T(8,128)(2,1)S(1)}, bf16[2,192,256]{2,1,0:T(8,128)(2,1)S(1)}, u32[]{:S(2)}, u32[]{:S(2)}) collective-permute-start(bf16[2,192,256]{2,1,0:T(8,128)(2,1)S(1)} %maximum_select_fusion.15), channel_id=1, source_target_pairs={{0,8},{2,10},{4,12},{6,14},{8,0},{10,2},{12,4},{14,6},{16,24},{18,... | collective-permute-start | bytes 589832 | tf_op jit(solution)/shard_map/ppermute | solution.py:366
  30.3 15.2 %copy-start.27 = (bf16[192,384]{1,0:T(8,128)(2,1)}, bf16[192,384]{1,0:T(8,128)(2,1)S(1)}, u32[]{:S(2)}) copy-start(bf16[192,384]{1,0:T(8,128)(2,1)S(1)} %collective-permute-done.3) | copy-start | bytes 442372
  30.4 13.5 %collective-permute-start.4 = (bf16[2,192,384]{2,1,0:T(8,128)(2,1)S(1)}, bf16[2,192,384]{2,1,0:T(8,128)(2,1)S(1)}, u32[]{:S(2)}, u32[]{:S(2)}) collective-permute-start(bf16[2,192,384]{2,1,0:T(8,128)(2,1)S(1)} %maximum_select_fusion.13), channel_id=1, source_target_pairs={{0,8},{2,10},{4,12},{6,14},{8,0},{10,2},{12,4},{14,6},{16,24},{18,... | collective-permute-start | bytes 884744 | tf_op jit(solution)/shard_map/ppermute | solution.py:366
  31.4 14.1 %copy-start.29 = (bf16[1,1,192,256]{3,2,0,1:T(8,128)(2,1)S(1)}, bf16[1,1,192,256]{3,2,0,1:T(8,128)(2,1)}, u32[]{:S(2)}) copy-start(bf16[1,1,192,256]{3,2,0,1:T(8,128)(2,1)} %copy-done.28) | copy-start | bytes 294916
  31.5 15.0 %copy-start.26 = (bf16[1,1,192,384]{3,2,0,1:T(8,128)(2,1)S(1)}, bf16[1,1,192,384]{3,2,0,1:T(8,128)(2,1)}, u32[]{:S(2)}) copy-start(bf16[1,1,192,384]{3,2,0,1:T(8,128)(2,1)} %copy-done.25) | copy-start | bytes 442372
  38.3 9.5 %copy-start.19 = (bf16[2,192,256]{2,1,0:T(8,128)(2,1)}, bf16[2,192,256]{2,1,0:T(8,128)(2,1)S(1)}, u32[]{:S(2)}) copy-start(bf16[2,192,256]{2,1,0:T(8,128)(2,1)S(1)} %collective-permute-done.1) | copy-start | bytes 589828
  38.3 12.5 %collective-permute-start.2 = (bf16[2,2,192,256]{3,2,0,1:T(8,128)(2,1)S(1)}, bf16[2,2,192,256]{3,2,0,1:T(8,128)(2,1)S(1)}, u32[]{:S(2)}, u32[]{:S(2)}) collective-permute-start(bf16[2,2,192,256]{3,2,0,1:T(8,128)(2,1)S(1)} %maximum_select_fusion.11), channel_id=1, source_target_pairs={{0,4},{2,6},{4,0},{6,2},{8,12},{10,14},{12,8},{14,10},{16,20},{18,... | collective-permute-start | bytes 1179656 | tf_op jit(solution)/shard_map/ppermute | solution.py:366
  44.0 21.1 %collective-permute-start.5 = (bf16[2,2,192,384]{3,2,0,1:T(8,128)(2,1)S(1)}, bf16[2,2,192,384]{3,2,0,1:T(8,128)(2,1)S(1)}, u32[]{:S(2)}, u32[]{:S(2)}) collective-permute-start(bf16[2,2,192,384]{3,2,0,1:T(8,128)(2,1)S(1)} %maximum_select_fusion.9), channel_id=1, source_target_pairs={{0,2},{2,0},{4,6},{6,4},{8,10},{10,8},{12,14},{14,12},{16,18},{18,... | collective-permute-start | bytes 1769480 | tf_op jit(solution)/shard_map/ppermute | solution.py:366
  50.8 14.2 %copy-start.23 = (bf16[2,2,192,256]{3,2,0,1:T(8,128)(2,1)}, bf16[2,2,192,256]{3,2,0,1:T(8,128)(2,1)S(1)}, u32[]{:S(2)}) copy-start(bf16[2,2,192,256]{3,2,0,1:T(8,128)(2,1)S(1)} %collective-permute-done.2) | copy-start | bytes 1179652
  65.0 36.4 %copy-start.15 = (bf16[2,2,192,384]{3,2,0,1:T(8,128)(2,1)}, bf16[2,2,192,384]{3,2,0,1:T(8,128)(2,1)S(1)}, u32[]{:S(2)}) copy-start(bf16[2,2,192,384]{3,2,0,1:T(8,128)(2,1)S(1)} %collective-permute-done.5) | copy-start | bytes 1769476
  101.4 7.1 %copy-start.20 = (bf16[2,192,256]{2,1,0:T(8,128)(2,1)S(1)}, bf16[2,192,256]{2,1,0:T(8,128)(2,1)}, u32[]{:S(2)}) copy-start(bf16[2,192,256]{2,1,0:T(8,128)(2,1)} %copy-done.19) | copy-start | bytes 589828
  101.4 7.1 %copy-start.22 = (bf16[2,1,1,192,256]{4,3,0,1,2:T(8,128)(2,1)S(1)}, bf16[2,1,1,192,256]{4,3,0,1,2:T(8,128)(2,1)}, u32[]{:S(2)}) copy-start(bf16[2,1,1,192,256]{4,3,0,1,2:T(8,128)(2,1)} %copy-done.21) | copy-start | bytes 589828
  108.2 9.8 %collective-permute-start.6 = (bf16[1024,1024]{1,0:T(8,128)(2,1)}, bf16[1024,1024]{1,0:T(8,128)(2,1)}, u32[]{:S(2)}, u32[]{:S(2)}) collective-permute-start(bf16[1024,1024]{1,0:T(8,128)(2,1)} %get-tuple-element.70), channel_id=1, source_target_pairs={{0,1},{1,0},{2,3},{3,2},{4,5},{5,4},{6,7},{7,6},{8,9},{9,8},{10,11... | collective-permute-start | bytes 6291464 | tf_op jit(solution)/shard_map/ppermute | solution.py:350
  108.7 48.2 %collective-permute-start.7 = (bf16[2,2,2,192,256]{4,3,0,1,2:T(8,128)(2,1)}, bf16[2,2,2,192,256]{4,3,0,1,2:T(8,128)(2,1)}, u32[]{:S(2)}, u32[]{:S(2)}) collective-permute-start(bf16[2,2,2,192,256]{4,3,0,1,2:T(8,128)(2,1)} %maximum_select_fusion.6), channel_id=1, source_target_pairs={{0,2},{2,0},{4,6},{6,4},{8,10},{10,8},{12,14},{14,12},{16,18},{18,... | collective-permute-start | bytes 2359304 | tf_op jit(solution)/shard_map/ppermute | solution.py:366
  110.3 46.6 %collective-permute-start.8 = (bf16[2,2,2,192,384]{4,3,0,1,2:T(8,128)(2,1)}, bf16[2,2,2,192,384]{4,3,0,1,2:T(8,128)(2,1)}, u32[]{:S(2)}, u32[]{:S(2)}) collective-permute-start(bf16[2,2,2,192,384]{4,3,0,1,2:T(8,128)(2,1)} %maximum_select_fusion.4), channel_id=1, source_target_pairs={{0,4},{2,6},{4,0},{6,2},{8,12},{10,14},{12,8},{14,10},{16,20},{18,... | collective-permute-start | bytes 3538952 | tf_op jit(solution)/shard_map/ppermute | solution.py:366
  162.6 5.5 %collective-permute-start.9 = (bf16[1024,640]{1,0:T(8,128)(2,1)S(1)}, bf16[1024,640]{1,0:T(8,128)(2,1)S(1)}, u32[]{:S(2)}, u32[]{:S(2)}) collective-permute-start(bf16[1024,640]{1,0:T(8,128)(2,1)S(1)} %copy-done.46), channel_id=1, source_target_pairs={{0,1},{1,0},{2,3},{3,2},{4,5},{5,4},{6,7},{7,6},{8,9},{9,8},{10,11... | collective-permute-start | bytes 3932168 | tf_op jit(solution)/shard_map/ppermute | solution.py:350
  164.8 18.6 %collective-permute-start.10 = (bf16[3072,640]{1,0:T(8,128)(2,1)}, bf16[3072,640]{1,0:T(8,128)(2,1)}, u32[]{:S(2)}, u32[]{:S(2)}) collective-permute-start(bf16[3072,640]{1,0:T(8,128)(2,1)} %pad_maximum_fusion.wd_mine), channel_id=1, source_target_pairs={{0,1},{1,0},{2,3},{3,2},{4,5},{5,4},{6,7},{7,6},{8,9},{9,8},{10,11... | collective-permute-start | bytes 11796488 | tf_op jit(solution)/shard_map/ppermute | solution.py:350
  296.8 16.9 %collective-permute-start.12 = (bf16[1152,1536]{1,0:T(8,128)(2,1)}, bf16[1152,1536]{1,0:T(8,128)(2,1)}, u32[]{:S(2)}, u32[]{:S(2)}) collective-permute-start(bf16[1152,1536]{1,0:T(8,128)(2,1)} %get-tuple-element.81), channel_id=1, source_target_pairs={{0,1},{1,0},{2,3},{3,2},{4,5},{5,4},{6,7},{7,6},{8,9},{9,8},{10,11... | collective-permute-start | bytes 10616840 | tf_op jit(solution)/shard_map/ppermute | solution.py:350
  297.1 18.9 %collective-permute-start.11 = (bf16[1152,1536]{1,0:T(8,128)(2,1)}, bf16[1152,1536]{1,0:T(8,128)(2,1)S(1)}, u32[]{:S(2)}, u32[]{:S(2)}) collective-permute-start(bf16[1152,1536]{1,0:T(8,128)(2,1)} %get-tuple-element.79), channel_id=1, source_target_pairs={{0,1},{1,0},{2,3},{3,2},{4,5},{5,4},{6,7},{7,6},{8,9},{9,8},{10,11... | collective-permute-start | bytes 10616840 | tf_op jit(solution)/shard_map/ppermute | solution.py:350
  297.4 33.3 %collective-permute-start.14 = (bf16[3072,640]{1,0:T(8,128)(2,1)}, bf16[3072,640]{1,0:T(8,128)(2,1)S(1)}, u32[]{:S(2)}, u32[]{:S(2)}) collective-permute-start(bf16[3072,640]{1,0:T(8,128)(2,1)} %get-tuple-element.84), channel_id=1, source_target_pairs={{0,1},{1,0},{2,3},{3,2},{4,5},{5,4},{6,7},{7,6},{8,9},{9,8},{10,11... | collective-permute-start | bytes 11796488 | tf_op jit(solution)/shard_map/ppermute | solution.py:350
  297.6 5.6 %copy-start.13 = (bf16[1152,1536]{1,0:T(8,128)(2,1)S(1)}, bf16[1152,1536]{1,0:T(8,128)(2,1)}, u32[]{:S(2)}) copy-start(bf16[1152,1536]{1,0:T(8,128)(2,1)} %get-tuple-element.80) | copy-start | bytes 10616836
  309.7 10.1 %copy-start.1 = (f32[1024,1152]{1,0:T(8,128)}, f32[1024,1152]{1,0:T(8,128)S(1)}, u32[]{:S(2)}) copy-start(f32[1024,1152]{1,0:T(8,128)S(1)} %subtract_add_fusion) | copy-start | bytes 14155780
  323.3 9.5 %collective-permute-start.13 = (bf16[1024,640]{1,0:T(8,128)(2,1)S(1)}, bf16[1024,640]{1,0:T(8,128)(2,1)S(1)}, u32[]{:S(2)}, u32[]{:S(2)}) collective-permute-start(bf16[1024,640]{1,0:T(8,128)(2,1)S(1)} %convolution_convert_fusion), channel_id=1, source_target_pairs={{0,1},{1,0},{2,3},{3,2},{4,5},{5,4},{6,7},{7,6},{8,9},{9,8},{10,11... | collective-permute-start | bytes 3932168 | tf_op jit(solution)/shard_map/ppermute | solution.py:350
  326.9 41.1 %collective-permute-start.15 = (bf16[2,2,2,72,1536]{4,3,0,2,1:T(8,128)(2,1)}, bf16[2,2,2,72,1536]{4,3,0,2,1:T(8,128)(2,1)}, u32[]{:S(2)}, u32[]{:S(2)}) collective-permute-start(bf16[2,2,2,72,1536]{4,3,0,2,1:T(8,128)(2,1)} %fusion.17), channel_id=1, source_target_pairs={{0,2},{2,0},{4,6},{6,4},{8,10},{10,8},{12,14},{14,12},{16,18},{18,... | collective-permute-start | bytes 5308424 | tf_op jit(solution)/shard_map/ppermute | solution.py:366
  328.3 40.8 %collective-permute-start.16 = (bf16[2,2,2,72,1536]{4,3,1,2,0:T(8,128)(2,1)}, bf16[2,2,2,72,1536]{4,3,1,2,0:T(8,128)(2,1)}, u32[]{:S(2)}, u32[]{:S(2)}) collective-permute-start(bf16[2,2,2,72,1536]{4,3,1,2,0:T(8,128)(2,1)} %fusion.18), channel_id=1, source_target_pairs={{0,4},{2,6},{4,0},{6,2},{8,12},{10,14},{12,8},{14,10},{16,20},{18,... | collective-permute-start | bytes 5308424 | tf_op jit(solution)/shard_map/ppermute | solution.py:366
  332.9 44.7 %collective-permute-start.17 = (bf16[2,2,2,192,640]{4,3,1,2,0:T(8,128)(2,1)}, bf16[2,2,2,192,640]{4,3,1,2,0:T(8,128)(2,1)}, u32[]{:S(2)}, u32[]{:S(2)}) collective-permute-start(bf16[2,2,2,192,640]{4,3,1,2,0:T(8,128)(2,1)} %fusion.14), channel_id=1, source_target_pairs={{0,8},{2,10},{4,12},{6,14},{8,0},{10,2},{12,4},{14,6},{16,24},{18,... | collective-permute-start | bytes 5898248 | tf_op jit(solution)/shard_map/ppermute | solution.py:366
  364.8 14.7 %copy-start.9 = (bf16[1024,1152]{1,0:T(8,128)(2,1)S(1)}, bf16[1024,1152]{1,0:T(8,128)(2,1)}, u32[]{:S(2)}) copy-start(bf16[1024,1152]{1,0:T(8,128)(2,1)} %copy-done.8) | copy-start | bytes 7077892
  364.8 14.7 %copy-start.52 = (pred[640]{0:T(1024)(128)(4,1)S(1)}, pred[640]{0:T(1024)(128)(4,1)}, u32[]{:S(2)}) copy-start(pred[640]{0:T(1024)(128)(4,1)} %constant.342.clone.1) | copy-start | bytes 1924
  386.8 11.8 %collective-permute-start.18 = (bf16[1152,640]{1,0:T(8,128)(2,1)S(1)}, bf16[1152,640]{1,0:T(8,128)(2,1)S(1)}, u32[]{:S(2)}, u32[]{:S(2)}) collective-permute-start(bf16[1152,640]{1,0:T(8,128)(2,1)S(1)} %maximum_select_fusion.3), channel_id=1, source_target_pairs={{0,1},{1,0},{2,3},{3,2},{4,5},{5,4},{6,7},{7,6},{8,9},{9,8},{10,11... | collective-permute-start | bytes 4423688 | tf_op jit(solution)/shard_map/ppermute | solution.py:350
  401.9 46.4 %collective-permute-start.21 = (bf16[2,2,192,640]{3,2,1,0:T(8,128)(2,1)}, bf16[2,2,192,640]{3,2,1,0:T(8,128)(2,1)}, u32[]{:S(2)}, u32[]{:S(2)}) collective-permute-start(bf16[2,2,192,640]{3,2,1,0:T(8,128)(2,1)} %copy.86), channel_id=1, source_target_pairs={{0,16},{2,18},{4,20},{6,22},{8,24},{10,26},{12,28},{14,30},{16,0},... | collective-permute-start | bytes 2949128 | tf_op jit(solution)/shard_map/ppermute | solution.py:366
  404.5 43.8 %copy-start.43 = (f32[1,4,2,128]{3,1,2,0:T(4,128)S(1)}, f32[1,4,2,128]{3,1,2,0:T(4,128)}, u32[]{:S(2)}) copy-start(f32[1,4,2,128]{3,1,2,0:T(4,128)} %copy-done.42) | copy-start | bytes 12292
  404.5 39.0 %collective-permute-start.19 = (bf16[2,2,72,1536]{3,2,1,0:T(8,128)(2,1)}, bf16[2,2,72,1536]{3,2,1,0:T(8,128)(2,1)}, u32[]{:S(2)}, u32[]{:S(2)}) collective-permute-start(bf16[2,2,72,1536]{3,2,1,0:T(8,128)(2,1)} %copy.85), channel_id=1, source_target_pairs={{0,4},{2,6},{4,0},{6,2},{8,12},{10,14},{12,8},{14,10},{16,20},{18,... | collective-permute-start | bytes 2654216 | tf_op jit(solution)/shard_map/ppermute | solution.py:366
  405.9 37.6 %collective-permute-start.20 = (bf16[2,2,72,1536]{3,2,1,0:T(8,128)(2,1)}, bf16[2,2,72,1536]{3,2,1,0:T(8,128)(2,1)}, u32[]{:S(2)}, u32[]{:S(2)}) collective-permute-start(bf16[2,2,72,1536]{3,2,1,0:T(8,128)(2,1)} %get-tuple-element.104), channel_id=1, source_target_pairs={{0,2},{2,0},{4,6},{6,4},{8,10},{10,8},{12,14},{14,12},{16,18},{18,... | collective-permute-start | bytes 2654216 | tf_op jit(solution)/shard_map/ppermute | solution.py:366
  406.6 37.0 %collective-permute-start.22 = (bf16[2,2,2,72,640]{4,3,0,2,1:T(8,128)(2,1)}, bf16[2,2,2,72,640]{4,3,0,2,1:T(8,128)(2,1)}, u32[]{:S(2)}, u32[]{:S(2)}) collective-permute-start(bf16[2,2,2,72,640]{4,3,0,2,1:T(8,128)(2,1)} %fusion.34), channel_id=1, source_target_pairs={{0,2},{2,0},{4,6},{6,4},{8,10},{10,8},{12,14},{14,12},{16,18},{18,... | collective-permute-start | bytes 2211848 | tf_op jit(solution)/shard_map/ppermute | solution.py:366
  448.3 11.7 %collective-permute-start.23 = (bf16[1024,1024]{1,0:T(8,128)(2,1)}, bf16[1024,1024]{1,0:T(8,128)(2,1)S(1)}, u32[]{:S(2)}, u32[]{:S(2)}) collective-permute-start(bf16[1024,1024]{1,0:T(8,128)(2,1)} %get-tuple-element.109), channel_id=1, source_target_pairs={{0,1},{1,0},{2,3},{3,2},{4,5},{5,4},{6,7},{7,6},{8,9},{9,8},{10,11... | collective-permute-start | bytes 6291464 | tf_op jit(solution)/shard_map/ppermute | solution.py:350
  451.2 27.5 %collective-permute-start.36 = (bf16[2,72,1536]{2,1,0:T(8,128)(2,1)S(1)}, bf16[2,72,1536]{2,1,0:T(8,128)(2,1)S(1)}, u32[]{:S(2)}, u32[]{:S(2)}) collective-permute-start(bf16[2,72,1536]{2,1,0:T(8,128)(2,1)S(1)} %get-tuple-element.182), channel_id=1, source_target_pairs={{0,16},{2,18},{4,20},{6,22},{8,24},{10,26},{12,28},{14,30},{16,0},... | collective-permute-start | bytes 1327112 | tf_op jit(solution)/shard_map/ppermute | solution.py:366
  452.7 5.2 copy-start.10
  452.7 26.1 %collective-permute-start.35 = (bf16[2,72,1536]{2,1,0:T(8,128)(2,1)S(1)}, bf16[2,72,1536]{2,1,0:T(8,128)(2,1)S(1)}, u32[]{:S(2)}, u32[]{:S(2)}) collective-permute-start(bf16[2,72,1536]{2,1,0:T(8,128)(2,1)S(1)} %get-tuple-element.184), channel_id=1, source_target_pairs={{0,8},{2,10},{4,12},{6,14},{8,0},{10,2},{12,4},{14,6},{16,24},{18,... | collective-permute-start | bytes 1327112 | tf_op jit(solution)/shard_map/ppermute | solution.py:366
  456.4 21.7 %collective-permute-start.34 = (bf16[2,2,72,640]{3,2,1,0:T(8,128)(2,1)S(1)}, bf16[2,2,72,640]{3,2,1,0:T(8,128)(2,1)S(1)}, u32[]{:S(2)}, u32[]{:S(2)}) collective-permute-start(bf16[2,2,72,640]{3,2,1,0:T(8,128)(2,1)S(1)} %copy.102), channel_id=1, source_target_pairs={{0,4},{2,6},{4,0},{6,2},{8,12},{10,14},{12,8},{14,10},{16,20},{18,... | collective-permute-start | bytes 1105928 | tf_op jit(solution)/shard_map/ppermute | solution.py:366
  459.3 19.5 %collective-permute-start.33 = (bf16[2,192,640]{2,1,0:T(8,128)(2,1)S(1)}, bf16[2,192,640]{2,1,0:T(8,128)(2,1)S(1)}, u32[]{:S(2)}, u32[]{:S(2)}) collective-permute-start(bf16[2,192,640]{2,1,0:T(8,128)(2,1)S(1)} %get-tuple-element.180), channel_id=1, source_target_pairs={{0,2},{2,0},{4,6},{6,4},{8,10},{10,8},{12,14},{14,12},{16,18},{18,... | collective-permute-start | bytes 1474568 | tf_op jit(solution)/shard_map/ppermute | solution.py:366
  466.7 6.5 %slice-start = ((s8[4718592]{0:T(1024)(128)(4,1)}), s8[4194304]{0:T(1024)(128)(4,1)S(1)}, s32[]{:S(2)}) async-start(s8[4718592]{0:T(1024)(128)(4,1)} %bitcast.323), calls=%async_computation.2 | async-start | bytes 8388608
  469.7 6.2 %collective-permute-start.24 = (bf16[1152,1024]{1,0:T(8,128)(2,1)S(1)}, bf16[1152,1024]{1,0:T(8,128)(2,1)S(1)}, u32[]{:S(2)}, u32[]{:S(2)}) collective-permute-start(bf16[1152,1024]{1,0:T(8,128)(2,1)S(1)} %add_convert_fusion), channel_id=1, source_target_pairs={{0,1},{1,0},{2,3},{3,2},{4,5},{5,4},{6,7},{7,6},{8,9},{9,8},{10,11... | collective-permute-start | bytes 7077896 | tf_op jit(solution)/shard_map/ppermute | solution.py:350
  476.4 15.8 %collective-permute-start.25 = (bf16[2,2,2,72,512]{4,3,0,2,1:T(8,128)(2,1)S(1)}, bf16[2,2,2,72,512]{4,3,0,2,1:T(8,128)(2,1)S(1)}, u32[]{:S(2)}, u32[]{:S(2)}) collective-permute-start(bf16[2,2,2,72,512]{4,3,0,2,1:T(8,128)(2,1)S(1)} %fusion.37), channel_id=1, source_target_pairs={{0,2},{2,0},{4,6},{6,4},{8,10},{10,8},{12,14},{14,12},{16,18},{18,... | collective-permute-start | bytes 1769480 | tf_op jit(solution)/shard_map/ppermute | solution.py:366
  478.1 16.3 %collective-permute-start.29 = (bf16[2,2,2,72,512]{4,3,1,2,0:T(8,128)(2,1)S(1)}, bf16[2,2,2,72,512]{4,3,1,2,0:T(8,128)(2,1)S(1)}, u32[]{:S(2)}, u32[]{:S(2)}) collective-permute-start(bf16[2,2,2,72,512]{4,3,1,2,0:T(8,128)(2,1)S(1)} %fusion.38), channel_id=1, source_target_pairs={{0,4},{2,6},{4,0},{6,2},{8,12},{10,14},{12,8},{14,10},{16,20},{18,... | collective-permute-start | bytes 1769480 | tf_op jit(solution)/shard_map/ppermute | solution.py:366
  478.9 19.5 %collective-permute-start.40 = (bf16[72,1536]{1,0:T(8,128)(2,1)S(1)}, bf16[72,1536]{1,0:T(8,128)(2,1)S(1)}, u32[]{:S(2)}, u32[]{:S(2)}) collective-permute-start(bf16[72,1536]{1,0:T(8,128)(2,1)S(1)} %fusion.70), channel_id=1, source_target_pairs={{0,8},{2,10},{4,12},{6,14},{8,0},{10,2},{12,4},{14,6},{16,24},{18,... | collective-permute-start | bytes 663560 | tf_op jit(solution)/shard_map/ppermute | solution.py:366
  479.1 19.3 %collective-permute-start.39 = (bf16[72,1536]{1,0:T(8,128)(2,1)S(1)}, bf16[72,1536]{1,0:T(8,128)(2,1)S(1)}, u32[]{:S(2)}, u32[]{:S(2)}) collective-permute-start(bf16[72,1536]{1,0:T(8,128)(2,1)S(1)} %fusion.69), channel_id=1, source_target_pairs={{0,16},{2,18},{4,20},{6,22},{8,24},{10,26},{12,28},{14,30},{16,0},... | collective-permute-start | bytes 663560 | tf_op jit(solution)/shard_map/ppermute | solution.py:366
  481.8 17.0 %collective-permute-start.37 = (bf16[192,640]{1,0:T(8,128)(2,1)S(1)}, bf16[192,640]{1,0:T(8,128)(2,1)S(1)}, u32[]{:S(2)}, u32[]{:S(2)}) collective-permute-start(bf16[192,640]{1,0:T(8,128)(2,1)S(1)} %get-tuple-element.208), channel_id=1, source_target_pairs={{0,4},{2,6},{4,0},{6,2},{8,12},{10,14},{12,8},{14,10},{16,20},{18,... | collective-permute-start | bytes 737288 | tf_op jit(solution)/shard_map/ppermute | solution.py:366
  492.2 6.2 %collective-permute-start.38 = (bf16[2,72,640]{2,1,0:T(8,128)(2,1)S(1)}, bf16[2,72,640]{2,1,0:T(8,128)(2,1)S(1)}, u32[]{:S(2)}, u32[]{:S(2)}) collective-permute-start(bf16[2,72,640]{2,1,0:T(8,128)(2,1)S(1)} %get-tuple-element.210), channel_id=1, source_target_pairs={{0,8},{2,10},{4,12},{6,14},{8,0},{10,2},{12,4},{14,6},{16,24},{18,... | collective-permute-start | bytes 552968 | tf_op jit(solution)/shard_map/ppermute | solution.py:366
  494.5 15.3 %collective-permute-start.30 = (bf16[2,2,72,512]{3,2,1,0:T(8,128)(2,1)S(1)}, bf16[2,2,72,512]{3,2,1,0:T(8,128)(2,1)S(1)}, u32[]{:S(2)}, u32[]{:S(2)}) collective-permute-start(bf16[2,2,72,512]{3,2,1,0:T(8,128)(2,1)S(1)} %get-tuple-element.202), channel_id=1, source_target_pairs={{0,2},{2,0},{4,6},{6,4},{8,10},{10,8},{12,14},{14,12},{16,18},{18,... | collective-permute-start | bytes 884744 | tf_op jit(solution)/shard_map/ppermute | solution.py:366
  498.9 11.4 %collective-permute-start.41 = (bf16[72,640]{1,0:T(8,128)(2,1)S(1)}, bf16[72,640]{1,0:T(8,128)(2,1)S(1)}, u32[]{:S(2)}, u32[]{:S(2)}) collective-permute-start(bf16[72,640]{1,0:T(8,128)(2,1)S(1)} %get-tuple-element.215), channel_id=1, source_target_pairs={{0,16},{2,18},{4,20},{6,22},{8,24},{10,26},{12,28},{14,30},{16,0},... | collective-permute-start | bytes 276488 | tf_op jit(solution)/shard_map/ppermute | solution.py:366
  499.7 8.0 %collective-permute-start.26 = (bf16[2,2,72,512]{3,2,1,0:T(8,128)(2,1)S(1)}, bf16[2,2,72,512]{3,2,1,0:T(8,128)(2,1)S(1)}, u32[]{:S(2)}, u32[]{:S(2)}) collective-permute-start(bf16[2,2,72,512]{3,2,1,0:T(8,128)(2,1)S(1)} %copy.92), channel_id=1, source_target_pairs={{0,4},{2,6},{4,0},{6,2},{8,12},{10,14},{12,8},{14,10},{16,20},{18,... | collective-permute-start | bytes 884744 | tf_op jit(solution)/shard_map/ppermute | solution.py:366
  507.8 10.0 %collective-permute-start.27 = (bf16[2,72,512]{2,1,0:T(8,128)(2,1)S(1)}, bf16[2,72,512]{2,1,0:T(8,128)(2,1)S(1)}, u32[]{:S(2)}, u32[]{:S(2)}) collective-permute-start(bf16[2,72,512]{2,1,0:T(8,128)(2,1)S(1)} %get-tuple-element.212), channel_id=1, source_target_pairs={{0,8},{2,10},{4,12},{6,14},{8,0},{10,2},{12,4},{14,6},{16,24},{18,... | collective-permute-start | bytes 442376 | tf_op jit(solution)/shard_map/ppermute | solution.py:366
  509.8 7.8 %collective-permute-start.31 = (bf16[2,72,512]{2,1,0:T(8,128)(2,1)S(1)}, bf16[2,72,512]{2,1,0:T(8,128)(2,1)S(1)}, u32[]{:S(2)}, u32[]{:S(2)}) collective-permute-start(bf16[2,72,512]{2,1,0:T(8,128)(2,1)S(1)} %get-tuple-element.214), channel_id=1, source_target_pairs={{0,16},{2,18},{4,20},{6,22},{8,24},{10,26},{12,28},{14,30},{16,0},... | collective-permute-start | bytes 442376 | tf_op jit(solution)/shard_map/ppermute | solution.py:366
  517.7 4.4 collective-permute-start.32
  517.8 5.7 %collective-permute-start.28 = (bf16[72,512]{1,0:T(8,128)(2,1)S(1)}, bf16[72,512]{1,0:T(8,128)(2,1)S(1)}, u32[]{:S(2)}, u32[]{:S(2)}) collective-permute-start(bf16[72,512]{1,0:T(8,128)(2,1)S(1)} %fusion.85), channel_id=1, source_target_pairs={{0,16},{2,18},{4,20},{6,22},{8,24},{10,26},{12,28},{14,30},{16,0},... | collective-permute-start | bytes 221192 | tf_op jit(solution)/shard_map/ppermute | solution.py:366
  (39 other events, 101.4 us)
Sparse Core Ops, SparseCore 0:
  11.5 84.8 all-gather.2
  99.8 105.1 all-gather.4

commit v9 on v8

--- a/solution.py
+++ b/solution.py
@@ -514,8 +514,8 @@
     )
     lins = back(0, ())
 
-    lins, grad_low, wide_sum.got, down_sum.got = tie((lins, grad_low, wide_sum.got, down_sum.got))
-    low = widen(grad_low[:, : D // 2]), widen(grad_low[:, D // 2 :])
+    lins, grad_low = tie((lins, grad_low))
+    parts_of = lambda u: (widen(u[:, : D // 2]), widen(u[:, D // 2 :]))
 
     def grad_out(columns):
         a, b = [
@@ -524,9 +524,13 @@
         ]
         return pick(jnp.concatenate([a, b], 0), jnp.concatenate([b, a], 0))
 
+    out_theirs_grad = grad_out(pick(*parts_of(grad_low)[::-1]))
+    out_theirs_grad, grad_low, wide_sum.got, down_sum.got = tie(
+        (out_theirs_grad, grad_low, wide_sum.got, down_sum.got)
+    )
     wide_sum.prepare(1)
     down_sum.prepare(1)
-    out_sum = Halving([(grad_out(pick(*low)), swap(grad_out(pick(*low[::-1]))), ORDERS[0])])
+    out_sum = Halving([(grad_out(pick(*parts_of(grad_low))), swap(out_theirs_grad), ORDERS[0])])
     out_sum.prepare(0)
     lins, wide_sum.send, down_sum.send, out_sum.send = tie(
         (lins, wide_sum.send, down_sum.send, out_sum.send)

time: 541 us -> 536 us (level)
    dynamic_slice x12, local copies, waits for them, and re-layouts: 6.5 us -> 12.8 us  [prepare(): at = lambda u, i: lax.dynamic_index_in_dim(u, i, axis, keepdims=False)]
    unnamed x118 -> x116, local copies, waits for them, and re-layouts: 14.1 us -> 10 us
  transfers between devices with their start and end apart: 44 -> 44, of which waited for: 19 -> 17; matrix products, arithmetic and copies ran while one was open for 20% -> 22% of each run, Pallas kernels for 21% -> 21%
where the time goes in v9:
time: 536 us; the launch traced here: 527 us
  Pallas kernels  201 us (38%)
  waiting for transfers between devices  134 us (25%)
  other arithmetic  68.2 us (13%)
  starting transfers between devices  40.9 us (8%)
  local copies, waits for them, and re-layouts  37.9 us (7%)
  matrix products  29.1 us (5%)
  between operations  15.4 us (3%)
    pallas_call x1, Pallas kernels, mlp(): pl.pallas_call(mlp_body, grid_spec=pltpu.PrefetchScalarGridSpec(num_scala...  91.8 us
    ppermute x32, waiting for transfers between devices, exchange(): lax.ppermute(a, 'dp', [(i, i ^ 1 << bit) for i in range(lax.axis_size('dp...  82.6 us
    pallas_call x2, Pallas kernels, attend_back(): pl.pallas_call(bwd_body, grid_spec=pltpu.PrefetchScalarGridSpec(num_scala...  57 us
    all_gather x2, waiting for transfers between devices, fetch(): lax.all_gather(w, BOTH, axis=0, tiled=True)  51.5 us
    pallas_call x1, Pallas kernels, attend(): pl.pallas_call(fwd_body, grid_spec=pltpu.PrefetchScalarGridSpec(num_scala...  38.9 us
    ppermute x32, starting transfers between devices, exchange(): lax.ppermute(a, 'dp', [(i, i ^ 1 << bit) for i in range(lax.axis_size('dp...  38.8 us
    convert_element_type x29, other arithmetic, prepare(): add(at(self.stay[p], i), at(self.got[p], i)).astype(self.kind)  26.6 us
    pallas_call x2, Pallas kernels, project(): pl.pallas_call(project_body, grid_spec=pltpu.PrefetchScalarGridSpec(num_s...  13.6 us
  transfers between devices with their start and end apart: 44, of which 17 were waited for; matrix products, arithmetic and copies ran while one was open for 22% of the time, Pallas kernels for 21%

profile of v9, /device:TPU:0, one launch (start us, length us, event | category | flops | bytes accessed | tf_op | source)
XLA Modules:
  0.0 527.0 jit_solution(15362105430415350271)
XLA Ops:
  8.1 1.8 concatenate.186
  10.0 2.0 pad_maximum_fusion.1
  12.0 4.1 collective-permute-start.3
  16.4 3.1 fusion.43
  20.1 9.1 %collective-permute-done = bf16[192,256]{1,0:T(8,128)(2,1)S(1)} collective-permute-done((bf16[192,256]{1,0:T(8,128)(2,1)S(1)}, bf16[192,256]{1,0:T(8,128)(2,1)S(1)}, u32[]{:S(2)}, u32[]{:S(2)}) %collective-permute-start) | collective-permute-done | bytes 98336 | tf_op jit(solution)/shard_map/ppermute | solution.py:366
  31.5 6.8 %collective-permute-done.1 = bf16[2,192,256]{2,1,0:T(8,128)(2,1)S(1)} collective-permute-done((bf16[2,192,256]{2,1,0:T(8,128)(2,1)S(1)}, bf16[2,192,256]{2,1,0:T(8,128)(2,1)S(1)}, u32[]{:S(2)}, u32[]{:S(2)}) %collective-permute-start.1) | collective-permute-done | bytes 196640 | tf_op jit(solution)/shard_map/ppermute | solution.py:366
  38.3 1.8 collective-permute-start.2
  40.2 3.7 collective-permute-done.4
  47.8 3.0 collective-permute-done.2
  51.8 13.2 %collective-permute-done.5 = bf16[2,2,192,384]{3,2,0,1:T(8,128)(2,1)S(1)} collective-permute-done((bf16[2,2,192,384]{3,2,0,1:T(8,128)(2,1)S(1)}, bf16[2,2,192,384]{3,2,0,1:T(8,128)(2,1)S(1)}, u32[]{:S(2)}, u32[]{:S(2)}) %collective-permute-start.5) | collective-permute-done | bytes 589856 | tf_op jit(solution)/shard_map/ppermute | solution.py:366
  66.3 30.0 %all-gather.3.cloned.1.call-done = bf16[2304,1600]{1,0:T(8,128)(2,1)} async-done(((bf16[72,1600]{1,0:T(8,128)(2,1)}), bf16[2304,1600]{1,0:T(8,128)(2,1)}) %all-gather.3.cloned.1.call-update) | async-done | bytes 7372816 | tf_op jit(solution)/shard_map/all_gather | solution.py:361
  96.3 2.2 convert_reduce_fusion
  99.4 2.0 fusion.2.n1
  101.4 6.8 %project.3 = (bf16[1024,1024]{1,0:T(8,128)(2,1)}, bf16[1152,1024]{1,0:T(8,128)(2,1)}) custom-call(s32[1]{0:T(128)} %bitcast.me, bf16[1024,1152]{1,0:T(8,128)(2,1)} %fusion.2.n1, bf16[16,2,72,1600]{3,2,1,0:T(8,128)(2,1)} %bitcast.352, f32[1024,128]{1,0:T(8,128)} %get-tuple-element.230.cosine, f32[1024,128]{1,0:T(8,128)} %get-tuple-element.229.sine), custom_call_target="tpu_custom_call" | custom-call | flops 3000000000 | bytes 12000000 | tf_op jit(solution)/shard_map/project/pallas_call | solution.py:66
  111.2 6.8 %project.2 = (bf16[1024,1024]{1,0:T(8,128)(2,1)}, bf16[1152,1024]{1,0:T(8,128)(2,1)}) custom-call(s32[1]{0:T(128)} %bitcast.me, bf16[1024,1152]{1,0:T(8,128)(2,1)} %fusion.2.n1, bf16[16,2,72,1600]{3,2,1,0:T(8,128)(2,1)} %bitcast.353, f32[1024,128]{1,0:T(8,128)} %get-tuple-element.230.cosine, f32[1024,128]{1,0:T(8,128)} %get-tuple-element.229.sine), custom_call_target="tpu_custom_call" | custom-call | flops 3000000000 | bytes 12000000 | tf_op jit(solution)/shard_map/project/pallas_call | solution.py:66
  118.0 38.9 %attend.1 = (bf16[1024,640]{1,0:T(8,128)(2,1)}, bf16[1024,640]{1,0:T(8,128)(2,1)}, f32[2048,128]{1,0:T(8,128)}) custom-call(s32[1]{0:T(128)} %bitcast.me, bf16[1024,1024]{1,0:T(8,128)(2,1)} %get-tuple-element.71.mine, bf16[1024,1024]{1,0:T(8,128)(2,1)} %collective-permute-done.6.got), custom_call_target="tpu_custom_call" | custom-call | flops 24000000000 | bytes 20000000 | tf_op jit(solution)/shard_map/attend/pallas_call | solution.py:200
  156.9 2.0 maximum_select_fusion
  159.2 2.1 maximum_select_fusion.1
  162.6 2.2 pad_maximum_fusion.wd_mine
  165.4 2.1 slice_bitcast_fusion
  168.1 2.1 fusion.62
  171.7 2.4 multiply_reduce_fusion.2
  174.1 2.1 copy-done
  176.6 2.6 copy.70.n2t
  179.2 4.2 multiply_convert_fusion.n2
  183.4 21.4 %all-gather.5.cloned.1.call-done = bf16[2304,3072]{1,0:T(8,128)(2,1)} async-done(((bf16[72,3072]{1,0:T(8,128)(2,1)}), bf16[2304,3072]{1,0:T(8,128)(2,1)}) %all-gather.5.cloned.1.call-update) | async-done | bytes 14155792 | tf_op jit(solution)/shard_map/all_gather | solution.py:361
  204.8 91.8 %mlp.1 = (bf16[1024,1152]{1,0:T(8,128)(2,1)}, f32[1024,1152]{1,0:T(8,128)}, bf16[1152,1536]{1,0:T(8,128)(2,1)}, bf16[1152,1536]{1,0:T(8,128)(2,1)}, bf16[1152,15...) custom-call(s32[1]{0:T(128)} %bitcast.me, ...), custom_call_target="tpu_custom_call" | custom-call | flops 65000001536 | bytes 60000000 | tf_op jit(solution)/shard_map/mlp/pallas_call | solution.py:312
  297.4 2.7 constant_dynamic-slice_fusion.13
  301.0 4.5 multiply_reduce_fusion
  305.4 2.5 constant_dynamic-slice_fusion.15
  310.7 1.9 subtract_add_fusion
  312.6 4.0 constant_dynamic-slice_fusion.14
  317.0 1.7 fusion.18
  318.7 1.7 fusion.17
  321.7 2.2 convolution_convert_fusion
  326.3 1.7 add_convert_fusion.4
  328.1 1.7 add_convert_fusion.5
  329.8 3.3 convolution_convert_fusion.1.do_mine
  333.5 1.9 fusion.14
  336.9 28.6 %attend_back.2 = (bf16[1024,1024]{1,0:T(8,128)(2,1)}, bf16[1024,1024]{1,0:T(8,128)(2,1)}) custom-call(s32[1]{0:T(128)} %bitcast.me, bf16[1024,1024]{1,0:T(8,128)(2,1)} %get-tuple-element.71.mine, bf16[1024,1024]{1,0:T(8,128)(2,1)} %collective-permute-done.6.got, bf16[1024,640]{1,0:T(8,128)(2,1)} %get-tuple-element.73.o_mine, ...), custom_call_target="tpu_custom_call" | custom-call | flops 12999999488 | bytes 20000000 | tf_op jit(solution)/shard_map/attend_back/pallas_call | solution.py:226
  365.6 2.1 slice.92
  367.7 2.7 fusion.89
  372.5 8.2 %collective-permute-done.17 = bf16[2,2,2,192,640]{4,3,1,2,0:T(8,128)(2,1)} collective-permute-done((bf16[2,2,2,192,640]{4,3,1,2,0:T(8,128)(2,1)}, bf16[2,2,2,192,640]{4,3,1,2,0:T(8,128)(2,1)}, u32[]{:S(2)}, u32[]{:S(2)}) %collective-permute-start.17) | collective-permute-done | bytes 1966112 | tf_op jit(solution)/shard_map/ppermute | solution.py:366
  384.1 3.0 fusion.15
  389.5 3.0 fusion.19
  392.4 1.9 fusion.20
  403.9 28.3 %attend_back.3 = (bf16[1024,1024]{1,0:T(8,128)(2,1)}, bf16[1024,1024]{1,0:T(8,128)(2,1)}) custom-call(s32[1]{0:T(128)} %bitcast.me, bf16[1024,1024]{1,0:T(8,128)(2,1)} %get-tuple-element.71.mine, bf16[1024,1024]{1,0:T(8,128)(2,1)} %collective-permute-done.6.got, ...), custom_call_target="tpu_custom_call", output_to_operand_aliasing={{0}: (10, {}), {1}: (11, {})} | custom-call | flops 12999999488 | bytes 20000000 | tf_op jit(solution)/shard_map/attend_back/pallas_call | solution.py:226
  432.2 7.2 %collective-permute-done.22 = bf16[2,2,2,72,640]{4,3,0,2,1:T(8,128)(2,1)} collective-permute-done((bf16[2,2,2,72,640]{4,3,0,2,1:T(8,128)(2,1)}, bf16[2,2,2,72,640]{4,3,0,2,1:T(8,128)(2,1)}, u32[]{:S(2)}, u32[]{:S(2)}) %collective-permute-start.22) | collective-permute-done | bytes 737312 | tf_op jit(solution)/shard_map/ppermute | solution.py:366
  439.4 4.6 collective-permute-done.21
  448.4 2.3 collective-permute-start.35
  455.8 2.9 fusion.114
  458.8 3.5 fusion.9
  462.3 3.0 add_convert_fusion
  465.4 3.0 add_convert_fusion.1
  468.9 2.7 fusion.6
  474.7 2.6 collective-permute-start.39
  479.4 8.4 %collective-permute-done.25 = bf16[2,2,2,72,512]{4,3,0,2,1:T(8,128)(2,1)S(1)} collective-permute-done((bf16[2,2,2,72,512]{4,3,0,2,1:T(8,128)(2,1)S(1)}, bf16[2,2,2,72,512]{4,3,0,2,1:T(8,128)(2,1)S(1)}, u32[]{:S(2)}, u32[]{:S(2)}) %collective-permute-start.25) | collective-permute-done | bytes 589856 | tf_op jit(solution)/shard_map/ppermute | solution.py:366
  488.1 1.9 collective-permute-done.29
  490.9 3.1 collective-permute-done.38
  498.2 5.1 collective-permute-done.26
  503.4 2.0 collective-permute-start.27
  507.5 5.9 %collective-permute-done.31 = bf16[2,72,512]{2,1,0:T(8,128)(2,1)S(1)} collective-permute-done((bf16[2,72,512]{2,1,0:T(8,128)(2,1)S(1)}, bf16[2,72,512]{2,1,0:T(8,128)(2,1)S(1)}, u32[]{:S(2)}, u32[]{:S(2)}) %collective-permute-start.31) | collective-permute-done | bytes 147488 | tf_op jit(solution)/shard_map/ppermute | solution.py:366
  513.5 2.3 collective-permute-start.28
  515.8 2.0 collective-permute-done.32
  (282 shorter events, 71.0 us)
Async XLA Ops:
  7.2 89.2 %all-gather.3.cloned.1.call-start = ((), (), s32[]{:S(2)}) async-start(), calls=%async_computation | async-start | bytes 7907328 | tf_op jit(solution)/shard_map/all_gather | solution.py:361
  9.9 9.6 %copy-start.2 = (bf16[2,1,512,1152]{3,2,1,0:T(8,128)(2,1)S(1)}, bf16[2,1,512,1152]{3,2,1,0:T(8,128)(2,1)}, u32[]{:S(2)}) copy-start(bf16[2,1,512,1152]{3,2,1,0:T(8,128)(2,1)} %param.11) | copy-start | bytes 7077892
  9.9 194.9 %all-gather.5.cloned.1.call-start = ((), (), s32[]{:S(2)}) async-start(), calls=%async_computation.1 | async-start | bytes 14598144 | tf_op jit(solution)/shard_map/all_gather | solution.py:361
  12.0 19.4 %copy-start.23 = (bf16[1,1,192,384]{3,2,0,1:T(8,128)(2,1)}, bf16[1,1,192,384]{3,2,0,1:T(8,128)(2,1)S(1)}, u32[]{:S(2)}) copy-start(bf16[1,1,192,384]{3,2,0,1:T(8,128)(2,1)S(1)} %get-tuple-element.221) | copy-start | bytes 442372
  12.0 18.3 %collective-permute-start.3 = (bf16[192,384]{1,0:T(8,128)(2,1)S(1)}, bf16[192,384]{1,0:T(8,128)(2,1)S(1)}, u32[]{:S(2)}, u32[]{:S(2)}) collective-permute-start(bf16[192,384]{1,0:T(8,128)(2,1)S(1)} %get-tuple-element.223), channel_id=1, source_target_pairs={{0,16},{2,18},{4,20},{6,22},{8,24},{10,26},{12,28},{14,30},{16,0},... | collective-permute-start | bytes 442376 | tf_op jit(solution)/shard_map/ppermute | solution.py:366
  16.2 15.2 %copy-start.26 = (bf16[1,1,192,256]{3,2,0,1:T(8,128)(2,1)}, bf16[1,1,192,256]{3,2,0,1:T(8,128)(2,1)S(1)}, u32[]{:S(2)}) copy-start(bf16[1,1,192,256]{3,2,0,1:T(8,128)(2,1)S(1)} %get-tuple-element.224) | copy-start | bytes 294916
  16.2 12.9 %collective-permute-start = (bf16[192,256]{1,0:T(8,128)(2,1)S(1)}, bf16[192,256]{1,0:T(8,128)(2,1)S(1)}, u32[]{:S(2)}, u32[]{:S(2)}) collective-permute-start(bf16[192,256]{1,0:T(8,128)(2,1)S(1)} %get-tuple-element.226), channel_id=1, source_target_pairs={{0,16},{2,18},{4,20},{6,22},{8,24},{10,26},{12,28},{14,30},{16,0},... | collective-permute-start | bytes 294920 | tf_op jit(solution)/shard_map/ppermute | solution.py:366
  20.1 79.3 %copy-start.40 = (f32[1,4,2,128]{3,1,2,0:T(4,128)}, f32[1,4,2,128]{3,1,2,0:T(4,128)S(1)}, u32[]{:S(2)}) copy-start(f32[1,4,2,128]{3,1,2,0:T(4,128)S(1)} %copy.135) | copy-start | bytes 12292
  29.1 14.7 %copy-start.28 = (bf16[192,256]{1,0:T(8,128)(2,1)}, bf16[192,256]{1,0:T(8,128)(2,1)S(1)}, u32[]{:S(2)}) copy-start(bf16[192,256]{1,0:T(8,128)(2,1)S(1)} %collective-permute-done) | copy-start | bytes 294916
  29.2 9.1 %collective-permute-start.1 = (bf16[2,192,256]{2,1,0:T(8,128)(2,1)S(1)}, bf16[2,192,256]{2,1,0:T(8,128)(2,1)S(1)}, u32[]{:S(2)}, u32[]{:S(2)}) collective-permute-start(bf16[2,192,256]{2,1,0:T(8,128)(2,1)S(1)} %maximum_select_fusion.15), channel_id=1, source_target_pairs={{0,8},{2,10},{4,12},{6,14},{8,0},{10,2},{12,4},{14,6},{16,24},{18,... | collective-permute-start | bytes 589832 | tf_op jit(solution)/shard_map/ppermute | solution.py:366
  30.3 15.2 %copy-start.25 = (bf16[192,384]{1,0:T(8,128)(2,1)}, bf16[192,384]{1,0:T(8,128)(2,1)S(1)}, u32[]{:S(2)}) copy-start(bf16[192,384]{1,0:T(8,128)(2,1)S(1)} %collective-permute-done.3) | copy-start | bytes 442372
  30.4 13.5 %collective-permute-start.4 = (bf16[2,192,384]{2,1,0:T(8,128)(2,1)S(1)}, bf16[2,192,384]{2,1,0:T(8,128)(2,1)S(1)}, u32[]{:S(2)}, u32[]{:S(2)}) collective-permute-start(bf16[2,192,384]{2,1,0:T(8,128)(2,1)S(1)} %maximum_select_fusion.13), channel_id=1, source_target_pairs={{0,8},{2,10},{4,12},{6,14},{8,0},{10,2},{12,4},{14,6},{16,24},{18,... | collective-permute-start | bytes 884744 | tf_op jit(solution)/shard_map/ppermute | solution.py:366
  31.4 14.1 %copy-start.27 = (bf16[1,1,192,256]{3,2,0,1:T(8,128)(2,1)S(1)}, bf16[1,1,192,256]{3,2,0,1:T(8,128)(2,1)}, u32[]{:S(2)}) copy-start(bf16[1,1,192,256]{3,2,0,1:T(8,128)(2,1)} %copy-done.26) | copy-start | bytes 294916
  31.5 15.0 %copy-start.24 = (bf16[1,1,192,384]{3,2,0,1:T(8,128)(2,1)S(1)}, bf16[1,1,192,384]{3,2,0,1:T(8,128)(2,1)}, u32[]{:S(2)}) copy-start(bf16[1,1,192,384]{3,2,0,1:T(8,128)(2,1)} %copy-done.23) | copy-start | bytes 442372
  38.3 9.5 %copy-start.17 = (bf16[2,192,256]{2,1,0:T(8,128)(2,1)}, bf16[2,192,256]{2,1,0:T(8,128)(2,1)S(1)}, u32[]{:S(2)}) copy-start(bf16[2,192,256]{2,1,0:T(8,128)(2,1)S(1)} %collective-permute-done.1) | copy-start | bytes 589828
  38.3 12.5 %collective-permute-start.2 = (bf16[2,2,192,256]{3,2,0,1:T(8,128)(2,1)S(1)}, bf16[2,2,192,256]{3,2,0,1:T(8,128)(2,1)S(1)}, u32[]{:S(2)}, u32[]{:S(2)}) collective-permute-start(bf16[2,2,192,256]{3,2,0,1:T(8,128)(2,1)S(1)} %maximum_select_fusion.11), channel_id=1, source_target_pairs={{0,4},{2,6},{4,0},{6,2},{8,12},{10,14},{12,8},{14,10},{16,20},{18,... | collective-permute-start | bytes 1179656 | tf_op jit(solution)/shard_map/ppermute | solution.py:366
  44.0 21.1 %collective-permute-start.5 = (bf16[2,2,192,384]{3,2,0,1:T(8,128)(2,1)S(1)}, bf16[2,2,192,384]{3,2,0,1:T(8,128)(2,1)S(1)}, u32[]{:S(2)}, u32[]{:S(2)}) collective-permute-start(bf16[2,2,192,384]{3,2,0,1:T(8,128)(2,1)S(1)} %maximum_select_fusion.9), channel_id=1, source_target_pairs={{0,2},{2,0},{4,6},{6,4},{8,10},{10,8},{12,14},{14,12},{16,18},{18,... | collective-permute-start | bytes 1769480 | tf_op jit(solution)/shard_map/ppermute | solution.py:366
  50.8 14.2 %copy-start.21 = (bf16[2,2,192,256]{3,2,0,1:T(8,128)(2,1)}, bf16[2,2,192,256]{3,2,0,1:T(8,128)(2,1)S(1)}, u32[]{:S(2)}) copy-start(bf16[2,2,192,256]{3,2,0,1:T(8,128)(2,1)S(1)} %collective-permute-done.2) | copy-start | bytes 1179652
  65.0 36.4 %copy-start.13 = (bf16[2,2,192,384]{3,2,0,1:T(8,128)(2,1)}, bf16[2,2,192,384]{3,2,0,1:T(8,128)(2,1)S(1)}, u32[]{:S(2)}) copy-start(bf16[2,2,192,384]{3,2,0,1:T(8,128)(2,1)S(1)} %collective-permute-done.5) | copy-start | bytes 1769476
  101.4 7.1 %copy-start.18 = (bf16[2,192,256]{2,1,0:T(8,128)(2,1)S(1)}, bf16[2,192,256]{2,1,0:T(8,128)(2,1)}, u32[]{:S(2)}) copy-start(bf16[2,192,256]{2,1,0:T(8,128)(2,1)} %copy-done.17) | copy-start | bytes 589828
  101.4 7.1 %copy-start.20 = (bf16[2,1,1,192,256]{4,3,0,1,2:T(8,128)(2,1)S(1)}, bf16[2,1,1,192,256]{4,3,0,1,2:T(8,128)(2,1)}, u32[]{:S(2)}) copy-start(bf16[2,1,1,192,256]{4,3,0,1,2:T(8,128)(2,1)} %copy-done.19) | copy-start | bytes 589828
  108.2 9.8 %collective-permute-start.6 = (bf16[1024,1024]{1,0:T(8,128)(2,1)}, bf16[1024,1024]{1,0:T(8,128)(2,1)}, u32[]{:S(2)}, u32[]{:S(2)}) collective-permute-start(bf16[1024,1024]{1,0:T(8,128)(2,1)} %get-tuple-element.72), channel_id=1, source_target_pairs={{0,1},{1,0},{2,3},{3,2},{4,5},{5,4},{6,7},{7,6},{8,9},{9,8},{10,11... | collective-permute-start | bytes 6291464 | tf_op jit(solution)/shard_map/ppermute | solution.py:350
  108.6 48.2 %collective-permute-start.7 = (bf16[2,2,2,192,256]{4,3,0,1,2:T(8,128)(2,1)}, bf16[2,2,2,192,256]{4,3,0,1,2:T(8,128)(2,1)}, u32[]{:S(2)}, u32[]{:S(2)}) collective-permute-start(bf16[2,2,2,192,256]{4,3,0,1,2:T(8,128)(2,1)} %maximum_select_fusion.6), channel_id=1, source_target_pairs={{0,2},{2,0},{4,6},{6,4},{8,10},{10,8},{12,14},{14,12},{16,18},{18,... | collective-permute-start | bytes 2359304 | tf_op jit(solution)/shard_map/ppermute | solution.py:366
  110.3 46.6 %collective-permute-start.8 = (bf16[2,2,2,192,384]{4,3,0,1,2:T(8,128)(2,1)}, bf16[2,2,2,192,384]{4,3,0,1,2:T(8,128)(2,1)}, u32[]{:S(2)}, u32[]{:S(2)}) collective-permute-start(bf16[2,2,2,192,384]{4,3,0,1,2:T(8,128)(2,1)} %maximum_select_fusion.4), channel_id=1, source_target_pairs={{0,4},{2,6},{4,0},{6,2},{8,12},{10,14},{12,8},{14,10},{16,20},{18,... | collective-permute-start | bytes 3538952 | tf_op jit(solution)/shard_map/ppermute | solution.py:366
  162.6 5.5 %collective-permute-start.9 = (bf16[1024,640]{1,0:T(8,128)(2,1)S(1)}, bf16[1024,640]{1,0:T(8,128)(2,1)S(1)}, u32[]{:S(2)}, u32[]{:S(2)}) collective-permute-start(bf16[1024,640]{1,0:T(8,128)(2,1)S(1)} %copy-done.44), channel_id=1, source_target_pairs={{0,1},{1,0},{2,3},{3,2},{4,5},{5,4},{6,7},{7,6},{8,9},{9,8},{10,11... | collective-permute-start | bytes 3932168 | tf_op jit(solution)/shard_map/ppermute | solution.py:350
  164.8 18.6 %collective-permute-start.10 = (bf16[3072,640]{1,0:T(8,128)(2,1)}, bf16[3072,640]{1,0:T(8,128)(2,1)}, u32[]{:S(2)}, u32[]{:S(2)}) collective-permute-start(bf16[3072,640]{1,0:T(8,128)(2,1)} %pad_maximum_fusion.wd_mine), channel_id=1, source_target_pairs={{0,1},{1,0},{2,3},{3,2},{4,5},{5,4},{6,7},{7,6},{8,9},{9,8},{10,11... | collective-permute-start | bytes 11796488 | tf_op jit(solution)/shard_map/ppermute | solution.py:350
  296.6 16.0 %collective-permute-start.12 = (bf16[1152,1536]{1,0:T(8,128)(2,1)}, bf16[1152,1536]{1,0:T(8,128)(2,1)}, u32[]{:S(2)}, u32[]{:S(2)}) collective-permute-start(bf16[1152,1536]{1,0:T(8,128)(2,1)} %get-tuple-element.83), channel_id=1, source_target_pairs={{0,1},{1,0},{2,3},{3,2},{4,5},{5,4},{6,7},{7,6},{8,9},{9,8},{10,11... | collective-permute-start | bytes 10616840 | tf_op jit(solution)/shard_map/ppermute | solution.py:350
  296.9 19.7 %collective-permute-start.11 = (bf16[1152,1536]{1,0:T(8,128)(2,1)}, bf16[1152,1536]{1,0:T(8,128)(2,1)S(1)}, u32[]{:S(2)}, u32[]{:S(2)}) collective-permute-start(bf16[1152,1536]{1,0:T(8,128)(2,1)} %get-tuple-element.81), channel_id=1, source_target_pairs={{0,1},{1,0},{2,3},{3,2},{4,5},{5,4},{6,7},{7,6},{8,9},{9,8},{10,11... | collective-permute-start | bytes 10616840 | tf_op jit(solution)/shard_map/ppermute | solution.py:350
  297.2 35.9 %collective-permute-start.14 = (bf16[3072,640]{1,0:T(8,128)(2,1)}, bf16[3072,640]{1,0:T(8,128)(2,1)S(1)}, u32[]{:S(2)}, u32[]{:S(2)}) collective-permute-start(bf16[3072,640]{1,0:T(8,128)(2,1)} %get-tuple-element.86), channel_id=1, source_target_pairs={{0,1},{1,0},{2,3},{3,2},{4,5},{5,4},{6,7},{7,6},{8,9},{9,8},{10,11... | collective-permute-start | bytes 11796488 | tf_op jit(solution)/shard_map/ppermute | solution.py:350
  301.0 7.8 %slice-start = ((s8[4718592]{0:T(1024)(128)(4,1)}), s8[524288]{0:T(1024)(128)(4,1)S(1)}, s32[]{:S(2)}) async-start(s8[4718592]{0:T(1024)(128)(4,1)} %bitcast.323), calls=%async_computation.2 | async-start | bytes 1048576
  312.6 7.8 %copy-start.1 = (f32[1024,1152]{1,0:T(8,128)}, f32[1024,1152]{1,0:T(8,128)S(1)}, u32[]{:S(2)}) copy-start(f32[1024,1152]{1,0:T(8,128)S(1)} %subtract_add_fusion) | copy-start | bytes 14155780
  321.7 8.0 %copy-start.6 = (bf16[1024,1152]{1,0:T(8,128)(2,1)}, bf16[1024,1152]{1,0:T(8,128)(2,1)S(1)}, u32[]{:S(2)}) copy-start(bf16[1024,1152]{1,0:T(8,128)(2,1)S(1)} %convert_element_type.928) | copy-start | bytes 7077892
  324.0 11.9 %collective-permute-start.13 = (bf16[1024,640]{1,0:T(8,128)(2,1)S(1)}, bf16[1024,640]{1,0:T(8,128)(2,1)}, u32[]{:S(2)}, u32[]{:S(2)}) collective-permute-start(bf16[1024,640]{1,0:T(8,128)(2,1)S(1)} %convolution_convert_fusion), channel_id=1, source_target_pairs={{0,1},{1,0},{2,3},{3,2},{4,5},{5,4},{6,7},{7,6},{8,9},{9,8},{10,11... | collective-permute-start | bytes 3932168 | tf_op jit(solution)/shard_map/ppermute | solution.py:350
  324.3 48.2 %collective-permute-start.15 = (bf16[2,2,2,72,1536]{4,3,0,2,1:T(8,128)(2,1)}, bf16[2,2,2,72,1536]{4,3,0,2,1:T(8,128)(2,1)}, u32[]{:S(2)}, u32[]{:S(2)}) collective-permute-start(bf16[2,2,2,72,1536]{4,3,0,2,1:T(8,128)(2,1)} %fusion.17), channel_id=1, source_target_pairs={{0,2},{2,0},{4,6},{6,4},{8,10},{10,8},{12,14},{14,12},{16,18},{18,... | collective-permute-start | bytes 5308424 | tf_op jit(solution)/shard_map/ppermute | solution.py:366
  325.7 46.8 %collective-permute-start.16 = (bf16[2,2,2,72,1536]{4,3,1,2,0:T(8,128)(2,1)}, bf16[2,2,2,72,1536]{4,3,1,2,0:T(8,128)(2,1)}, u32[]{:S(2)}, u32[]{:S(2)}) collective-permute-start(bf16[2,2,2,72,1536]{4,3,1,2,0:T(8,128)(2,1)} %fusion.18), channel_id=1, source_target_pairs={{0,4},{2,6},{4,0},{6,2},{8,12},{10,14},{12,8},{14,10},{16,20},{18,... | collective-permute-start | bytes 5308424 | tf_op jit(solution)/shard_map/ppermute | solution.py:366
  335.9 44.8 %collective-permute-start.17 = (bf16[2,2,2,192,640]{4,3,1,2,0:T(8,128)(2,1)}, bf16[2,2,2,192,640]{4,3,1,2,0:T(8,128)(2,1)}, u32[]{:S(2)}, u32[]{:S(2)}) collective-permute-start(bf16[2,2,2,192,640]{4,3,1,2,0:T(8,128)(2,1)} %fusion.14), channel_id=1, source_target_pairs={{0,8},{2,10},{4,12},{6,14},{8,0},{10,2},{12,4},{14,6},{16,24},{18,... | collective-permute-start | bytes 5898248 | tf_op jit(solution)/shard_map/ppermute | solution.py:366
  372.5 8.8 %copy-start.51 = (bf16[1024,640]{1,0:T(8,128)(2,1)S(1)}, bf16[1024,640]{1,0:T(8,128)(2,1)}, u32[]{:S(2)}) copy-start(bf16[1024,640]{1,0:T(8,128)(2,1)} %get-tuple-element.73.o_mine) | copy-start | bytes 3932164
  382.6 11.7 %collective-permute-start.18 = (bf16[1152,640]{1,0:T(8,128)(2,1)S(1)}, bf16[1152,640]{1,0:T(8,128)(2,1)S(1)}, u32[]{:S(2)}, u32[]{:S(2)}) collective-permute-start(bf16[1152,640]{1,0:T(8,128)(2,1)S(1)} %maximum_select_fusion.2), channel_id=1, source_target_pairs={{0,1},{1,0},{2,3},{3,2},{4,5},{5,4},{6,7},{7,6},{8,9},{9,8},{10,11... | collective-permute-start | bytes 4423688 | tf_op jit(solution)/shard_map/ppermute | solution.py:350
  397.6 46.4 %collective-permute-start.21 = (bf16[2,2,192,640]{3,2,1,0:T(8,128)(2,1)}, bf16[2,2,192,640]{3,2,1,0:T(8,128)(2,1)}, u32[]{:S(2)}, u32[]{:S(2)}) collective-permute-start(bf16[2,2,192,640]{3,2,1,0:T(8,128)(2,1)} %copy.86), channel_id=1, source_target_pairs={{0,16},{2,18},{4,20},{6,22},{8,24},{10,26},{12,28},{14,30},{16,0},... | collective-permute-start | bytes 2949128 | tf_op jit(solution)/shard_map/ppermute | solution.py:366
  400.3 43.8 %copy-start.41 = (f32[1,4,2,128]{3,1,2,0:T(4,128)S(1)}, f32[1,4,2,128]{3,1,2,0:T(4,128)}, u32[]{:S(2)}) copy-start(f32[1,4,2,128]{3,1,2,0:T(4,128)} %copy-done.40) | copy-start | bytes 12292
  400.3 39.2 %collective-permute-start.19 = (bf16[2,2,72,1536]{3,2,1,0:T(8,128)(2,1)}, bf16[2,2,72,1536]{3,2,1,0:T(8,128)(2,1)}, u32[]{:S(2)}, u32[]{:S(2)}) collective-permute-start(bf16[2,2,72,1536]{3,2,1,0:T(8,128)(2,1)} %copy.85), channel_id=1, source_target_pairs={{0,4},{2,6},{4,0},{6,2},{8,12},{10,14},{12,8},{14,10},{16,20},{18,... | collective-permute-start | bytes 2654216 | tf_op jit(solution)/shard_map/ppermute | solution.py:366
  401.8 37.6 %collective-permute-start.20 = (bf16[2,2,72,1536]{3,2,1,0:T(8,128)(2,1)}, bf16[2,2,72,1536]{3,2,1,0:T(8,128)(2,1)}, u32[]{:S(2)}, u32[]{:S(2)}) collective-permute-start(bf16[2,2,72,1536]{3,2,1,0:T(8,128)(2,1)} %get-tuple-element.108), channel_id=1, source_target_pairs={{0,2},{2,0},{4,6},{6,4},{8,10},{10,8},{12,14},{14,12},{16,18},{18,... | collective-permute-start | bytes 2654216 | tf_op jit(solution)/shard_map/ppermute | solution.py:366
  402.5 37.0 %collective-permute-start.22 = (bf16[2,2,2,72,640]{4,3,0,2,1:T(8,128)(2,1)}, bf16[2,2,2,72,640]{4,3,0,2,1:T(8,128)(2,1)}, u32[]{:S(2)}, u32[]{:S(2)}) collective-permute-start(bf16[2,2,2,72,640]{4,3,0,2,1:T(8,128)(2,1)} %fusion.34), channel_id=1, source_target_pairs={{0,2},{2,0},{4,6},{6,4},{8,10},{10,8},{12,14},{14,12},{16,18},{18,... | collective-permute-start | bytes 2211848 | tf_op jit(solution)/shard_map/ppermute | solution.py:366
  444.0 11.7 %collective-permute-start.23 = (bf16[1024,1024]{1,0:T(8,128)(2,1)}, bf16[1024,1024]{1,0:T(8,128)(2,1)S(1)}, u32[]{:S(2)}, u32[]{:S(2)}) collective-permute-start(bf16[1024,1024]{1,0:T(8,128)(2,1)} %get-tuple-element.113), channel_id=1, source_target_pairs={{0,1},{1,0},{2,3},{3,2},{4,5},{5,4},{6,7},{7,6},{8,9},{9,8},{10,11... | collective-permute-start | bytes 6291464 | tf_op jit(solution)/shard_map/ppermute | solution.py:350
  446.9 27.5 %collective-permute-start.36 = (bf16[2,72,1536]{2,1,0:T(8,128)(2,1)S(1)}, bf16[2,72,1536]{2,1,0:T(8,128)(2,1)S(1)}, u32[]{:S(2)}, u32[]{:S(2)}) collective-permute-start(bf16[2,72,1536]{2,1,0:T(8,128)(2,1)S(1)} %get-tuple-element.186), channel_id=1, source_target_pairs={{0,16},{2,18},{4,20},{6,22},{8,24},{10,26},{12,28},{14,30},{16,0},... | collective-permute-start | bytes 1327112 | tf_op jit(solution)/shard_map/ppermute | solution.py:366
  448.4 5.2 copy-start.10
  448.4 26.1 %collective-permute-start.35 = (bf16[2,72,1536]{2,1,0:T(8,128)(2,1)S(1)}, bf16[2,72,1536]{2,1,0:T(8,128)(2,1)S(1)}, u32[]{:S(2)}, u32[]{:S(2)}) collective-permute-start(bf16[2,72,1536]{2,1,0:T(8,128)(2,1)S(1)} %get-tuple-element.188), channel_id=1, source_target_pairs={{0,8},{2,10},{4,12},{6,14},{8,0},{10,2},{12,4},{14,6},{16,24},{18,... | collective-permute-start | bytes 1327112 | tf_op jit(solution)/shard_map/ppermute | solution.py:366
  452.1 21.7 %collective-permute-start.34 = (bf16[2,2,72,640]{3,2,1,0:T(8,128)(2,1)S(1)}, bf16[2,2,72,640]{3,2,1,0:T(8,128)(2,1)S(1)}, u32[]{:S(2)}, u32[]{:S(2)}) collective-permute-start(bf16[2,2,72,640]{3,2,1,0:T(8,128)(2,1)S(1)} %copy.102), channel_id=1, source_target_pairs={{0,4},{2,6},{4,0},{6,2},{8,12},{10,14},{12,8},{14,10},{16,20},{18,... | collective-permute-start | bytes 1105928 | tf_op jit(solution)/shard_map/ppermute | solution.py:366
  455.0 19.5 %collective-permute-start.33 = (bf16[2,192,640]{2,1,0:T(8,128)(2,1)S(1)}, bf16[2,192,640]{2,1,0:T(8,128)(2,1)S(1)}, u32[]{:S(2)}, u32[]{:S(2)}) collective-permute-start(bf16[2,192,640]{2,1,0:T(8,128)(2,1)S(1)} %get-tuple-element.184), channel_id=1, source_target_pairs={{0,2},{2,0},{4,6},{6,4},{8,10},{10,8},{12,14},{14,12},{16,18},{18,... | collective-permute-start | bytes 1474568 | tf_op jit(solution)/shard_map/ppermute | solution.py:366
  462.3 6.5 %slice-start.2 = ((s8[4718592]{0:T(1024)(128)(4,1)}), s8[4194304]{0:T(1024)(128)(4,1)S(1)}, s32[]{:S(2)}) async-start(s8[4718592]{0:T(1024)(128)(4,1)} %bitcast.325), calls=%async_computation.4 | async-start | bytes 8388608
  465.4 6.2 %collective-permute-start.24 = (bf16[1152,1024]{1,0:T(8,128)(2,1)S(1)}, bf16[1152,1024]{1,0:T(8,128)(2,1)S(1)}, u32[]{:S(2)}, u32[]{:S(2)}) collective-permute-start(bf16[1152,1024]{1,0:T(8,128)(2,1)S(1)} %add_convert_fusion), channel_id=1, source_target_pairs={{0,1},{1,0},{2,3},{3,2},{4,5},{5,4},{6,7},{7,6},{8,9},{9,8},{10,11... | collective-permute-start | bytes 7077896 | tf_op jit(solution)/shard_map/ppermute | solution.py:350
  472.1 15.8 %collective-permute-start.25 = (bf16[2,2,2,72,512]{4,3,0,2,1:T(8,128)(2,1)S(1)}, bf16[2,2,2,72,512]{4,3,0,2,1:T(8,128)(2,1)S(1)}, u32[]{:S(2)}, u32[]{:S(2)}) collective-permute-start(bf16[2,2,2,72,512]{4,3,0,2,1:T(8,128)(2,1)S(1)} %fusion.37), channel_id=1, source_target_pairs={{0,2},{2,0},{4,6},{6,4},{8,10},{10,8},{12,14},{14,12},{16,18},{18,... | collective-permute-start | bytes 1769480 | tf_op jit(solution)/shard_map/ppermute | solution.py:366
  473.7 16.3 %collective-permute-start.29 = (bf16[2,2,2,72,512]{4,3,1,2,0:T(8,128)(2,1)S(1)}, bf16[2,2,2,72,512]{4,3,1,2,0:T(8,128)(2,1)S(1)}, u32[]{:S(2)}, u32[]{:S(2)}) collective-permute-start(bf16[2,2,2,72,512]{4,3,1,2,0:T(8,128)(2,1)S(1)} %fusion.38), channel_id=1, source_target_pairs={{0,4},{2,6},{4,0},{6,2},{8,12},{10,14},{12,8},{14,10},{16,20},{18,... | collective-permute-start | bytes 1769480 | tf_op jit(solution)/shard_map/ppermute | solution.py:366
  474.5 19.5 %collective-permute-start.40 = (bf16[72,1536]{1,0:T(8,128)(2,1)S(1)}, bf16[72,1536]{1,0:T(8,128)(2,1)S(1)}, u32[]{:S(2)}, u32[]{:S(2)}) collective-permute-start(bf16[72,1536]{1,0:T(8,128)(2,1)S(1)} %fusion.70), channel_id=1, source_target_pairs={{0,8},{2,10},{4,12},{6,14},{8,0},{10,2},{12,4},{14,6},{16,24},{18,... | collective-permute-start | bytes 663560 | tf_op jit(solution)/shard_map/ppermute | solution.py:366
  474.7 19.3 %collective-permute-start.39 = (bf16[72,1536]{1,0:T(8,128)(2,1)S(1)}, bf16[72,1536]{1,0:T(8,128)(2,1)S(1)}, u32[]{:S(2)}, u32[]{:S(2)}) collective-permute-start(bf16[72,1536]{1,0:T(8,128)(2,1)S(1)} %fusion.69), channel_id=1, source_target_pairs={{0,16},{2,18},{4,20},{6,22},{8,24},{10,26},{12,28},{14,30},{16,0},... | collective-permute-start | bytes 663560 | tf_op jit(solution)/shard_map/ppermute | solution.py:366
  477.5 17.0 %collective-permute-start.37 = (bf16[192,640]{1,0:T(8,128)(2,1)S(1)}, bf16[192,640]{1,0:T(8,128)(2,1)S(1)}, u32[]{:S(2)}, u32[]{:S(2)}) collective-permute-start(bf16[192,640]{1,0:T(8,128)(2,1)S(1)} %get-tuple-element.212), channel_id=1, source_target_pairs={{0,4},{2,6},{4,0},{6,2},{8,12},{10,14},{12,8},{14,10},{16,20},{18,... | collective-permute-start | bytes 737288 | tf_op jit(solution)/shard_map/ppermute | solution.py:366
  487.8 6.2 %collective-permute-start.38 = (bf16[2,72,640]{2,1,0:T(8,128)(2,1)S(1)}, bf16[2,72,640]{2,1,0:T(8,128)(2,1)S(1)}, u32[]{:S(2)}, u32[]{:S(2)}) collective-permute-start(bf16[2,72,640]{2,1,0:T(8,128)(2,1)S(1)} %get-tuple-element.214), channel_id=1, source_target_pairs={{0,8},{2,10},{4,12},{6,14},{8,0},{10,2},{12,4},{14,6},{16,24},{18,... | collective-permute-start | bytes 552968 | tf_op jit(solution)/shard_map/ppermute | solution.py:366
  490.2 15.3 %collective-permute-start.30 = (bf16[2,2,72,512]{3,2,1,0:T(8,128)(2,1)S(1)}, bf16[2,2,72,512]{3,2,1,0:T(8,128)(2,1)S(1)}, u32[]{:S(2)}, u32[]{:S(2)}) collective-permute-start(bf16[2,2,72,512]{3,2,1,0:T(8,128)(2,1)S(1)} %get-tuple-element.206), channel_id=1, source_target_pairs={{0,2},{2,0},{4,6},{6,4},{8,10},{10,8},{12,14},{14,12},{16,18},{18,... | collective-permute-start | bytes 884744 | tf_op jit(solution)/shard_map/ppermute | solution.py:366
  494.6 11.4 %collective-permute-start.41 = (bf16[72,640]{1,0:T(8,128)(2,1)S(1)}, bf16[72,640]{1,0:T(8,128)(2,1)S(1)}, u32[]{:S(2)}, u32[]{:S(2)}) collective-permute-start(bf16[72,640]{1,0:T(8,128)(2,1)S(1)} %get-tuple-element.219), channel_id=1, source_target_pairs={{0,16},{2,18},{4,20},{6,22},{8,24},{10,26},{12,28},{14,30},{16,0},... | collective-permute-start | bytes 276488 | tf_op jit(solution)/shard_map/ppermute | solution.py:366
  495.4 8.0 %collective-permute-start.26 = (bf16[2,2,72,512]{3,2,1,0:T(8,128)(2,1)S(1)}, bf16[2,2,72,512]{3,2,1,0:T(8,128)(2,1)S(1)}, u32[]{:S(2)}, u32[]{:S(2)}) collective-permute-start(bf16[2,2,72,512]{3,2,1,0:T(8,128)(2,1)S(1)} %copy.92), channel_id=1, source_target_pairs={{0,4},{2,6},{4,0},{6,2},{8,12},{10,14},{12,8},{14,10},{16,20},{18,... | collective-permute-start | bytes 884744 | tf_op jit(solution)/shard_map/ppermute | solution.py:366
  503.4 10.0 %collective-permute-start.27 = (bf16[2,72,512]{2,1,0:T(8,128)(2,1)S(1)}, bf16[2,72,512]{2,1,0:T(8,128)(2,1)S(1)}, u32[]{:S(2)}, u32[]{:S(2)}) collective-permute-start(bf16[2,72,512]{2,1,0:T(8,128)(2,1)S(1)} %get-tuple-element.216), channel_id=1, source_target_pairs={{0,8},{2,10},{4,12},{6,14},{8,0},{10,2},{12,4},{14,6},{16,24},{18,... | collective-permute-start | bytes 442376 | tf_op jit(solution)/shard_map/ppermute | solution.py:366
  505.5 7.8 %collective-permute-start.31 = (bf16[2,72,512]{2,1,0:T(8,128)(2,1)S(1)}, bf16[2,72,512]{2,1,0:T(8,128)(2,1)S(1)}, u32[]{:S(2)}, u32[]{:S(2)}) collective-permute-start(bf16[2,72,512]{2,1,0:T(8,128)(2,1)S(1)} %get-tuple-element.218), channel_id=1, source_target_pairs={{0,16},{2,18},{4,20},{6,22},{8,24},{10,26},{12,28},{14,30},{16,0},... | collective-permute-start | bytes 442376 | tf_op jit(solution)/shard_map/ppermute | solution.py:366
  513.4 4.4 collective-permute-start.32
  513.5 5.7 %collective-permute-start.28 = (bf16[72,512]{1,0:T(8,128)(2,1)S(1)}, bf16[72,512]{1,0:T(8,128)(2,1)S(1)}, u32[]{:S(2)}, u32[]{:S(2)}) collective-permute-start(bf16[72,512]{1,0:T(8,128)(2,1)S(1)} %fusion.85), channel_id=1, source_target_pairs={{0,16},{2,18},{4,20},{6,22},{8,24},{10,26},{12,28},{14,30},{16,0},... | collective-permute-start | bytes 221192 | tf_op jit(solution)/shard_map/ppermute | solution.py:366
  (38 other events, 97.9 us)
Sparse Core Ops, SparseCore 0:
  11.5 84.8 all-gather.2
  99.8 104.9 all-gather.4

commit v10 on v9

--- a/solution.py
+++ b/solution.py
@@ -540,9 +540,8 @@
     out_sum.move(0)
     for b in range(1, batch):
         lins = back(b, lins)
-    (lin_mine, lin_out), wide_sum.got, down_sum.got, out_sum.got = tie(
-        (lins, wide_sum.got, down_sum.got, out_sum.got)
-    )
+    (lin_mine, lin_out), wide_sum.got, down_sum.got = tie((lins, wide_sum.got, down_sum.got))
+    _, out_sum.got = tie((lin_mine, out_sum.got))
     lin_got = swap(lin_out)
     down_sum.advance(2)
     out_sum.advance(1)

time: 536 us -> 547 us (1.021)
  waiting for transfers between devices: 134 us -> 146 us
    ppermute x32, waiting for transfers between devices: 82.6 us -> 94.8 us  [exchange(): lax.ppermute(a, 'dp', [(i, i ^ 1 << bit) for i in range(lax.axis_size('dp...]
  transfers between devices with their start and end apart: 44 -> 44, of which waited for: 17 -> 17; matrix products, arithmetic and copies ran while one was open for 22% -> 22% of each run, Pallas kernels for 21% -> 20%
where the time goes in v10:
time: 547 us; the launch traced here: 538 us
  Pallas kernels  201 us (37%)
  waiting for transfers between devices  146 us (27%)
  other arithmetic  67.2 us (12%)
  starting transfers between devices  40.9 us (7%)
  local copies, waits for them, and re-layouts  37.8 us (7%)
  matrix products  29.1 us (5%)
  between operations  15.5 us (3%)
    ppermute x32, waiting for transfers between devices, exchange(): lax.ppermute(a, 'dp', [(i, i ^ 1 << bit) for i in range(lax.axis_size('dp...  94.8 us
    pallas_call x1, Pallas kernels, mlp(): pl.pallas_call(mlp_body, grid_spec=pltpu.PrefetchScalarGridSpec(num_scala...  91.8 us
    pallas_call x2, Pallas kernels, attend_back(): pl.pallas_call(bwd_body, grid_spec=pltpu.PrefetchScalarGridSpec(num_scala...  57 us
    all_gather x2, waiting for transfers between devices, fetch(): lax.all_gather(w, BOTH, axis=0, tiled=True)  51.5 us
    pallas_call x1, Pallas kernels, attend(): pl.pallas_call(fwd_body, grid_spec=pltpu.PrefetchScalarGridSpec(num_scala...  38.9 us
    ppermute x32, starting transfers between devices, exchange(): lax.ppermute(a, 'dp', [(i, i ^ 1 << bit) for i in range(lax.axis_size('dp...  38.8 us
    convert_element_type x29, other arithmetic, prepare(): add(at(self.stay[p], i), at(self.got[p], i)).astype(self.kind)  25.5 us
    pallas_call x2, Pallas kernels, project(): pl.pallas_call(project_body, grid_spec=pltpu.PrefetchScalarGridSpec(num_s...  13.6 us
  transfers between devices with their start and end apart: 44, of which 17 were waited for; matrix products, arithmetic and copies ran while one was open for 22% of the time, Pallas kernels for 20%

profile of v10, /device:TPU:0, one launch (start us, length us, event | category | flops | bytes accessed | tf_op | source)
XLA Modules:
  0.0 538.0 jit_solution(8978296771040354138)
XLA Ops:
  8.1 1.8 concatenate.186
  10.0 2.0 pad_maximum_fusion.1
  12.0 4.1 collective-permute-start.3
  16.4 3.1 fusion.43
  20.1 9.1 %collective-permute-done = bf16[192,256]{1,0:T(8,128)(2,1)S(1)} collective-permute-done((bf16[192,256]{1,0:T(8,128)(2,1)S(1)}, bf16[192,256]{1,0:T(8,128)(2,1)S(1)}, u32[]{:S(2)}, u32[]{:S(2)}) %collective-permute-start) | collective-permute-done | bytes 98336 | tf_op jit(solution)/shard_map/ppermute | solution.py:366
  31.5 6.8 %collective-permute-done.1 = bf16[2,192,256]{2,1,0:T(8,128)(2,1)S(1)} collective-permute-done((bf16[2,192,256]{2,1,0:T(8,128)(2,1)S(1)}, bf16[2,192,256]{2,1,0:T(8,128)(2,1)S(1)}, u32[]{:S(2)}, u32[]{:S(2)}) %collective-permute-start.1) | collective-permute-done | bytes 196640 | tf_op jit(solution)/shard_map/ppermute | solution.py:366
  38.3 1.8 collective-permute-start.2
  40.2 3.7 collective-permute-done.4
  47.8 3.0 collective-permute-done.2
  51.8 13.2 %collective-permute-done.5 = bf16[2,2,192,384]{3,2,0,1:T(8,128)(2,1)S(1)} collective-permute-done((bf16[2,2,192,384]{3,2,0,1:T(8,128)(2,1)S(1)}, bf16[2,2,192,384]{3,2,0,1:T(8,128)(2,1)S(1)}, u32[]{:S(2)}, u32[]{:S(2)}) %collective-permute-start.5) | collective-permute-done | bytes 589856 | tf_op jit(solution)/shard_map/ppermute | solution.py:366
  66.3 30.0 %all-gather.3.cloned.1.call-done = bf16[2304,1600]{1,0:T(8,128)(2,1)} async-done(((bf16[72,1600]{1,0:T(8,128)(2,1)}), bf16[2304,1600]{1,0:T(8,128)(2,1)}) %all-gather.3.cloned.1.call-update) | async-done | bytes 7372816 | tf_op jit(solution)/shard_map/all_gather | solution.py:361
  96.3 2.2 convert_reduce_fusion
  99.4 2.0 fusion.2.n1
  101.4 6.8 %project.3 = (bf16[1024,1024]{1,0:T(8,128)(2,1)}, bf16[1152,1024]{1,0:T(8,128)(2,1)}) custom-call(s32[1]{0:T(128)} %bitcast.me, bf16[1024,1152]{1,0:T(8,128)(2,1)} %fusion.2.n1, bf16[16,2,72,1600]{3,2,1,0:T(8,128)(2,1)} %bitcast.352, f32[1024,128]{1,0:T(8,128)} %get-tuple-element.230.cosine, f32[1024,128]{1,0:T(8,128)} %get-tuple-element.229.sine), custom_call_target="tpu_custom_call" | custom-call | flops 3000000000 | bytes 12000000 | tf_op jit(solution)/shard_map/project/pallas_call | solution.py:66
  111.2 6.8 %project.2 = (bf16[1024,1024]{1,0:T(8,128)(2,1)}, bf16[1152,1024]{1,0:T(8,128)(2,1)}) custom-call(s32[1]{0:T(128)} %bitcast.me, bf16[1024,1152]{1,0:T(8,128)(2,1)} %fusion.2.n1, bf16[16,2,72,1600]{3,2,1,0:T(8,128)(2,1)} %bitcast.353, f32[1024,128]{1,0:T(8,128)} %get-tuple-element.230.cosine, f32[1024,128]{1,0:T(8,128)} %get-tuple-element.229.sine), custom_call_target="tpu_custom_call" | custom-call | flops 3000000000 | bytes 12000000 | tf_op jit(solution)/shard_map/project/pallas_call | solution.py:66
  118.0 38.9 %attend.1 = (bf16[1024,640]{1,0:T(8,128)(2,1)}, bf16[1024,640]{1,0:T(8,128)(2,1)}, f32[2048,128]{1,0:T(8,128)}) custom-call(s32[1]{0:T(128)} %bitcast.me, bf16[1024,1024]{1,0:T(8,128)(2,1)} %get-tuple-element.71.mine, bf16[1024,1024]{1,0:T(8,128)(2,1)} %collective-permute-done.6.got), custom_call_target="tpu_custom_call" | custom-call | flops 24000000000 | bytes 20000000 | tf_op jit(solution)/shard_map/attend/pallas_call | solution.py:200
  156.9 2.0 maximum_select_fusion
  159.2 2.1 maximum_select_fusion.1
  162.6 2.2 pad_maximum_fusion.wd_mine
  165.4 2.1 slice_bitcast_fusion
  168.1 2.1 fusion.62
  171.7 2.4 multiply_reduce_fusion.2
  174.1 2.1 copy-done
  176.6 2.6 copy.70.n2t
  179.2 4.2 multiply_convert_fusion.n2
  183.4 21.4 %all-gather.5.cloned.1.call-done = bf16[2304,3072]{1,0:T(8,128)(2,1)} async-done(((bf16[72,3072]{1,0:T(8,128)(2,1)}), bf16[2304,3072]{1,0:T(8,128)(2,1)}) %all-gather.5.cloned.1.call-update) | async-done | bytes 14155792 | tf_op jit(solution)/shard_map/all_gather | solution.py:361
  204.8 91.8 %mlp.1 = (bf16[1024,1152]{1,0:T(8,128)(2,1)}, f32[1024,1152]{1,0:T(8,128)}, bf16[1152,1536]{1,0:T(8,128)(2,1)}, bf16[1152,1536]{1,0:T(8,128)(2,1)}, bf16[1152,15...) custom-call(s32[1]{0:T(128)} %bitcast.me, ...), custom_call_target="tpu_custom_call" | custom-call | flops 65000001536 | bytes 60000000 | tf_op jit(solution)/shard_map/mlp/pallas_call | solution.py:312
  297.4 2.7 constant_dynamic-slice_fusion.13
  301.0 4.5 multiply_reduce_fusion
  305.4 2.5 constant_dynamic-slice_fusion.15
  310.7 1.9 subtract_add_fusion
  312.6 4.0 constant_dynamic-slice_fusion.14
  317.0 1.7 fusion.18
  318.7 1.7 fusion.17
  321.7 2.2 convolution_convert_fusion
  326.3 1.7 add_convert_fusion.4
  328.1 1.7 add_convert_fusion.5
  329.8 3.3 convolution_convert_fusion.1.do_mine
  333.5 1.9 fusion.14
  336.9 28.6 %attend_back.2 = (bf16[1024,1024]{1,0:T(8,128)(2,1)}, bf16[1024,1024]{1,0:T(8,128)(2,1)}) custom-call(s32[1]{0:T(128)} %bitcast.me, bf16[1024,1024]{1,0:T(8,128)(2,1)} %get-tuple-element.71.mine, bf16[1024,1024]{1,0:T(8,128)(2,1)} %collective-permute-done.6.got, bf16[1024,640]{1,0:T(8,128)(2,1)} %get-tuple-element.73.o_mine, ...), custom_call_target="tpu_custom_call" | custom-call | flops 12999999488 | bytes 20000000 | tf_op jit(solution)/shard_map/attend_back/pallas_call | solution.py:226
  365.6 2.1 slice.92
  367.7 2.7 fusion.89
  372.5 8.2 %collective-permute-done.17 = bf16[2,2,2,192,640]{4,3,1,2,0:T(8,128)(2,1)} collective-permute-done((bf16[2,2,2,192,640]{4,3,1,2,0:T(8,128)(2,1)}, bf16[2,2,2,192,640]{4,3,1,2,0:T(8,128)(2,1)}, u32[]{:S(2)}, u32[]{:S(2)}) %collective-permute-start.17) | collective-permute-done | bytes 1966112 | tf_op jit(solution)/shard_map/ppermute | solution.py:366
  384.1 3.0 fusion.15
  389.5 3.0 fusion.19
  392.4 1.9 fusion.20
  397.5 1.7 collective-permute-start.21
  402.4 28.3 %attend_back.3 = (bf16[1024,1024]{1,0:T(8,128)(2,1)}, bf16[1024,1024]{1,0:T(8,128)(2,1)}) custom-call(s32[1]{0:T(128)} %bitcast.me, bf16[1024,1024]{1,0:T(8,128)(2,1)} %get-tuple-element.71.mine, bf16[1024,1024]{1,0:T(8,128)(2,1)} %collective-permute-done.6.got, ...), custom_call_target="tpu_custom_call", output_to_operand_aliasing={{0}: (10, {}), {1}: (11, {})} | custom-call | flops 12999999488 | bytes 20000000 | tf_op jit(solution)/shard_map/attend_back/pallas_call | solution.py:226
  430.8 13.2 %collective-permute-done.21 = bf16[2,2,192,640]{3,2,1,0:T(8,128)(2,1)} collective-permute-done((bf16[2,2,192,640]{3,2,1,0:T(8,128)(2,1)}, bf16[2,2,192,640]{3,2,1,0:T(8,128)(2,1)}, u32[]{:S(2)}, u32[]{:S(2)}) %collective-permute-start.21) | collective-permute-done | bytes 983072 | tf_op jit(solution)/shard_map/ppermute | solution.py:366
  449.9 2.3 collective-permute-start.35
  452.3 10.9 %collective-permute-done.32 = bf16[2,2,2,72,640]{4,3,0,2,1:T(8,128)(2,1)S(1)} collective-permute-done((bf16[2,2,2,72,640]{4,3,0,2,1:T(8,128)(2,1)}, bf16[2,2,2,72,640]{4,3,0,2,1:T(8,128)(2,1)S(1)}, u32[]{:S(2)}, u32[]{:S(2)}) %collective-permute-start.32) | collective-permute-done | bytes 737312 | tf_op jit(solution)/shard_map/ppermute | solution.py:366
  467.1 2.9 fusion.114
  470.1 3.5 fusion.9
  473.7 3.0 add_convert_fusion
  476.8 3.0 add_convert_fusion.1
  480.2 2.7 fusion.6
  486.0 2.3 collective-permute-start.39
  490.4 8.8 %collective-permute-done.24 = bf16[2,2,2,72,512]{4,3,0,2,1:T(8,128)(2,1)S(1)} collective-permute-done((bf16[2,2,2,72,512]{4,3,0,2,1:T(8,128)(2,1)S(1)}, bf16[2,2,2,72,512]{4,3,0,2,1:T(8,128)(2,1)S(1)}, u32[]{:S(2)}, u32[]{:S(2)}) %collective-permute-start.24) | collective-permute-done | bytes 589856 | tf_op jit(solution)/shard_map/ppermute | solution.py:366
  499.4 2.0 collective-permute-done.28
  502.3 3.1 collective-permute-done.38
  509.2 5.1 collective-permute-done.25
  514.4 2.0 collective-permute-start.26
  518.8 5.6 %collective-permute-done.30 = bf16[2,72,512]{2,1,0:T(8,128)(2,1)S(1)} collective-permute-done((bf16[2,72,512]{2,1,0:T(8,128)(2,1)S(1)}, bf16[2,72,512]{2,1,0:T(8,128)(2,1)S(1)}, u32[]{:S(2)}, u32[]{:S(2)}) %collective-permute-start.30) | collective-permute-done | bytes 147488 | tf_op jit(solution)/shard_map/ppermute | solution.py:366
  524.5 2.7 collective-permute-start.27
  (282 shorter events, 69.8 us)
Async XLA Ops:
  7.2 89.2 %all-gather.3.cloned.1.call-start = ((), (), s32[]{:S(2)}) async-start(), calls=%async_computation | async-start | bytes 7907328 | tf_op jit(solution)/shard_map/all_gather | solution.py:361
  9.9 9.6 %copy-start.2 = (bf16[2,1,512,1152]{3,2,1,0:T(8,128)(2,1)S(1)}, bf16[2,1,512,1152]{3,2,1,0:T(8,128)(2,1)}, u32[]{:S(2)}) copy-start(bf16[2,1,512,1152]{3,2,1,0:T(8,128)(2,1)} %param.11) | copy-start | bytes 7077892
  9.9 194.9 %all-gather.5.cloned.1.call-start = ((), (), s32[]{:S(2)}) async-start(), calls=%async_computation.1 | async-start | bytes 14598144 | tf_op jit(solution)/shard_map/all_gather | solution.py:361
  12.0 19.4 %copy-start.23 = (bf16[1,1,192,384]{3,2,0,1:T(8,128)(2,1)}, bf16[1,1,192,384]{3,2,0,1:T(8,128)(2,1)S(1)}, u32[]{:S(2)}) copy-start(bf16[1,1,192,384]{3,2,0,1:T(8,128)(2,1)S(1)} %get-tuple-element.221) | copy-start | bytes 442372
  12.0 18.3 %collective-permute-start.3 = (bf16[192,384]{1,0:T(8,128)(2,1)S(1)}, bf16[192,384]{1,0:T(8,128)(2,1)S(1)}, u32[]{:S(2)}, u32[]{:S(2)}) collective-permute-start(bf16[192,384]{1,0:T(8,128)(2,1)S(1)} %get-tuple-element.223), channel_id=1, source_target_pairs={{0,16},{2,18},{4,20},{6,22},{8,24},{10,26},{12,28},{14,30},{16,0},... | collective-permute-start | bytes 442376 | tf_op jit(solution)/shard_map/ppermute | solution.py:366
  16.2 15.2 %copy-start.26 = (bf16[1,1,192,256]{3,2,0,1:T(8,128)(2,1)}, bf16[1,1,192,256]{3,2,0,1:T(8,128)(2,1)S(1)}, u32[]{:S(2)}) copy-start(bf16[1,1,192,256]{3,2,0,1:T(8,128)(2,1)S(1)} %get-tuple-element.224) | copy-start | bytes 294916
  16.2 12.9 %collective-permute-start = (bf16[192,256]{1,0:T(8,128)(2,1)S(1)}, bf16[192,256]{1,0:T(8,128)(2,1)S(1)}, u32[]{:S(2)}, u32[]{:S(2)}) collective-permute-start(bf16[192,256]{1,0:T(8,128)(2,1)S(1)} %get-tuple-element.226), channel_id=1, source_target_pairs={{0,16},{2,18},{4,20},{6,22},{8,24},{10,26},{12,28},{14,30},{16,0},... | collective-permute-start | bytes 294920 | tf_op jit(solution)/shard_map/ppermute | solution.py:366
  20.1 79.3 %copy-start.40 = (f32[1,4,2,128]{3,1,2,0:T(4,128)}, f32[1,4,2,128]{3,1,2,0:T(4,128)S(1)}, u32[]{:S(2)}) copy-start(f32[1,4,2,128]{3,1,2,0:T(4,128)S(1)} %copy.135) | copy-start | bytes 12292
  29.1 14.7 %copy-start.28 = (bf16[192,256]{1,0:T(8,128)(2,1)}, bf16[192,256]{1,0:T(8,128)(2,1)S(1)}, u32[]{:S(2)}) copy-start(bf16[192,256]{1,0:T(8,128)(2,1)S(1)} %collective-permute-done) | copy-start | bytes 294916
  29.2 9.1 %collective-permute-start.1 = (bf16[2,192,256]{2,1,0:T(8,128)(2,1)S(1)}, bf16[2,192,256]{2,1,0:T(8,128)(2,1)S(1)}, u32[]{:S(2)}, u32[]{:S(2)}) collective-permute-start(bf16[2,192,256]{2,1,0:T(8,128)(2,1)S(1)} %maximum_select_fusion.15), channel_id=1, source_target_pairs={{0,8},{2,10},{4,12},{6,14},{8,0},{10,2},{12,4},{14,6},{16,24},{18,... | collective-permute-start | bytes 589832 | tf_op jit(solution)/shard_map/ppermute | solution.py:366
  30.3 15.2 %copy-start.25 = (bf16[192,384]{1,0:T(8,128)(2,1)}, bf16[192,384]{1,0:T(8,128)(2,1)S(1)}, u32[]{:S(2)}) copy-start(bf16[192,384]{1,0:T(8,128)(2,1)S(1)} %collective-permute-done.3) | copy-start | bytes 442372
  30.4 13.5 %collective-permute-start.4 = (bf16[2,192,384]{2,1,0:T(8,128)(2,1)S(1)}, bf16[2,192,384]{2,1,0:T(8,128)(2,1)S(1)}, u32[]{:S(2)}, u32[]{:S(2)}) collective-permute-start(bf16[2,192,384]{2,1,0:T(8,128)(2,1)S(1)} %maximum_select_fusion.13), channel_id=1, source_target_pairs={{0,8},{2,10},{4,12},{6,14},{8,0},{10,2},{12,4},{14,6},{16,24},{18,... | collective-permute-start | bytes 884744 | tf_op jit(solution)/shard_map/ppermute | solution.py:366
  31.4 14.1 %copy-start.27 = (bf16[1,1,192,256]{3,2,0,1:T(8,128)(2,1)S(1)}, bf16[1,1,192,256]{3,2,0,1:T(8,128)(2,1)}, u32[]{:S(2)}) copy-start(bf16[1,1,192,256]{3,2,0,1:T(8,128)(2,1)} %copy-done.26) | copy-start | bytes 294916
  31.5 15.0 %copy-start.24 = (bf16[1,1,192,384]{3,2,0,1:T(8,128)(2,1)S(1)}, bf16[1,1,192,384]{3,2,0,1:T(8,128)(2,1)}, u32[]{:S(2)}) copy-start(bf16[1,1,192,384]{3,2,0,1:T(8,128)(2,1)} %copy-done.23) | copy-start | bytes 442372
  38.3 9.5 %copy-start.17 = (bf16[2,192,256]{2,1,0:T(8,128)(2,1)}, bf16[2,192,256]{2,1,0:T(8,128)(2,1)S(1)}, u32[]{:S(2)}) copy-start(bf16[2,192,256]{2,1,0:T(8,128)(2,1)S(1)} %collective-permute-done.1) | copy-start | bytes 589828
  38.3 12.5 %collective-permute-start.2 = (bf16[2,2,192,256]{3,2,0,1:T(8,128)(2,1)S(1)}, bf16[2,2,192,256]{3,2,0,1:T(8,128)(2,1)S(1)}, u32[]{:S(2)}, u32[]{:S(2)}) collective-permute-start(bf16[2,2,192,256]{3,2,0,1:T(8,128)(2,1)S(1)} %maximum_select_fusion.11), channel_id=1, source_target_pairs={{0,4},{2,6},{4,0},{6,2},{8,12},{10,14},{12,8},{14,10},{16,20},{18,... | collective-permute-start | bytes 1179656 | tf_op jit(solution)/shard_map/ppermute | solution.py:366
  44.0 21.1 %collective-permute-start.5 = (bf16[2,2,192,384]{3,2,0,1:T(8,128)(2,1)S(1)}, bf16[2,2,192,384]{3,2,0,1:T(8,128)(2,1)S(1)}, u32[]{:S(2)}, u32[]{:S(2)}) collective-permute-start(bf16[2,2,192,384]{3,2,0,1:T(8,128)(2,1)S(1)} %maximum_select_fusion.9), channel_id=1, source_target_pairs={{0,2},{2,0},{4,6},{6,4},{8,10},{10,8},{12,14},{14,12},{16,18},{18,... | collective-permute-start | bytes 1769480 | tf_op jit(solution)/shard_map/ppermute | solution.py:366
  50.8 14.2 %copy-start.21 = (bf16[2,2,192,256]{3,2,0,1:T(8,128)(2,1)}, bf16[2,2,192,256]{3,2,0,1:T(8,128)(2,1)S(1)}, u32[]{:S(2)}) copy-start(bf16[2,2,192,256]{3,2,0,1:T(8,128)(2,1)S(1)} %collective-permute-done.2) | copy-start | bytes 1179652
  65.0 36.4 %copy-start.13 = (bf16[2,2,192,384]{3,2,0,1:T(8,128)(2,1)}, bf16[2,2,192,384]{3,2,0,1:T(8,128)(2,1)S(1)}, u32[]{:S(2)}) copy-start(bf16[2,2,192,384]{3,2,0,1:T(8,128)(2,1)S(1)} %collective-permute-done.5) | copy-start | bytes 1769476
  101.4 7.1 %copy-start.18 = (bf16[2,192,256]{2,1,0:T(8,128)(2,1)S(1)}, bf16[2,192,256]{2,1,0:T(8,128)(2,1)}, u32[]{:S(2)}) copy-start(bf16[2,192,256]{2,1,0:T(8,128)(2,1)} %copy-done.17) | copy-start | bytes 589828
  101.4 7.1 %copy-start.20 = (bf16[2,1,1,192,256]{4,3,0,1,2:T(8,128)(2,1)S(1)}, bf16[2,1,1,192,256]{4,3,0,1,2:T(8,128)(2,1)}, u32[]{:S(2)}) copy-start(bf16[2,1,1,192,256]{4,3,0,1,2:T(8,128)(2,1)} %copy-done.19) | copy-start | bytes 589828
  108.2 9.8 %collective-permute-start.6 = (bf16[1024,1024]{1,0:T(8,128)(2,1)}, bf16[1024,1024]{1,0:T(8,128)(2,1)}, u32[]{:S(2)}, u32[]{:S(2)}) collective-permute-start(bf16[1024,1024]{1,0:T(8,128)(2,1)} %get-tuple-element.72), channel_id=1, source_target_pairs={{0,1},{1,0},{2,3},{3,2},{4,5},{5,4},{6,7},{7,6},{8,9},{9,8},{10,11... | collective-permute-start | bytes 6291464 | tf_op jit(solution)/shard_map/ppermute | solution.py:350
  108.6 48.2 %collective-permute-start.7 = (bf16[2,2,2,192,256]{4,3,0,1,2:T(8,128)(2,1)}, bf16[2,2,2,192,256]{4,3,0,1,2:T(8,128)(2,1)}, u32[]{:S(2)}, u32[]{:S(2)}) collective-permute-start(bf16[2,2,2,192,256]{4,3,0,1,2:T(8,128)(2,1)} %maximum_select_fusion.6), channel_id=1, source_target_pairs={{0,2},{2,0},{4,6},{6,4},{8,10},{10,8},{12,14},{14,12},{16,18},{18,... | collective-permute-start | bytes 2359304 | tf_op jit(solution)/shard_map/ppermute | solution.py:366
  110.3 46.6 %collective-permute-start.8 = (bf16[2,2,2,192,384]{4,3,0,1,2:T(8,128)(2,1)}, bf16[2,2,2,192,384]{4,3,0,1,2:T(8,128)(2,1)}, u32[]{:S(2)}, u32[]{:S(2)}) collective-permute-start(bf16[2,2,2,192,384]{4,3,0,1,2:T(8,128)(2,1)} %maximum_select_fusion.4), channel_id=1, source_target_pairs={{0,4},{2,6},{4,0},{6,2},{8,12},{10,14},{12,8},{14,10},{16,20},{18,... | collective-permute-start | bytes 3538952 | tf_op jit(solution)/shard_map/ppermute | solution.py:366
  162.6 5.5 %collective-permute-start.9 = (bf16[1024,640]{1,0:T(8,128)(2,1)S(1)}, bf16[1024,640]{1,0:T(8,128)(2,1)S(1)}, u32[]{:S(2)}, u32[]{:S(2)}) collective-permute-start(bf16[1024,640]{1,0:T(8,128)(2,1)S(1)} %copy-done.44), channel_id=1, source_target_pairs={{0,1},{1,0},{2,3},{3,2},{4,5},{5,4},{6,7},{7,6},{8,9},{9,8},{10,11... | collective-permute-start | bytes 3932168 | tf_op jit(solution)/shard_map/ppermute | solution.py:350
  164.8 18.6 %collective-permute-start.10 = (bf16[3072,640]{1,0:T(8,128)(2,1)}, bf16[3072,640]{1,0:T(8,128)(2,1)}, u32[]{:S(2)}, u32[]{:S(2)}) collective-permute-start(bf16[3072,640]{1,0:T(8,128)(2,1)} %pad_maximum_fusion.wd_mine), channel_id=1, source_target_pairs={{0,1},{1,0},{2,3},{3,2},{4,5},{5,4},{6,7},{7,6},{8,9},{9,8},{10,11... | collective-permute-start | bytes 11796488 | tf_op jit(solution)/shard_map/ppermute | solution.py:350
  296.6 16.0 %collective-permute-start.12 = (bf16[1152,1536]{1,0:T(8,128)(2,1)}, bf16[1152,1536]{1,0:T(8,128)(2,1)}, u32[]{:S(2)}, u32[]{:S(2)}) collective-permute-start(bf16[1152,1536]{1,0:T(8,128)(2,1)} %get-tuple-element.83), channel_id=1, source_target_pairs={{0,1},{1,0},{2,3},{3,2},{4,5},{5,4},{6,7},{7,6},{8,9},{9,8},{10,11... | collective-permute-start | bytes 10616840 | tf_op jit(solution)/shard_map/ppermute | solution.py:350
  296.9 19.7 %collective-permute-start.11 = (bf16[1152,1536]{1,0:T(8,128)(2,1)}, bf16[1152,1536]{1,0:T(8,128)(2,1)S(1)}, u32[]{:S(2)}, u32[]{:S(2)}) collective-permute-start(bf16[1152,1536]{1,0:T(8,128)(2,1)} %get-tuple-element.81), channel_id=1, source_target_pairs={{0,1},{1,0},{2,3},{3,2},{4,5},{5,4},{6,7},{7,6},{8,9},{9,8},{10,11... | collective-permute-start | bytes 10616840 | tf_op jit(solution)/shard_map/ppermute | solution.py:350
  297.2 35.9 %collective-permute-start.14 = (bf16[3072,640]{1,0:T(8,128)(2,1)}, bf16[3072,640]{1,0:T(8,128)(2,1)S(1)}, u32[]{:S(2)}, u32[]{:S(2)}) collective-permute-start(bf16[3072,640]{1,0:T(8,128)(2,1)} %get-tuple-element.86), channel_id=1, source_target_pairs={{0,1},{1,0},{2,3},{3,2},{4,5},{5,4},{6,7},{7,6},{8,9},{9,8},{10,11... | collective-permute-start | bytes 11796488 | tf_op jit(solution)/shard_map/ppermute | solution.py:350
  301.0 7.8 %slice-start = ((s8[4718592]{0:T(1024)(128)(4,1)}), s8[524288]{0:T(1024)(128)(4,1)S(1)}, s32[]{:S(2)}) async-start(s8[4718592]{0:T(1024)(128)(4,1)} %bitcast.323), calls=%async_computation.2 | async-start | bytes 1048576
  312.6 7.8 %copy-start.1 = (f32[1024,1152]{1,0:T(8,128)}, f32[1024,1152]{1,0:T(8,128)S(1)}, u32[]{:S(2)}) copy-start(f32[1024,1152]{1,0:T(8,128)S(1)} %subtract_add_fusion) | copy-start | bytes 14155780
  321.7 8.0 %copy-start.6 = (bf16[1024,1152]{1,0:T(8,128)(2,1)}, bf16[1024,1152]{1,0:T(8,128)(2,1)S(1)}, u32[]{:S(2)}) copy-start(bf16[1024,1152]{1,0:T(8,128)(2,1)S(1)} %convert_element_type.928) | copy-start | bytes 7077892
  324.0 11.9 %collective-permute-start.13 = (bf16[1024,640]{1,0:T(8,128)(2,1)S(1)}, bf16[1024,640]{1,0:T(8,128)(2,1)}, u32[]{:S(2)}, u32[]{:S(2)}) collective-permute-start(bf16[1024,640]{1,0:T(8,128)(2,1)S(1)} %convolution_convert_fusion), channel_id=1, source_target_pairs={{0,1},{1,0},{2,3},{3,2},{4,5},{5,4},{6,7},{7,6},{8,9},{9,8},{10,11... | collective-permute-start | bytes 3932168 | tf_op jit(solution)/shard_map/ppermute | solution.py:350
  324.3 48.2 %collective-permute-start.15 = (bf16[2,2,2,72,1536]{4,3,0,2,1:T(8,128)(2,1)}, bf16[2,2,2,72,1536]{4,3,0,2,1:T(8,128)(2,1)}, u32[]{:S(2)}, u32[]{:S(2)}) collective-permute-start(bf16[2,2,2,72,1536]{4,3,0,2,1:T(8,128)(2,1)} %fusion.17), channel_id=1, source_target_pairs={{0,2},{2,0},{4,6},{6,4},{8,10},{10,8},{12,14},{14,12},{16,18},{18,... | collective-permute-start | bytes 5308424 | tf_op jit(solution)/shard_map/ppermute | solution.py:366
  325.7 46.8 %collective-permute-start.16 = (bf16[2,2,2,72,1536]{4,3,1,2,0:T(8,128)(2,1)}, bf16[2,2,2,72,1536]{4,3,1,2,0:T(8,128)(2,1)}, u32[]{:S(2)}, u32[]{:S(2)}) collective-permute-start(bf16[2,2,2,72,1536]{4,3,1,2,0:T(8,128)(2,1)} %fusion.18), channel_id=1, source_target_pairs={{0,4},{2,6},{4,0},{6,2},{8,12},{10,14},{12,8},{14,10},{16,20},{18,... | collective-permute-start | bytes 5308424 | tf_op jit(solution)/shard_map/ppermute | solution.py:366
  335.9 44.8 %collective-permute-start.17 = (bf16[2,2,2,192,640]{4,3,1,2,0:T(8,128)(2,1)}, bf16[2,2,2,192,640]{4,3,1,2,0:T(8,128)(2,1)}, u32[]{:S(2)}, u32[]{:S(2)}) collective-permute-start(bf16[2,2,2,192,640]{4,3,1,2,0:T(8,128)(2,1)} %fusion.14), channel_id=1, source_target_pairs={{0,8},{2,10},{4,12},{6,14},{8,0},{10,2},{12,4},{14,6},{16,24},{18,... | collective-permute-start | bytes 5898248 | tf_op jit(solution)/shard_map/ppermute | solution.py:366
  372.5 8.8 %copy-start.51 = (bf16[1024,640]{1,0:T(8,128)(2,1)S(1)}, bf16[1024,640]{1,0:T(8,128)(2,1)}, u32[]{:S(2)}) copy-start(bf16[1024,640]{1,0:T(8,128)(2,1)} %get-tuple-element.73.o_mine) | copy-start | bytes 3932164
  382.6 11.7 %collective-permute-start.18 = (bf16[1152,640]{1,0:T(8,128)(2,1)S(1)}, bf16[1152,640]{1,0:T(8,128)(2,1)S(1)}, u32[]{:S(2)}, u32[]{:S(2)}) collective-permute-start(bf16[1152,640]{1,0:T(8,128)(2,1)S(1)} %maximum_select_fusion.2), channel_id=1, source_target_pairs={{0,1},{1,0},{2,3},{3,2},{4,5},{5,4},{6,7},{7,6},{8,9},{9,8},{10,11... | collective-permute-start | bytes 4423688 | tf_op jit(solution)/shard_map/ppermute | solution.py:350
  397.5 46.4 %collective-permute-start.21 = (bf16[2,2,192,640]{3,2,1,0:T(8,128)(2,1)}, bf16[2,2,192,640]{3,2,1,0:T(8,128)(2,1)}, u32[]{:S(2)}, u32[]{:S(2)}) collective-permute-start(bf16[2,2,192,640]{3,2,1,0:T(8,128)(2,1)} %copy.86), channel_id=1, source_target_pairs={{0,16},{2,18},{4,20},{6,22},{8,24},{10,26},{12,28},{14,30},{16,0},... | collective-permute-start | bytes 2949128 | tf_op jit(solution)/shard_map/ppermute | solution.py:366
  400.2 43.8 %copy-start.41 = (f32[1,4,2,128]{3,1,2,0:T(4,128)S(1)}, f32[1,4,2,128]{3,1,2,0:T(4,128)}, u32[]{:S(2)}) copy-start(f32[1,4,2,128]{3,1,2,0:T(4,128)} %copy-done.40) | copy-start | bytes 12292
  400.2 30.5 %collective-permute-start.19 = (bf16[2,2,72,1536]{3,2,1,0:T(8,128)(2,1)}, bf16[2,2,72,1536]{3,2,1,0:T(8,128)(2,1)}, u32[]{:S(2)}, u32[]{:S(2)}) collective-permute-start(bf16[2,2,72,1536]{3,2,1,0:T(8,128)(2,1)} %copy.85), channel_id=1, source_target_pairs={{0,4},{2,6},{4,0},{6,2},{8,12},{10,14},{12,8},{14,10},{16,20},{18,... | collective-permute-start | bytes 2654216 | tf_op jit(solution)/shard_map/ppermute | solution.py:366
  401.8 29.0 %collective-permute-start.20 = (bf16[2,2,72,1536]{3,2,1,0:T(8,128)(2,1)}, bf16[2,2,72,1536]{3,2,1,0:T(8,128)(2,1)}, u32[]{:S(2)}, u32[]{:S(2)}) collective-permute-start(bf16[2,2,72,1536]{3,2,1,0:T(8,128)(2,1)} %get-tuple-element.108), channel_id=1, source_target_pairs={{0,2},{2,0},{4,6},{6,4},{8,10},{10,8},{12,14},{14,12},{16,18},{18,... | collective-permute-start | bytes 2654216 | tf_op jit(solution)/shard_map/ppermute | solution.py:366
  444.0 23.1 %collective-permute-start.22 = (bf16[1024,1024]{1,0:T(8,128)(2,1)}, bf16[1024,1024]{1,0:T(8,128)(2,1)S(1)}, u32[]{:S(2)}, u32[]{:S(2)}) collective-permute-start(bf16[1024,1024]{1,0:T(8,128)(2,1)} %get-tuple-element.112), channel_id=1, source_target_pairs={{0,1},{1,0},{2,3},{3,2},{4,5},{5,4},{6,7},{7,6},{8,9},{9,8},{10,11... | collective-permute-start | bytes 6291464 | tf_op jit(solution)/shard_map/ppermute | solution.py:350
  444.0 19.2 %collective-permute-start.32 = (bf16[2,2,2,72,640]{4,3,0,2,1:T(8,128)(2,1)}, bf16[2,2,2,72,640]{4,3,0,2,1:T(8,128)(2,1)S(1)}, u32[]{:S(2)}, u32[]{:S(2)}) collective-permute-start(bf16[2,2,2,72,640]{4,3,0,2,1:T(8,128)(2,1)} %fusion.34), channel_id=1, source_target_pairs={{0,2},{2,0},{4,6},{6,4},{8,10},{10,8},{12,14},{14,12},{16,18},{18,... | collective-permute-start | bytes 2211848 | tf_op jit(solution)/shard_map/ppermute | solution.py:366
  448.4 37.3 %collective-permute-start.36 = (bf16[2,72,1536]{2,1,0:T(8,128)(2,1)S(1)}, bf16[2,72,1536]{2,1,0:T(8,128)(2,1)S(1)}, u32[]{:S(2)}, u32[]{:S(2)}) collective-permute-start(bf16[2,72,1536]{2,1,0:T(8,128)(2,1)S(1)} %get-tuple-element.186), channel_id=1, source_target_pairs={{0,16},{2,18},{4,20},{6,22},{8,24},{10,26},{12,28},{14,30},{16,0},... | collective-permute-start | bytes 1327112 | tf_op jit(solution)/shard_map/ppermute | solution.py:366
  449.9 15.0 %copy-start.10 = (bf16[1,2,2,192,640]{4,3,1,2,0:T(8,128)(2,1)S(1)}, bf16[1,2,2,192,640]{4,3,1,2,0:T(8,128)(2,1)}, u32[]{:S(2)}) copy-start(bf16[1,2,2,192,640]{4,3,1,2,0:T(8,128)(2,1)} %get-tuple-element.159) | copy-start | bytes 2949124
  449.9 35.9 %collective-permute-start.35 = (bf16[2,72,1536]{2,1,0:T(8,128)(2,1)S(1)}, bf16[2,72,1536]{2,1,0:T(8,128)(2,1)S(1)}, u32[]{:S(2)}, u32[]{:S(2)}) collective-permute-start(bf16[2,72,1536]{2,1,0:T(8,128)(2,1)S(1)} %get-tuple-element.188), channel_id=1, source_target_pairs={{0,8},{2,10},{4,12},{6,14},{8,0},{10,2},{12,4},{14,6},{16,24},{18,... | collective-permute-start | bytes 1327112 | tf_op jit(solution)/shard_map/ppermute | solution.py:366
  463.4 21.7 %collective-permute-start.34 = (bf16[2,2,72,640]{3,2,1,0:T(8,128)(2,1)S(1)}, bf16[2,2,72,640]{3,2,1,0:T(8,128)(2,1)S(1)}, u32[]{:S(2)}, u32[]{:S(2)}) collective-permute-start(bf16[2,2,72,640]{3,2,1,0:T(8,128)(2,1)S(1)} %copy.102), channel_id=1, source_target_pairs={{0,4},{2,6},{4,0},{6,2},{8,12},{10,14},{12,8},{14,10},{16,20},{18,... | collective-permute-start | bytes 1105928 | tf_op jit(solution)/shard_map/ppermute | solution.py:366
  466.3 19.4 %collective-permute-start.33 = (bf16[2,192,640]{2,1,0:T(8,128)(2,1)S(1)}, bf16[2,192,640]{2,1,0:T(8,128)(2,1)S(1)}, u32[]{:S(2)}, u32[]{:S(2)}) collective-permute-start(bf16[2,192,640]{2,1,0:T(8,128)(2,1)S(1)} %get-tuple-element.184), channel_id=1, source_target_pairs={{0,2},{2,0},{4,6},{6,4},{8,10},{10,8},{12,14},{14,12},{16,18},{18,... | collective-permute-start | bytes 1474568 | tf_op jit(solution)/shard_map/ppermute | solution.py:366
  473.7 6.5 %slice-start.2 = ((s8[4718592]{0:T(1024)(128)(4,1)}), s8[4194304]{0:T(1024)(128)(4,1)S(1)}, s32[]{:S(2)}) async-start(s8[4718592]{0:T(1024)(128)(4,1)} %bitcast.325), calls=%async_computation.4 | async-start | bytes 8388608
  476.7 6.2 %collective-permute-start.23 = (bf16[1152,1024]{1,0:T(8,128)(2,1)S(1)}, bf16[1152,1024]{1,0:T(8,128)(2,1)S(1)}, u32[]{:S(2)}, u32[]{:S(2)}) collective-permute-start(bf16[1152,1024]{1,0:T(8,128)(2,1)S(1)} %add_convert_fusion), channel_id=1, source_target_pairs={{0,1},{1,0},{2,3},{3,2},{4,5},{5,4},{6,7},{7,6},{8,9},{9,8},{10,11... | collective-permute-start | bytes 7077896 | tf_op jit(solution)/shard_map/ppermute | solution.py:350
  483.4 15.8 %collective-permute-start.24 = (bf16[2,2,2,72,512]{4,3,0,2,1:T(8,128)(2,1)S(1)}, bf16[2,2,2,72,512]{4,3,0,2,1:T(8,128)(2,1)S(1)}, u32[]{:S(2)}, u32[]{:S(2)}) collective-permute-start(bf16[2,2,2,72,512]{4,3,0,2,1:T(8,128)(2,1)S(1)} %fusion.37), channel_id=1, source_target_pairs={{0,2},{2,0},{4,6},{6,4},{8,10},{10,8},{12,14},{14,12},{16,18},{18,... | collective-permute-start | bytes 1769480 | tf_op jit(solution)/shard_map/ppermute | solution.py:366
  485.1 16.3 %collective-permute-start.28 = (bf16[2,2,2,72,512]{4,3,1,2,0:T(8,128)(2,1)S(1)}, bf16[2,2,2,72,512]{4,3,1,2,0:T(8,128)(2,1)S(1)}, u32[]{:S(2)}, u32[]{:S(2)}) collective-permute-start(bf16[2,2,2,72,512]{4,3,1,2,0:T(8,128)(2,1)S(1)} %fusion.38), channel_id=1, source_target_pairs={{0,4},{2,6},{4,0},{6,2},{8,12},{10,14},{12,8},{14,10},{16,20},{18,... | collective-permute-start | bytes 1769480 | tf_op jit(solution)/shard_map/ppermute | solution.py:366
  485.9 19.5 %collective-permute-start.40 = (bf16[72,1536]{1,0:T(8,128)(2,1)S(1)}, bf16[72,1536]{1,0:T(8,128)(2,1)S(1)}, u32[]{:S(2)}, u32[]{:S(2)}) collective-permute-start(bf16[72,1536]{1,0:T(8,128)(2,1)S(1)} %fusion.70), channel_id=1, source_target_pairs={{0,8},{2,10},{4,12},{6,14},{8,0},{10,2},{12,4},{14,6},{16,24},{18,... | collective-permute-start | bytes 663560 | tf_op jit(solution)/shard_map/ppermute | solution.py:366
  486.0 19.3 %collective-permute-start.39 = (bf16[72,1536]{1,0:T(8,128)(2,1)S(1)}, bf16[72,1536]{1,0:T(8,128)(2,1)S(1)}, u32[]{:S(2)}, u32[]{:S(2)}) collective-permute-start(bf16[72,1536]{1,0:T(8,128)(2,1)S(1)} %fusion.69), channel_id=1, source_target_pairs={{0,16},{2,18},{4,20},{6,22},{8,24},{10,26},{12,28},{14,30},{16,0},... | collective-permute-start | bytes 663560 | tf_op jit(solution)/shard_map/ppermute | solution.py:366
  488.5 17.4 %collective-permute-start.37 = (bf16[192,640]{1,0:T(8,128)(2,1)S(1)}, bf16[192,640]{1,0:T(8,128)(2,1)S(1)}, u32[]{:S(2)}, u32[]{:S(2)}) collective-permute-start(bf16[192,640]{1,0:T(8,128)(2,1)S(1)} %get-tuple-element.212), channel_id=1, source_target_pairs={{0,4},{2,6},{4,0},{6,2},{8,12},{10,14},{12,8},{14,10},{16,20},{18,... | collective-permute-start | bytes 737288 | tf_op jit(solution)/shard_map/ppermute | solution.py:366
  499.2 6.2 %collective-permute-start.38 = (bf16[2,72,640]{2,1,0:T(8,128)(2,1)S(1)}, bf16[2,72,640]{2,1,0:T(8,128)(2,1)S(1)}, u32[]{:S(2)}, u32[]{:S(2)}) collective-permute-start(bf16[2,72,640]{2,1,0:T(8,128)(2,1)S(1)} %get-tuple-element.214), channel_id=1, source_target_pairs={{0,8},{2,10},{4,12},{6,14},{8,0},{10,2},{12,4},{14,6},{16,24},{18,... | collective-permute-start | bytes 552968 | tf_op jit(solution)/shard_map/ppermute | solution.py:366
  501.5 14.9 %collective-permute-start.29 = (bf16[2,2,72,512]{3,2,1,0:T(8,128)(2,1)S(1)}, bf16[2,2,72,512]{3,2,1,0:T(8,128)(2,1)S(1)}, u32[]{:S(2)}, u32[]{:S(2)}) collective-permute-start(bf16[2,2,72,512]{3,2,1,0:T(8,128)(2,1)S(1)} %get-tuple-element.206), channel_id=1, source_target_pairs={{0,2},{2,0},{4,6},{6,4},{8,10},{10,8},{12,14},{14,12},{16,18},{18,... | collective-permute-start | bytes 884744 | tf_op jit(solution)/shard_map/ppermute | solution.py:366
  505.9 11.3 %collective-permute-start.41 = (bf16[72,640]{1,0:T(8,128)(2,1)S(1)}, bf16[72,640]{1,0:T(8,128)(2,1)S(1)}, u32[]{:S(2)}, u32[]{:S(2)}) collective-permute-start(bf16[72,640]{1,0:T(8,128)(2,1)S(1)} %get-tuple-element.219), channel_id=1, source_target_pairs={{0,16},{2,18},{4,20},{6,22},{8,24},{10,26},{12,28},{14,30},{16,0},... | collective-permute-start | bytes 276488 | tf_op jit(solution)/shard_map/ppermute | solution.py:366
  506.1 8.3 %collective-permute-start.25 = (bf16[2,2,72,512]{3,2,1,0:T(8,128)(2,1)S(1)}, bf16[2,2,72,512]{3,2,1,0:T(8,128)(2,1)S(1)}, u32[]{:S(2)}, u32[]{:S(2)}) collective-permute-start(bf16[2,2,72,512]{3,2,1,0:T(8,128)(2,1)S(1)} %copy.92), channel_id=1, source_target_pairs={{0,4},{2,6},{4,0},{6,2},{8,12},{10,14},{12,8},{14,10},{16,20},{18,... | collective-permute-start | bytes 884744 | tf_op jit(solution)/shard_map/ppermute | solution.py:366
  514.4 10.0 %collective-permute-start.26 = (bf16[2,72,512]{2,1,0:T(8,128)(2,1)S(1)}, bf16[2,72,512]{2,1,0:T(8,128)(2,1)S(1)}, u32[]{:S(2)}, u32[]{:S(2)}) collective-permute-start(bf16[2,72,512]{2,1,0:T(8,128)(2,1)S(1)} %get-tuple-element.216), channel_id=1, source_target_pairs={{0,8},{2,10},{4,12},{6,14},{8,0},{10,2},{12,4},{14,6},{16,24},{18,... | collective-permute-start | bytes 442376 | tf_op jit(solution)/shard_map/ppermute | solution.py:366
  516.5 7.8 %collective-permute-start.30 = (bf16[2,72,512]{2,1,0:T(8,128)(2,1)S(1)}, bf16[2,72,512]{2,1,0:T(8,128)(2,1)S(1)}, u32[]{:S(2)}, u32[]{:S(2)}) collective-permute-start(bf16[2,72,512]{2,1,0:T(8,128)(2,1)S(1)} %get-tuple-element.218), channel_id=1, source_target_pairs={{0,16},{2,18},{4,20},{6,22},{8,24},{10,26},{12,28},{14,30},{16,0},... | collective-permute-start | bytes 442376 | tf_op jit(solution)/shard_map/ppermute | solution.py:366
  524.4 4.4 collective-permute-start.31
  524.5 5.7 %collective-permute-start.27 = (bf16[72,512]{1,0:T(8,128)(2,1)S(1)}, bf16[72,512]{1,0:T(8,128)(2,1)S(1)}, u32[]{:S(2)}, u32[]{:S(2)}) collective-permute-start(bf16[72,512]{1,0:T(8,128)(2,1)S(1)} %fusion.85), channel_id=1, source_target_pairs={{0,16},{2,18},{4,20},{6,22},{8,24},{10,26},{12,28},{14,30},{16,0},... | collective-permute-start | bytes 221192 | tf_op jit(solution)/shard_map/ppermute | solution.py:366
  (38 other events, 97.9 us)
Sparse Core Ops, SparseCore 0:
  11.5 84.8 all-gather.2
  99.8 104.9 all-gather.4
